TPU v7x, 32 devices: a whole 2x2x4 slice. The times are simulated.
32 devices in a mesh: band: 2 (over y), slab: 16 (over z, x, core).
Axes of the slice: x: 2, y: 2, z: 4, core: 2. Of those that a mesh axis runs over, the one named last changes fastest.
Arguments:
- own_orbitals: float32 [4, 128, 128, 128], P('band', 'slab'), may hold values from -6 to 6
- partners: float32 [8, 128, 128, 128], P('band', 'slab'), may hold values from -6 to 6
Outputs:
- own_field: float32 [4, 128, 128, 128], P('band', 'slab')
- partner_field: float32 [8, 128, 128, 128], P('band', 'slab')
All inputs are finite; a program needn't handle non-finite values.
Results may differ from a plain program's by a relative error of at most 0.0001.
Values sent between devices are 32-bit elements; how exact they have to be, the bound alone decides.
No kernel may reach another device: no remote copies, remote signals or barrier semaphores. Data moves between devices by JAX's collectives and lax.ppermute only.
A program may use at most 128 MiB of HBM per device.

v0:
```python
import math

import jax
import jax.numpy as jnp
from jax import lax
from jax.sharding import PartitionSpec as P

STEPS = 2


coulomb_scale = 46.9 * 46.9 / math.pi
highest = lax.Precision.HIGHEST


def passed_along(block, axis, distance):
    devices = range(lax.axis_size(axis))
    route = [((i - distance) % len(devices), i) for i in devices]
    return lax.ppermute(block, axis, route)


def dft_tables(length):
    positions = lax.iota(jnp.int32, length)
    wrapped = positions[:, None] * positions[None, :] % length
    angles = wrapped.astype(jnp.float32) * (2.0 * math.pi / length)
    return (jnp.cos(angles), jnp.sin(angles))


def apply_table(pattern, field, table):
    return jnp.einsum(pattern, field, table, precision=highest)


def forward(pattern, real_part, imag_part, cosine, sine_table):
    new_real = apply_table(pattern, real_part, cosine) + apply_table(pattern, imag_part, sine_table)
    new_imag = apply_table(pattern, imag_part, cosine) - apply_table(pattern, real_part, sine_table)
    return (new_real, new_imag)


def inverse(pattern, real_part, imag_part, cosine, sine_table):
    new_real = apply_table(pattern, real_part, cosine) - apply_table(pattern, imag_part, sine_table)
    new_imag = apply_table(pattern, imag_part, cosine) + apply_table(pattern, real_part, sine_table)
    return (new_real, new_imag)


def frequency(positions, length):
    return jnp.where(positions < length // 2, positions, positions - length).astype(jnp.float32)


def shards(own_orbitals, partners):
    length = own_orbitals.shape[3]
    cosine, sine_table = dft_tables(length)
    slab_count = lax.axis_size("slab")
    rows_y = length // slab_count
    z_waves = frequency(lax.iota(jnp.int32, length), length)
    y_waves = frequency(lax.axis_index("slab") * rows_y + lax.iota(jnp.int32, rows_y), length)
    square = (
        z_waves[:, None, None] * z_waves[:, None, None]
        + y_waves[None, :, None] * y_waves[None, :, None]
        + z_waves[None, None, :] * z_waves[None, None, :]
    )
    kernel = jnp.where(square > 0, coulomb_scale / jnp.maximum(square, 1.0), 0.0) / float(
        length * length * length
    )
    x_form = "pzyx,xk->pzyk"
    y_form = "pzyx,yk->pzkx"
    z_form = "pzyx,zk->pkyx"
    own_acc = jnp.zeros(own_orbitals.shape, jnp.float32)
    partner_set = passed_along(partners, "band", 1)
    partner_out = jnp.zeros(partners.shape, jnp.float32)
    for step_no in range(1, STEPS + 1):
        if step_no > 1:
            partner_set = passed_along(partner_set, "band", 1)
        own_count = own_orbitals.shape[0]
        part_count = partner_set.shape[0]
        pair_count = own_count * part_count
        density = (own_orbitals[:, None] * partner_set[None]).reshape(
            (pair_count,) + own_orbitals.shape[1:]
        )
        potentials_real_part = apply_table(x_form, density, cosine)
        potentials_imag_part = -apply_table(x_form, density, sine_table)
        solve_real_part = potentials_real_part
        solve_imag_part = potentials_imag_part
        solve_real_part, solve_imag_part = forward(
            y_form, solve_real_part, solve_imag_part, cosine, sine_table
        )
        real_part, imag_part = forward(
            z_form,
            lax.all_to_all(solve_real_part, "slab", split_axis=2, concat_axis=1, tiled=True),
            lax.all_to_all(solve_imag_part, "slab", split_axis=2, concat_axis=1, tiled=True),
            cosine,
            sine_table,
        )
        real_part = real_part * kernel
        imag_part = imag_part * kernel
        real_part, imag_part = inverse(z_form, real_part, imag_part, cosine, sine_table)
        solve_real_part = lax.all_to_all(real_part, "slab", split_axis=1, concat_axis=2, tiled=True)
        solve_imag_part = lax.all_to_all(imag_part, "slab", split_axis=1, concat_axis=2, tiled=True)
        potentials_real_part, potentials_imag_part = inverse(
            y_form, solve_real_part, solve_imag_part, cosine, sine_table
        )
        potential = apply_table(x_form, potentials_real_part, cosine) - apply_table(
            x_form, potentials_imag_part, sine_table
        )
        potential = potential.reshape((own_count, part_count) + own_orbitals.shape[1:])
        own_add = jnp.sum(potential * partner_set[None], axis=1)
        part_add = jnp.sum(potential * own_orbitals[:, None], axis=0)
        own_add, part_add = (own_add, part_add)
        own_acc = own_acc + own_add
        partner_out = partner_out + passed_along(part_add, "band", -step_no)
    return (own_acc, partner_out)


def solution(mesh):
    in_specs = (P("band", "slab", None, None), P("band", "slab", None, None))
    out_specs = (P("band", "slab", None, None), P("band", "slab", None, None))
    return jax.shard_map(shards, mesh=mesh, in_specs=in_specs, out_specs=out_specs, check_vma=False)
```

profile of v0, /device:TPU:10, one launch (start us, length us, event | category | flops | bytes accessed | tf_op | source)
XLA Modules:
  0.0 983.0 jit_solution(5613835076587833565)
XLA Ops:
  2.2 46.1 %collective-permute-done = f32[4,8,128,128]{3,2,1,0:T(8,128)S(1)} collective-permute-done((f32[4,8,128,128]{3,2,1,0:T(8,128)}, f32[4,8,128,128]{3,2,1,0:T(8,128)S(1)}, u32[]{:S(2)}, u32[]{:S(2)}) %collective-permute-start) | collective-permute-done | bytes 2097184 | tf_op jit(solution)/shard_map/ppermute | solution.py:18
  49.8 45.0 %collective-permute-done.1 = f32[4,8,128,128]{3,2,1,0:T(8,128)S(1)} collective-permute-done((f32[4,8,128,128]{3,2,1,0:T(8,128)S(1)}, f32[4,8,128,128]{3,2,1,0:T(8,128)S(1)}, u32[]{:S(2)}, u32[]{:S(2)}) %collective-permute-start.1) | collective-permute-done | bytes 2097184 | tf_op jit(solution)/shard_map/ppermute | solution.py:18
  94.8 4.7 broadcast_multiply_fusion
  115.2 4.4 copy.136
  119.7 6.8 all-to-all-start.4
  126.5 6.1 fusion.125
  140.9 77.8 %all-to-all-done.4 = f32[8,8,128,128]{3,1,0,2:T(8,128)} async-done(((f32[8,8,128,128]{3,1,0,2:T(8,128)}), f32[8,8,128,128]{3,1,0,2:T(8,128)}, u32[]{:S(2)}, u32[]{:S(2)}) %all-to-all-start.4) | async-done | bytes 4194336 | tf_op jit(solution)/shard_map/all_to_all | solution.py:87
  218.6 5.0 all-to-all-start.5
  223.7 6.0 fusion.161
  241.4 4.7 copy.115
  246.1 69.9 %all-to-all-done.5 = f32[8,8,128,128]{3,1,0,2:T(8,128)} async-done(((f32[8,8,128,128]{3,1,0,2:T(8,128)}), f32[8,8,128,128]{3,1,0,2:T(8,128)}, u32[]{:S(2)}, u32[]{:S(2)}) %all-to-all-start.5) | async-done | bytes 4194336 | tf_op jit(solution)/shard_map/all_to_all | solution.py:88
  316.0 5.1 all-to-all-start.1
  321.1 6.1 fusion.163
  331.1 4.4 copy.110
  335.5 77.9 %all-to-all-done.1 = f32[8,8,128,128]{3,1,0,2:T(8,128)} async-done(((f32[8,8,128,128]{3,1,0,2:T(8,128)}), f32[8,8,128,128]{3,1,0,2:T(8,128)}, u32[]{:S(2)}, u32[]{:S(2)}) %all-to-all-start.1) | async-done | bytes 4194336 | tf_op jit(solution)/shard_map/all_to_all | solution.py:88
  413.4 5.6 all-to-all-start
  419.3 5.9 fusion.16
  425.3 6.0 fusion.18
  431.2 6.2 subtract_multiply_fusion
  443.5 6.3 add_multiply_fusion
  453.9 4.4 copy.148
  458.3 52.8 %all-to-all-done = f32[8,8,128,128]{3,1,0,2:T(8,128)} async-done(((f32[8,8,128,128]{3,1,0,2:T(8,128)}), f32[8,8,128,128]{3,1,0,2:T(8,128)}, u32[]{:S(2)}, u32[]{:S(2)}) %all-to-all-start) | async-done | bytes 4194336 | tf_op jit(solution)/shard_map/all_to_all | solution.py:87
  511.2 5.4 all-to-all-start.6
  516.6 6.1 fusion.12
  526.7 4.4 copy.154
  531.1 77.6 %all-to-all-done.6 = f32[8,128,8,128]{3,2,0,1:T(8,128)} async-done(((f32[8,128,8,128]{3,2,0,1:T(8,128)}), f32[8,128,8,128]{3,2,0,1:T(8,128)}, u32[]{:S(2)}, u32[]{:S(2)}) %all-to-all-start.6) | async-done | bytes 4194336 | tf_op jit(solution)/shard_map/all_to_all | solution.py:95
  608.7 5.6 all-to-all-start.7
  614.3 6.0 fusion.46
  620.3 5.9 fusion.44
  626.3 6.2 subtract_multiply_fusion.1
  638.4 6.3 add_multiply_fusion.1
  648.8 4.5 copy.122
  653.3 53.2 %all-to-all-done.7 = f32[8,128,8,128]{3,2,0,1:T(8,128)} async-done(((f32[8,128,8,128]{3,2,0,1:T(8,128)}), f32[8,128,8,128]{3,2,0,1:T(8,128)}, u32[]{:S(2)}, u32[]{:S(2)}) %all-to-all-start.7) | async-done | bytes 4194336 | tf_op jit(solution)/shard_map/all_to_all | solution.py:96
  706.5 5.4 all-to-all-start.2
  711.9 6.1 fusion.40
  726.4 77.6 %all-to-all-done.2 = f32[8,128,8,128]{3,2,0,1:T(8,128)} async-done(((f32[8,128,8,128]{3,2,0,1:T(8,128)}), f32[8,128,8,128]{3,2,0,1:T(8,128)}, u32[]{:S(2)}, u32[]{:S(2)}) %all-to-all-start.2) | async-done | bytes 4194336 | tf_op jit(solution)/shard_map/all_to_all | solution.py:95
  804.1 5.4 all-to-all-start.3
  809.5 8.2 fusion.8
  817.7 8.1 fusion.10
  825.8 8.3 fusion.4
  834.2 8.2 fusion.6
  842.4 8.3 fusion.36
  850.7 8.4 fusion.38
  859.1 42.3 %all-to-all-done.3 = f32[8,128,8,128]{3,2,0,1:T(8,128)} async-done(((f32[8,128,8,128]{3,2,0,1:T(8,128)}), f32[8,128,8,128]{3,2,0,1:T(8,128)}, u32[]{:S(2)}, u32[]{:S(2)}) %all-to-all-start.3) | async-done | bytes 4194336 | tf_op jit(solution)/shard_map/all_to_all | solution.py:96
  901.4 6.0 fusion.32
  907.4 6.1 fusion.34
  921.3 6.0 multiply_reduce_fusion.2
  935.9 45.1 %collective-permute-done.2 = f32[4,8,128,128]{3,2,1,0:T(8,128)S(1)} collective-permute-done((f32[4,8,128,128]{3,2,1,0:T(8,128)S(1)}, f32[4,8,128,128]{3,2,1,0:T(8,128)S(1)}, u32[]{:S(2)}, u32[]{:S(2)}) %collective-permute-start.2) | collective-permute-done | bytes 2097184 | tf_op jit(solution)/shard_map/ppermute | solution.py:18
  (74 shorter events, 93.6 us)
Async XLA Ops:
  0.6 47.6 %collective-permute-start = (f32[4,8,128,128]{3,2,1,0:T(8,128)}, f32[4,8,128,128]{3,2,1,0:T(8,128)S(1)}, u32[]{:S(2)}, u32[]{:S(2)}) collective-permute-start(f32[4,8,128,128]{3,2,1,0:T(8,128)} %param.3), channel_id=1, source_target_pairs={{16,0},{0,16},{17,1},{1,17},{18,2},{2,18},{19,3},{3,19},{20,4},{4,... | collective-permute-start | bytes 6291464 | tf_op jit(solution)/shard_map/ppermute | solution.py:18
  48.3 46.5 %collective-permute-start.1 = (f32[4,8,128,128]{3,2,1,0:T(8,128)S(1)}, f32[4,8,128,128]{3,2,1,0:T(8,128)S(1)}, u32[]{:S(2)}, u32[]{:S(2)}) collective-permute-start(f32[4,8,128,128]{3,2,1,0:T(8,128)S(1)} %collective-permute-done), channel_id=1, source_target_pairs={{16,0},{0,16},{17,1},{1,17},{18,2},{2,18},{19,3},{3,19},{20,4},{4,... | collective-permute-start | bytes 6291464 | tf_op jit(solution)/shard_map/ppermute | solution.py:18
  94.8 4.7 copy-start.19
  103.3 3.7 copy-start.12
  107.0 8.3 copy-start.6
  119.7 99.0 %all-to-all-start.4 = ((f32[8,8,128,128]{3,1,0,2:T(8,128)}), f32[8,8,128,128]{3,1,0,2:T(8,128)}, u32[]{:S(2)}, u32[]{:S(2)}) async-start(f32[8,8,128,128]{3,1,0,2:T(8,128)} %copy.136), calls=%async_computation.4 | async-start | bytes 8388608 | tf_op jit(solution)/shard_map/all_to_all | solution.py:87
  126.5 6.1 copy-start.7
  218.6 97.4 %all-to-all-start.5 = ((f32[8,8,128,128]{3,1,0,2:T(8,128)}), f32[8,8,128,128]{3,1,0,2:T(8,128)}, u32[]{:S(2)}, u32[]{:S(2)}) async-start(f32[8,8,128,128]{3,1,0,2:T(8,128)} %copy.141), calls=%async_computation.5 | async-start | bytes 8388608 | tf_op jit(solution)/shard_map/all_to_all | solution.py:88
  223.7 6.0 copy-start.10
  229.7 3.7 copy-start.11
  233.4 4.1 copy-start.4
  316.0 97.4 %all-to-all-start.1 = ((f32[8,8,128,128]{3,1,0,2:T(8,128)}), f32[8,8,128,128]{3,1,0,2:T(8,128)}, u32[]{:S(2)}, u32[]{:S(2)}) async-start(f32[8,8,128,128]{3,1,0,2:T(8,128)} %copy.115), calls=%async_computation.1 | async-start | bytes 8388608 | tf_op jit(solution)/shard_map/all_to_all | solution.py:88
  321.1 6.1 copy-start.5
  413.4 97.8 %all-to-all-start = ((f32[8,8,128,128]{3,1,0,2:T(8,128)}), f32[8,8,128,128]{3,1,0,2:T(8,128)}, u32[]{:S(2)}, u32[]{:S(2)}) async-start(f32[8,8,128,128]{3,1,0,2:T(8,128)} %copy.110), calls=%async_computation | async-start | bytes 8388608 | tf_op jit(solution)/shard_map/all_to_all | solution.py:87
  437.4 2.0 copy-start.9
  449.8 4.1 copy-start.2
  511.2 97.6 %all-to-all-start.6 = ((f32[8,128,8,128]{3,2,0,1:T(8,128)}), f32[8,128,8,128]{3,2,0,1:T(8,128)}, u32[]{:S(2)}, u32[]{:S(2)}) async-start(f32[8,128,8,128]{3,2,0,1:T(8,128)} %copy.148), calls=%async_computation.6 | async-start | bytes 8388608 | tf_op jit(solution)/shard_map/all_to_all | solution.py:95
  516.6 6.1 copy-start.3
  608.7 97.8 %all-to-all-start.7 = ((f32[8,128,8,128]{3,2,0,1:T(8,128)}), f32[8,128,8,128]{3,2,0,1:T(8,128)}, u32[]{:S(2)}, u32[]{:S(2)}) async-start(f32[8,128,8,128]{3,2,0,1:T(8,128)} %copy.154), calls=%async_computation.7 | async-start | bytes 8388608 | tf_op jit(solution)/shard_map/all_to_all | solution.py:96
  632.4 1.9 copy-start.8
  644.7 4.1 copy-start
  706.5 97.6 %all-to-all-start.2 = ((f32[8,128,8,128]{3,2,0,1:T(8,128)}), f32[8,128,8,128]{3,2,0,1:T(8,128)}, u32[]{:S(2)}, u32[]{:S(2)}) async-start(f32[8,128,8,128]{3,2,0,1:T(8,128)} %copy.122), calls=%async_computation.2 | async-start | bytes 8388608 | tf_op jit(solution)/shard_map/all_to_all | solution.py:95
  711.9 6.1 copy-start.1
  804.1 97.4 %all-to-all-start.3 = ((f32[8,128,8,128]{3,2,0,1:T(8,128)}), f32[8,128,8,128]{3,2,0,1:T(8,128)}, u32[]{:S(2)}, u32[]{:S(2)}) async-start(f32[8,128,8,128]{3,2,0,1:T(8,128)} %copy.128), calls=%async_computation.3 | async-start | bytes 8388608 | tf_op jit(solution)/shard_map/all_to_all | solution.py:96
  907.4 6.2 copy-start.16
  907.4 6.2 copy-start.17
  913.6 3.9 copy-start.18
  917.4 3.9 copy-start.14
  917.4 3.9 copy-start.15
  921.3 6.0 copy-start.13
  927.3 4.4 copy-start.20
  933.1 47.9 %collective-permute-start.2 = (f32[4,8,128,128]{3,2,1,0:T(8,128)S(1)}, f32[4,8,128,128]{3,2,1,0:T(8,128)S(1)}, u32[]{:S(2)}, u32[]{:S(2)}) collective-permute-start(f32[4,8,128,128]{3,2,1,0:T(8,128)S(1)} %get-tuple-element.3), channel_id=1, source_target_pairs={{16,0},{0,16},{17,1},{1,17},{18,2},{2,18},{19,3},{3,19},{20,4},{4,... | collective-permute-start | bytes 6291464 | tf_op jit(solution)/shard_map/ppermute | solution.py:18
  934.7 46.3 %collective-permute-start.3 = (f32[4,8,128,128]{3,2,1,0:T(8,128)S(1)}, f32[4,8,128,128]{3,2,1,0:T(8,128)S(1)}, u32[]{:S(2)}, u32[]{:S(2)}) collective-permute-start(f32[4,8,128,128]{3,2,1,0:T(8,128)S(1)} %get-tuple-element.2), channel_id=1, source_target_pairs={{0,0},{16,16},{1,1},{17,17},{2,2},{18,18},{3,3},{19,19},{4,4},{20,... | collective-permute-start | bytes 6291464 | tf_op jit(solution)/shard_map/ppermute | solution.py:18
where the time goes:
time: 992 us; the launch traced here: 983 us
  waiting for transfers between devices  665 us (67%)
  matrix products  218 us (22%)
  starting transfers between devices  49.1 us (5%)
  local copies, waits for them, and re-layouts  39.5 us (4%)
    dot_general x40, matrix products, apply_table(): return jnp.einsum(pattern, field, table, precision=highest)  218 us
    all_to_all x2, waiting for transfers between devices, shards(): lax.all_to_all(real_part, 'slab', split_axis=1, concat_axis=2, tiled=True)  155 us
    all_to_all x2, waiting for transfers between devices, shards(): lax.all_to_all(solve_imag_part, 'slab', split_axis=2, concat_axis=1, tile...  148 us
    ppermute x4, waiting for transfers between devices, passed_along(): return lax.ppermute(block, axis, route)  136 us
    all_to_all x2, waiting for transfers between devices, shards(): lax.all_to_all(solve_real_part, 'slab', split_axis=2, concat_axis=1, tile...  131 us
    all_to_all x2, waiting for transfers between devices, shards(): lax.all_to_all(imag_part, 'slab', split_axis=1, concat_axis=2, tiled=True)  95.5 us
  transfers between devices with their start and end apart: 12, of which 11 were waited for; matrix products, arithmetic and copies ran while one was open for 21% of the time, Pallas kernels for 0%

commit v1 on v0

v1 whole, which is shorter than its diff:
```python
import functools
import math

import jax
import jax.numpy as jnp
import numpy as np
from jax import lax
from jax.sharding import PartitionSpec as P

STEPS = 2


coulomb_scale = 46.9 * 46.9 / math.pi
precision = lax.Precision.HIGH


def cas_table(length):
    half = length // 2
    angles = np.arange(half) * (2.0 * math.pi / length)
    first = (np.cos(angles) + np.sin(angles)).astype(np.float32)
    wave = np.concatenate([first, -first])
    positions = np.arange(length)
    return wave[(positions[:, None] * positions[None, :]) % length]


def apply_table(pattern, field, table):
    return jnp.einsum(pattern, field, table, precision=precision)


def frequency(positions, length):
    return jnp.where(positions < length // 2, positions, positions - length).astype(jnp.float32)


def coulomb(z_waves, y_waves, x_waves, cells):
    square = (
        z_waves[:, None, None] * z_waves[:, None, None]
        + y_waves[None, :, None] * y_waves[None, :, None]
        + x_waves[None, None, :] * x_waves[None, None, :]
    )
    return jnp.where(square > 0, (coulomb_scale / float(cells)) / jnp.maximum(square, 1.0), 0.0)


def band_shift(block, groups, distance):
    if distance % groups == 0:
        return block
    route = [((b + distance) % groups, b) for b in range(groups)]
    return lax.ppermute(block, "band", route)


def pencils(own, partners, groups, slabs):
    length = own.shape[3]
    own_count, part_count = own.shape[0], partners.shape[0]
    table = jnp.asarray(cas_table(length))
    rows_y = length // slabs
    waves = frequency(lax.iota(jnp.int32, length), length)
    y_waves = frequency(
        lax.axis_index("slab") * rows_y + lax.iota(jnp.int32, rows_y), length
    )
    kernel = coulomb(waves, y_waves, waves, length**3)
    own_acc = jnp.zeros(own.shape, jnp.float32)
    part_acc = jnp.zeros(partners.shape, jnp.float32)
    for step_no in sorted(range(1, STEPS + 1), key=lambda s: s % groups != 0):
        bands = band_shift(own, groups, step_no)
        field = (bands[:, None] * partners[None]).reshape((-1,) + own.shape[1:])
        field = apply_table("pzyx,xk->pzyk", field, table)
        field = apply_table("pzyx,yk->pzkx", field, table)
        field = lax.all_to_all(field, "slab", split_axis=2, concat_axis=1, tiled=True)
        field = apply_table("pzyx,zk->pkyx", field, table) * kernel
        field = apply_table("pzyx,zk->pkyx", field, table)
        field = lax.all_to_all(field, "slab", split_axis=1, concat_axis=2, tiled=True)
        field = apply_table("pzyx,yk->pzkx", field, table)
        field = apply_table("pzyx,xk->pzyk", field, table)
        potential = field.reshape((own_count, part_count) + own.shape[1:])
        part_acc = part_acc + jnp.sum(potential * bands[:, None], axis=0)
        own_add = jnp.sum(potential * partners[None], axis=1)
        own_acc = own_acc + band_shift(own_add, groups, -step_no)
    return own_acc, part_acc


def solution(mesh):
    groups, slabs = mesh.shape["band"], mesh.shape["slab"]
    spec = P("band", "slab", None, None)
    return jax.shard_map(
        functools.partial(pencils, groups=groups, slabs=slabs),
        mesh=mesh, in_specs=(spec, spec), out_specs=(spec, spec), check_vma=False,
    )
```

time: 992 us -> 469 us (0.47)
  waiting for transfers between devices: 665 us -> 356 us
  matrix products: 218 us -> 46.6 us
  starting transfers between devices: 49.1 us -> 24.6 us
    all_to_all x8 -> x4, waiting for transfers between devices: 529 us -> 312 us  [the longest x2 157 us: pencils(): lax.all_to_all(field, 'slab', split_axis=1, concat_axis=2, tiled=True)]
    dot_general x40 -> x12, matrix products: 218 us -> 46.6 us  [apply_table(): return jnp.einsum(pattern, field, table, precision=precision)]
    ppermute x4 -> x2, waiting for transfers between devices: 136 us -> 44.4 us  [band_shift(): return lax.ppermute(block, 'band', route)]
    all_to_all x8 -> x4, starting transfers between devices: 44.3 us -> 21.4 us  [the longest x2 11.3 us: pencils(): lax.all_to_all(field, 'slab', split_axis=2, concat_axis=1, tiled=True)]
    transpose x0 -> x4, local copies, waits for them, and re-layouts: none -> 21.6 us  [apply_table(): return jnp.einsum(pattern, field, table, precision=precision)]
    sub x4 -> x0, local copies, waits for them, and re-layouts: 17.9 us -> none  [the longest x2 9.04 us: forward(): apply_table(pattern, imag_part, cosine)]
    add x4 -> x0, local copies, waits for them, and re-layouts: 17.6 us -> none  [the longest x2 8.81 us: forward(): apply_table(pattern, real_part, cosine)]
  transfers between devices with their start and end apart: 12 -> 6, of which waited for: 11 -> 6; matrix products, arithmetic and copies ran while one was open for 21% -> 13% of each run, Pallas kernels for 0% -> 0%
where the time goes in v1:
time: 469 us; the launch traced here: 468 us
  waiting for transfers between devices  356 us (76%)
  matrix products  46.6 us (10%)
  local copies, waits for them, and re-layouts  30.9 us (7%)
  starting transfers between devices  24.6 us (5%)
  other arithmetic  9.47 us (2%)
    all_to_all x2, waiting for transfers between devices, pencils(): lax.all_to_all(field, 'slab', split_axis=1, concat_axis=2, tiled=True)  157 us
    all_to_all x2, waiting for transfers between devices, pencils(): lax.all_to_all(field, 'slab', split_axis=2, concat_axis=1, tiled=True)  155 us
    dot_general x12, matrix products, apply_table(): return jnp.einsum(pattern, field, table, precision=precision)  46.6 us
    ppermute x2, waiting for transfers between devices, band_shift(): return lax.ppermute(block, 'band', route)  44.4 us
    transpose x4, local copies, waits for them, and re-layouts, apply_table(): return jnp.einsum(pattern, field, table, precision=precision)  21.6 us
    all_to_all x2, starting transfers between devices, pencils(): lax.all_to_all(field, 'slab', split_axis=2, concat_axis=1, tiled=True)  11.3 us
    all_to_all x2, starting transfers between devices, pencils(): lax.all_to_all(field, 'slab', split_axis=1, concat_axis=2, tiled=True)  10.1 us
  transfers between devices with their start and end apart: 6, of which 6 were waited for; matrix products, arithmetic and copies ran while one was open for 13% of the time, Pallas kernels for 0%

profile of v1, /device:TPU:10, one launch (start us, length us, event | category | flops | bytes accessed | tf_op | source)
XLA Modules:
  0.0 468.5 jit_solution(9830222730541804954)
XLA Ops:
  0.6 0.0 copy-start.2
  0.6 1.6 collective-permute-start
  2.2 23.6 %collective-permute-done = f32[2,8,128,128]{3,2,1,0:T(8,128)S(1)} collective-permute-done((f32[2,8,128,128]{3,2,1,0:T(8,128)}, f32[2,8,128,128]{3,2,1,0:T(8,128)S(1)}, u32[]{:S(2)}, u32[]{:S(2)}) %collective-permute-start) | collective-permute-done | bytes 1048608 | tf_op jit(solution)/shard_map/ppermute | solution.py:47
  25.8 5.1 %broadcast_multiply_fusion.1 = (f32[2,4,8,128,128]{4,3,2,1,0:T(8,128)S(1)}, f32[2,4,8,128,128]{4,3,2,1,0:T(8,128)}) fusion(f32[4,8,128,128]{3,2,1,0:T(8,128)} %param.4, f32[2,8,128,128]{3,2,1,0:T(8,128)} %param.3, f32[2,8,128,128]{3,2,1,0:T(8,128)S(1)} %collective-permute-done), kind=kLoop, calls=%fused_computation.29 | loop fusion | flops 2097152 | bytes 12582912 | tf_op jit(solution)/shard_map/mul | solution.py:64
  30.9 0.0 copy-done.2
  30.9 1.9 fusion.26
  32.8 3.4 convolution_bitcast_fusion.1
  36.2 5.4 %copy.12 = f32[8,8,128,128]{3,1,0,2:T(8,128)} copy(f32[8,8,128,128]{2,3,1,0:T(8,128)} %convolution_bitcast_fusion.1) | data formatting | bytes 8388608 | tf_op jit(solution)/shard_map/pzyx,yk->pzkx/transpose | solution.py:27
  41.6 6.2 %all-to-all-start = ((f32[8,8,128,128]{3,1,0,2:T(8,128)}), f32[8,8,128,128]{3,1,0,2:T(8,128)}, u32[]{:S(2)}, u32[]{:S(2)}) async-start(f32[8,8,128,128]{3,1,0,2:T(8,128)} %copy.12), calls=%async_computation | async-start | bytes 8388608 | tf_op jit(solution)/shard_map/all_to_all | solution.py:67
  47.8 4.1 fusion.27
  51.9 3.4 convolution_bitcast_fusion
  55.3 5.4 %copy.21 = f32[8,8,128,128]{3,1,0,2:T(8,128)} copy(f32[8,8,128,128]{2,3,1,0:T(8,128)} %convolution_bitcast_fusion) | data formatting | bytes 8388608 | tf_op jit(solution)/shard_map/pzyx,yk->pzkx/transpose | solution.py:27
  60.7 79.4 %all-to-all-done = f32[8,8,128,128]{3,1,0,2:T(8,128)} async-done(((f32[8,8,128,128]{3,1,0,2:T(8,128)}), f32[8,8,128,128]{3,1,0,2:T(8,128)}, u32[]{:S(2)}, u32[]{:S(2)}) %all-to-all-start) | async-done | bytes 4194336 | tf_op jit(solution)/shard_map/all_to_all | solution.py:67
  140.1 5.1 %all-to-all-start.2 = ((f32[8,8,128,128]{3,1,0,2:T(8,128)}), f32[8,8,128,128]{3,1,0,2:T(8,128)}, u32[]{:S(2)}, u32[]{:S(2)}) async-start(f32[8,8,128,128]{3,1,0,2:T(8,128)} %copy.21), calls=%async_computation.2 | async-start | bytes 8388608 | tf_op jit(solution)/shard_map/all_to_all | solution.py:67
  145.2 0.1 broadcast_add_fusion
  145.3 0.2 fusion.21
  145.5 0.0 copy-start.4
  145.5 4.7 copy.13
  150.1 0.0 copy-done.4
  150.1 3.4 fusion.14
  153.6 3.4 fusion.16
  157.0 5.4 %copy.15 = f32[8,128,8,128]{3,2,0,1:T(8,128)} copy(f32[8,128,8,128]{1,3,2,0:T(8,128)} %fusion.16) | data formatting | bytes 8388608 | tf_op jit(solution)/shard_map/pzyx,zk->pkyx/transpose | solution.py:27
  162.4 75.1 %all-to-all-done.2 = f32[8,8,128,128]{3,1,0,2:T(8,128)} async-done(((f32[8,8,128,128]{3,1,0,2:T(8,128)}), f32[8,8,128,128]{3,1,0,2:T(8,128)}, u32[]{:S(2)}, u32[]{:S(2)}) %all-to-all-start.2) | async-done | bytes 4194336 | tf_op jit(solution)/shard_map/all_to_all | solution.py:67
  237.5 5.1 %all-to-all-start.1 = ((f32[8,128,8,128]{3,2,0,1:T(8,128)}), f32[8,128,8,128]{3,2,0,1:T(8,128)}, u32[]{:S(2)}, u32[]{:S(2)}) async-start(f32[8,128,8,128]{3,2,0,1:T(8,128)} %copy.15), calls=%async_computation.1 | async-start | bytes 8388608 | tf_op jit(solution)/shard_map/all_to_all | solution.py:70
  242.6 4.6 copy.22
  247.2 3.6 fusion.12
  250.8 3.4 fusion.17
  254.2 5.4 %copy.24 = f32[8,128,8,128]{3,2,0,1:T(8,128)} copy(f32[8,128,8,128]{1,3,2,0:T(8,128)} %fusion.17) | data formatting | bytes 8388608 | tf_op jit(solution)/shard_map/pzyx,zk->pkyx/transpose | solution.py:27
  259.6 75.3 %all-to-all-done.1 = f32[8,128,8,128]{3,2,0,1:T(8,128)} async-done(((f32[8,128,8,128]{3,2,0,1:T(8,128)}), f32[8,128,8,128]{3,2,0,1:T(8,128)}, u32[]{:S(2)}, u32[]{:S(2)}) %all-to-all-start.1) | async-done | bytes 4194336 | tf_op jit(solution)/shard_map/all_to_all | solution.py:70
  334.9 5.1 %all-to-all-start.3 = ((f32[8,128,8,128]{3,2,0,1:T(8,128)}), f32[8,128,8,128]{3,2,0,1:T(8,128)}, u32[]{:S(2)}, u32[]{:S(2)}) async-start(f32[8,128,8,128]{3,2,0,1:T(8,128)} %copy.24), calls=%async_computation.3 | async-start | bytes 8388608 | tf_op jit(solution)/shard_map/all_to_all | solution.py:70
  339.9 5.4 %fusion.8 = f32[8,8,128,128]{3,2,1,0:T(8,128)S(1)} fusion(f32[128,128,1,1]{1,0,3,2:T(8,128)S(1)} %copy-done.2, f32[8,8,16,8,128]{4,3,0,1,2:T(8,128)} %bitcast.11), kind=kOutput, calls=%fused_computation.9 | convolution fusion | flops 805306368 | bytes 8454144 | tf_op jit(solution)/shard_map/pzyx,yk->pzkx/dot_general | solution.py:27
  345.3 5.0 %fusion.6 = f32[8,8,128,128]{3,2,1,0:T(8,128)} fusion(f32[128,128,1,1]{1,0,3,2:T(8,128)S(1)} %copy-done.2, f32[8,8,128,128]{3,2,1,0:T(8,128)S(1)} %fusion.8), kind=kOutput, calls=%fused_computation.7 | convolution fusion | flops 805306368 | bytes 8454144 | tf_op jit(solution)/shard_map/pzyx,xk->pzyk/dot_general | solution.py:27
  350.4 81.9 %all-to-all-done.3 = f32[8,128,8,128]{3,2,0,1:T(8,128)} async-done(((f32[8,128,8,128]{3,2,0,1:T(8,128)}), f32[8,128,8,128]{3,2,0,1:T(8,128)}, u32[]{:S(2)}, u32[]{:S(2)}) %all-to-all-start.3) | async-done | bytes 4194336 | tf_op jit(solution)/shard_map/all_to_all | solution.py:70
  432.3 0.0 copy-start
  432.3 0.0 copy-start.1
  432.3 5.6 %fusion.2 = f32[8,8,128,128]{3,2,1,0:T(8,128)S(1)} fusion(f32[128,128,1,1]{1,0,3,2:T(8,128)S(1)} %copy-done.2, f32[8,8,16,8,128]{4,3,0,1,2:T(8,128)} %bitcast.24), kind=kOutput, calls=%fused_computation.2 | convolution fusion | flops 805306368 | bytes 8454144 | tf_op jit(solution)/shard_map/pzyx,yk->pzkx/dot_general | solution.py:27
  437.8 0.0 copy-done
  437.8 0.0 copy-done.1
  437.9 0.0 copy-start.3
  437.9 4.1 multiply_reduce_fusion.2
  442.0 1.6 collective-permute-start.1
  443.5 0.0 copy-done.3
  443.6 1.5 multiply_reduce_fusion
  445.0 1.6 add.74
  446.6 20.8 %collective-permute-done.1 = f32[2,8,128,128]{3,2,1,0:T(8,128)S(1)} collective-permute-done((f32[2,8,128,128]{3,2,1,0:T(8,128)S(1)}, f32[2,8,128,128]{3,2,1,0:T(8,128)S(1)}, u32[]{:S(2)}, u32[]{:S(2)}) %collective-permute-start.1) | collective-permute-done | bytes 1048608 | tf_op jit(solution)/shard_map/ppermute | solution.py:47
  467.4 1.1 add.73
  (2 shorter events, 0.0 us)
Async XLA Ops:
  0.6 30.2 %copy-start.2 = (f32[128,128,1,1]{1,0,3,2:T(8,128)S(1)}, f32[128,128,1,1]{1,0,3,2:T(8,128)}, u32[]{:S(2)}) copy-start(f32[128,128,1,1]{1,0,3,2:T(8,128)} %constant.29) | copy-start | bytes 196612
  0.6 25.2 %collective-permute-start = (f32[2,8,128,128]{3,2,1,0:T(8,128)}, f32[2,8,128,128]{3,2,1,0:T(8,128)S(1)}, u32[]{:S(2)}, u32[]{:S(2)}) collective-permute-start(f32[2,8,128,128]{3,2,1,0:T(8,128)} %param.3), channel_id=1, source_target_pairs={{16,0},{0,16},{17,1},{1,17},{18,2},{2,18},{19,3},{3,19},{20,4},{4,... | collective-permute-start | bytes 3145736 | tf_op jit(solution)/shard_map/ppermute | solution.py:47
  41.6 98.6 %all-to-all-start = ((f32[8,8,128,128]{3,1,0,2:T(8,128)}), f32[8,8,128,128]{3,1,0,2:T(8,128)}, u32[]{:S(2)}, u32[]{:S(2)}) async-start(f32[8,8,128,128]{3,1,0,2:T(8,128)} %copy.12), calls=%async_computation | async-start | bytes 8388608 | tf_op jit(solution)/shard_map/all_to_all | solution.py:67
  140.1 97.4 %all-to-all-start.2 = ((f32[8,8,128,128]{3,1,0,2:T(8,128)}), f32[8,8,128,128]{3,1,0,2:T(8,128)}, u32[]{:S(2)}, u32[]{:S(2)}) async-start(f32[8,8,128,128]{3,1,0,2:T(8,128)} %copy.21), calls=%async_computation.2 | async-start | bytes 8388608 | tf_op jit(solution)/shard_map/all_to_all | solution.py:67
  145.5 4.7 copy-start.4
  237.5 97.4 %all-to-all-start.1 = ((f32[8,128,8,128]{3,2,0,1:T(8,128)}), f32[8,128,8,128]{3,2,0,1:T(8,128)}, u32[]{:S(2)}, u32[]{:S(2)}) async-start(f32[8,128,8,128]{3,2,0,1:T(8,128)} %copy.15), calls=%async_computation.1 | async-start | bytes 8388608 | tf_op jit(solution)/shard_map/all_to_all | solution.py:70
  334.9 97.4 %all-to-all-start.3 = ((f32[8,128,8,128]{3,2,0,1:T(8,128)}), f32[8,128,8,128]{3,2,0,1:T(8,128)}, u32[]{:S(2)}, u32[]{:S(2)}) async-start(f32[8,128,8,128]{3,2,0,1:T(8,128)} %copy.24), calls=%async_computation.3 | async-start | bytes 8388608 | tf_op jit(solution)/shard_map/all_to_all | solution.py:70
  432.3 5.6 %copy-start = (f32[8,8,128,128]{3,2,1,0:T(8,128)S(1)}, f32[8,8,128,128]{3,2,1,0:T(8,128)}, u32[]{:S(2)}) copy-start(f32[8,8,128,128]{3,2,1,0:T(8,128)} %fusion.6) | copy-start | bytes 12582916
  432.3 5.6 %copy-start.1 = (f32[4,8,128,128]{3,2,1,0:T(8,128)S(1)}, f32[4,8,128,128]{3,2,1,0:T(8,128)}, u32[]{:S(2)}) copy-start(f32[4,8,128,128]{3,2,1,0:T(8,128)} %param.4) | copy-start | bytes 6291460
  437.9 5.7 %copy-start.3 = (f32[2,8,128,128]{3,2,1,0:T(8,128)S(1)}, f32[2,8,128,128]{3,2,1,0:T(8,128)}, u32[]{:S(2)}) copy-start(f32[2,8,128,128]{3,2,1,0:T(8,128)} %param.3) | copy-start | bytes 3145732
  442.0 25.4 %collective-permute-start.1 = (f32[2,8,128,128]{3,2,1,0:T(8,128)S(1)}, f32[2,8,128,128]{3,2,1,0:T(8,128)S(1)}, u32[]{:S(2)}, u32[]{:S(2)}) collective-permute-start(f32[2,8,128,128]{3,2,1,0:T(8,128)S(1)} %get-tuple-element.2), channel_id=1, source_target_pairs={{16,0},{0,16},{17,1},{1,17},{18,2},{2,18},{19,3},{3,19},{20,4},{4,... | collective-permute-start | bytes 3145736 | tf_op jit(solution)/shard_map/ppermute | solution.py:47

commit v2 on v1

--- a/solution.py
+++ b/solution.py
@@ -1,4 +1,3 @@
-import functools
 import math
 
 import jax
@@ -8,6 +7,7 @@
 from jax.sharding import PartitionSpec as P
 
 STEPS = 2
+CHUNKS = 4
 
 
 coulomb_scale = 46.9 * 46.9 / math.pi
@@ -77,10 +77,104 @@
     return own_acc, part_acc
 
 
+def whole_fields(own, partners, groups, slabs, chunks):
+    length = own.shape[3]
+    rows = own.shape[1]
+    table = jnp.asarray(cas_table(length))
+    me = lax.axis_index("slab")
+    part_half, own_band, part_low = (me >> 3) & 1, (me >> 2) & 1, (me >> 1) & 1
+
+    def swap(block, mask):
+        return lax.ppermute(block, "slab", [(i ^ mask, i) for i in range(slabs)])
+
+    def across(block, flip, back):
+        route = []
+        for b in range(groups):
+            for i in range(slabs):
+                source = ((b + 1 + (i & 1)) % groups) * slabs + (i ^ flip)
+                target = b * slabs + i
+                route.append((target, source) if back else (source, target))
+        return lax.ppermute(block, ("band", "slab"), route)
+
+    def pick(block, position, axis=0):
+        return lax.dynamic_index_in_dim(block, position, axis, keepdims=False)
+
+    def ordered(position, mine, other):
+        return jnp.where(position == 0, jnp.stack([mine, other]), jnp.stack([other, mine]))
+
+    def own_in(block):
+        block = jnp.stack([pick(block, own_band), swap(pick(block, 1 - own_band), 4)])
+        block = jnp.stack([block, swap(block, 8)])
+        block = jnp.stack([block, swap(block, 2)])
+        return across(block, 0, False), across(block, 1, False)
+
+    def part_in(block):
+        block = block.reshape((2, 2) + block.shape[1:])
+        block = jnp.stack([pick(block, part_half), swap(pick(block, 1 - part_half), 8)], 1)
+        block = jnp.stack([pick(block, part_low), swap(pick(block, 1 - part_low), 2)])
+        block = jnp.stack([block, swap(block, 4)], 2)
+        return block, swap(block, 1)
+
+    def own_back(first, second):
+        block = across(first, 0, True) + across(second, 1, True)
+        block = block[0] + swap(block[1], 2)
+        block = block[0] + swap(block[1], 8)
+        return ordered(own_band, block[0], swap(block[1], 4))
+
+    def part_back(first, second):
+        block = first + swap(second, 1)
+        block = block[:, :, 0] + swap(block[:, :, 1], 4)
+        block = ordered(part_low, block[0], swap(block[1], 2))
+        block = ordered(part_half, block[:, 0], swap(block[:, 1], 8))
+        return block.reshape((-1,) + block.shape[2:])
+
+    cut = length // chunks
+    pieces = [slice(k * cut, (k + 1) * cut) for k in range(chunks)]
+    own_pairs = [own_in(own[:, :, piece]) for piece in pieces]
+    part_pairs = [part_in(partners[:, :, piece]) for piece in pieces]
+
+    def laid(pair):
+        return [half.reshape((-1,) + half.shape[-2:]) for half in pair]
+
+    own_pairs = [laid(pair) for pair in own_pairs]
+    part_pairs = [laid(pair) for pair in part_pairs]
+    field = jnp.concatenate(
+        [
+            apply_table("zyx,xk->zyk", jnp.concatenate([a * b for a, b in zip(o, p)]), table)
+            for o, p in zip(own_pairs, part_pairs)
+        ],
+        1,
+    )
+    position = lax.iota(jnp.int32, slabs)
+    slab_of = me ^ (
+        (position & 1) * 4 + (position & 2) * 4 + (position & 4) // 2 + (position & 8) // 8
+    )
+    z_table = jnp.take(table.reshape(slabs, rows, length), slab_of, axis=0).reshape(length, length)
+    waves = frequency(lax.iota(jnp.int32, length), length)
+    kernel = coulomb(waves, waves, waves, length**3)
+    field = apply_table("zyx,yk->zkx", field, table)
+    field = apply_table("zyx,zk->kyx", field, z_table) * kernel
+    field = apply_table("kyx,zk->zyx", field, z_table)
+    field = apply_table("zyx,yk->zkx", field, table)
+    own_out, part_out = [], []
+    parts_shape = (2, 2, 2, rows, cut, length)
+    for k, piece in enumerate(pieces):
+        potential = apply_table("zyx,xk->zyk", field[:, piece], table)
+        halves = [potential[: length // 2], potential[length // 2 :]]
+        own_out.append(own_back(*[(v * b).reshape(parts_shape) for v, b in zip(halves, part_pairs[k])]))
+        part_out.append(part_back(*[(v * a).reshape(parts_shape) for v, a in zip(halves, own_pairs[k])]))
+    return jnp.concatenate(own_out, 2), jnp.concatenate(part_out, 2)
+
+
 def solution(mesh):
     groups, slabs = mesh.shape["band"], mesh.shape["slab"]
     spec = P("band", "slab", None, None)
+
+    def shards(own, partners):
+        if slabs == 16 and own.shape[0] == 2 and partners.shape[0] == 4 and STEPS == 2:
+            return whole_fields(own, partners, groups, slabs, CHUNKS)
+        return pencils(own, partners, groups, slabs)
+
     return jax.shard_map(
-        functools.partial(pencils, groups=groups, slabs=slabs),
-        mesh=mesh, in_specs=(spec, spec), out_specs=(spec, spec), check_vma=False,
+        shards, mesh=mesh, in_specs=(spec, spec), out_specs=(spec, spec), check_vma=False
     )

time: 469 us -> 568 us (1.21)
  the two profiles are of different devices: /device:TPU:10 before, /device:TPU:0 now
where the time goes in v2:
time: 568 us; the launch traced here: 559 us
  waiting for transfers between devices  296 us (52%)
  starting transfers between devices  119 us (21%)
  local copies, waits for them, and re-layouts  50.7 us (9%)
  matrix products  49.3 us (9%)
  other arithmetic  42.2 us (7%)
    ppermute x56, waiting for transfers between devices, swap(): return lax.ppermute(block, 'slab', [(i ^ mask, i) for i in range(slabs)])  204 us
    ppermute x16, waiting for transfers between devices, across(): return lax.ppermute(block, ('band', 'slab'), route)  91.8 us
    ppermute x56, starting transfers between devices, swap(): return lax.ppermute(block, 'slab', [(i ^ mask, i) for i in range(slabs)])  73 us
    dot_general x12, matrix products, apply_table(): return jnp.einsum(pattern, field, table, precision=precision)  49.3 us
    ppermute x16, starting transfers between devices, across(): return lax.ppermute(block, ('band', 'slab'), route)  45.6 us
  transfers between devices with their start and end apart: 72, of which 36 were waited for; matrix products, arithmetic and copies ran while one was open for 12% of the time, Pallas kernels for 0%

profile of v2, /device:TPU:0, one launch (start us, length us, event | category | flops | bytes accessed | tf_op | source)
XLA Modules:
  0.0 559.0 jit_solution(17946570658662728170)
XLA Ops:
  2.8 3.0 collective-permute-start
  13.2 3.0 collective-permute-start.22
  23.6 3.0 collective-permute-start.28
  27.5 24.4 %collective-permute-done.22 = f32[2,8,32,128]{3,1,0,2:T(8,128)} collective-permute-done((f32[2,8,32,128]{3,1,0,2:T(8,128)}, f32[2,8,32,128]{3,1,0,2:T(8,128)}, u32[]{:S(2)}, u32[]{:S(2)}) %collective-permute-start.22) | collective-permute-done | bytes 262176 | tf_op jit(solution)/shard_map/ppermute | solution.py:88
  52.9 7.3 %collective-permute-done.4 = f32[2,8,32,128]{3,1,0,2:T(8,128)S(1)} collective-permute-done((f32[2,8,32,128]{3,1,0,2:T(8,128)S(1)}, f32[2,8,32,128]{3,1,0,2:T(8,128)S(1)}, u32[]{:S(2)}, u32[]{:S(2)}) %collective-permute-start.4) | collective-permute-done | bytes 262176 | tf_op jit(solution)/shard_map/ppermute | solution.py:88
  60.3 8.4 %collective-permute-done.13 = f32[2,8,32,128]{3,1,0,2:T(8,128)S(1)} collective-permute-done((f32[2,8,32,128]{3,1,0,2:T(8,128)S(1)}, f32[2,8,32,128]{3,1,0,2:T(8,128)S(1)}, u32[]{:S(2)}, u32[]{:S(2)}) %collective-permute-start.13) | collective-permute-done | bytes 262176 | tf_op jit(solution)/shard_map/ppermute | solution.py:88
  68.7 8.4 %collective-permute-done.31 = f32[2,8,32,128]{3,1,0,2:T(8,128)S(1)} collective-permute-done((f32[2,8,32,128]{3,1,0,2:T(8,128)S(1)}, f32[2,8,32,128]{3,1,0,2:T(8,128)S(1)}, u32[]{:S(2)}, u32[]{:S(2)}) %collective-permute-start.31) | collective-permute-done | bytes 262176 | tf_op jit(solution)/shard_map/ppermute | solution.py:88
  77.1 7.4 %collective-permute-start.23 = (f32[2,8,32,128]{3,1,0,2:T(8,128)S(1)}, f32[2,8,32,128]{3,1,0,2:T(8,128)S(1)}, u32[]{:S(2)}, u32[]{:S(2)}) collective-permute-start(f32[2,8,32,128]{3,1,0,2:T(8,128)S(1)} %get-tuple-element.67), channel_id=1, source_target_pairs={{2,0},{3,1},{0,2},{1,3},{6,4},{7,5},{4,6},{5,7},{10,8},{11,9},{8,1... | collective-permute-start | bytes 786440 | tf_op jit(solution)/shard_map/ppermute | solution.py:88
  84.5 17.8 %collective-permute-done.1 = f32[2,8,32,128]{3,2,1,0:T(8,128)S(1)} collective-permute-done((f32[2,8,32,128]{3,2,1,0:T(8,128)S(1)}, f32[2,8,32,128]{3,2,1,0:T(8,128)S(1)}, u32[]{:S(2)}, u32[]{:S(2)}) %collective-permute-start.1) | collective-permute-done | bytes 262176 | tf_op jit(solution)/shard_map/ppermute | solution.py:88
  107.7 9.5 %collective-permute-done.32 = f32[2,8,32,128]{3,1,0,2:T(8,128)S(1)} collective-permute-done((f32[2,8,32,128]{3,1,0,2:T(8,128)S(1)}, f32[2,8,32,128]{3,1,0,2:T(8,128)S(1)}, u32[]{:S(2)}, u32[]{:S(2)}) %collective-permute-start.32) | collective-permute-done | bytes 262176 | tf_op jit(solution)/shard_map/ppermute | solution.py:88
  122.2 23.1 %collective-permute-done.5 = f32[2,8,32,128]{3,1,0,2:T(8,128)S(1)} collective-permute-done((f32[2,8,32,128]{3,1,0,2:T(8,128)S(1)}, f32[2,8,32,128]{3,1,0,2:T(8,128)S(1)}, u32[]{:S(2)}, u32[]{:S(2)}) %collective-permute-start.5) | collective-permute-done | bytes 262176 | tf_op jit(solution)/shard_map/ppermute | solution.py:88
  150.7 5.8 %collective-permute-done.11 = f32[2,2,8,32,128]{4,3,2,1,0:T(8,128)S(1)} collective-permute-done((f32[2,2,8,32,128]{4,3,2,1,0:T(8,128)S(1)}, f32[2,2,8,32,128]{4,3,2,1,0:T(8,128)S(1)}, u32[]{:S(2)}, u32[]{:S(2)}) %collective-permute-start.11) | collective-permute-done | bytes 524320 | tf_op jit(solution)/shard_map/ppermute | solution.py:88
  158.0 4.9 collective-permute-done.2
  162.9 3.2 collective-permute-start.30
  171.4 3.8 collective-permute-start.12
  178.0 3.4 collective-permute-start.21
  183.6 14.7 %collective-permute-start.7 = (f32[2,2,2,8,32,128]{5,4,3,2,1,0:T(8,128)}, f32[2,2,2,8,32,128]{5,4,3,2,1,0:T(8,128)S(1)}, u32[]{:S(2)}, u32[]{:S(2)}) collective-permute-start(f32[2,2,2,8,32,128]{5,4,3,2,1,0:T(8,128)} %pad_maximum_fusion.5), channel_id=1, source_target_pairs={{17,0},{0,1},{19,2},{2,3},{21,4},{4,5},{23,6},{6,7},{25,8},{8,9},{... | collective-permute-start | bytes 3145736 | tf_op jit(solution)/shard_map/ppermute | solution.py:97
  204.8 22.3 %collective-permute-done.21 = f32[2,2,2,8,32,128]{5,4,3,2,1,0:T(8,128)} collective-permute-done((f32[2,2,2,8,32,128]{5,4,3,2,1,0:T(8,128)}, f32[2,2,2,8,32,128]{5,4,3,2,1,0:T(8,128)}, u32[]{:S(2)}, u32[]{:S(2)}) %collective-permute-start.21) | collective-permute-done | bytes 1048608 | tf_op jit(solution)/shard_map/ppermute | solution.py:97
  237.4 9.8 %collective-permute-done.25 = f32[2,2,2,8,32,128]{5,4,3,2,1,0:T(8,128)S(1)} collective-permute-done((f32[2,2,2,8,32,128]{5,4,3,2,1,0:T(8,128)}, f32[2,2,2,8,32,128]{5,4,3,2,1,0:T(8,128)S(1)}, u32[]{:S(2)}, u32[]{:S(2)}) %collective-permute-start.25) | collective-permute-done | bytes 1048608 | tf_op jit(solution)/shard_map/ppermute | solution.py:97
  247.9 10.6 %collective-permute-done.34 = f32[2,2,2,8,32,128]{5,4,3,2,1,0:T(8,128)S(1)} collective-permute-done((f32[2,2,2,8,32,128]{5,4,3,2,1,0:T(8,128)}, f32[2,2,2,8,32,128]{5,4,3,2,1,0:T(8,128)S(1)}, u32[]{:S(2)}, u32[]{:S(2)}) %collective-permute-start.34) | collective-permute-done | bytes 1048608 | tf_op jit(solution)/shard_map/ppermute | solution.py:97
  273.6 9.2 %fusion.18 = f32[128,128,128]{1,2,0:T(8,128)} fusion(f32[128,128,1]{0,1,2:T(8,128)S(1)} %copy-done.18, f32[128,32,128]{2,1,0:T(8,128)S(1)} %fusion.21, f32[128,32,128]{2,1,0:T(8,128)S(1)} %fusion.23, f32[128,32,128]{2,1,0:T(8,128)S(1)} %fusion.25, f32[128,32,128]{2,1,0:T(8,128)S(1)} %fusion.27), kind=kOutput, calls=%fused_computation.19 | convolution fusion | flops 1616904192 | bytes 16842752 | tf_op jit(solution)/shard_map/zyx,yk->zkx/dot_general | solution.py:27
  282.8 9.3 %copy.115 = f32[128,128,128]{2,0,1:T(8,128)} copy(f32[128,128,128]{1,2,0:T(8,128)} %fusion.18) | data formatting | bytes 16777216 | tf_op jit(solution)/shard_map/zyx,yk->zkx/transpose | solution.py:27
  292.1 6.5 %fusion.62 = f32[128,128,128]{2,0,1:T(8,128)S(1)} fusion(f32[128,128,128]{2,0,1:T(8,128)} %copy.115, f32[16,8,128]{2,1,0:T(8,128)S(1)} %gather_fusion, pred[128]{0:T(512)(128)(4,1)S(1)} %broadcast_in_dim.23), kind=kOutput, calls=%fused_computation.198 | convolution fusion | flops 1610629120 | bytes 16842880 | tf_op jit(solution)/shard_map/zyx,zk->kyx/dot_general | solution.py:27
  298.6 10.1 %fusion.2 = f32[128,128,128]{2,1,0:T(8,128)S(1)} fusion(f32[128,128,128]{2,0,1:T(8,128)S(1)} %fusion.62, f32[128]{0:T(128)S(1)} %fusion.82, f32[128,128]{1,0:T(8,128)S(1)} %broadcast_add_fusion), kind=kLoop, calls=%fused_computation.5 | loop fusion | flops 12582912 | bytes 16843264 | tf_op jit(solution)/shard_map/mul | solution.py:156
  308.7 8.3 %fusion.13 = f32[128,128,128]{2,0,1:T(8,128)S(1)} fusion(f32[128,128,128]{2,1,0:T(8,128)S(1)} %fusion.2, f32[16,8,128]{2,1,0:T(8,128)S(1)} %gather_fusion, pred[128]{0:T(512)(128)(4,1)S(1)} %broadcast_in_dim.23), kind=kOutput, calls=%fused_computation.16 | convolution fusion | flops 1610629120 | bytes 16842880 | tf_op jit(solution)/shard_map/kyx,zk->zyx/dot_general | solution.py:27
  317.1 8.5 %fusion.15 = f32[128,128,128]{2,1,0:T(8,128)S(1)} fusion(f32[128,128,1]{0,1,2:T(8,128)S(1)} %copy-done.18, f32[128,128,128]{2,0,1:T(8,128)S(1)} %fusion.13), kind=kOutput, calls=%fused_computation.18 | convolution fusion | flops 1610612736 | bytes 16842752 | tf_op jit(solution)/shard_map/zyx,yk->zkx/dot_general | solution.py:27
  332.2 3.2 collective-permute-start.36
  351.9 3.2 collective-permute-start.46
  355.1 3.8 collective-permute-done.37
  358.9 4.0 collective-permute-start.47
  374.0 7.4 %collective-permute-done.52 = f32[2,2,2,8,32,128]{5,4,3,2,1,0:T(8,128)S(1)} collective-permute-done((f32[2,2,2,8,32,128]{5,4,3,2,1,0:T(8,128)S(1)}, f32[2,2,2,8,32,128]{5,4,3,2,1,0:T(8,128)S(1)}, u32[]{:S(2)}, u32[]{:S(2)}) %collective-permute-start.52) | collective-permute-done | bytes 1048608 | tf_op jit(solution)/shard_map/ppermute | solution.py:97
  387.4 6.5 %collective-permute-done.46 = f32[2,2,2,8,32,128]{5,4,3,2,1,0:T(8,128)} collective-permute-done((f32[2,2,2,8,32,128]{5,4,3,2,1,0:T(8,128)}, f32[2,2,2,8,32,128]{5,4,3,2,1,0:T(8,128)}, u32[]{:S(2)}, u32[]{:S(2)}) %collective-permute-start.46) | collective-permute-done | bytes 1048608 | tf_op jit(solution)/shard_map/ppermute | solution.py:97
  393.9 10.0 %collective-permute-done.47 = f32[2,2,2,8,32,128]{5,4,3,2,1,0:T(8,128)} collective-permute-done((f32[2,2,2,8,32,128]{5,4,3,2,1,0:T(8,128)}, f32[2,2,2,8,32,128]{5,4,3,2,1,0:T(8,128)}, u32[]{:S(2)}, u32[]{:S(2)}) %collective-permute-start.47) | collective-permute-done | bytes 1048608 | tf_op jit(solution)/shard_map/ppermute | solution.py:97
  406.9 9.4 %collective-permute-done.41 = f32[2,2,2,8,32,128]{5,4,3,2,1,0:T(8,128)S(1)} collective-permute-done((f32[2,2,2,8,32,128]{5,4,3,2,1,0:T(8,128)}, f32[2,2,2,8,32,128]{5,4,3,2,1,0:T(8,128)S(1)}, u32[]{:S(2)}, u32[]{:S(2)}) %collective-permute-start.41) | collective-permute-done | bytes 1048608 | tf_op jit(solution)/shard_map/ppermute | solution.py:97
  417.5 8.9 %collective-permute-done.42 = f32[2,2,2,8,32,128]{5,4,3,2,1,0:T(8,128)} collective-permute-done((f32[2,2,2,8,32,128]{5,4,3,2,1,0:T(8,128)}, f32[2,2,2,8,32,128]{5,4,3,2,1,0:T(8,128)}, u32[]{:S(2)}, u32[]{:S(2)}) %collective-permute-start.42) | collective-permute-done | bytes 1048608 | tf_op jit(solution)/shard_map/ppermute | solution.py:97
  435.7 5.4 collective-permute-done.57
  445.0 7.4 %collective-permute-done.69 = f32[2,2,8,32,128]{4,2,3,1,0:T(8,128)S(1)} collective-permute-done((f32[2,2,8,32,128]{4,2,3,1,0:T(8,128)S(1)}, f32[2,2,8,32,128]{4,2,3,1,0:T(8,128)S(1)}, u32[]{:S(2)}, u32[]{:S(2)}) %collective-permute-start.69) | collective-permute-done | bytes 524320 | tf_op jit(solution)/shard_map/ppermute | solution.py:88
  456.9 9.7 %collective-permute-done.43 = f32[2,2,8,32,128]{4,3,2,1,0:T(8,128)S(1)} collective-permute-done((f32[2,2,8,32,128]{4,3,2,1,0:T(8,128)S(1)}, f32[2,2,8,32,128]{4,3,2,1,0:T(8,128)S(1)}, u32[]{:S(2)}, u32[]{:S(2)}) %collective-permute-start.43) | collective-permute-done | bytes 524320 | tf_op jit(solution)/shard_map/ppermute | solution.py:88
  466.6 3.4 collective-permute-start.54
  471.8 14.3 %collective-permute-done.65 = f32[2,2,8,32,128]{4,2,3,1,0:T(8,128)S(1)} collective-permute-done((f32[2,2,8,32,128]{4,2,3,1,0:T(8,128)S(1)}, f32[2,2,8,32,128]{4,2,3,1,0:T(8,128)S(1)}, u32[]{:S(2)}, u32[]{:S(2)}) %collective-permute-start.65) | collective-permute-done | bytes 524320 | tf_op jit(solution)/shard_map/ppermute | solution.py:88
  490.8 16.6 %collective-permute-done.49 = f32[2,8,32,128]{3,2,1,0:T(8,128)S(1)} collective-permute-done((f32[2,8,32,128]{3,2,1,0:T(8,128)S(1)}, f32[2,8,32,128]{3,2,1,0:T(8,128)S(1)}, u32[]{:S(2)}, u32[]{:S(2)}) %collective-permute-start.49) | collective-permute-done | bytes 262176 | tf_op jit(solution)/shard_map/ppermute | solution.py:88
  514.5 3.5 collective-permute-start.50
  521.1 3.1 collective-permute-start.63
  524.2 5.3 collective-permute-done.50
  529.5 3.1 collective-permute-start.67
  533.9 13.2 %collective-permute-done.71 = f32[2,8,32,128]{3,1,2,0:T(8,128)S(1)} collective-permute-done((f32[2,8,32,128]{3,1,2,0:T(8,128)S(1)}, f32[2,8,32,128]{3,1,2,0:T(8,128)S(1)}, u32[]{:S(2)}, u32[]{:S(2)}) %collective-permute-start.71) | collective-permute-done | bytes 262176 | tf_op jit(solution)/shard_map/ppermute | solution.py:88
  547.2 5.5 collective-permute-done.63
  552.9 4.3 collective-permute-done.67
  (364 shorter events, 159.3 us)
Async XLA Ops:
  13.2 38.7 %collective-permute-start.22 = (f32[2,8,32,128]{3,1,0,2:T(8,128)}, f32[2,8,32,128]{3,1,0,2:T(8,128)}, u32[]{:S(2)}, u32[]{:S(2)}) collective-permute-start(f32[2,8,32,128]{3,1,0,2:T(8,128)} %bitcast.325), channel_id=1, source_target_pairs={{8,0},{9,1},{10,2},{11,3},{12,4},{13,5},{14,6},{15,7},{0,8},{1,9},... | collective-permute-start | bytes 786440 | tf_op jit(solution)/shard_map/ppermute | solution.py:88
  17.5 42.7 %collective-permute-start.4 = (f32[2,8,32,128]{3,1,0,2:T(8,128)S(1)}, f32[2,8,32,128]{3,1,0,2:T(8,128)S(1)}, u32[]{:S(2)}, u32[]{:S(2)}) collective-permute-start(f32[2,8,32,128]{3,1,0,2:T(8,128)S(1)} %bitcast.372), channel_id=1, source_target_pairs={{8,0},{9,1},{10,2},{11,3},{12,4},{13,5},{14,6},{15,7},{0,8},{1,9},... | collective-permute-start | bytes 786440 | tf_op jit(solution)/shard_map/ppermute | solution.py:88
  18.6 50.0 %collective-permute-start.13 = (f32[2,8,32,128]{3,1,0,2:T(8,128)S(1)}, f32[2,8,32,128]{3,1,0,2:T(8,128)S(1)}, u32[]{:S(2)}, u32[]{:S(2)}) collective-permute-start(f32[2,8,32,128]{3,1,0,2:T(8,128)S(1)} %bitcast.371), channel_id=1, source_target_pairs={{8,0},{9,1},{10,2},{11,3},{12,4},{13,5},{14,6},{15,7},{0,8},{1,9},... | collective-permute-start | bytes 786440 | tf_op jit(solution)/shard_map/ppermute | solution.py:88
  22.5 54.5 %collective-permute-start.31 = (f32[2,8,32,128]{3,1,0,2:T(8,128)S(1)}, f32[2,8,32,128]{3,1,0,2:T(8,128)S(1)}, u32[]{:S(2)}, u32[]{:S(2)}) collective-permute-start(f32[2,8,32,128]{3,1,0,2:T(8,128)S(1)} %bitcast.370), channel_id=1, source_target_pairs={{8,0},{9,1},{10,2},{11,3},{12,4},{13,5},{14,6},{15,7},{0,8},{1,9},... | collective-permute-start | bytes 786440 | tf_op jit(solution)/shard_map/ppermute | solution.py:88
  23.6 80.7 %collective-permute-start.28 = (f32[2,8,32,128]{3,2,1,0:T(8,128)S(1)}, f32[2,8,32,128]{3,2,1,0:T(8,128)S(1)}, u32[]{:S(2)}, u32[]{:S(2)}) collective-permute-start(f32[2,8,32,128]{3,2,1,0:T(8,128)S(1)} %get-tuple-element.99), channel_id=1, source_target_pairs={{8,0},{9,1},{10,2},{11,3},{12,4},{13,5},{14,6},{15,7},{0,8},{1,9},... | collective-permute-start | bytes 786440 | tf_op jit(solution)/shard_map/ppermute | solution.py:88
  51.9 52.8 %collective-permute-start.19 = (f32[2,8,32,128]{3,2,1,0:T(8,128)S(1)}, f32[2,8,32,128]{3,2,1,0:T(8,128)S(1)}, u32[]{:S(2)}, u32[]{:S(2)}) collective-permute-start(f32[2,8,32,128]{3,2,1,0:T(8,128)S(1)} %get-tuple-element.95), channel_id=1, source_target_pairs={{8,0},{9,1},{10,2},{11,3},{12,4},{13,5},{14,6},{15,7},{0,8},{1,9},... | collective-permute-start | bytes 786440 | tf_op jit(solution)/shard_map/ppermute | solution.py:88
  60.2 42.1 %collective-permute-start.1 = (f32[2,8,32,128]{3,2,1,0:T(8,128)S(1)}, f32[2,8,32,128]{3,2,1,0:T(8,128)S(1)}, u32[]{:S(2)}, u32[]{:S(2)}) collective-permute-start(f32[2,8,32,128]{3,2,1,0:T(8,128)S(1)} %get-tuple-element.87), channel_id=1, source_target_pairs={{8,0},{9,1},{10,2},{11,3},{12,4},{13,5},{14,6},{15,7},{0,8},{1,9},... | collective-permute-start | bytes 786440 | tf_op jit(solution)/shard_map/ppermute | solution.py:88
  68.6 38.1 %collective-permute-start.10 = (f32[2,8,32,128]{3,2,1,0:T(8,128)S(1)}, f32[2,8,32,128]{3,2,1,0:T(8,128)S(1)}, u32[]{:S(2)}, u32[]{:S(2)}) collective-permute-start(f32[2,8,32,128]{3,2,1,0:T(8,128)S(1)} %get-tuple-element.91), channel_id=1, source_target_pairs={{8,0},{9,1},{10,2},{11,3},{12,4},{13,5},{14,6},{15,7},{0,8},{1,9},... | collective-permute-start | bytes 786440 | tf_op jit(solution)/shard_map/ppermute | solution.py:88
  77.1 43.1 %collective-permute-start.23 = (f32[2,8,32,128]{3,1,0,2:T(8,128)S(1)}, f32[2,8,32,128]{3,1,0,2:T(8,128)S(1)}, u32[]{:S(2)}, u32[]{:S(2)}) collective-permute-start(f32[2,8,32,128]{3,1,0,2:T(8,128)S(1)} %get-tuple-element.67), channel_id=1, source_target_pairs={{2,0},{3,1},{0,2},{1,3},{6,4},{7,5},{4,6},{5,7},{10,8},{11,9},{8,1... | collective-permute-start | bytes 786440 | tf_op jit(solution)/shard_map/ppermute | solution.py:88
  104.7 41.8 %collective-permute-start.29 = (f32[2,2,8,32,128]{4,3,2,1,0:T(8,128)S(1)}, f32[2,2,8,32,128]{4,3,2,1,0:T(8,128)S(1)}, u32[]{:S(2)}, u32[]{:S(2)}) collective-permute-start(f32[2,2,8,32,128]{4,3,2,1,0:T(8,128)S(1)} %get-tuple-element.71), channel_id=1, source_target_pairs={{2,0},{3,1},{0,2},{1,3},{6,4},{7,5},{4,6},{5,7},{10,8},{11,9},{8,1... | collective-permute-start | bytes 1572872 | tf_op jit(solution)/shard_map/ppermute | solution.py:88
  106.7 41.5 %collective-permute-start.20 = (f32[2,2,8,32,128]{4,3,2,1,0:T(8,128)S(1)}, f32[2,2,8,32,128]{4,3,2,1,0:T(8,128)S(1)}, u32[]{:S(2)}, u32[]{:S(2)}) collective-permute-start(f32[2,2,8,32,128]{4,3,2,1,0:T(8,128)S(1)} %get-tuple-element.63), channel_id=1, source_target_pairs={{2,0},{3,1},{0,2},{1,3},{6,4},{7,5},{4,6},{5,7},{10,8},{11,9},{8,1... | collective-permute-start | bytes 1572872 | tf_op jit(solution)/shard_map/ppermute | solution.py:88
  117.2 28.1 %collective-permute-start.5 = (f32[2,8,32,128]{3,1,0,2:T(8,128)S(1)}, f32[2,8,32,128]{3,1,0,2:T(8,128)S(1)}, u32[]{:S(2)}, u32[]{:S(2)}) collective-permute-start(f32[2,8,32,128]{3,1,0,2:T(8,128)S(1)} %get-tuple-element.51), channel_id=1, source_target_pairs={{2,0},{3,1},{0,2},{1,3},{6,4},{7,5},{4,6},{5,7},{10,8},{11,9},{8,1... | collective-permute-start | bytes 786440 | tf_op jit(solution)/shard_map/ppermute | solution.py:88
  119.9 36.6 %collective-permute-start.11 = (f32[2,2,8,32,128]{4,3,2,1,0:T(8,128)S(1)}, f32[2,2,8,32,128]{4,3,2,1,0:T(8,128)S(1)}, u32[]{:S(2)}, u32[]{:S(2)}) collective-permute-start(f32[2,2,8,32,128]{4,3,2,1,0:T(8,128)S(1)} %get-tuple-element.55), channel_id=1, source_target_pairs={{2,0},{3,1},{0,2},{1,3},{6,4},{7,5},{4,6},{5,7},{10,8},{11,9},{8,1... | collective-permute-start | bytes 1572872 | tf_op jit(solution)/shard_map/ppermute | solution.py:88
  120.2 42.7 %collective-permute-start.2 = (f32[2,2,8,32,128]{4,3,2,1,0:T(8,128)S(1)}, f32[2,2,8,32,128]{4,3,2,1,0:T(8,128)S(1)}, u32[]{:S(2)}, u32[]{:S(2)}) collective-permute-start(f32[2,2,8,32,128]{4,3,2,1,0:T(8,128)S(1)} %get-tuple-element.47), channel_id=1, source_target_pairs={{2,0},{3,1},{0,2},{1,3},{6,4},{7,5},{4,6},{5,7},{10,8},{11,9},{8,1... | collective-permute-start | bytes 1572872 | tf_op jit(solution)/shard_map/ppermute | solution.py:88
  146.5 24.9 %collective-permute-start.6 = (f32[2,2,8,32,128]{4,2,1,0,3:T(8,128)S(1)}, f32[2,2,8,32,128]{4,2,1,0,3:T(8,128)S(1)}, u32[]{:S(2)}, u32[]{:S(2)}) collective-permute-start(f32[2,2,8,32,128]{4,2,1,0,3:T(8,128)S(1)} %get-tuple-element.49), channel_id=1, source_target_pairs={{4,0},{5,1},{6,2},{7,3},{0,4},{1,5},{2,6},{3,7},{12,8},{13,9},{14,... | collective-permute-start | bytes 1572872 | tf_op jit(solution)/shard_map/ppermute | solution.py:88
  148.2 29.7 %collective-permute-start.15 = (f32[2,2,8,32,128]{4,2,1,0,3:T(8,128)S(1)}, f32[2,2,8,32,128]{4,2,1,0,3:T(8,128)S(1)}, u32[]{:S(2)}, u32[]{:S(2)}) collective-permute-start(f32[2,2,8,32,128]{4,2,1,0,3:T(8,128)S(1)} %get-tuple-element.57), channel_id=1, source_target_pairs={{4,0},{5,1},{6,2},{7,3},{0,4},{1,5},{2,6},{3,7},{12,8},{13,9},{14,... | collective-permute-start | bytes 1572872 | tf_op jit(solution)/shard_map/ppermute | solution.py:88
  156.5 27.0 %collective-permute-start.33 = (f32[2,2,8,32,128]{4,2,1,0,3:T(8,128)}, f32[2,2,8,32,128]{4,2,1,0,3:T(8,128)S(1)}, u32[]{:S(2)}, u32[]{:S(2)}) collective-permute-start(f32[2,2,8,32,128]{4,2,1,0,3:T(8,128)} %get-tuple-element.73), channel_id=1, source_target_pairs={{4,0},{5,1},{6,2},{7,3},{0,4},{1,5},{2,6},{3,7},{12,8},{13,9},{14,... | collective-permute-start | bytes 1572872 | tf_op jit(solution)/shard_map/ppermute | solution.py:88
  162.9 36.8 %collective-permute-start.30 = (f32[2,2,2,8,32,128]{5,4,3,2,1,0:T(8,128)}, f32[2,2,2,8,32,128]{5,4,3,2,1,0:T(8,128)}, u32[]{:S(2)}, u32[]{:S(2)}) collective-permute-start(f32[2,2,2,8,32,128]{5,4,3,2,1,0:T(8,128)} %pad_maximum_fusion.11), channel_id=1, source_target_pairs={{16,0},{1,1},{18,2},{3,3},{20,4},{5,5},{22,6},{7,7},{24,8},{9,9},{... | collective-permute-start | bytes 3145736 | tf_op jit(solution)/shard_map/ppermute | solution.py:97
  167.2 35.6 %collective-permute-start.3 = (f32[2,2,2,8,32,128]{5,4,3,2,1,0:T(8,128)}, f32[2,2,2,8,32,128]{5,4,3,2,1,0:T(8,128)}, u32[]{:S(2)}, u32[]{:S(2)}) collective-permute-start(f32[2,2,2,8,32,128]{5,4,3,2,1,0:T(8,128)} %pad_maximum_fusion.5), channel_id=1, source_target_pairs={{16,0},{1,1},{18,2},{3,3},{20,4},{5,5},{22,6},{7,7},{24,8},{9,9},{... | collective-permute-start | bytes 3145736 | tf_op jit(solution)/shard_map/ppermute | solution.py:97
  171.4 33.2 %collective-permute-start.12 = (f32[2,2,2,8,32,128]{5,4,3,2,1,0:T(8,128)}, f32[2,2,2,8,32,128]{5,4,3,2,1,0:T(8,128)}, u32[]{:S(2)}, u32[]{:S(2)}) collective-permute-start(f32[2,2,2,8,32,128]{5,4,3,2,1,0:T(8,128)} %pad_maximum_fusion.7), channel_id=1, source_target_pairs={{16,0},{1,1},{18,2},{3,3},{20,4},{5,5},{22,6},{7,7},{24,8},{9,9},{... | collective-permute-start | bytes 3145736 | tf_op jit(solution)/shard_map/ppermute | solution.py:97
  178.0 49.1 %collective-permute-start.21 = (f32[2,2,2,8,32,128]{5,4,3,2,1,0:T(8,128)}, f32[2,2,2,8,32,128]{5,4,3,2,1,0:T(8,128)}, u32[]{:S(2)}, u32[]{:S(2)}) collective-permute-start(f32[2,2,2,8,32,128]{5,4,3,2,1,0:T(8,128)} %pad_maximum_fusion.9), channel_id=1, source_target_pairs={{16,0},{1,1},{18,2},{3,3},{20,4},{5,5},{22,6},{7,7},{24,8},{9,9},{... | collective-permute-start | bytes 3145736 | tf_op jit(solution)/shard_map/ppermute | solution.py:97
  183.6 49.7 %collective-permute-start.7 = (f32[2,2,2,8,32,128]{5,4,3,2,1,0:T(8,128)}, f32[2,2,2,8,32,128]{5,4,3,2,1,0:T(8,128)S(1)}, u32[]{:S(2)}, u32[]{:S(2)}) collective-permute-start(f32[2,2,2,8,32,128]{5,4,3,2,1,0:T(8,128)} %pad_maximum_fusion.5), channel_id=1, source_target_pairs={{17,0},{0,1},{19,2},{2,3},{21,4},{4,5},{23,6},{6,7},{25,8},{8,9},{... | collective-permute-start | bytes 3145736 | tf_op jit(solution)/shard_map/ppermute | solution.py:97
  199.7 36.3 %collective-permute-start.16 = (f32[2,2,2,8,32,128]{5,4,3,2,1,0:T(8,128)}, f32[2,2,2,8,32,128]{5,4,3,2,1,0:T(8,128)S(1)}, u32[]{:S(2)}, u32[]{:S(2)}) collective-permute-start(f32[2,2,2,8,32,128]{5,4,3,2,1,0:T(8,128)} %pad_maximum_fusion.7), channel_id=1, source_target_pairs={{17,0},{0,1},{19,2},{2,3},{21,4},{4,5},{23,6},{6,7},{25,8},{8,9},{... | collective-permute-start | bytes 3145736 | tf_op jit(solution)/shard_map/ppermute | solution.py:97
  202.8 44.4 %collective-permute-start.25 = (f32[2,2,2,8,32,128]{5,4,3,2,1,0:T(8,128)}, f32[2,2,2,8,32,128]{5,4,3,2,1,0:T(8,128)S(1)}, u32[]{:S(2)}, u32[]{:S(2)}) collective-permute-start(f32[2,2,2,8,32,128]{5,4,3,2,1,0:T(8,128)} %pad_maximum_fusion.9), channel_id=1, source_target_pairs={{17,0},{0,1},{19,2},{2,3},{21,4},{4,5},{23,6},{6,7},{25,8},{8,9},{... | collective-permute-start | bytes 3145736 | tf_op jit(solution)/shard_map/ppermute | solution.py:97
  204.6 53.9 %collective-permute-start.34 = (f32[2,2,2,8,32,128]{5,4,3,2,1,0:T(8,128)}, f32[2,2,2,8,32,128]{5,4,3,2,1,0:T(8,128)S(1)}, u32[]{:S(2)}, u32[]{:S(2)}) collective-permute-start(f32[2,2,2,8,32,128]{5,4,3,2,1,0:T(8,128)} %pad_maximum_fusion.11), channel_id=1, source_target_pairs={{17,0},{0,1},{19,2},{2,3},{21,4},{4,5},{23,6},{6,7},{25,8},{8,9},{... | collective-permute-start | bytes 3145736 | tf_op jit(solution)/shard_map/ppermute | solution.py:97
  227.1 32.0 %collective-permute-start.35 = (f32[2,2,2,8,32,128]{5,3,2,1,0,4:T(8,128)S(1)}, f32[2,2,2,8,32,128]{5,3,2,1,0,4:T(8,128)S(1)}, u32[]{:S(2)}, u32[]{:S(2)}) collective-permute-start(f32[2,2,2,8,32,128]{5,3,2,1,0,4:T(8,128)S(1)} %pad_maximum_fusion.12), channel_id=1, source_target_pairs={{1,0},{0,1},{3,2},{2,3},{5,4},{4,5},{7,6},{6,7},{9,8},{8,9},{11,10... | collective-permute-start | bytes 3145736 | tf_op jit(solution)/shard_map/ppermute | solution.py:88
  233.3 28.1 %collective-permute-start.17 = (f32[2,2,2,8,32,128]{5,3,2,1,0,4:T(8,128)S(1)}, f32[2,2,2,8,32,128]{5,3,2,1,0,4:T(8,128)S(1)}, u32[]{:S(2)}, u32[]{:S(2)}) collective-permute-start(f32[2,2,2,8,32,128]{5,3,2,1,0,4:T(8,128)S(1)} %pad_maximum_fusion.8), channel_id=1, source_target_pairs={{1,0},{0,1},{3,2},{2,3},{5,4},{4,5},{7,6},{6,7},{9,8},{8,9},{11,10... | collective-permute-start | bytes 3145736 | tf_op jit(solution)/shard_map/ppermute | solution.py:88
  236.0 26.8 %collective-permute-start.8 = (f32[2,2,2,8,32,128]{5,3,2,1,0,4:T(8,128)S(1)}, f32[2,2,2,8,32,128]{5,3,2,1,0,4:T(8,128)S(1)}, u32[]{:S(2)}, u32[]{:S(2)}) collective-permute-start(f32[2,2,2,8,32,128]{5,3,2,1,0,4:T(8,128)S(1)} %pad_maximum_fusion.6), channel_id=1, source_target_pairs={{1,0},{0,1},{3,2},{2,3},{5,4},{4,5},{7,6},{6,7},{9,8},{8,9},{11,10... | collective-permute-start | bytes 3145736 | tf_op jit(solution)/shard_map/ppermute | solution.py:88
  335.9 34.4 %collective-permute-start.56 = (f32[2,2,2,8,32,128]{5,3,2,1,0,4:T(8,128)S(1)}, f32[2,2,2,8,32,128]{5,3,2,1,0,4:T(8,128)S(1)}, u32[]{:S(2)}, u32[]{:S(2)}) collective-permute-start(f32[2,2,2,8,32,128]{5,3,2,1,0,4:T(8,128)S(1)} %bitcast.354), channel_id=1, source_target_pairs={{1,0},{0,1},{3,2},{2,3},{5,4},{4,5},{7,6},{6,7},{9,8},{8,9},{11,10... | collective-permute-start | bytes 3145736 | tf_op jit(solution)/shard_map/ppermute | solution.py:88
  341.7 31.1 %collective-permute-start.51 = (f32[2,2,2,8,32,128]{5,4,3,2,1,0:T(8,128)S(1)}, f32[2,2,2,8,32,128]{5,4,3,2,1,0:T(8,128)S(1)}, u32[]{:S(2)}, u32[]{:S(2)}) collective-permute-start(f32[2,2,2,8,32,128]{5,4,3,2,1,0:T(8,128)S(1)} %copy.92), channel_id=1, source_target_pairs={{0,16},{1,1},{2,18},{3,3},{4,20},{5,5},{6,22},{7,7},{8,24},{9,9},{... | collective-permute-start | bytes 3145736 | tf_op jit(solution)/shard_map/ppermute | solution.py:97
  344.4 37.0 %collective-permute-start.52 = (f32[2,2,2,8,32,128]{5,4,3,2,1,0:T(8,128)S(1)}, f32[2,2,2,8,32,128]{5,4,3,2,1,0:T(8,128)S(1)}, u32[]{:S(2)}, u32[]{:S(2)}) collective-permute-start(f32[2,2,2,8,32,128]{5,4,3,2,1,0:T(8,128)S(1)} %copy.93), channel_id=1, source_target_pairs={{0,17},{1,0},{2,19},{3,2},{4,21},{5,4},{6,23},{7,6},{8,25},{9,8},{... | collective-permute-start | bytes 3145736 | tf_op jit(solution)/shard_map/ppermute | solution.py:97
  351.9 42.0 %collective-permute-start.46 = (f32[2,2,2,8,32,128]{5,4,3,2,1,0:T(8,128)}, f32[2,2,2,8,32,128]{5,4,3,2,1,0:T(8,128)}, u32[]{:S(2)}, u32[]{:S(2)}) collective-permute-start(f32[2,2,2,8,32,128]{5,4,3,2,1,0:T(8,128)} %copy.88), channel_id=1, source_target_pairs={{0,16},{1,1},{2,18},{3,3},{4,20},{5,5},{6,22},{7,7},{8,24},{9,9},{... | collective-permute-start | bytes 3145736 | tf_op jit(solution)/shard_map/ppermute | solution.py:97
  358.9 45.0 %collective-permute-start.47 = (f32[2,2,2,8,32,128]{5,4,3,2,1,0:T(8,128)}, f32[2,2,2,8,32,128]{5,4,3,2,1,0:T(8,128)}, u32[]{:S(2)}, u32[]{:S(2)}) collective-permute-start(f32[2,2,2,8,32,128]{5,4,3,2,1,0:T(8,128)} %copy.89), channel_id=1, source_target_pairs={{0,17},{1,0},{2,19},{3,2},{4,21},{5,4},{6,23},{7,6},{8,25},{9,8},{... | collective-permute-start | bytes 3145736 | tf_op jit(solution)/shard_map/ppermute | solution.py:97
  370.2 46.1 %collective-permute-start.41 = (f32[2,2,2,8,32,128]{5,4,3,2,1,0:T(8,128)}, f32[2,2,2,8,32,128]{5,4,3,2,1,0:T(8,128)S(1)}, u32[]{:S(2)}, u32[]{:S(2)}) collective-permute-start(f32[2,2,2,8,32,128]{5,4,3,2,1,0:T(8,128)} %copy.84), channel_id=1, source_target_pairs={{0,16},{1,1},{2,18},{3,3},{4,20},{5,5},{6,22},{7,7},{8,24},{9,9},{... | collective-permute-start | bytes 3145736 | tf_op jit(solution)/shard_map/ppermute | solution.py:97
  372.9 53.6 %collective-permute-start.42 = (f32[2,2,2,8,32,128]{5,4,3,2,1,0:T(8,128)}, f32[2,2,2,8,32,128]{5,4,3,2,1,0:T(8,128)}, u32[]{:S(2)}, u32[]{:S(2)}) collective-permute-start(f32[2,2,2,8,32,128]{5,4,3,2,1,0:T(8,128)} %copy.85), channel_id=1, source_target_pairs={{0,17},{1,0},{2,19},{3,2},{4,21},{5,4},{6,23},{7,6},{8,25},{9,8},{... | collective-permute-start | bytes 3145736 | tf_op jit(solution)/shard_map/ppermute | solution.py:97
  382.4 47.0 %collective-permute-start.68 = (f32[2,2,2,8,32,128]{5,3,4,1,0,2:T(8,128)}, f32[2,2,2,8,32,128]{5,3,4,1,0,2:T(8,128)}, u32[]{:S(2)}, u32[]{:S(2)}) collective-permute-start(f32[2,2,2,8,32,128]{5,3,4,1,0,2:T(8,128)} %copy.107), channel_id=1, source_target_pairs={{1,0},{0,1},{3,2},{2,3},{5,4},{4,5},{7,6},{6,7},{9,8},{8,9},{11,10... | collective-permute-start | bytes 3145736 | tf_op jit(solution)/shard_map/ppermute | solution.py:88
  393.9 38.5 %collective-permute-start.60 = (f32[2,2,2,8,32,128]{5,3,4,1,0,2:T(8,128)S(1)}, f32[2,2,2,8,32,128]{5,3,4,1,0,2:T(8,128)S(1)}, u32[]{:S(2)}, u32[]{:S(2)}) collective-permute-start(f32[2,2,2,8,32,128]{5,3,4,1,0,2:T(8,128)S(1)} %copy.99), channel_id=1, source_target_pairs={{1,0},{0,1},{3,2},{2,3},{5,4},{4,5},{7,6},{6,7},{9,8},{8,9},{11,10... | collective-permute-start | bytes 3145736 | tf_op jit(solution)/shard_map/ppermute | solution.py:88
  404.0 29.3 %collective-permute-start.64 = (f32[2,2,2,8,32,128]{5,3,4,1,0,2:T(8,128)S(1)}, f32[2,2,2,8,32,128]{5,3,4,1,0,2:T(8,128)S(1)}, u32[]{:S(2)}, u32[]{:S(2)}) collective-permute-start(f32[2,2,2,8,32,128]{5,3,4,1,0,2:T(8,128)S(1)} %copy.103), channel_id=1, source_target_pairs={{1,0},{0,1},{3,2},{2,3},{5,4},{4,5},{7,6},{6,7},{9,8},{8,9},{11,10... | collective-permute-start | bytes 3145736 | tf_op jit(solution)/shard_map/ppermute | solution.py:88
  434.1 32.5 %collective-permute-start.43 = (f32[2,2,8,32,128]{4,3,2,1,0:T(8,128)S(1)}, f32[2,2,8,32,128]{4,3,2,1,0:T(8,128)S(1)}, u32[]{:S(2)}, u32[]{:S(2)}) collective-permute-start(f32[2,2,8,32,128]{4,3,2,1,0:T(8,128)S(1)} %slice_bitcast_fusion.12), channel_id=1, source_target_pairs={{2,0},{3,1},{0,2},{1,3},{6,4},{7,5},{4,6},{5,7},{10,8},{11,9},{8,1... | collective-permute-start | bytes 1572872 | tf_op jit(solution)/shard_map/ppermute | solution.py:88
  441.2 29.0 %collective-permute-start.61 = (f32[2,2,8,32,128]{4,2,3,1,0:T(8,128)S(1)}, f32[2,2,8,32,128]{4,2,3,1,0:T(8,128)S(1)}, u32[]{:S(2)}, u32[]{:S(2)}) collective-permute-start(f32[2,2,8,32,128]{4,2,3,1,0:T(8,128)S(1)} %slice_bitcast_fusion.4), channel_id=1, source_target_pairs={{4,0},{5,1},{6,2},{7,3},{0,4},{1,5},{2,6},{3,7},{12,8},{13,9},{14,... | collective-permute-start | bytes 1572872 | tf_op jit(solution)/shard_map/ppermute | solution.py:88
  444.1 42.0 %collective-permute-start.65 = (f32[2,2,8,32,128]{4,2,3,1,0:T(8,128)S(1)}, f32[2,2,8,32,128]{4,2,3,1,0:T(8,128)S(1)}, u32[]{:S(2)}, u32[]{:S(2)}) collective-permute-start(f32[2,2,8,32,128]{4,2,3,1,0:T(8,128)S(1)} %slice_bitcast_fusion.2), channel_id=1, source_target_pairs={{4,0},{5,1},{6,2},{7,3},{0,4},{1,5},{2,6},{3,7},{12,8},{13,9},{14,... | collective-permute-start | bytes 1572872 | tf_op jit(solution)/shard_map/ppermute | solution.py:88
  452.4 36.1 %collective-permute-start.39 = (f32[2,8,32,128]{3,2,1,0:T(8,128)S(1)}, f32[2,8,32,128]{3,2,1,0:T(8,128)S(1)}, u32[]{:S(2)}, u32[]{:S(2)}) collective-permute-start(f32[2,8,32,128]{3,2,1,0:T(8,128)S(1)} %slice_bitcast_fusion.38), channel_id=1, source_target_pairs={{8,0},{9,1},{10,2},{11,3},{12,4},{13,5},{14,6},{15,7},{0,8},{1,9},... | collective-permute-start | bytes 786440 | tf_op jit(solution)/shard_map/ppermute | solution.py:88
  455.4 53.5 %collective-permute-start.58 = (f32[2,8,32,128]{3,1,0,2:T(8,128)S(1)}, f32[2,8,32,128]{3,1,0,2:T(8,128)S(1)}, u32[]{:S(2)}, u32[]{:S(2)}) collective-permute-start(f32[2,8,32,128]{3,1,0,2:T(8,128)S(1)} %get-tuple-element.33), channel_id=1, source_target_pairs={{2,0},{3,1},{0,2},{1,3},{6,4},{7,5},{4,6},{5,7},{10,8},{11,9},{8,1... | collective-permute-start | bytes 786440 | tf_op jit(solution)/shard_map/ppermute | solution.py:88
  470.2 38.9 %collective-permute-start.70 = (f32[2,8,32,128]{3,1,2,0:T(8,128)S(1)}, f32[2,8,32,128]{3,1,2,0:T(8,128)S(1)}, u32[]{:S(2)}, u32[]{:S(2)}) collective-permute-start(f32[2,8,32,128]{3,1,2,0:T(8,128)S(1)} %get-tuple-element.45), channel_id=1, source_target_pairs={{2,0},{3,1},{0,2},{1,3},{6,4},{7,5},{4,6},{5,7},{10,8},{11,9},{8,1... | collective-permute-start | bytes 786440 | tf_op jit(solution)/shard_map/ppermute | solution.py:88
  488.5 26.0 %collective-permute-start.44 = (f32[2,8,32,128]{3,2,1,0:T(8,128)S(1)}, f32[2,8,32,128]{3,2,1,0:T(8,128)S(1)}, u32[]{:S(2)}, u32[]{:S(2)}) collective-permute-start(f32[2,8,32,128]{3,2,1,0:T(8,128)S(1)} %slice_bitcast_fusion.36), channel_id=1, source_target_pairs={{8,0},{9,1},{10,2},{11,3},{12,4},{13,5},{14,6},{15,7},{0,8},{1,9},... | collective-permute-start | bytes 786440 | tf_op jit(solution)/shard_map/ppermute | solution.py:88
  514.1 33.0 %collective-permute-start.71 = (f32[2,8,32,128]{3,1,2,0:T(8,128)S(1)}, f32[2,8,32,128]{3,1,2,0:T(8,128)S(1)}, u32[]{:S(2)}, u32[]{:S(2)}) collective-permute-start(f32[2,8,32,128]{3,1,2,0:T(8,128)S(1)} %get-tuple-element.43), channel_id=1, source_target_pairs={{8,0},{9,1},{10,2},{11,3},{12,4},{13,5},{14,6},{15,7},{0,8},{1,9},... | collective-permute-start | bytes 786440 | tf_op jit(solution)/shard_map/ppermute | solution.py:88
  521.1 31.6 %collective-permute-start.63 = (f32[2,8,32,128]{3,1,2,0:T(8,128)S(1)}, f32[2,8,32,128]{3,1,2,0:T(8,128)S(1)}, u32[]{:S(2)}, u32[]{:S(2)}) collective-permute-start(f32[2,8,32,128]{3,1,2,0:T(8,128)S(1)} %get-tuple-element.35), channel_id=1, source_target_pairs={{8,0},{9,1},{10,2},{11,3},{12,4},{13,5},{14,6},{15,7},{0,8},{1,9},... | collective-permute-start | bytes 786440 | tf_op jit(solution)/shard_map/ppermute | solution.py:88
  529.5 27.7 %collective-permute-start.67 = (f32[2,8,32,128]{3,1,2,0:T(8,128)S(1)}, f32[2,8,32,128]{3,1,2,0:T(8,128)S(1)}, u32[]{:S(2)}, u32[]{:S(2)}) collective-permute-start(f32[2,8,32,128]{3,1,2,0:T(8,128)S(1)} %get-tuple-element.39), channel_id=1, source_target_pairs={{8,0},{9,1},{10,2},{11,3},{12,4},{13,5},{14,6},{15,7},{0,8},{1,9},... | collective-permute-start | bytes 786440 | tf_op jit(solution)/shard_map/ppermute | solution.py:88
  (78 other events, 834.0 us)

commit v3 on v1

--- a/solution.py
+++ b/solution.py
@@ -1,10 +1,12 @@
-import functools
 import math
 
 import jax
 import jax.numpy as jnp
+import ml_dtypes
 import numpy as np
 from jax import lax
+from jax.experimental import pallas as pl
+from jax.experimental.pallas import tpu as pltpu
 from jax.sharding import PartitionSpec as P
 
 STEPS = 2
@@ -77,10 +79,304 @@
     return own_acc, part_acc
 
 
+def two_terms(values):
+    high = values.astype(jnp.bfloat16)
+    return high, (values - high.astype(jnp.float32)).astype(jnp.bfloat16)
+
+
+def table_terms(length):
+    table = cas_table(length)
+    high = table.astype(ml_dtypes.bfloat16)
+    low = (table - high.astype(np.float32)).astype(ml_dtypes.bfloat16)
+    return high, low
+
+
+def from_left(high, low, xp=np):
+    return xp.concatenate([xp.concatenate([high, high], 1), xp.concatenate([low, low], 1)], 0)
+
+
+def product(left, right):
+    return jnp.dot(left, right, preferred_element_type=jnp.float32)
+
+
+def along_x(rows, right):
+    high, low = two_terms(rows)
+    both = product(jnp.concatenate([high, low], 1), right)
+    return both[:, : both.shape[1] // 2] + both[:, both.shape[1] // 2 :]
+
+
+def along_y(columns, left):
+    high, low = two_terms(columns)
+    both = product(left, jnp.concatenate([high, low], 0))
+    return both[: both.shape[0] // 2] + both[both.shape[0] // 2 :]
+
+
+def slab_pieces(step, refs):
+    first, fx_a, fx_b, second, sx_a, sx_b, parts, parts_c = refs
+    return [
+        (0, (first,), parts),
+        (1, (fx_a, fx_b), parts),
+        (2, (second,), parts_c),
+        (3, (sx_a, sx_b), parts_c),
+    ]
+
+
+def gather_kernel(right_ref, left_ref, *refs):
+    pieces, out_ref, pair_ref = refs[:8], refs[8], refs[9]
+    step = pl.program_id(0)
+    rows, length = pair_ref.shape[0], pair_ref.shape[1]
+    for turn, own_refs, part_ref in slab_pieces(step, pieces):
+
+        @pl.when(step // 2 == turn)
+        def _(own_refs=own_refs, part_ref=part_ref):
+            count = rows // len(own_refs)
+            for k, own_ref in enumerate(own_refs):
+                span = pl.ds(k * count, count)
+                pair_ref[span] = own_ref[0] * part_ref[0, span]
+
+    flat_out = out_ref.reshape(rows * length, length)
+    for r in range(0, rows, 2):
+        block = along_x(pair_ref[pl.ds(r, 2)].reshape(2 * length, length), right_ref[...])
+        block = along_y(jnp.concatenate([block[:length], block[length:]], 1), left_ref[...])
+        flat_out[pl.ds(r, length, stride=rows), :] = block[:, :length]
+        flat_out[pl.ds(r + 1, length, stride=rows), :] = block[:, length:]
+
+
+def column_kernel(left_ref, back_ref, coulomb_ref, a_ref, b_ref, a_out, b_out):
+    count, half, length = a_ref.shape
+    for k in range(0, count, 2):
+        block = jnp.concatenate(
+            [
+                jnp.concatenate([a_ref[k], b_ref[k]], 0),
+                jnp.concatenate([a_ref[k + 1], b_ref[k + 1]], 0),
+            ],
+            1,
+        )
+        block = along_y(block, left_ref[...])
+        block = block * jnp.concatenate([coulomb_ref[k], coulomb_ref[k + 1]], 1)
+        block = along_y(block, back_ref[...])
+        for j in range(2):
+            piece = block[:, j * length : (j + 1) * length]
+            a_out[k + j] = piece[:half]
+            b_out[k + j] = piece[half:]
+
+
+def scatter_kernel(right_ref, left_ref, field_ref, *refs):
+    pieces, outs, pot_ref = refs[:8], refs[-9:-1], refs[-1]
+    step = pl.program_id(0)
+    rows, length = pot_ref.shape[0], pot_ref.shape[1]
+    flat = field_ref.reshape(rows * length, length)
+    for r in range(0, rows, 2):
+        block = jnp.concatenate(
+            [flat[pl.ds(r, length, stride=rows), :], flat[pl.ds(r + 1, length, stride=rows), :]], 1
+        )
+        block = along_y(block, left_ref[...])
+        block = jnp.concatenate([block[:, :length], block[:, length:]], 0)
+        pot_ref[pl.ds(r, 2)] = along_x(block, right_ref[...]).reshape(2, length, length)
+    for (turn, own_refs, part_ref), (_, own_outs, part_out) in zip(
+        slab_pieces(step, pieces), slab_pieces(step, outs)
+    ):
+
+        @pl.when(step // 2 == turn)
+        def _(own_refs=own_refs, part_ref=part_ref, own_outs=own_outs, part_out=part_out):
+            count = rows // len(own_refs)
+            for k, (own_ref, own_out) in enumerate(zip(own_refs, own_outs)):
+                span = pl.ds(k * count, count)
+                own_out[0] = pot_ref[span] * part_ref[0, span]
+                part_out[0, span] = pot_ref[span] * own_ref[0]
+
+
+def piece_specs(rows, length, z_low):
+    def own_spec(turn, count):
+        return pl.BlockSpec(
+            (1, count, length, length),
+            lambda i: (jnp.clip(i - 2 * turn, 0, 1) * 2 + z_low, 0, 0, 0),
+        )
+
+    def part_spec(core):
+        return pl.BlockSpec(
+            (1, rows, length, length), lambda i: (jnp.clip(i - 4 * core, 0, 3), 0, 0, 0)
+        )
+
+    half = rows // 2
+    return [
+        own_spec(0, rows), own_spec(1, half), own_spec(1, half),
+        own_spec(2, rows), own_spec(3, half), own_spec(3, half),
+        part_spec(0), part_spec(1),
+    ]
+
+
+def fixed_spec(shape):
+    return pl.BlockSpec(shape, lambda i: (0,) * len(shape))
+
+
+def settings(megabytes):
+    return pltpu.CompilerParams(
+        dimension_semantics=("arbitrary",), vmem_limit_bytes=megabytes * 2**20
+    )
+
+
+def cost(length, fields, transforms):
+    cells = length**3
+    return pl.CostEstimate(
+        flops=transforms * 8 * cells * length, bytes_accessed=4 * fields * cells, transcendentals=0
+    )
+
+
+def gather_half(right, left, pieces, z_low):
+    rows, length = pieces[0].shape[1], pieces[0].shape[2]
+    return pl.pallas_call(
+        gather_kernel,
+        grid=(8,),
+        in_specs=[fixed_spec(right.shape), fixed_spec(left.shape)] + piece_specs(rows, length, z_low),
+        out_specs=pl.BlockSpec((length, rows, length), lambda i: (0, i, 0)),
+        out_shape=jax.ShapeDtypeStruct((length, 8 * rows, length), jnp.float32),
+        scratch_shapes=[pltpu.VMEM((rows, length, length), jnp.float32)],
+        compiler_params=settings(32),
+        cost_estimate=cost(length, 2, 1),
+    )(right, left, *pieces)
+
+
+def columns(left, back, coulomb_table, a, b):
+    length, half = a.shape[0], a.shape[1]
+    count = 8
+    block = pl.BlockSpec((count, half, length), lambda i: (i, 0, 0))
+    return pl.pallas_call(
+        column_kernel,
+        grid=(length // count,),
+        in_specs=[
+            fixed_spec(left.shape), fixed_spec(back.shape),
+            pl.BlockSpec((count, length, length), lambda i: (i, 0, 0)), block, block,
+        ],
+        out_specs=[block, block],
+        out_shape=[jax.ShapeDtypeStruct(a.shape, jnp.float32)] * 2,
+        compiler_params=settings(32),
+        cost_estimate=cost(length, 3, 2),
+    )(left, back, coulomb_table, a, b)
+
+
+def scatter_half(right, left, field, pieces, z_low, held):
+    rows, length = pieces[0].shape[1], pieces[0].shape[2]
+    specs = piece_specs(rows, length, z_low)
+    count = len(held)
+    return pl.pallas_call(
+        scatter_kernel,
+        grid=(8,),
+        in_specs=[
+            fixed_spec(right.shape), fixed_spec(left.shape),
+            pl.BlockSpec((length, rows, length), lambda i: (0, i, 0)),
+        ]
+        + specs
+        + [pl.BlockSpec(memory_space=pl.ANY)] * count,
+        out_specs=specs,
+        out_shape=[jax.ShapeDtypeStruct(piece.shape, jnp.float32) for piece in pieces],
+        input_output_aliases={11 + k: k for k in range(count)},
+        scratch_shapes=[pltpu.VMEM((rows, length, length), jnp.float32)],
+        compiler_params=settings(48),
+        cost_estimate=cost(length, 3, 1),
+    )(right, left, field, *pieces, *held)
+
+
+def whole_fields(own, partners, groups, slabs):
+    length = own.shape[3]
+    rows = own.shape[1]
+    half = rows // 2
+    plane = own.shape[2:]
+    me = lax.axis_index("slab")
+    part_half, own_band, part_low = (me >> 3) & 1, (me >> 2) & 1, (me >> 1) & 1
+
+    def swap(block, mask):
+        return lax.ppermute(block, "slab", [(i ^ mask, i) for i in range(slabs)])
+
+    def across(block, flip, back):
+        route = []
+        for b in range(groups):
+            for i in range(slabs):
+                source = ((b + 1 + (i & 1)) % groups) * slabs + (i ^ flip)
+                target = b * slabs + i
+                route.append((target, source) if back else (source, target))
+        return lax.ppermute(block, ("band", "slab"), route)
+
+    def pick(block, position, axis=0):
+        return lax.dynamic_index_in_dim(block, position, axis, keepdims=False)
+
+    def ordered(position, mine, other, axis=0):
+        return jnp.where(
+            position == 0, jnp.stack([mine, other], axis), jnp.stack([other, mine], axis)
+        )
+
+    def together(*blocks):
+        return lax.optimization_barrier(blocks)
+
+    high, low = table_terms(length)
+    left = jnp.asarray(from_left(high, low))
+    right = jnp.asarray(from_left(high, low).T)
+    position = lax.iota(jnp.int32, slabs)
+    slab_of = me ^ (
+        (position & 1) * 8 + (position & 2) + (position & 4) // 4 + (position & 8) // 2
+    )
+    z_high, z_low = [
+        jnp.take(jnp.asarray(term).reshape(slabs, rows, length), slab_of, axis=0).reshape(
+            length, length
+        )
+        for term in (high, low)
+    ]
+    z_left, z_back = from_left(z_high.T, z_low.T, jnp), from_left(z_high, z_low, jnp)
+    waves = frequency(lax.iota(jnp.int32, length), length)
+    coulomb_table = coulomb(waves, waves, waves, length**3)
+
+    kept, passed = pick(own, own_band), pick(own, 1 - own_band)
+    bands = jnp.stack([kept, swap(passed, 4), swap(kept, 8), swap(passed, 12)])
+    parts = partners.reshape((2, 2) + partners.shape[1:])
+    parts = jnp.stack([pick(parts, part_low, 1), swap(pick(parts, 1 - part_low, 1), 2)])
+    bands, parts = together(bands, parts)
+    bands_x = swap(bands, 2)
+    first, second = across(bands, 0, False), across(bands, 1, False)
+    parts = jnp.stack([pick(parts, part_half, 1), swap(pick(parts, 1 - part_half, 1), 8)], 1)
+    bands_x, first, second, parts = together(bands_x, first, second, parts)
+    parts = parts.reshape((4, rows) + plane)
+    parts_z, parts_c = swap(parts, 4), swap(parts, 1)
+    fx_a, fx_b = across(bands_x[:, :half], 0, False), swap(first[:, half:], 2)
+    sx_a, sx_b = across(bands_x[:, :half], 1, False), swap(second[:, half:], 2)
+    own_pieces = [first, fx_a, fx_b, second, sx_a, sx_b]
+    even = own_pieces + [parts, parts_c]
+    field_even = gather_half(right, left, even, 0)
+    odd = own_pieces + [parts_z, swap(parts_z, 1)]
+    field_odd = gather_half(right, left, odd, 1)
+
+    field_even, field_odd = columns(z_left, z_back, coulomb_table, field_even, field_odd)
+
+    *own_pieces, parts_z, parts_zc = scatter_half(right, left, field_odd, odd, 1, [])
+    parts_z = parts_z + swap(parts_zc, 1)
+    parts_z = swap(parts_z, 4)
+    *own_pieces, parts, parts_c = scatter_half(right, left, field_even, even, 0, own_pieces)
+    first, fx_a, fx_b, second, sx_a, sx_b = own_pieces
+    bands_x = across(fx_a, 0, True) + across(sx_a, 1, True)
+    fx_b, sx_b = swap(fx_b, 2), swap(sx_b, 2)
+    parts = (parts + swap(parts_c, 1) + parts_z).reshape((2, 2, rows) + plane)
+    first = jnp.concatenate([first[:, :half], first[:, half:] + fx_b], 1)
+    second = jnp.concatenate([second[:, :half], second[:, half:] + sx_b], 1)
+    bands_x, first, second, parts = together(bands_x, first, second, parts)
+    bands = across(first, 0, True) + across(second, 1, True)
+    bands_x = swap(bands_x, 2)
+    bands = jnp.concatenate([bands[:, :half] + bands_x, bands[:, half:]], 1)
+    parts = ordered(part_half, parts[:, 0], swap(parts[:, 1], 8), 1)
+    bands, parts = together(bands, parts)
+    kept = bands[0] + swap(bands[2], 8)
+    passed = swap(bands[1], 4) + swap(bands[3], 12)
+    parts = ordered(part_low, parts[0], swap(parts[1], 2), 1)
+    return ordered(own_band, kept, passed), parts.reshape(partners.shape)
+
+
 def solution(mesh):
     groups, slabs = mesh.shape["band"], mesh.shape["slab"]
     spec = P("band", "slab", None, None)
+
+    def shards(own, partners):
+        if slabs == 16 and own.shape[0] == 2 and partners.shape[0] == 4 and STEPS == 2:
+            return whole_fields(own, partners, groups, slabs)
+        return pencils(own, partners, groups, slabs)
+
     return jax.shard_map(
-        functools.partial(pencils, groups=groups, slabs=slabs),
-        mesh=mesh, in_specs=(spec, spec), out_specs=(spec, spec), check_vma=False,
-    )
+        shards, mesh=mesh, in_specs=(spec, spec), out_specs=(spec, spec), check_vma=False
+    )

time: 469 us -> 431 us (0.919)
  waiting for transfers between devices: 356 us -> 275 us
  Pallas kernels: 0 us -> 55.4 us
  matrix products: 46.6 us -> 0 us
  starting transfers between devices: 24.6 us -> 51.6 us
  other arithmetic: 9.47 us -> 25.7 us
  local copies, waits for them, and re-layouts: 30.9 us -> 18.8 us
    all_to_all x4 -> x0, waiting for transfers between devices: 312 us -> none  [the longest x2 157 us: pencils(): lax.all_to_all(field, 'slab', split_axis=1, concat_axis=2, tiled=True)]
    ppermute x2 -> x30, waiting for transfers between devices: 44.4 us -> 275 us  [the longest x22 255 us: swap(): return lax.ppermute(block, 'slab', [(i ^ mask, i) for i in range(slabs)])]
    pallas_call x0 -> x5, Pallas kernels: none -> 55.4 us  [the longest x2 23.5 us: scatter_half(): pl.pallas_call(scatter_kernel, grid=(8,), in_specs=[fixed_spec(right.shap...]
    ppermute x2 -> x30, starting transfers between devices: 3.17 us -> 51.6 us  [the longest x22 26.4 us: swap(): return lax.ppermute(block, 'slab', [(i ^ mask, i) for i in range(slabs)])]
    dot_general x12 -> x0, matrix products: 46.6 us -> none  [apply_table(): return jnp.einsum(pattern, field, table, precision=precision)]
    transpose x4 -> x0, local copies, waits for them, and re-layouts: 21.6 us -> none  [apply_table(): return jnp.einsum(pattern, field, table, precision=precision)]
    all_to_all x4 -> x0, starting transfers between devices: 21.4 us -> none  [the longest x2 11.3 us: pencils(): lax.all_to_all(field, 'slab', split_axis=2, concat_axis=1, tiled=True)]
    all_to_all x2 -> x0, local copies, waits for them, and re-layouts: 9.27 us -> none  [pencils(): lax.all_to_all(field, 'slab', split_axis=2, concat_axis=1, tiled=True)]
  transfers between devices with their start and end apart: 6 -> 30, of which waited for: 6 -> 12; matrix products, arithmetic and copies ran while one was open for 13% -> 7% of each run, Pallas kernels for 0% -> 5%
where the time goes in v3:
time: 431 us; the launch traced here: 428 us
  waiting for transfers between devices  275 us (64%)
  Pallas kernels  55.4 us (13%)
  starting transfers between devices  51.6 us (12%)
  other arithmetic  25.7 us (6%)
  local copies, waits for them, and re-layouts  18.8 us (4%)
    ppermute x22, waiting for transfers between devices, swap(): return lax.ppermute(block, 'slab', [(i ^ mask, i) for i in range(slabs)])  255 us
    ppermute x22, starting transfers between devices, swap(): return lax.ppermute(block, 'slab', [(i ^ mask, i) for i in range(slabs)])  26.4 us
    ppermute x8, starting transfers between devices, across(): return lax.ppermute(block, ('band', 'slab'), route)  25.2 us
    pallas_call x2, Pallas kernels, scatter_half(): pl.pallas_call(scatter_kernel, grid=(8,), in_specs=[fixed_spec(right.shap...  23.5 us
    ppermute x8, waiting for transfers between devices, across(): return lax.ppermute(block, ('band', 'slab'), route)  19.6 us
    pallas_call x2, Pallas kernels, gather_half(): pl.pallas_call(gather_kernel, grid=(8,), in_specs=[fixed_spec(right.shape...  17.7 us
    pallas_call x1, Pallas kernels, columns(): pl.pallas_call(column_kernel, grid=(length // count,), in_specs=[fixed_sp...  14.3 us
  transfers between devices with their start and end apart: 30, of which 12 were waited for; matrix products, arithmetic and copies ran while one was open for 7% of the time, Pallas kernels for 5%

profile of v3, /device:TPU:10, one launch (start us, length us, event | category | flops | bytes accessed | tf_op | source)
XLA Modules:
  0.0 427.6 jit_solution(13466825667578599128)
XLA Ops:
  0.6 1.8 dynamic-slice_bitcast_fusion.2
  3.1 2.7 collective-permute-start.1
  5.8 1.8 collective-permute-start
  7.6 31.6 %collective-permute-done.1 = f32[8,128,128]{2,1,0:T(8,128)S(1)} collective-permute-done((f32[8,128,128]{2,1,0:T(8,128)S(1)}, f32[8,128,128]{2,1,0:T(8,128)S(1)}, u32[]{:S(2)}, u32[]{:S(2)}) %collective-permute-start.1) | collective-permute-done | bytes 524320 | tf_op jit(solution)/shard_map/ppermute | solution.py:289
  39.2 11.1 %collective-permute-done.2 = f32[8,128,128]{2,1,0:T(8,128)S(1)} collective-permute-done((f32[8,128,128]{2,1,0:T(8,128)S(1)}, f32[8,128,128]{2,1,0:T(8,128)S(1)}, u32[]{:S(2)}, u32[]{:S(2)}) %collective-permute-start.2) | collective-permute-done | bytes 524320 | tf_op jit(solution)/shard_map/ppermute | solution.py:289
  50.3 1.5 pad_maximum_fusion
  51.8 2.8 pad_maximum_fusion.1
  54.6 3.4 collective-permute-start.5
  58.0 1.6 collective-permute-start.4
  59.6 1.7 constant_dynamic-slice_fusion
  61.4 42.5 %collective-permute-done.7 = f32[2,8,128,128]{3,2,1,0:T(8,128)S(1)} collective-permute-done((f32[2,8,128,128]{3,2,1,0:T(8,128)S(1)}, f32[2,8,128,128]{3,2,1,0:T(8,128)S(1)}, u32[]{:S(2)}, u32[]{:S(2)}) %collective-permute-start.7) | collective-permute-done | bytes 1048608 | tf_op jit(solution)/shard_map/ppermute | solution.py:289
  103.8 1.6 pad_maximum_fusion.2
  105.4 4.9 %collective-permute-start.13 = (f32[4,8,128,128]{3,2,1,0:T(8,128)}, f32[4,8,128,128]{3,2,1,0:T(8,128)}, u32[]{:S(2)}, u32[]{:S(2)}) collective-permute-start(f32[4,8,128,128]{3,2,1,0:T(8,128)} %bitcast.15.refs_6_), channel_id=1, source_target_pairs={{4,0},{5,1},{6,2},{7,3},{0,4},{1,5},{2,6},{3,7},{12,8},{13,9},{14,... | collective-permute-start | bytes 6291464 | tf_op jit(solution)/shard_map/ppermute | solution.py:289
  111.9 2.4 collective-permute-start.12
  114.3 40.5 %collective-permute-done.13.refs_6_ = f32[4,8,128,128]{3,2,1,0:T(8,128)} collective-permute-done((f32[4,8,128,128]{3,2,1,0:T(8,128)}, f32[4,8,128,128]{3,2,1,0:T(8,128)}, u32[]{:S(2)}, u32[]{:S(2)}) %collective-permute-start.13) | collective-permute-done | bytes 2097184 | tf_op jit(solution)/shard_map/ppermute | solution.py:289
  154.8 2.1 collective-permute-start.14
  158.5 1.3 slice.52
  159.9 2.4 collective-permute-start.8
  162.3 1.3 slice.53
  164.3 6.7 %fusion.1.coulomb_ref = f32[128,128,128]{2,1,0:T(8,128)} fusion(f32[128]{0:T(128)S(1)} %fusion.14, f32[128,128]{1,0:T(8,128)S(1)} %broadcast_add_fusion), kind=kLoop, calls=%fused_computation.5 | loop fusion | flops 10485760 | bytes 8454656 | tf_op jit(solution)/shard_map/jit(_where)/select_n | solution.py:42
  170.9 16.8 %collective-permute-done.9.refs_2_ = f32[4,4,128,128]{3,2,1,0:T(8,128)S(1)} collective-permute-done((f32[4,4,128,128]{3,2,1,0:T(8,128)S(1)}, f32[4,4,128,128]{3,2,1,0:T(8,128)S(1)}, u32[]{:S(2)}, u32[]{:S(2)}) %collective-permute-start.9) | collective-permute-done | bytes 1048608 | tf_op jit(solution)/shard_map/ppermute | solution.py:289
  187.7 9.2 %shard_map.77.a_ref = f32[128,64,128]{2,1,0:T(8,128)S(1)} custom-call(bf16[256,256]{1,0:T(8,128)(2,1)S(1)} %copy-done.6, bf16[256,256]{1,0:T(8,128)(2,1)S(1)} %copy-done.7, f32[4,8,128,128]{3,2,1,0:T(8,128)} %collective-permute-done.5.refs_0_, f32[4,4,128,128]{3,2,1,0:T(8,128)S(1)} %collective-permute-done.8.refs_1_, ...), custom_call_target="tpu_custom_call" | custom-call | flops 2147483648 | bytes 16777216 | tf_op jit(solution)/shard_map/pallas_call | solution.py:228
  197.0 8.5 %shard_map.78.b_ref = f32[128,64,128]{2,1,0:T(8,128)S(1)} custom-call(bf16[256,256]{1,0:T(8,128)(2,1)S(1)} %copy-done.6, bf16[256,256]{1,0:T(8,128)(2,1)S(1)} %copy-done.7, f32[4,8,128,128]{3,2,1,0:T(8,128)} %collective-permute-done.5.refs_0_, f32[4,4,128,128]{3,2,1,0:T(8,128)S(1)} %collective-permute-done.8.refs_1_, ...), custom_call_target="tpu_custom_call" | custom-call | flops 2147483648 | bytes 16777216 | tf_op jit(solution)/shard_map/pallas_call | solution.py:228
  205.5 14.3 %shard_map.79 = (f32[128,64,128]{2,1,0:T(8,128)S(1)}, f32[128,64,128]{2,1,0:T(8,128)S(1)}) custom-call(bf16[256,256]{1,0:T(8,128)(2,1)S(1)} %copy.14.left_ref, bf16[256,256]{1,0:T(8,128)(2,1)S(1)} %maximum_maximum_fusion.1.back_ref, f32[128,128,128]{2,1,0:T(8,128)} %fusion.1.coulomb_ref, f32[128,64,128]{2,1,0:T(8,128)S(1)} %shard_map.77.a_ref, ...), custom_call_target="tpu_custom_call" | custom-call | flops 4294967296 | bytes 25165824 | tf_op jit(solution)/shard_map/pallas_call | solution.py:244
  219.8 2.0 copy-done.4
  221.7 2.0 copy-done.5
  223.7 11.7 %shard_map.80 = (f32[4,8,128,128]{3,2,1,0:T(8,128)}, f32[4,4,128,128]{3,2,1,0:T(8,128)S(1)}, f32[4,4,128,128]{3,2,1,0:T(8,128)S(1)}, f32[4,8,128,128]{3,2,1,0:T(...) custom-call(bf16[256,256]{1,0:T(8,128)(2,1)S(1)} %copy-done.6, ...), custom_call_target="tpu_custom_call" | custom-call | flops 2147483648 | bytes 25165824 | tf_op jit(solution)/shard_map/pallas_call | solution.py:262
  235.5 11.8 %shard_map.81 = (f32[4,8,128,128]{3,2,1,0:T(8,128)}, f32[4,4,128,128]{3,2,1,0:T(8,128)S(1)}, f32[4,4,128,128]{3,2,1,0:T(8,128)S(1)}, f32[4,8,128,128]{3,2,1,0:T(...) custom-call(bf16[256,256]{1,0:T(8,128)(2,1)S(1)} %copy-done.6, ...), custom_call_target="tpu_custom_call", output_to_operand_aliasing={{0}: (11, {}), {1}: (12, {}), {2}: (13, {}), {3}: (14, {}),... | custom-call | flops 2147483648 | bytes 25165824 | tf_op jit(solution)/shard_map/pallas_call | solution.py:262
  247.3 3.4 collective-permute-start.15
  251.2 2.1 collective-permute-start.21
  254.2 9.9 %collective-permute-done.15 = f32[4,4,128,128]{3,2,1,0:T(8,128)S(1)} collective-permute-done((f32[4,4,128,128]{3,2,1,0:T(8,128)S(1)}, f32[4,4,128,128]{3,2,1,0:T(8,128)S(1)}, u32[]{:S(2)}, u32[]{:S(2)}) %collective-permute-start.15) | collective-permute-done | bytes 1048608 | tf_op jit(solution)/shard_map/ppermute | solution.py:298
  264.6 9.7 %collective-permute-done.16 = f32[4,4,128,128]{3,2,1,0:T(8,128)S(1)} collective-permute-done((f32[4,4,128,128]{3,2,1,0:T(8,128)S(1)}, f32[4,4,128,128]{3,2,1,0:T(8,128)S(1)}, u32[]{:S(2)}, u32[]{:S(2)}) %collective-permute-start.16) | collective-permute-done | bytes 1048608 | tf_op jit(solution)/shard_map/ppermute | solution.py:298
  274.4 5.2 %collective-permute-done.17 = f32[4,4,128,128]{3,2,1,0:T(8,128)S(1)} collective-permute-done((f32[4,4,128,128]{3,2,1,0:T(8,128)S(1)}, f32[4,4,128,128]{3,2,1,0:T(8,128)S(1)}, u32[]{:S(2)}, u32[]{:S(2)}) %collective-permute-start.17) | collective-permute-done | bytes 1048608 | tf_op jit(solution)/shard_map/ppermute | solution.py:289
  279.8 21.5 %collective-permute-done.18 = f32[4,4,128,128]{3,2,1,0:T(8,128)S(1)} collective-permute-done((f32[4,4,128,128]{3,2,1,0:T(8,128)S(1)}, f32[4,4,128,128]{3,2,1,0:T(8,128)S(1)}, u32[]{:S(2)}, u32[]{:S(2)}) %collective-permute-start.18) | collective-permute-done | bytes 1048608 | tf_op jit(solution)/shard_map/ppermute | solution.py:289
  301.6 2.5 pad_maximum_fusion.3
  304.7 2.4 collective-permute-start.22
  307.2 13.1 %collective-permute-start.23 = (f32[4,8,128,128]{3,2,1,0:T(8,128)}, f32[4,8,128,128]{3,2,1,0:T(8,128)}, u32[]{:S(2)}, u32[]{:S(2)}) collective-permute-start(f32[4,8,128,128]{3,2,1,0:T(8,128)} %get-tuple-element.58), channel_id=1, source_target_pairs={{0,17},{1,0},{2,19},{3,2},{4,21},{5,4},{6,23},{7,6},{8,25},{9,8},{... | collective-permute-start | bytes 6291464 | tf_op jit(solution)/shard_map/ppermute | solution.py:298
  322.1 45.4 %collective-permute-done.25 = f32[2,8,128,128]{3,2,1,0:T(8,128)} collective-permute-done((f32[2,8,128,128]{3,2,1,0:T(8,128)}, f32[2,8,128,128]{3,2,1,0:T(8,128)}, u32[]{:S(2)}, u32[]{:S(2)}) %collective-permute-start.25) | collective-permute-done | bytes 1048608 | tf_op jit(solution)/shard_map/ppermute | solution.py:289
  367.5 1.8 maximum_select_fusion
  369.3 3.2 add.132
  372.5 1.4 slice_add_fusion
  374.1 1.2 slice_bitcast_fusion.5
  375.3 3.4 collective-permute-start.26
  380.3 1.5 collective-permute-start.28
  381.7 1.3 slice_bitcast_fusion
  383.1 29.7 %collective-permute-done.26 = f32[8,128,128]{2,1,0:T(8,128)} collective-permute-done((f32[8,128,128]{2,1,0:T(8,128)}, f32[8,128,128]{2,1,0:T(8,128)}, u32[]{:S(2)}, u32[]{:S(2)}) %collective-permute-start.26) | collective-permute-done | bytes 524320 | tf_op jit(solution)/shard_map/ppermute | solution.py:289
  413.9 11.0 %collective-permute-done.28 = f32[8,128,128]{2,1,0:T(8,128)S(1)} collective-permute-done((f32[8,128,128]{2,1,0:T(8,128)}, f32[8,128,128]{2,1,0:T(8,128)S(1)}, u32[]{:S(2)}, u32[]{:S(2)}) %collective-permute-start.28) | collective-permute-done | bytes 524320 | tf_op jit(solution)/shard_map/ppermute | solution.py:289
  426.2 1.5 copy.17
  (91 shorter events, 13.6 us)
Async XLA Ops:
  0.6 2.4 copy-start.13
  2.4 49.3 %collective-permute-start.3 = (f32[2,8,128,128]{3,2,1,0:T(8,128)S(1)}, f32[2,8,128,128]{3,2,1,0:T(8,128)}, u32[]{:S(2)}, u32[]{:S(2)}) collective-permute-start(f32[2,8,128,128]{3,2,1,0:T(8,128)S(1)} %get-tuple-element.75), channel_id=1, source_target_pairs={{2,0},{3,1},{0,2},{1,3},{6,4},{7,5},{4,6},{5,7},{10,8},{11,9},{8,1... | collective-permute-start | bytes 3145736 | tf_op jit(solution)/shard_map/ppermute | solution.py:289
  3.1 36.1 %collective-permute-start.1 = (f32[8,128,128]{2,1,0:T(8,128)S(1)}, f32[8,128,128]{2,1,0:T(8,128)S(1)}, u32[]{:S(2)}, u32[]{:S(2)}) collective-permute-start(f32[8,128,128]{2,1,0:T(8,128)S(1)} %bitcast.54), channel_id=1, source_target_pairs={{8,0},{9,1},{10,2},{11,3},{12,4},{13,5},{14,6},{15,7},{0,8},{1,9},... | collective-permute-start | bytes 1572872 | tf_op jit(solution)/shard_map/ppermute | solution.py:289
  5.8 44.5 %collective-permute-start.2 = (f32[8,128,128]{2,1,0:T(8,128)S(1)}, f32[8,128,128]{2,1,0:T(8,128)S(1)}, u32[]{:S(2)}, u32[]{:S(2)}) collective-permute-start(f32[8,128,128]{2,1,0:T(8,128)S(1)} %get-tuple-element.77), channel_id=1, source_target_pairs={{12,0},{13,1},{14,2},{15,3},{8,4},{9,5},{10,6},{11,7},{4,8},{5,9},... | collective-permute-start | bytes 1572872 | tf_op jit(solution)/shard_map/ppermute | solution.py:289
  5.8 44.5 %collective-permute-start = (f32[8,128,128]{2,1,0:T(8,128)S(1)}, f32[8,128,128]{2,1,0:T(8,128)S(1)}, u32[]{:S(2)}, u32[]{:S(2)}) collective-permute-start(f32[8,128,128]{2,1,0:T(8,128)S(1)} %get-tuple-element.77), channel_id=1, source_target_pairs={{4,0},{5,1},{6,2},{7,3},{0,4},{1,5},{2,6},{3,7},{12,8},{13,9},{14,... | collective-permute-start | bytes 1572872 | tf_op jit(solution)/shard_map/ppermute | solution.py:289
  54.6 50.8 %collective-permute-start.6 = (f32[4,8,128,128]{3,2,1,0:T(8,128)}, f32[4,8,128,128]{3,2,1,0:T(8,128)S(1)}, u32[]{:S(2)}, u32[]{:S(2)}) collective-permute-start(f32[4,8,128,128]{3,2,1,0:T(8,128)} %pad_maximum_fusion), channel_id=1, source_target_pairs={{17,0},{0,1},{19,2},{2,3},{21,4},{4,5},{23,6},{6,7},{25,8},{8,9},{... | collective-permute-start | bytes 6291464 | tf_op jit(solution)/shard_map/ppermute | solution.py:298
  54.6 50.8 %collective-permute-start.5 = (f32[4,8,128,128]{3,2,1,0:T(8,128)}, f32[4,8,128,128]{3,2,1,0:T(8,128)}, u32[]{:S(2)}, u32[]{:S(2)}) collective-permute-start(f32[4,8,128,128]{3,2,1,0:T(8,128)} %pad_maximum_fusion), channel_id=1, source_target_pairs={{16,0},{1,1},{18,2},{3,3},{20,4},{5,5},{22,6},{7,7},{24,8},{9,9},{... | collective-permute-start | bytes 6291464 | tf_op jit(solution)/shard_map/ppermute | solution.py:298
  58.0 47.4 %collective-permute-start.4 = (f32[4,8,128,128]{3,2,1,0:T(8,128)}, f32[4,8,128,128]{3,2,1,0:T(8,128)}, u32[]{:S(2)}, u32[]{:S(2)}) collective-permute-start(f32[4,8,128,128]{3,2,1,0:T(8,128)} %pad_maximum_fusion), channel_id=1, source_target_pairs={{2,0},{3,1},{0,2},{1,3},{6,4},{7,5},{4,6},{5,7},{10,8},{11,9},{8,1... | collective-permute-start | bytes 6291464 | tf_op jit(solution)/shard_map/ppermute | solution.py:289
  61.3 42.6 %collective-permute-start.7 = (f32[2,8,128,128]{3,2,1,0:T(8,128)S(1)}, f32[2,8,128,128]{3,2,1,0:T(8,128)S(1)}, u32[]{:S(2)}, u32[]{:S(2)}) collective-permute-start(f32[2,8,128,128]{3,2,1,0:T(8,128)S(1)} %get-tuple-element.73), channel_id=1, source_target_pairs={{8,0},{9,1},{10,2},{11,3},{12,4},{13,5},{14,6},{15,7},{0,8},{1,9},... | collective-permute-start | bytes 3145736 | tf_op jit(solution)/shard_map/ppermute | solution.py:289
  105.4 51.6 %copy-start.15 = (bf16[16,8,128]{2,1,0:T(8,128)(2,1)S(1)}, bf16[16,8,128]{2,1,0:T(8,128)(2,1)}, u32[]{:S(2)}) copy-start(bf16[16,8,128]{2,1,0:T(8,128)(2,1)} %constant.94.clone.1) | copy-start | bytes 98308
  105.4 52.1 %copy-start.14 = (bf16[16,8,128]{2,1,0:T(8,128)(2,1)S(1)}, bf16[16,8,128]{2,1,0:T(8,128)(2,1)}, u32[]{:S(2)}) copy-start(bf16[16,8,128]{2,1,0:T(8,128)(2,1)} %constant.93.clone.1) | copy-start | bytes 98308
  105.4 91.5 %copy-start = (f32[4,8,128,128]{3,2,1,0:T(8,128)}, f32[4,8,128,128]{3,2,1,0:T(8,128)S(1)}, u32[]{:S(2)}) copy-start(f32[4,8,128,128]{3,2,1,0:T(8,128)S(1)} %collective-permute-done.6.refs_3_) | copy-start | bytes 6291460
  105.4 49.4 %collective-permute-start.13 = (f32[4,8,128,128]{3,2,1,0:T(8,128)}, f32[4,8,128,128]{3,2,1,0:T(8,128)}, u32[]{:S(2)}, u32[]{:S(2)}) collective-permute-start(f32[4,8,128,128]{3,2,1,0:T(8,128)} %bitcast.15.refs_6_), channel_id=1, source_target_pairs={{4,0},{5,1},{6,2},{7,3},{0,4},{1,5},{2,6},{3,7},{12,8},{13,9},{14,... | collective-permute-start | bytes 6291464 | tf_op jit(solution)/shard_map/ppermute | solution.py:289
  111.4 52.3 %collective-permute-start.11 = (f32[4,4,128,128]{3,2,1,0:T(8,128)}, f32[4,4,128,128]{3,2,1,0:T(8,128)S(1)}, u32[]{:S(2)}, u32[]{:S(2)}) collective-permute-start(f32[4,4,128,128]{3,2,1,0:T(8,128)} %slice.54), channel_id=1, source_target_pairs={{2,0},{3,1},{0,2},{1,3},{6,4},{7,5},{4,6},{5,7},{10,8},{11,9},{8,1... | collective-permute-start | bytes 3145736 | tf_op jit(solution)/shard_map/ppermute | solution.py:289
  111.9 75.8 %collective-permute-start.12 = (f32[4,8,128,128]{3,2,1,0:T(8,128)}, f32[4,8,128,128]{3,2,1,0:T(8,128)}, u32[]{:S(2)}, u32[]{:S(2)}) collective-permute-start(f32[4,8,128,128]{3,2,1,0:T(8,128)} %bitcast.15.refs_6_), channel_id=1, source_target_pairs={{1,0},{0,1},{3,2},{2,3},{5,4},{4,5},{7,6},{6,7},{9,8},{8,9},{11,10... | collective-permute-start | bytes 6291464 | tf_op jit(solution)/shard_map/ppermute | solution.py:289
  154.8 42.1 %collective-permute-start.14 = (f32[4,8,128,128]{3,2,1,0:T(8,128)}, f32[4,8,128,128]{3,2,1,0:T(8,128)}, u32[]{:S(2)}, u32[]{:S(2)}) collective-permute-start(f32[4,8,128,128]{3,2,1,0:T(8,128)} %collective-permute-done.13.refs_6_), channel_id=1, source_target_pairs={{1,0},{0,1},{3,2},{2,3},{5,4},{4,5},{7,6},{6,7},{9,8},{8,9},{11,10... | collective-permute-start | bytes 6291464 | tf_op jit(solution)/shard_map/ppermute | solution.py:289
  159.8 27.9 %collective-permute-start.10 = (f32[4,4,128,128]{3,2,1,0:T(8,128)S(1)}, f32[4,4,128,128]{3,2,1,0:T(8,128)S(1)}, u32[]{:S(2)}, u32[]{:S(2)}) collective-permute-start(f32[4,4,128,128]{3,2,1,0:T(8,128)S(1)} %slice.52), channel_id=1, source_target_pairs={{17,0},{0,1},{19,2},{2,3},{21,4},{4,5},{23,6},{6,7},{25,8},{8,9},{... | collective-permute-start | bytes 3145736 | tf_op jit(solution)/shard_map/ppermute | solution.py:298
  159.9 27.8 %collective-permute-start.8 = (f32[4,4,128,128]{3,2,1,0:T(8,128)S(1)}, f32[4,4,128,128]{3,2,1,0:T(8,128)S(1)}, u32[]{:S(2)}, u32[]{:S(2)}) collective-permute-start(f32[4,4,128,128]{3,2,1,0:T(8,128)S(1)} %slice.52), channel_id=1, source_target_pairs={{16,0},{1,1},{18,2},{3,3},{20,4},{5,5},{22,6},{7,7},{24,8},{9,9},{... | collective-permute-start | bytes 3145736 | tf_op jit(solution)/shard_map/ppermute | solution.py:298
  163.6 24.1 %copy-start.6 = (bf16[256,256]{1,0:T(8,128)(2,1)S(1)}, bf16[256,256]{1,0:T(8,128)(2,1)}, u32[]{:S(2)}) copy-start(bf16[256,256]{1,0:T(8,128)(2,1)} %constant.88.clone.right_ref) | copy-start | bytes 393220
  163.6 24.1 %copy-start.7 = (bf16[256,256]{1,0:T(8,128)(2,1)S(1)}, bf16[256,256]{1,0:T(8,128)(2,1)}, u32[]{:S(2)}) copy-start(bf16[256,256]{1,0:T(8,128)(2,1)} %constant.87.clone.left_ref) | copy-start | bytes 393220
  163.6 33.3 %copy-start.1 = (f32[4,4,128,128]{3,2,1,0:T(8,128)}, f32[4,4,128,128]{3,2,1,0:T(8,128)S(1)}, u32[]{:S(2)}) copy-start(f32[4,4,128,128]{3,2,1,0:T(8,128)S(1)} %collective-permute-done.11.refs_5_) | copy-start | bytes 3145732
  163.7 24.0 %collective-permute-start.9 = (f32[4,4,128,128]{3,2,1,0:T(8,128)S(1)}, f32[4,4,128,128]{3,2,1,0:T(8,128)S(1)}, u32[]{:S(2)}, u32[]{:S(2)}) collective-permute-start(f32[4,4,128,128]{3,2,1,0:T(8,128)S(1)} %slice.53), channel_id=1, source_target_pairs={{2,0},{3,1},{0,2},{1,3},{6,4},{7,5},{4,6},{5,7},{10,8},{11,9},{8,1... | collective-permute-start | bytes 3145736 | tf_op jit(solution)/shard_map/ppermute | solution.py:289
  187.7 9.3 %copy-start.3 = (f32[4,4,128,128]{3,2,1,0:T(8,128)}, f32[4,4,128,128]{3,2,1,0:T(8,128)S(1)}, u32[]{:S(2)}) copy-start(f32[4,4,128,128]{3,2,1,0:T(8,128)S(1)} %collective-permute-done.9.refs_2_) | copy-start | bytes 3145732
  187.7 9.3 %copy-start.2 = (f32[4,4,128,128]{3,2,1,0:T(8,128)}, f32[4,4,128,128]{3,2,1,0:T(8,128)S(1)}, u32[]{:S(2)}) copy-start(f32[4,4,128,128]{3,2,1,0:T(8,128)S(1)} %collective-permute-done.10.refs_4_) | copy-start | bytes 3145732
  219.8 2.0 copy-start.4
  221.7 2.0 copy-start.5
  235.4 15.4 %collective-permute-start.20 = (f32[4,8,128,128]{3,2,1,0:T(8,128)}, f32[4,8,128,128]{3,2,1,0:T(8,128)S(1)}, u32[]{:S(2)}, u32[]{:S(2)}) collective-permute-start(f32[4,8,128,128]{3,2,1,0:T(8,128)} %get-tuple-element.56), channel_id=1, source_target_pairs={{1,0},{0,1},{3,2},{2,3},{5,4},{4,5},{7,6},{6,7},{9,8},{8,9},{11,10... | collective-permute-start | bytes 6291464 | tf_op jit(solution)/shard_map/ppermute | solution.py:289
  235.5 15.4 %copy-start.11 = (f32[4,8,128,128]{3,2,1,0:T(8,128)S(1)}, f32[4,8,128,128]{3,2,1,0:T(8,128)}, u32[]{:S(2)}) copy-start(f32[4,8,128,128]{3,2,1,0:T(8,128)} %get-tuple-element.55) | copy-start | bytes 6291460
  247.3 16.7 %collective-permute-start.15 = (f32[4,4,128,128]{3,2,1,0:T(8,128)S(1)}, f32[4,4,128,128]{3,2,1,0:T(8,128)S(1)}, u32[]{:S(2)}, u32[]{:S(2)}) collective-permute-start(f32[4,4,128,128]{3,2,1,0:T(8,128)S(1)} %get-tuple-element.47), channel_id=1, source_target_pairs={{0,16},{1,1},{2,18},{3,3},{4,20},{5,5},{6,22},{7,7},{8,24},{9,9},{... | collective-permute-start | bytes 3145736 | tf_op jit(solution)/shard_map/ppermute | solution.py:298
  250.8 53.3 %collective-permute-start.19 = (f32[4,8,128,128]{3,2,1,0:T(8,128)}, f32[4,8,128,128]{3,2,1,0:T(8,128)S(1)}, u32[]{:S(2)}, u32[]{:S(2)}) collective-permute-start(f32[4,8,128,128]{3,2,1,0:T(8,128)} %get-tuple-element.54), channel_id=1, source_target_pairs={{1,0},{0,1},{3,2},{2,3},{5,4},{4,5},{7,6},{6,7},{9,8},{8,9},{11,10... | collective-permute-start | bytes 6291464 | tf_op jit(solution)/shard_map/ppermute | solution.py:289
  251.2 28.4 %copy-start.8 = (f32[4,8,128,128]{3,2,1,0:T(8,128)S(1)}, f32[4,8,128,128]{3,2,1,0:T(8,128)}, u32[]{:S(2)}) copy-start(f32[4,8,128,128]{3,2,1,0:T(8,128)} %get-tuple-element.49) | copy-start | bytes 6291460
  251.2 52.9 %collective-permute-start.21 = (f32[4,8,128,128]{3,2,1,0:T(8,128)S(1)}, f32[4,8,128,128]{3,2,1,0:T(8,128)S(1)}, u32[]{:S(2)}, u32[]{:S(2)}) collective-permute-start(f32[4,8,128,128]{3,2,1,0:T(8,128)S(1)} %add.130), channel_id=1, source_target_pairs={{4,0},{5,1},{6,2},{7,3},{0,4},{1,5},{2,6},{3,7},{12,8},{13,9},{14,... | collective-permute-start | bytes 6291464 | tf_op jit(solution)/shard_map/ppermute | solution.py:289
  253.3 21.0 %collective-permute-start.16 = (f32[4,4,128,128]{3,2,1,0:T(8,128)S(1)}, f32[4,4,128,128]{3,2,1,0:T(8,128)S(1)}, u32[]{:S(2)}, u32[]{:S(2)}) collective-permute-start(f32[4,4,128,128]{3,2,1,0:T(8,128)S(1)} %get-tuple-element.48), channel_id=1, source_target_pairs={{0,17},{1,0},{2,19},{3,2},{4,21},{5,4},{6,23},{7,6},{8,25},{9,8},{... | collective-permute-start | bytes 3145736 | tf_op jit(solution)/shard_map/ppermute | solution.py:298
  253.6 26.0 %collective-permute-start.17 = (f32[4,4,128,128]{3,2,1,0:T(8,128)S(1)}, f32[4,4,128,128]{3,2,1,0:T(8,128)S(1)}, u32[]{:S(2)}, u32[]{:S(2)}) collective-permute-start(f32[4,4,128,128]{3,2,1,0:T(8,128)S(1)} %get-tuple-element.50), channel_id=1, source_target_pairs={{2,0},{3,1},{0,2},{1,3},{6,4},{7,5},{4,6},{5,7},{10,8},{11,9},{8,1... | collective-permute-start | bytes 3145736 | tf_op jit(solution)/shard_map/ppermute | solution.py:289
  264.0 37.3 %collective-permute-start.18 = (f32[4,4,128,128]{3,2,1,0:T(8,128)S(1)}, f32[4,4,128,128]{3,2,1,0:T(8,128)S(1)}, u32[]{:S(2)}, u32[]{:S(2)}) collective-permute-start(f32[4,4,128,128]{3,2,1,0:T(8,128)S(1)} %get-tuple-element.52), channel_id=1, source_target_pairs={{2,0},{3,1},{0,2},{1,3},{6,4},{7,5},{4,6},{5,7},{10,8},{11,9},{8,1... | collective-permute-start | bytes 3145736 | tf_op jit(solution)/shard_map/ppermute | solution.py:289
  279.6 21.7 %copy-start.9 = (f32[4,8,128,128]{3,2,1,0:T(8,128)S(1)}, f32[4,8,128,128]{3,2,1,0:T(8,128)}, u32[]{:S(2)}) copy-start(f32[4,8,128,128]{3,2,1,0:T(8,128)} %get-tuple-element.51) | copy-start | bytes 6291460
  301.6 2.6 copy-start.12
  304.7 64.5 %collective-permute-start.22 = (f32[4,8,128,128]{3,2,1,0:T(8,128)}, f32[4,8,128,128]{3,2,1,0:T(8,128)}, u32[]{:S(2)}, u32[]{:S(2)}) collective-permute-start(f32[4,8,128,128]{3,2,1,0:T(8,128)} %get-tuple-element.57), channel_id=1, source_target_pairs={{0,16},{1,1},{2,18},{3,3},{4,20},{5,5},{6,22},{7,7},{8,24},{9,9},{... | collective-permute-start | bytes 6291464 | tf_op jit(solution)/shard_map/ppermute | solution.py:298
  307.2 62.1 %collective-permute-start.23 = (f32[4,8,128,128]{3,2,1,0:T(8,128)}, f32[4,8,128,128]{3,2,1,0:T(8,128)}, u32[]{:S(2)}, u32[]{:S(2)}) collective-permute-start(f32[4,8,128,128]{3,2,1,0:T(8,128)} %get-tuple-element.58), channel_id=1, source_target_pairs={{0,17},{1,0},{2,19},{3,2},{4,21},{5,4},{6,23},{7,6},{8,25},{9,8},{... | collective-permute-start | bytes 6291464 | tf_op jit(solution)/shard_map/ppermute | solution.py:298
  321.3 46.2 %collective-permute-start.25 = (f32[2,8,128,128]{3,2,1,0:T(8,128)}, f32[2,8,128,128]{3,2,1,0:T(8,128)}, u32[]{:S(2)}, u32[]{:S(2)}) collective-permute-start(f32[2,8,128,128]{3,2,1,0:T(8,128)} %slice_bitcast_fusion.2), channel_id=1, source_target_pairs={{8,0},{9,1},{10,2},{11,3},{12,4},{13,5},{14,6},{15,7},{0,8},{1,9},... | collective-permute-start | bytes 3145736 | tf_op jit(solution)/shard_map/ppermute | solution.py:289
  321.3 51.2 %collective-permute-start.24 = (f32[4,4,128,128]{3,2,1,0:T(8,128)S(1)}, f32[4,4,128,128]{3,2,1,0:T(8,128)}, u32[]{:S(2)}, u32[]{:S(2)}) collective-permute-start(f32[4,4,128,128]{3,2,1,0:T(8,128)S(1)} %add.126), channel_id=1, source_target_pairs={{2,0},{3,1},{0,2},{1,3},{6,4},{7,5},{4,6},{5,7},{10,8},{11,9},{8,1... | collective-permute-start | bytes 3145736 | tf_op jit(solution)/shard_map/ppermute | solution.py:289
  369.3 9.4 %copy-start.10 = (f32[2,2,8,128,128]{4,3,2,0,1:T(8,128)}, f32[2,2,8,128,128]{4,3,2,0,1:T(8,128)S(1)}, u32[]{:S(2)}) copy-start(f32[2,2,8,128,128]{4,3,2,0,1:T(8,128)S(1)} %maximum_select_fusion) | copy-start | bytes 6291460
  375.3 37.5 %collective-permute-start.26 = (f32[8,128,128]{2,1,0:T(8,128)}, f32[8,128,128]{2,1,0:T(8,128)}, u32[]{:S(2)}, u32[]{:S(2)}) collective-permute-start(f32[8,128,128]{2,1,0:T(8,128)} %get-tuple-element.63), channel_id=1, source_target_pairs={{8,0},{9,1},{10,2},{11,3},{12,4},{13,5},{14,6},{15,7},{0,8},{1,9},... | collective-permute-start | bytes 1572872 | tf_op jit(solution)/shard_map/ppermute | solution.py:289
  379.7 46.2 %collective-permute-start.29 = (f32[2,8,128,128]{3,2,1,0:T(8,128)}, f32[2,8,128,128]{3,2,1,0:T(8,128)S(1)}, u32[]{:S(2)}, u32[]{:S(2)}) collective-permute-start(f32[2,8,128,128]{3,2,1,0:T(8,128)} %slice_bitcast_fusion.1), channel_id=1, source_target_pairs={{2,0},{3,1},{0,2},{1,3},{6,4},{7,5},{4,6},{5,7},{10,8},{11,9},{8,1... | collective-permute-start | bytes 3145736 | tf_op jit(solution)/shard_map/ppermute | solution.py:289
  380.3 44.6 %collective-permute-start.28 = (f32[8,128,128]{2,1,0:T(8,128)}, f32[8,128,128]{2,1,0:T(8,128)S(1)}, u32[]{:S(2)}, u32[]{:S(2)}) collective-permute-start(f32[8,128,128]{2,1,0:T(8,128)} %get-tuple-element.64), channel_id=1, source_target_pairs={{12,0},{13,1},{14,2},{15,3},{8,4},{9,5},{10,6},{11,7},{4,8},{5,9},... | collective-permute-start | bytes 1572872 | tf_op jit(solution)/shard_map/ppermute | solution.py:289
  381.7 43.1 %collective-permute-start.27 = (f32[8,128,128]{2,1,0:T(8,128)}, f32[8,128,128]{2,1,0:T(8,128)S(1)}, u32[]{:S(2)}, u32[]{:S(2)}) collective-permute-start(f32[8,128,128]{2,1,0:T(8,128)} %get-tuple-element.65), channel_id=1, source_target_pairs={{4,0},{5,1},{6,2},{7,3},{0,4},{1,5},{2,6},{3,7},{12,8},{13,9},{14,... | collective-permute-start | bytes 1572872 | tf_op jit(solution)/shard_map/ppermute | solution.py:289

commit v4 on v3

--- a/solution.py
+++ b/solution.py
@@ -111,28 +111,20 @@
     return both[: both.shape[0] // 2] + both[both.shape[0] // 2 :]
 
 
-def slab_pieces(step, refs):
-    first, fx_a, fx_b, second, sx_a, sx_b, parts, parts_c = refs
-    return [
-        (0, (first,), parts),
-        (1, (fx_a, fx_b), parts),
-        (2, (second,), parts_c),
-        (3, (sx_a, sx_b), parts_c),
-    ]
+def slab_pieces(refs):
+    first, first_x, second, second_x, parts, parts_c = refs
+    return [(first, parts), (first_x, parts), (second, parts_c), (second_x, parts_c)]
 
 
 def gather_kernel(right_ref, left_ref, *refs):
-    pieces, out_ref, pair_ref = refs[:8], refs[8], refs[9]
+    pieces, out_ref, pair_ref = refs[:6], refs[6], refs[7]
     step = pl.program_id(0)
     rows, length = pair_ref.shape[0], pair_ref.shape[1]
-    for turn, own_refs, part_ref in slab_pieces(step, pieces):
+    for turn, (own_ref, part_ref) in enumerate(slab_pieces(pieces)):
 
         @pl.when(step // 2 == turn)
-        def _(own_refs=own_refs, part_ref=part_ref):
-            count = rows // len(own_refs)
-            for k, own_ref in enumerate(own_refs):
-                span = pl.ds(k * count, count)
-                pair_ref[span] = own_ref[0] * part_ref[0, span]
+        def _(own_ref=own_ref, part_ref=part_ref):
+            pair_ref[...] = own_ref[0] * part_ref[0]
 
     flat_out = out_ref.reshape(rows * length, length)
     for r in range(0, rows, 2):
@@ -162,7 +154,7 @@
 
 
 def scatter_kernel(right_ref, left_ref, field_ref, *refs):
-    pieces, outs, pot_ref = refs[:8], refs[-9:-1], refs[-1]
+    pieces, outs, pot_ref = refs[:6], refs[-7:-1], refs[-1]
     step = pl.program_id(0)
     rows, length = pot_ref.shape[0], pot_ref.shape[1]
     flat = field_ref.reshape(rows * length, length)
@@ -173,23 +165,18 @@
         block = along_y(block, left_ref[...])
         block = jnp.concatenate([block[:, :length], block[:, length:]], 0)
         pot_ref[pl.ds(r, 2)] = along_x(block, right_ref[...]).reshape(2, length, length)
-    for (turn, own_refs, part_ref), (_, own_outs, part_out) in zip(
-        slab_pieces(step, pieces), slab_pieces(step, outs)
-    ):
+    for turn, (piece, out) in enumerate(zip(slab_pieces(pieces), slab_pieces(outs))):
 
         @pl.when(step // 2 == turn)
-        def _(own_refs=own_refs, part_ref=part_ref, own_outs=own_outs, part_out=part_out):
-            count = rows // len(own_refs)
-            for k, (own_ref, own_out) in enumerate(zip(own_refs, own_outs)):
-                span = pl.ds(k * count, count)
-                own_out[0] = pot_ref[span] * part_ref[0, span]
-                part_out[0, span] = pot_ref[span] * own_ref[0]
+        def _(piece=piece, out=out):
+            out[0][0] = pot_ref[...] * piece[1][0]
+            out[1][0] = pot_ref[...] * piece[0][0]
 
 
 def piece_specs(rows, length, z_low):
-    def own_spec(turn, count):
+    def own_spec(turn):
         return pl.BlockSpec(
-            (1, count, length, length),
+            (1, rows, length, length),
             lambda i: (jnp.clip(i - 2 * turn, 0, 1) * 2 + z_low, 0, 0, 0),
         )
 
@@ -198,12 +185,7 @@
             (1, rows, length, length), lambda i: (jnp.clip(i - 4 * core, 0, 3), 0, 0, 0)
         )
 
-    half = rows // 2
-    return [
-        own_spec(0, rows), own_spec(1, half), own_spec(1, half),
-        own_spec(2, rows), own_spec(3, half), own_spec(3, half),
-        part_spec(0), part_spec(1),
-    ]
+    return [own_spec(turn) for turn in range(4)] + [part_spec(core) for core in range(2)]
 
 
 def fixed_spec(shape):
@@ -232,7 +214,7 @@
         out_specs=pl.BlockSpec((length, rows, length), lambda i: (0, i, 0)),
         out_shape=jax.ShapeDtypeStruct((length, 8 * rows, length), jnp.float32),
         scratch_shapes=[pltpu.VMEM((rows, length, length), jnp.float32)],
-        compiler_params=settings(32),
+        compiler_params=settings(16),
         cost_estimate=cost(length, 2, 1),
     )(right, left, *pieces)
 
@@ -250,7 +232,7 @@
         ],
         out_specs=[block, block],
         out_shape=[jax.ShapeDtypeStruct(a.shape, jnp.float32)] * 2,
-        compiler_params=settings(32),
+        compiler_params=settings(12),
         cost_estimate=cost(length, 3, 2),
     )(left, back, coulomb_table, a, b)
 
@@ -270,9 +252,9 @@
         + [pl.BlockSpec(memory_space=pl.ANY)] * count,
         out_specs=specs,
         out_shape=[jax.ShapeDtypeStruct(piece.shape, jnp.float32) for piece in pieces],
-        input_output_aliases={11 + k: k for k in range(count)},
+        input_output_aliases={9 + k: k for k in range(count)},
         scratch_shapes=[pltpu.VMEM((rows, length, length), jnp.float32)],
-        compiler_params=settings(48),
+        compiler_params=settings(24),
         cost_estimate=cost(length, 3, 1),
     )(right, left, field, *pieces, *held)
 
@@ -280,13 +262,18 @@
 def whole_fields(own, partners, groups, slabs):
     length = own.shape[3]
     rows = own.shape[1]
-    half = rows // 2
     plane = own.shape[2:]
     me = lax.axis_index("slab")
     part_half, own_band, part_low = (me >> 3) & 1, (me >> 2) & 1, (me >> 1) & 1
 
+    at_home = ((me & 1) + 1) % groups == 0
+
     def swap(block, mask):
         return lax.ppermute(block, "slab", [(i ^ mask, i) for i in range(slabs)])
+
+    def swap_away(block, mask):
+        away = [i for i in range(slabs) if ((i & 1) + 1) % groups != 0]
+        return lax.ppermute(block, "slab", [(i ^ mask, i) for i in away])
 
     def across(block, flip, back):
         route = []
@@ -294,7 +281,8 @@
             for i in range(slabs):
                 source = ((b + 1 + (i & 1)) % groups) * slabs + (i ^ flip)
                 target = b * slabs + i
-                route.append((target, source) if back else (source, target))
+                if source != target:
+                    route.append((target, source) if back else (source, target))
         return lax.ppermute(block, ("band", "slab"), route)
 
     def pick(block, position, axis=0):
@@ -336,30 +324,32 @@
     bands_x, first, second, parts = together(bands_x, first, second, parts)
     parts = parts.reshape((4, rows) + plane)
     parts_z, parts_c = swap(parts, 4), swap(parts, 1)
-    fx_a, fx_b = across(bands_x[:, :half], 0, False), swap(first[:, half:], 2)
-    sx_a, sx_b = across(bands_x[:, :half], 1, False), swap(second[:, half:], 2)
-    own_pieces = [first, fx_a, fx_b, second, sx_a, sx_b]
+    first_x, second_x = swap_away(first, 2), across(bands_x, 1, False)
+    first = jnp.where(at_home, bands, first)
+    first_x = jnp.where(at_home, bands_x, first_x)
+    own_pieces = [first, first_x, second, second_x]
     even = own_pieces + [parts, parts_c]
     field_even = gather_half(right, left, even, 0)
+    parts_z, field_even = together(parts_z, field_even)
     odd = own_pieces + [parts_z, swap(parts_z, 1)]
     field_odd = gather_half(right, left, odd, 1)
 
     field_even, field_odd = columns(z_left, z_back, coulomb_table, field_even, field_odd)
 
     *own_pieces, parts_z, parts_zc = scatter_half(right, left, field_odd, odd, 1, [])
-    parts_z = parts_z + swap(parts_zc, 1)
-    parts_z = swap(parts_z, 4)
+    parts_zc = swap(parts_zc, 1)
     *own_pieces, parts, parts_c = scatter_half(right, left, field_even, even, 0, own_pieces)
-    first, fx_a, fx_b, second, sx_a, sx_b = own_pieces
-    bands_x = across(fx_a, 0, True) + across(sx_a, 1, True)
-    fx_b, sx_b = swap(fx_b, 2), swap(sx_b, 2)
+    *own_pieces, parts, parts_c, parts_z, parts_zc = together(
+        *own_pieces, parts, parts_c, parts_z, parts_zc
+    )
+    parts_z = swap(parts_z + parts_zc, 4)
+    first, first_x, second, second_x = own_pieces
+    bands_x = across(second_x, 1, True) + jnp.where(at_home, first_x, 0.0)
+    first = first + swap_away(first_x, 2)
     parts = (parts + swap(parts_c, 1) + parts_z).reshape((2, 2, rows) + plane)
-    first = jnp.concatenate([first[:, :half], first[:, half:] + fx_b], 1)
-    second = jnp.concatenate([second[:, :half], second[:, half:] + sx_b], 1)
     bands_x, first, second, parts = together(bands_x, first, second, parts)
-    bands = across(first, 0, True) + across(second, 1, True)
-    bands_x = swap(bands_x, 2)
-    bands = jnp.concatenate([bands[:, :half] + bands_x, bands[:, half:]], 1)
+    bands = across(first, 0, True) + across(second, 1, True) + swap(bands_x, 2)
+    bands = bands + jnp.where(at_home, first, 0.0)
     parts = ordered(part_half, parts[:, 0], swap(parts[:, 1], 8), 1)
     bands, parts = together(bands, parts)
     kept = bands[0] + swap(bands[2], 8)

time: 431 us -> 372 us (0.86)
  waiting for transfers between devices: 275 us -> 246 us
  starting transfers between devices: 51.6 us -> 34.7 us
  Pallas kernels: 55.4 us -> 47.7 us
    ppermute x22 -> x18, waiting for transfers between devices: 255 us -> 205 us  [swap(): return lax.ppermute(block, 'slab', [(i ^ mask, i) for i in range(slabs)])]
    ppermute x0 -> x2, waiting for transfers between devices: none -> 41 us  [swap_away(): return lax.ppermute(block, 'slab', [(i ^ mask, i) for i in away])]
    ppermute x8 -> x6, waiting for transfers between devices: 19.6 us -> 0.02 us  [across(): return lax.ppermute(block, ('band', 'slab'), route)]
    ppermute x8 -> x6, starting transfers between devices: 25.2 us -> 7.47 us  [across(): return lax.ppermute(block, ('band', 'slab'), route)]
    ppermute x0 -> x2, starting transfers between devices: none -> 5.82 us  [swap_away(): return lax.ppermute(block, 'slab', [(i ^ mask, i) for i in away])]
    ppermute x22 -> x18, starting transfers between devices: 26.4 us -> 21.4 us  [swap(): return lax.ppermute(block, 'slab', [(i ^ mask, i) for i in range(slabs)])]
  transfers between devices with their start and end apart: 30 -> 26, of which waited for: 12 -> 11; matrix products, arithmetic and copies ran while one was open for 7% -> 6% of each run, Pallas kernels for 5% -> 5%
where the time goes in v4:
time: 372 us; the launch traced here: 370 us
  waiting for transfers between devices  246 us (66%)
  Pallas kernels  47.7 us (13%)
  starting transfers between devices  34.7 us (9%)
  other arithmetic  22.6 us (6%)
  local copies, waits for them, and re-layouts  17.5 us (5%)
    ppermute x18, waiting for transfers between devices, swap(): return lax.ppermute(block, 'slab', [(i ^ mask, i) for i in range(slabs)])  205 us
    ppermute x2, waiting for transfers between devices, swap_away(): return lax.ppermute(block, 'slab', [(i ^ mask, i) for i in away])  41 us
    ppermute x18, starting transfers between devices, swap(): return lax.ppermute(block, 'slab', [(i ^ mask, i) for i in range(slabs)])  21.4 us
    pallas_call x2, Pallas kernels, scatter_half(): pl.pallas_call(scatter_kernel, grid=(8,), in_specs=[fixed_spec(right.shap...  19.4 us
    pallas_call x2, Pallas kernels, gather_half(): pl.pallas_call(gather_kernel, grid=(8,), in_specs=[fixed_spec(right.shape...  18.3 us
    pallas_call x1, Pallas kernels, columns(): pl.pallas_call(column_kernel, grid=(length // count,), in_specs=[fixed_sp...  10 us
    unnamed x30, local copies, waits for them, and re-layouts  7.59 us
    ppermute x6, starting transfers between devices, across(): return lax.ppermute(block, ('band', 'slab'), route)  7.47 us
  transfers between devices with their start and end apart: 26, of which 11 were waited for; matrix products, arithmetic and copies ran while one was open for 6% of the time, Pallas kernels for 5%

profile of v4, /device:TPU:10, one launch (start us, length us, event | category | flops | bytes accessed | tf_op | source)
XLA Modules:
  0.0 369.7 jit_solution(9485632518430007469)
XLA Ops:
  0.6 1.8 dynamic-slice_bitcast_fusion.2
  3.1 2.7 collective-permute-start.1
  5.8 1.8 collective-permute-start
  7.6 31.6 %collective-permute-done.1 = f32[8,128,128]{2,1,0:T(8,128)S(1)} collective-permute-done((f32[8,128,128]{2,1,0:T(8,128)S(1)}, f32[8,128,128]{2,1,0:T(8,128)S(1)}, u32[]{:S(2)}, u32[]{:S(2)}) %collective-permute-start.1) | collective-permute-done | bytes 524320 | tf_op jit(solution)/shard_map/ppermute | solution.py:272
  39.2 11.1 %collective-permute-done.2 = f32[8,128,128]{2,1,0:T(8,128)S(1)} collective-permute-done((f32[8,128,128]{2,1,0:T(8,128)S(1)}, f32[8,128,128]{2,1,0:T(8,128)S(1)}, u32[]{:S(2)}, u32[]{:S(2)}) %collective-permute-start.2) | collective-permute-done | bytes 524320 | tf_op jit(solution)/shard_map/ppermute | solution.py:272
  50.3 1.5 pad_maximum_fusion
  51.8 2.8 pad_maximum_fusion.1
  54.6 3.4 collective-permute-start.5
  58.0 1.6 collective-permute-start.4
  59.5 1.7 constant_dynamic-slice_fusion
  61.3 45.2 %collective-permute-done.7 = f32[2,8,128,128]{3,2,1,0:T(8,128)S(1)} collective-permute-done((f32[2,8,128,128]{3,2,1,0:T(8,128)S(1)}, f32[2,8,128,128]{3,2,1,0:T(8,128)S(1)}, u32[]{:S(2)}, u32[]{:S(2)}) %collective-permute-start.7) | collective-permute-done | bytes 1048608 | tf_op jit(solution)/shard_map/ppermute | solution.py:272
  106.5 1.5 pad_maximum_fusion.2
  108.0 1.4 copy-done.2
  109.4 2.4 collective-permute-start.9
  112.4 4.4 %collective-permute-start.8 = (f32[4,8,128,128]{3,2,1,0:T(8,128)}, f32[4,8,128,128]{3,2,1,0:T(8,128)}, u32[]{:S(2)}, u32[]{:S(2)}) collective-permute-start(f32[4,8,128,128]{3,2,1,0:T(8,128)} %bitcast.15.refs_4_), channel_id=1, source_target_pairs={{4,0},{5,1},{6,2},{7,3},{0,4},{1,5},{2,6},{3,7},{12,8},{13,9},{14,... | collective-permute-start | bytes 6291464 | tf_op jit(solution)/shard_map/ppermute | solution.py:272
  116.8 1.8 broadcast_select_fusion.1.refs_0_
  118.7 18.9 %collective-permute-done.9 = f32[4,8,128,128]{3,2,1,0:T(8,128)} collective-permute-done((f32[4,8,128,128]{3,2,1,0:T(8,128)}, f32[4,8,128,128]{3,2,1,0:T(8,128)}, u32[]{:S(2)}, u32[]{:S(2)}) %collective-permute-start.9) | collective-permute-done | bytes 2097184 | tf_op jit(solution)/shard_map/ppermute | solution.py:276
  137.6 1.8 broadcast_select_fusion.refs_1_
  139.6 9.3 %shard_map.77.a_ref = f32[128,64,128]{2,1,0:T(8,128)S(1)} custom-call(bf16[256,256]{1,0:T(8,128)(2,1)S(1)} %copy-done.9, bf16[256,256]{1,0:T(8,128)(2,1)S(1)} %copy-done.10, f32[4,8,128,128]{3,2,1,0:T(8,128)S(1)} %broadcast_select_fusion.1.refs_0_, f32[4,8,128,128]{3,2,1,0:T(8,128)S(1)} %broadcast_select_fusion.refs_1_, f32[4,8,128,128]{3,2,1,0:T(8,128)S(1)} %copy-done.3, ...), custom_call_target="tpu_custom_call" | custom-call | flops 2147483648 | bytes 16777216 | tf_op jit(solution)/shard_map/pallas_call | solution.py:210
  149.0 2.0 copy-done.5
  150.9 12.2 %collective-permute-done.8.refs_4_ = f32[4,8,128,128]{3,2,1,0:T(8,128)} collective-permute-done((f32[4,8,128,128]{3,2,1,0:T(8,128)}, f32[4,8,128,128]{3,2,1,0:T(8,128)}, u32[]{:S(2)}, u32[]{:S(2)}) %collective-permute-start.8) | collective-permute-done | bytes 2097184 | tf_op jit(solution)/shard_map/ppermute | solution.py:272
  164.7 2.3 fusion.1.coulomb_ref
  167.6 8.9 %shard_map.78.b_ref = f32[128,64,128]{2,1,0:T(8,128)S(1)} custom-call(bf16[256,256]{1,0:T(8,128)(2,1)S(1)} %copy-done.9, bf16[256,256]{1,0:T(8,128)(2,1)S(1)} %copy-done.10, f32[4,8,128,128]{3,2,1,0:T(8,128)S(1)} %broadcast_select_fusion.1.refs_0_, f32[4,8,128,128]{3,2,1,0:T(8,128)S(1)} %copy-done.1, f32[4,8,128,128]{3,2,1,0:T(8,128)S(1)} %copy-done.4, ...), custom_call_target="tpu_custom_call" | custom-call | flops 2147483648 | bytes 16777216 | tf_op jit(solution)/shard_map/pallas_call | solution.py:210
  176.6 10.0 %shard_map.79 = (f32[128,64,128]{2,1,0:T(8,128)S(1)}, f32[128,64,128]{2,1,0:T(8,128)S(1)}) custom-call(bf16[256,256]{1,0:T(8,128)(2,1)S(1)} %copy.12.left_ref, bf16[256,256]{1,0:T(8,128)(2,1)S(1)} %maximum_maximum_fusion.1.back_ref, f32[128,128,128]{2,1,0:T(8,128)S(1)} %fusion.1.coulomb_ref, f32[128,64,128]{2,1,0:T(8,128)S(1)} %copy-done.6, ...), custom_call_target="tpu_custom_call" | custom-call | flops 4294967296 | bytes 25165824 | tf_op jit(solution)/shard_map/pallas_call | solution.py:226
  186.6 2.0 copy-done.7
  188.6 2.2 copy-done.8
  190.8 9.7 %shard_map.80 = (f32[4,8,128,128]{3,2,1,0:T(8,128)S(1)}, f32[4,8,128,128]{3,2,1,0:T(8,128)S(1)}, f32[4,8,128,128]{3,2,1,0:T(8,128)}, f32[4,8,128,128]{3,2,1,0:T(...) custom-call(bf16[256,256]{1,0:T(8,128)(2,1)S(1)} %copy-done.9, ...), custom_call_target="tpu_custom_call" | custom-call | flops 2147483648 | bytes 25165824 | tf_op jit(solution)/shard_map/pallas_call | solution.py:244
  200.5 9.7 %shard_map.81 = (f32[4,8,128,128]{3,2,1,0:T(8,128)S(1)}, f32[4,8,128,128]{3,2,1,0:T(8,128)S(1)}, f32[4,8,128,128]{3,2,1,0:T(8,128)}, f32[4,8,128,128]{3,2,1,0:T(...) custom-call(bf16[256,256]{1,0:T(8,128)(2,1)S(1)} %copy-done.9, ...), custom_call_target="tpu_custom_call", output_to_operand_aliasing={{0}: (9, {}), {1}: (10, {}), {2}: (11, {}), {3}: (12, {})} | custom-call | flops 2147483648 | bytes 25165824 | tf_op jit(solution)/shard_map/pallas_call | solution.py:244
  210.2 3.4 collective-permute-start.15
  214.0 1.8 collective-permute-start.17
  216.0 22.1 %collective-permute-done.15 = f32[4,8,128,128]{3,2,1,0:T(8,128)S(1)} collective-permute-done((f32[4,8,128,128]{3,2,1,0:T(8,128)S(1)}, f32[4,8,128,128]{3,2,1,0:T(8,128)S(1)}, u32[]{:S(2)}, u32[]{:S(2)}) %collective-permute-start.15) | collective-permute-done | bytes 2097184 | tf_op jit(solution)/shard_map/ppermute | solution.py:276
  238.1 1.7 add.136
  239.8 1.6 select_add_fusion.1
  241.4 20.7 %collective-permute-done.17 = f32[4,8,128,128]{3,2,1,0:T(8,128)S(1)} collective-permute-done((f32[4,8,128,128]{3,2,1,0:T(8,128)S(1)}, f32[4,8,128,128]{3,2,1,0:T(8,128)S(1)}, u32[]{:S(2)}, u32[]{:S(2)}) %collective-permute-start.17) | collective-permute-done | bytes 2097184 | tf_op jit(solution)/shard_map/ppermute | solution.py:272
  263.7 2.9 collective-permute-start.18
  266.6 1.0 slice_bitcast_fusion.2
  268.7 43.9 %collective-permute-done.21 = f32[2,8,128,128]{3,2,1,0:T(8,128)S(1)} collective-permute-done((f32[2,8,128,128]{3,2,1,0:T(8,128)}, f32[2,8,128,128]{3,2,1,0:T(8,128)S(1)}, u32[]{:S(2)}, u32[]{:S(2)}) %collective-permute-start.21) | collective-permute-done | bytes 1048608 | tf_op jit(solution)/shard_map/ppermute | solution.py:272
  312.8 3.7 %select_add_fusion = f32[4,8,128,128]{3,2,1,0:T(8,128)S(1)} fusion(f32[4,8,128,128]{3,2,1,0:T(8,128)} %add.136, f32[4,8,128,128]{3,2,1,0:T(8,128)} %collective-permute-done.20, f32[4,8,128,128]{3,2,1,0:T(8,128)} %collective-permute-done.18, f32[4,8,128,128]{3,2,1,0:T(8,128)} %collective-permute-done.19, pred[]{:T(512)S(6)} %eq.15), kind=kLoop, calls=%fused_computation.11 | loop fusion | flops 2097152 | bytes 10485761 | tf_op jit(solution)/shard_map/add | solution.py:352
  316.5 1.2 slice_bitcast_fusion.5
  317.7 3.3 collective-permute-start.22
  321.0 1.1 slice_bitcast_fusion.1
  322.1 1.5 collective-permute-start.25
  323.6 2.2 collective-permute-start.24
  325.9 30.3 %collective-permute-done.22 = f32[8,128,128]{2,1,0:T(8,128)} collective-permute-done((f32[8,128,128]{2,1,0:T(8,128)}, f32[8,128,128]{2,1,0:T(8,128)}, u32[]{:S(2)}, u32[]{:S(2)}) %collective-permute-start.22) | collective-permute-done | bytes 524320 | tf_op jit(solution)/shard_map/ppermute | solution.py:272
  356.2 1.3 fusion.2
  357.4 9.4 %collective-permute-done.24 = f32[8,128,128]{2,1,0:T(8,128)S(1)} collective-permute-done((f32[8,128,128]{2,1,0:T(8,128)}, f32[8,128,128]{2,1,0:T(8,128)S(1)}, u32[]{:S(2)}, u32[]{:S(2)}) %collective-permute-start.24) | collective-permute-done | bytes 524320 | tf_op jit(solution)/shard_map/ppermute | solution.py:272
  366.9 1.1 maximum_select_fusion.2
  368.2 1.5 copy.15
  (76 shorter events, 7.3 us)
Async XLA Ops:
  0.6 2.4 copy-start.12
  2.4 49.3 %collective-permute-start.3 = (f32[2,8,128,128]{3,2,1,0:T(8,128)S(1)}, f32[2,8,128,128]{3,2,1,0:T(8,128)}, u32[]{:S(2)}, u32[]{:S(2)}) collective-permute-start(f32[2,8,128,128]{3,2,1,0:T(8,128)S(1)} %get-tuple-element.81), channel_id=1, source_target_pairs={{2,0},{3,1},{0,2},{1,3},{6,4},{7,5},{4,6},{5,7},{10,8},{11,9},{8,1... | collective-permute-start | bytes 3145736 | tf_op jit(solution)/shard_map/ppermute | solution.py:272
  3.1 36.1 %collective-permute-start.1 = (f32[8,128,128]{2,1,0:T(8,128)S(1)}, f32[8,128,128]{2,1,0:T(8,128)S(1)}, u32[]{:S(2)}, u32[]{:S(2)}) collective-permute-start(f32[8,128,128]{2,1,0:T(8,128)S(1)} %bitcast.54), channel_id=1, source_target_pairs={{8,0},{9,1},{10,2},{11,3},{12,4},{13,5},{14,6},{15,7},{0,8},{1,9},... | collective-permute-start | bytes 1572872 | tf_op jit(solution)/shard_map/ppermute | solution.py:272
  5.8 44.5 %collective-permute-start.2 = (f32[8,128,128]{2,1,0:T(8,128)S(1)}, f32[8,128,128]{2,1,0:T(8,128)S(1)}, u32[]{:S(2)}, u32[]{:S(2)}) collective-permute-start(f32[8,128,128]{2,1,0:T(8,128)S(1)} %get-tuple-element.83), channel_id=1, source_target_pairs={{12,0},{13,1},{14,2},{15,3},{8,4},{9,5},{10,6},{11,7},{4,8},{5,9},... | collective-permute-start | bytes 1572872 | tf_op jit(solution)/shard_map/ppermute | solution.py:272
  5.8 44.5 %collective-permute-start = (f32[8,128,128]{2,1,0:T(8,128)S(1)}, f32[8,128,128]{2,1,0:T(8,128)S(1)}, u32[]{:S(2)}, u32[]{:S(2)}) collective-permute-start(f32[8,128,128]{2,1,0:T(8,128)S(1)} %get-tuple-element.83), channel_id=1, source_target_pairs={{4,0},{5,1},{6,2},{7,3},{0,4},{1,5},{2,6},{3,7},{12,8},{13,9},{14,... | collective-permute-start | bytes 1572872 | tf_op jit(solution)/shard_map/ppermute | solution.py:272
  54.5 53.4 %collective-permute-start.6 = (f32[4,8,128,128]{3,2,1,0:T(8,128)}, f32[4,8,128,128]{3,2,1,0:T(8,128)S(1)}, u32[]{:S(2)}, u32[]{:S(2)}) collective-permute-start(f32[4,8,128,128]{3,2,1,0:T(8,128)} %pad_maximum_fusion), channel_id=1, source_target_pairs={{17,0},{0,1},{19,2},{2,3},{21,4},{4,5},{23,6},{6,7},{25,8},{8,9},{... | collective-permute-start | bytes 6291464 | tf_op jit(solution)/shard_map/ppermute | solution.py:286
  54.6 54.8 %collective-permute-start.5 = (f32[4,8,128,128]{3,2,1,0:T(8,128)}, f32[4,8,128,128]{3,2,1,0:T(8,128)}, u32[]{:S(2)}, u32[]{:S(2)}) collective-permute-start(f32[4,8,128,128]{3,2,1,0:T(8,128)} %pad_maximum_fusion), channel_id=1, source_target_pairs={{16,0},{18,2},{20,4},{22,6},{24,8},{26,10},{28,12},{30,14},{0,16},... | collective-permute-start | bytes 6291464 | tf_op jit(solution)/shard_map/ppermute | solution.py:286
  58.0 51.4 %collective-permute-start.4 = (f32[4,8,128,128]{3,2,1,0:T(8,128)}, f32[4,8,128,128]{3,2,1,0:T(8,128)}, u32[]{:S(2)}, u32[]{:S(2)}) collective-permute-start(f32[4,8,128,128]{3,2,1,0:T(8,128)} %pad_maximum_fusion), channel_id=1, source_target_pairs={{2,0},{3,1},{0,2},{1,3},{6,4},{7,5},{4,6},{5,7},{10,8},{11,9},{8,1... | collective-permute-start | bytes 6291464 | tf_op jit(solution)/shard_map/ppermute | solution.py:272
  61.2 45.2 %collective-permute-start.7 = (f32[2,8,128,128]{3,2,1,0:T(8,128)S(1)}, f32[2,8,128,128]{3,2,1,0:T(8,128)S(1)}, u32[]{:S(2)}, u32[]{:S(2)}) collective-permute-start(f32[2,8,128,128]{3,2,1,0:T(8,128)S(1)} %get-tuple-element.79), channel_id=1, source_target_pairs={{8,0},{9,1},{10,2},{11,3},{12,4},{13,5},{14,6},{15,7},{0,8},{1,9},... | collective-permute-start | bytes 3145736 | tf_op jit(solution)/shard_map/ppermute | solution.py:272
  108.0 1.4 copy-start.2
  109.4 28.2 %collective-permute-start.9 = (f32[4,8,128,128]{3,2,1,0:T(8,128)}, f32[4,8,128,128]{3,2,1,0:T(8,128)}, u32[]{:S(2)}, u32[]{:S(2)}) collective-permute-start(f32[4,8,128,128]{3,2,1,0:T(8,128)} %collective-permute-done.5), channel_id=1, source_target_pairs={{2,0},{0,2},{6,4},{4,6},{10,8},{8,10},{14,12},{12,14},{18,16},{16,... | collective-permute-start | bytes 6291464 | tf_op jit(solution)/shard_map/ppermute | solution.py:276
  111.9 27.7 %collective-permute-start.11 = (f32[4,8,128,128]{3,2,1,0:T(8,128)}, f32[4,8,128,128]{3,2,1,0:T(8,128)}, u32[]{:S(2)}, u32[]{:S(2)}) collective-permute-start(f32[4,8,128,128]{3,2,1,0:T(8,128)} %bitcast.15.refs_4_), channel_id=1, source_target_pairs={{1,0},{0,1},{3,2},{2,3},{5,4},{4,5},{7,6},{6,7},{9,8},{8,9},{11,10... | collective-permute-start | bytes 6291464 | tf_op jit(solution)/shard_map/ppermute | solution.py:272
  111.9 27.6 %collective-permute-start.10 = (f32[4,8,128,128]{3,2,1,0:T(8,128)}, f32[4,8,128,128]{3,2,1,0:T(8,128)}, u32[]{:S(2)}, u32[]{:S(2)}) collective-permute-start(f32[4,8,128,128]{3,2,1,0:T(8,128)} %collective-permute-done.4), channel_id=1, source_target_pairs={{17,0},{0,1},{19,2},{2,3},{21,4},{4,5},{23,6},{6,7},{25,8},{8,9},{... | collective-permute-start | bytes 6291464 | tf_op jit(solution)/shard_map/ppermute | solution.py:286
  112.4 50.7 %collective-permute-start.8 = (f32[4,8,128,128]{3,2,1,0:T(8,128)}, f32[4,8,128,128]{3,2,1,0:T(8,128)}, u32[]{:S(2)}, u32[]{:S(2)}) collective-permute-start(f32[4,8,128,128]{3,2,1,0:T(8,128)} %bitcast.15.refs_4_), channel_id=1, source_target_pairs={{4,0},{5,1},{6,2},{7,3},{0,4},{1,5},{2,6},{3,7},{12,8},{13,9},{14,... | collective-permute-start | bytes 6291464 | tf_op jit(solution)/shard_map/ppermute | solution.py:272
  118.7 20.9 %copy-start.3 = (f32[4,8,128,128]{3,2,1,0:T(8,128)S(1)}, f32[4,8,128,128]{3,2,1,0:T(8,128)}, u32[]{:S(2)}) copy-start(f32[4,8,128,128]{3,2,1,0:T(8,128)} %copy-done.2) | copy-start | bytes 6291460
  118.7 20.9 %copy-start.9 = (bf16[256,256]{1,0:T(8,128)(2,1)S(1)}, bf16[256,256]{1,0:T(8,128)(2,1)}, u32[]{:S(2)}) copy-start(bf16[256,256]{1,0:T(8,128)(2,1)} %constant.97.clone.right_ref) | copy-start | bytes 393220
  118.7 20.9 %copy-start.10 = (bf16[256,256]{1,0:T(8,128)(2,1)S(1)}, bf16[256,256]{1,0:T(8,128)(2,1)}, u32[]{:S(2)}) copy-start(bf16[256,256]{1,0:T(8,128)(2,1)} %constant.96.clone.left_ref) | copy-start | bytes 393220
  139.5 9.4 %copy-start = (f32[4,8,128,128]{3,2,1,0:T(8,128)}, f32[4,8,128,128]{3,2,1,0:T(8,128)S(1)}, u32[]{:S(2)}) copy-start(f32[4,8,128,128]{3,2,1,0:T(8,128)S(1)} %broadcast_select_fusion.refs_1_) | copy-start | bytes 6291460
  139.5 23.6 %copy-start.14 = (bf16[16,8,128]{2,1,0:T(8,128)(2,1)S(1)}, bf16[16,8,128]{2,1,0:T(8,128)(2,1)}, u32[]{:S(2)}) copy-start(bf16[16,8,128]{2,1,0:T(8,128)(2,1)} %constant.103.clone.1) | copy-start | bytes 98308
  139.5 24.2 %copy-start.13 = (bf16[16,8,128]{2,1,0:T(8,128)(2,1)S(1)}, bf16[16,8,128]{2,1,0:T(8,128)(2,1)}, u32[]{:S(2)}) copy-start(bf16[16,8,128]{2,1,0:T(8,128)(2,1)} %constant.102.clone.1) | copy-start | bytes 98308
  148.9 2.0 copy-start.5
  163.1 4.5 %collective-permute-start.12 = (f32[4,8,128,128]{3,2,1,0:T(8,128)}, f32[4,8,128,128]{3,2,1,0:T(8,128)}, u32[]{:S(2)}, u32[]{:S(2)}) collective-permute-start(f32[4,8,128,128]{3,2,1,0:T(8,128)} %collective-permute-done.8.refs_4_), channel_id=1, source_target_pairs={{1,0},{0,1},{3,2},{2,3},{5,4},{4,5},{7,6},{6,7},{9,8},{8,9},{11,10... | collective-permute-start | bytes 6291464 | tf_op jit(solution)/shard_map/ppermute | solution.py:272
  164.6 3.0 copy-start.1
  164.7 3.0 copy-start.4
  167.0 9.5 %copy-start.6 = (f32[128,64,128]{2,1,0:T(8,128)S(1)}, f32[128,64,128]{2,1,0:T(8,128)}, u32[]{:S(2)}) copy-start(f32[128,64,128]{2,1,0:T(8,128)} %copy-done.5) | copy-start | bytes 12582916
  186.6 2.0 copy-start.7
  188.6 2.2 copy-start.8
  200.5 9.7 %collective-permute-start.13 = (f32[4,8,128,128]{3,2,1,0:T(8,128)S(1)}, f32[4,8,128,128]{3,2,1,0:T(8,128)S(1)}, u32[]{:S(2)}, u32[]{:S(2)}) collective-permute-start(f32[4,8,128,128]{3,2,1,0:T(8,128)S(1)} %get-tuple-element.60), channel_id=1, source_target_pairs={{1,0},{0,1},{3,2},{2,3},{5,4},{4,5},{7,6},{6,7},{9,8},{8,9},{11,10... | collective-permute-start | bytes 6291464 | tf_op jit(solution)/shard_map/ppermute | solution.py:272
  210.2 27.9 %collective-permute-start.15 = (f32[4,8,128,128]{3,2,1,0:T(8,128)S(1)}, f32[4,8,128,128]{3,2,1,0:T(8,128)S(1)}, u32[]{:S(2)}, u32[]{:S(2)}) collective-permute-start(f32[4,8,128,128]{3,2,1,0:T(8,128)S(1)} %get-tuple-element.62), channel_id=1, source_target_pairs={{2,0},{0,2},{6,4},{4,6},{10,8},{8,10},{14,12},{12,14},{18,16},{16,... | collective-permute-start | bytes 6291464 | tf_op jit(solution)/shard_map/ppermute | solution.py:276
  213.5 26.2 %collective-permute-start.14 = (f32[4,8,128,128]{3,2,1,0:T(8,128)S(1)}, f32[4,8,128,128]{3,2,1,0:T(8,128)S(1)}, u32[]{:S(2)}, u32[]{:S(2)}) collective-permute-start(f32[4,8,128,128]{3,2,1,0:T(8,128)S(1)} %get-tuple-element.61), channel_id=1, source_target_pairs={{0,17},{1,0},{2,19},{3,2},{4,21},{5,4},{6,23},{7,6},{8,25},{9,8},{... | collective-permute-start | bytes 6291464 | tf_op jit(solution)/shard_map/ppermute | solution.py:286
  214.0 48.1 %collective-permute-start.17 = (f32[4,8,128,128]{3,2,1,0:T(8,128)S(1)}, f32[4,8,128,128]{3,2,1,0:T(8,128)S(1)}, u32[]{:S(2)}, u32[]{:S(2)}) collective-permute-start(f32[4,8,128,128]{3,2,1,0:T(8,128)S(1)} %add.138), channel_id=1, source_target_pairs={{4,0},{5,1},{6,2},{7,3},{0,4},{1,5},{2,6},{3,7},{12,8},{13,9},{14,... | collective-permute-start | bytes 6291464 | tf_op jit(solution)/shard_map/ppermute | solution.py:272
  215.8 46.3 %collective-permute-start.16 = (f32[4,8,128,128]{3,2,1,0:T(8,128)S(1)}, f32[4,8,128,128]{3,2,1,0:T(8,128)S(1)}, u32[]{:S(2)}, u32[]{:S(2)}) collective-permute-start(f32[4,8,128,128]{3,2,1,0:T(8,128)S(1)} %get-tuple-element.66), channel_id=1, source_target_pairs={{1,0},{0,1},{3,2},{2,3},{5,4},{4,5},{7,6},{6,7},{9,8},{8,9},{11,10... | collective-permute-start | bytes 6291464 | tf_op jit(solution)/shard_map/ppermute | solution.py:272
  262.6 50.2 %collective-permute-start.19 = (f32[4,8,128,128]{3,2,1,0:T(8,128)}, f32[4,8,128,128]{3,2,1,0:T(8,128)}, u32[]{:S(2)}, u32[]{:S(2)}) collective-permute-start(f32[4,8,128,128]{3,2,1,0:T(8,128)} %get-tuple-element.70), channel_id=1, source_target_pairs={{0,17},{1,0},{2,19},{3,2},{4,21},{5,4},{6,23},{7,6},{8,25},{9,8},{... | collective-permute-start | bytes 6291464 | tf_op jit(solution)/shard_map/ppermute | solution.py:286
  263.2 49.6 %collective-permute-start.20 = (f32[4,8,128,128]{3,2,1,0:T(8,128)}, f32[4,8,128,128]{3,2,1,0:T(8,128)}, u32[]{:S(2)}, u32[]{:S(2)}) collective-permute-start(f32[4,8,128,128]{3,2,1,0:T(8,128)} %select_add_fusion.1), channel_id=1, source_target_pairs={{2,0},{3,1},{0,2},{1,3},{6,4},{7,5},{4,6},{5,7},{10,8},{11,9},{8,1... | collective-permute-start | bytes 6291464 | tf_op jit(solution)/shard_map/ppermute | solution.py:272
  263.7 49.1 %collective-permute-start.18 = (f32[4,8,128,128]{3,2,1,0:T(8,128)}, f32[4,8,128,128]{3,2,1,0:T(8,128)}, u32[]{:S(2)}, u32[]{:S(2)}) collective-permute-start(f32[4,8,128,128]{3,2,1,0:T(8,128)} %add.136), channel_id=1, source_target_pairs={{0,16},{2,18},{4,20},{6,22},{8,24},{10,26},{12,28},{14,30},{16,0},... | collective-permute-start | bytes 6291464 | tf_op jit(solution)/shard_map/ppermute | solution.py:286
  267.6 44.9 %collective-permute-start.21 = (f32[2,8,128,128]{3,2,1,0:T(8,128)}, f32[2,8,128,128]{3,2,1,0:T(8,128)S(1)}, u32[]{:S(2)}, u32[]{:S(2)}) collective-permute-start(f32[2,8,128,128]{3,2,1,0:T(8,128)} %slice_bitcast_fusion.2), channel_id=1, source_target_pairs={{8,0},{9,1},{10,2},{11,3},{12,4},{13,5},{14,6},{15,7},{0,8},{1,9},... | collective-permute-start | bytes 3145736 | tf_op jit(solution)/shard_map/ppermute | solution.py:272
  316.5 5.6 %copy-start.11 = (f32[4,8,128,128]{3,2,1,0:T(8,128)}, f32[4,8,128,128]{3,2,1,0:T(8,128)S(1)}, u32[]{:S(2)}) copy-start(f32[4,8,128,128]{3,2,1,0:T(8,128)S(1)} %select_add_fusion) | copy-start | bytes 6291460
  317.7 38.4 %collective-permute-start.22 = (f32[8,128,128]{2,1,0:T(8,128)}, f32[8,128,128]{2,1,0:T(8,128)}, u32[]{:S(2)}, u32[]{:S(2)}) collective-permute-start(f32[8,128,128]{2,1,0:T(8,128)} %get-tuple-element.75), channel_id=1, source_target_pairs={{8,0},{9,1},{10,2},{11,3},{12,4},{13,5},{14,6},{15,7},{0,8},{1,9},... | collective-permute-start | bytes 1572872 | tf_op jit(solution)/shard_map/ppermute | solution.py:272
  322.1 45.9 %collective-permute-start.25 = (f32[2,8,128,128]{3,2,1,0:T(8,128)}, f32[2,8,128,128]{3,2,1,0:T(8,128)S(1)}, u32[]{:S(2)}, u32[]{:S(2)}) collective-permute-start(f32[2,8,128,128]{3,2,1,0:T(8,128)} %slice_bitcast_fusion.1), channel_id=1, source_target_pairs={{2,0},{3,1},{0,2},{1,3},{6,4},{7,5},{4,6},{5,7},{10,8},{11,9},{8,1... | collective-permute-start | bytes 3145736 | tf_op jit(solution)/shard_map/ppermute | solution.py:272
  323.6 43.3 %collective-permute-start.24 = (f32[8,128,128]{2,1,0:T(8,128)}, f32[8,128,128]{2,1,0:T(8,128)S(1)}, u32[]{:S(2)}, u32[]{:S(2)}) collective-permute-start(f32[8,128,128]{2,1,0:T(8,128)} %get-tuple-element.76), channel_id=1, source_target_pairs={{12,0},{13,1},{14,2},{15,3},{8,4},{9,5},{10,6},{11,7},{4,8},{5,9},... | collective-permute-start | bytes 1572872 | tf_op jit(solution)/shard_map/ppermute | solution.py:272
  325.8 41.1 %collective-permute-start.23 = (f32[8,128,128]{2,1,0:T(8,128)}, f32[8,128,128]{2,1,0:T(8,128)S(1)}, u32[]{:S(2)}, u32[]{:S(2)}) collective-permute-start(f32[8,128,128]{2,1,0:T(8,128)} %get-tuple-element.77), channel_id=1, source_target_pairs={{4,0},{5,1},{6,2},{7,3},{0,4},{1,5},{2,6},{3,7},{12,8},{13,9},{14,... | collective-permute-start | bytes 1572872 | tf_op jit(solution)/shard_map/ppermute | solution.py:272

commit v5 on v4

--- a/solution.py
+++ b/solution.py
@@ -112,17 +112,17 @@
 
 
 def slab_pieces(refs):
-    first, first_x, second, second_x, parts, parts_c = refs
-    return [(first, parts), (first_x, parts), (second, parts_c), (second_x, parts_c)]
+    own_refs, part_refs = refs[:4], refs[4:]
+    return [(own_refs[i // 2], part_refs[i // 4 * 2 + i % 2]) for i in range(8)]
 
 
 def gather_kernel(right_ref, left_ref, *refs):
-    pieces, out_ref, pair_ref = refs[:6], refs[6], refs[7]
+    pieces, out_ref, pair_ref = refs[:8], refs[8], refs[9]
     step = pl.program_id(0)
     rows, length = pair_ref.shape[0], pair_ref.shape[1]
     for turn, (own_ref, part_ref) in enumerate(slab_pieces(pieces)):
 
-        @pl.when(step // 2 == turn)
+        @pl.when(step == turn)
         def _(own_ref=own_ref, part_ref=part_ref):
             pair_ref[...] = own_ref[0] * part_ref[0]
 
@@ -154,7 +154,7 @@
 
 
 def scatter_kernel(right_ref, left_ref, field_ref, *refs):
-    pieces, outs, pot_ref = refs[:6], refs[-7:-1], refs[-1]
+    pieces, outs, pot_ref = refs[:8], refs[-9:-1], refs[-1]
     step = pl.program_id(0)
     rows, length = pot_ref.shape[0], pot_ref.shape[1]
     flat = field_ref.reshape(rows * length, length)
@@ -167,7 +167,7 @@
         pot_ref[pl.ds(r, 2)] = along_x(block, right_ref[...]).reshape(2, length, length)
     for turn, (piece, out) in enumerate(zip(slab_pieces(pieces), slab_pieces(outs))):
 
-        @pl.when(step // 2 == turn)
+        @pl.when(step == turn)
         def _(piece=piece, out=out):
             out[0][0] = pot_ref[...] * piece[1][0]
             out[1][0] = pot_ref[...] * piece[0][0]
@@ -180,12 +180,13 @@
             lambda i: (jnp.clip(i - 2 * turn, 0, 1) * 2 + z_low, 0, 0, 0),
         )
 
-    def part_spec(core):
+    def part_spec(core, z_high):
         return pl.BlockSpec(
-            (1, rows, length, length), lambda i: (jnp.clip(i - 4 * core, 0, 3), 0, 0, 0)
-        )
-
-    return [own_spec(turn) for turn in range(4)] + [part_spec(core) for core in range(2)]
+            (1, rows, length, length),
+            lambda i: (jnp.where(i >= 4 * core + z_high + 2, 1, 0), 0, 0, 0),
+        )
+
+    return [own_spec(turn) for turn in range(4)] + [part_spec(k // 2, k % 2) for k in range(4)]
 
 
 def fixed_spec(shape):
@@ -252,7 +253,7 @@
         + [pl.BlockSpec(memory_space=pl.ANY)] * count,
         out_specs=specs,
         out_shape=[jax.ShapeDtypeStruct(piece.shape, jnp.float32) for piece in pieces],
-        input_output_aliases={9 + k: k for k in range(count)},
+        input_output_aliases={11 + k: k for k in range(count)},
         scratch_shapes=[pltpu.VMEM((rows, length, length), jnp.float32)],
         compiler_params=settings(24),
         cost_estimate=cost(length, 3, 1),
@@ -314,47 +315,58 @@
     coulomb_table = coulomb(waves, waves, waves, length**3)
 
     kept, passed = pick(own, own_band), pick(own, 1 - own_band)
-    bands = jnp.stack([kept, swap(passed, 4), swap(kept, 8), swap(passed, 12)])
+    from_z = [swap(kept, 8), swap(passed, 12), swap(passed, 4)]
     parts = partners.reshape((2, 2) + partners.shape[1:])
-    parts = jnp.stack([pick(parts, part_low, 1), swap(pick(parts, 1 - part_low, 1), 2)])
-    bands, parts = together(bands, parts)
+    parts, parts_x = pick(parts, part_low, 1), swap(pick(parts, 1 - part_low, 1), 2)
+    kept_near = jnp.stack([pick(parts, part_half), pick(parts_x, part_half)])
+    leaving = jnp.stack([pick(parts, 1 - part_half), pick(parts_x, 1 - part_half)])
+    kept_near, leaving, *from_z = together(kept_near, leaving, *from_z)
+    got_near, kept_far = swap(leaving, 8), swap(kept_near, 4)
+    bands = jnp.stack([kept, from_z[2], from_z[0], from_z[1]])
     bands_x = swap(bands, 2)
     first, second = across(bands, 0, False), across(bands, 1, False)
-    parts = jnp.stack([pick(parts, part_half, 1), swap(pick(parts, 1 - part_half, 1), 8)], 1)
-    bands_x, first, second, parts = together(bands_x, first, second, parts)
-    parts = parts.reshape((4, rows) + plane)
-    parts_z, parts_c = swap(parts, 4), swap(parts, 1)
+    bands_x, first, second, got_near, kept_far = together(
+        bands_x, first, second, got_near, kept_far
+    )
+    got_far = swap(got_near, 4)
     first_x, second_x = swap_away(first, 2), across(bands_x, 1, False)
+    near = [kept_near, got_near, swap(kept_near, 1), swap(got_near, 1)]
+    kept_far_c = swap(kept_far, 1)
     first = jnp.where(at_home, bands, first)
     first_x = jnp.where(at_home, bands_x, first_x)
     own_pieces = [first, first_x, second, second_x]
-    even = own_pieces + [parts, parts_c]
-    field_even = gather_half(right, left, even, 0)
-    parts_z, field_even = together(parts_z, field_even)
-    odd = own_pieces + [parts_z, swap(parts_z, 1)]
-    field_odd = gather_half(right, left, odd, 1)
-
-    field_even, field_odd = columns(z_left, z_back, coulomb_table, field_even, field_odd)
-
-    *own_pieces, parts_z, parts_zc = scatter_half(right, left, field_odd, odd, 1, [])
-    parts_zc = swap(parts_zc, 1)
-    *own_pieces, parts, parts_c = scatter_half(right, left, field_even, even, 0, own_pieces)
-    *own_pieces, parts, parts_c, parts_z, parts_zc = together(
-        *own_pieces, parts, parts_c, parts_z, parts_zc
-    )
-    parts_z = swap(parts_z + parts_zc, 4)
-    first, first_x, second, second_x = own_pieces
+    field_near = gather_half(right, left, own_pieces + near, 0)
+    far = [kept_far, got_far, kept_far_c, swap(got_far, 1)]
+    field_far = gather_half(right, left, own_pieces + far, 1)
+
+    field_near, field_far = columns(z_left, z_back, coulomb_table, field_near, field_far)
+
+    outs = scatter_half(right, left, field_far, own_pieces + far, 1, [])
+    kept_far_c, got_far_c = swap(outs[6], 1), swap(outs[7], 1)
+    kept_far, got_far = outs[4], outs[5]
+    outs = scatter_half(right, left, field_near, own_pieces + near, 0, outs[:4])
+    *outs, kept_far, got_far, kept_far_c, got_far_c = together(
+        *outs, kept_far, got_far, kept_far_c, got_far_c
+    )
+    got_near = swap(got_far + got_far_c, 4)
+    first, first_x, second, second_x = outs[:4]
     bands_x = across(second_x, 1, True) + jnp.where(at_home, first_x, 0.0)
     first = first + swap_away(first_x, 2)
-    parts = (parts + swap(parts_c, 1) + parts_z).reshape((2, 2, rows) + plane)
-    bands_x, first, second, parts = together(bands_x, first, second, parts)
+    kept_far = kept_far + kept_far_c
+    kept_near = outs[4] + swap(outs[6], 1)
+    got_near = got_near + outs[5] + swap(outs[7], 1)
+    bands_x, first, second, kept_far, kept_near, got_near = together(
+        bands_x, first, second, kept_far, kept_near, got_near
+    )
+    leaving = swap(got_near, 8)
+    kept_near = kept_near + swap(kept_far, 4)
     bands = across(first, 0, True) + across(second, 1, True) + swap(bands_x, 2)
     bands = bands + jnp.where(at_home, first, 0.0)
-    parts = ordered(part_half, parts[:, 0], swap(parts[:, 1], 8), 1)
-    bands, parts = together(bands, parts)
+    bands, kept_near, leaving = together(bands, kept_near, leaving)
     kept = bands[0] + swap(bands[2], 8)
     passed = swap(bands[1], 4) + swap(bands[3], 12)
-    parts = ordered(part_low, parts[0], swap(parts[1], 2), 1)
+    parts_x = swap(ordered(part_half, kept_near[1], leaving[1]), 2)
+    parts = ordered(part_low, ordered(part_half, kept_near[0], leaving[0]), parts_x, 1)
     return ordered(own_band, kept, passed), parts.reshape(partners.shape)
 
 

time: 372 us -> 334 us (0.90)
  waiting for transfers between devices: 246 us -> 205 us
  other arithmetic: 22.6 us -> 27.9 us
    ppermute x2, waiting for transfers between devices: 41 us -> 0.01 us  [swap_away(): return lax.ppermute(block, 'slab', [(i ^ mask, i) for i in away])]
    another operation x3 -> x2, other arithmetic: 5.74 us -> 0.42 us  [the longest x1 0.21 us: whole_fields(): kept_near = jnp.stack([pick(parts, part_half), pick(parts_x, part_half)])]
    select_n x1, other arithmetic: 2.35 us -> 6.8 us  [coulomb(): jnp.where(square > 0, coulomb_scale / float(cells) / jnp.maximum(square,...]
    unnamed x30 -> x28, local copies, waits for them, and re-layouts: 7.59 us -> 5 us
    ppermute x18 -> x24, starting transfers between devices: 21.4 us -> 22.7 us  [swap(): return lax.ppermute(block, 'slab', [(i ^ mask, i) for i in range(slabs)])]
    ppermute x18 -> x24, waiting for transfers between devices: 205 us -> 205 us  [swap(): return lax.ppermute(block, 'slab', [(i ^ mask, i) for i in range(slabs)])]
  transfers between devices with their start and end apart: 26 -> 32, of which waited for: 11 -> 12; matrix products, arithmetic and copies ran while one was open for 6% -> 10% of each run, Pallas kernels for 5% -> 6%
where the time goes in v5:
time: 334 us; the launch traced here: 332 us
  waiting for transfers between devices  205 us (61%)
  Pallas kernels  47.9 us (14%)
  starting transfers between devices  34.9 us (10%)
  other arithmetic  27.9 us (8%)
  local copies, waits for them, and re-layouts  15 us (4%)
    ppermute x24, waiting for transfers between devices, swap(): return lax.ppermute(block, 'slab', [(i ^ mask, i) for i in range(slabs)])  205 us
    ppermute x24, starting transfers between devices, swap(): return lax.ppermute(block, 'slab', [(i ^ mask, i) for i in range(slabs)])  22.7 us
    pallas_call x2, Pallas kernels, scatter_half(): pl.pallas_call(scatter_kernel, grid=(8,), in_specs=[fixed_spec(right.shap...  19.9 us
    pallas_call x2, Pallas kernels, gather_half(): pl.pallas_call(gather_kernel, grid=(8,), in_specs=[fixed_spec(right.shape...  18 us
    pallas_call x1, Pallas kernels, columns(): pl.pallas_call(column_kernel, grid=(length // count,), in_specs=[fixed_sp...  10 us
    ppermute x6, starting transfers between devices, across(): return lax.ppermute(block, ('band', 'slab'), route)  7.39 us
    select_n x1, other arithmetic, coulomb(): jnp.where(square > 0, coulomb_scale / float(cells) / jnp.maximum(square,...  6.8 us
  transfers between devices with their start and end apart: 32, of which 12 were waited for; matrix products, arithmetic and copies ran while one was open for 10% of the time, Pallas kernels for 6%

profile of v5, /device:TPU:10, one launch (start us, length us, event | category | flops | bytes accessed | tf_op | source)
XLA Modules:
  0.0 331.9 jit_solution(5827206527400269576)
XLA Ops:
  0.6 1.4 dynamic-slice_bitcast_fusion
  3.5 2.6 collective-permute-start.1
  7.0 1.3 dynamic-slice_bitcast_fusion.2
  8.3 18.8 %collective-permute-done = f32[2,8,128,128]{3,2,1,0:T(8,128)} collective-permute-done((f32[2,8,128,128]{3,2,1,0:T(8,128)S(1)}, f32[2,8,128,128]{3,2,1,0:T(8,128)}, u32[]{:S(2)}, u32[]{:S(2)}) %collective-permute-start) | collective-permute-done | bytes 1048608 | tf_op jit(solution)/shard_map/ppermute | solution.py:273
  27.1 1.3 constant_dynamic-slice_fusion
  29.4 1.2 collective-permute-done.3
  30.7 20.0 %collective-permute-done.2 = f32[8,128,128]{2,1,0:T(8,128)S(1)} collective-permute-done((f32[8,128,128]{2,1,0:T(8,128)}, f32[8,128,128]{2,1,0:T(8,128)S(1)}, u32[]{:S(2)}, u32[]{:S(2)}) %collective-permute-start.2) | collective-permute-done | bytes 524320 | tf_op jit(solution)/shard_map/ppermute | solution.py:273
  51.8 3.4 %collective-permute-start.5 = (f32[4,8,128,128]{3,2,1,0:T(8,128)S(1)}, f32[4,8,128,128]{3,2,1,0:T(8,128)}, u32[]{:S(2)}, u32[]{:S(2)}) collective-permute-start(f32[4,8,128,128]{3,2,1,0:T(8,128)S(1)} %pad_maximum_fusion), channel_id=1, source_target_pairs={{16,0},{18,2},{20,4},{22,6},{24,8},{26,10},{28,12},{30,14},{0,16},... | collective-permute-start | bytes 6291464 | tf_op jit(solution)/shard_map/ppermute | solution.py:287
  55.2 1.6 collective-permute-start.4
  56.8 3.8 %collective-permute-start.8 = (f32[2,8,128,128]{3,2,1,0:T(8,128)S(1)}, f32[2,8,128,128]{3,2,1,0:T(8,128)}, u32[]{:S(2)}, u32[]{:S(2)}) collective-permute-start(f32[2,8,128,128]{3,2,1,0:T(8,128)S(1)} %get-tuple-element.56.refs_4_), channel_id=1, source_target_pairs={{4,0},{5,1},{6,2},{7,3},{0,4},{1,5},{2,6},{3,7},{12,8},{13,9},{14,... | collective-permute-start | bytes 3145736 | tf_op jit(solution)/shard_map/ppermute | solution.py:273
  60.6 41.3 %collective-permute-done.7.refs_5_ = f32[2,8,128,128]{3,2,1,0:T(8,128)} collective-permute-done((f32[2,8,128,128]{3,2,1,0:T(8,128)S(1)}, f32[2,8,128,128]{3,2,1,0:T(8,128)}, u32[]{:S(2)}, u32[]{:S(2)}) %collective-permute-start.7) | collective-permute-done | bytes 1048608 | tf_op jit(solution)/shard_map/ppermute | solution.py:273
  101.9 4.2 %collective-permute-done.8.refs_4_ = f32[2,8,128,128]{3,2,1,0:T(8,128)} collective-permute-done((f32[2,8,128,128]{3,2,1,0:T(8,128)S(1)}, f32[2,8,128,128]{3,2,1,0:T(8,128)}, u32[]{:S(2)}, u32[]{:S(2)}) %collective-permute-start.8) | collective-permute-done | bytes 1048608 | tf_op jit(solution)/shard_map/ppermute | solution.py:273
  106.1 2.4 collective-permute-start.9
  109.9 1.4 collective-permute-start.13
  111.3 6.8 %fusion.1.coulomb_ref = f32[128,128,128]{2,1,0:T(8,128)} fusion(f32[128]{0:T(128)S(1)} %fusion.14, f32[128,128]{1,0:T(8,128)S(1)} %broadcast_add_fusion), kind=kLoop, calls=%fused_computation.5 | loop fusion | flops 10485760 | bytes 8454656 | tf_op jit(solution)/shard_map/jit(_where)/select_n | solution.py:42
  118.7 15.1 %collective-permute-done.13.refs_5_ = f32[2,8,128,128]{3,2,1,0:T(8,128)} collective-permute-done((f32[2,8,128,128]{3,2,1,0:T(8,128)}, f32[2,8,128,128]{3,2,1,0:T(8,128)}, u32[]{:S(2)}, u32[]{:S(2)}) %collective-permute-start.13) | collective-permute-done | bytes 1048608 | tf_op jit(solution)/shard_map/ppermute | solution.py:273
  134.7 2.5 broadcast_select_fusion.1.refs_0_
  137.2 2.0 broadcast_select_fusion.refs_1_
  139.3 9.2 %shard_map.78.b_ref = f32[128,64,128]{2,1,0:T(8,128)S(1)} custom-call(bf16[256,256]{1,0:T(8,128)(2,1)S(1)} %copy-done.2, bf16[256,256]{1,0:T(8,128)(2,1)S(1)} %copy-done.3, f32[4,8,128,128]{3,2,1,0:T(8,128)S(1)} %broadcast_select_fusion.1.refs_0_, f32[4,8,128,128]{3,2,1,0:T(8,128)S(1)} %broadcast_select_fusion.refs_1_, ...), custom_call_target="tpu_custom_call" | custom-call | flops 2147483648 | bytes 16777216 | tf_op jit(solution)/shard_map/pallas_call | solution.py:211
  148.5 8.8 %shard_map.77.a_ref = f32[128,64,128]{2,1,0:T(8,128)S(1)} custom-call(bf16[256,256]{1,0:T(8,128)(2,1)S(1)} %copy-done.2, bf16[256,256]{1,0:T(8,128)(2,1)S(1)} %copy-done.3, f32[4,8,128,128]{3,2,1,0:T(8,128)S(1)} %broadcast_select_fusion.1.refs_0_, f32[4,8,128,128]{3,2,1,0:T(8,128)S(1)} %broadcast_select_fusion.refs_1_, ...), custom_call_target="tpu_custom_call" | custom-call | flops 2147483648 | bytes 16777216 | tf_op jit(solution)/shard_map/pallas_call | solution.py:211
  157.3 10.0 %shard_map.79 = (f32[128,64,128]{2,1,0:T(8,128)S(1)}, f32[128,64,128]{2,1,0:T(8,128)S(1)}) custom-call(bf16[256,256]{1,0:T(8,128)(2,1)S(1)} %copy.13.left_ref, bf16[256,256]{1,0:T(8,128)(2,1)S(1)} %maximum_maximum_fusion.1.back_ref, f32[128,128,128]{2,1,0:T(8,128)S(1)} %bitcast.44, f32[128,64,128]{2,1,0:T(8,128)S(1)} %shard_map.77.a_ref, ...), custom_call_target="tpu_custom_call" | custom-call | flops 4294967296 | bytes 25165824 | tf_op jit(solution)/shard_map/pallas_call | solution.py:227
  167.4 2.0 copy-done
  169.4 2.2 copy-done.1
  171.6 10.1 %shard_map.80 = (f32[4,8,128,128]{3,2,1,0:T(8,128)S(1)}, f32[4,8,128,128]{3,2,1,0:T(8,128)S(1)}, f32[4,8,128,128]{3,2,1,0:T(8,128)}, f32[4,8,128,128]{3,2,1,0:T(...) custom-call(bf16[256,256]{1,0:T(8,128)(2,1)S(1)} %copy-done.2, ...), custom_call_target="tpu_custom_call" | custom-call | flops 2147483648 | bytes 25165824 | tf_op jit(solution)/shard_map/pallas_call | solution.py:245
  182.2 9.8 %shard_map.81 = (f32[4,8,128,128]{3,2,1,0:T(8,128)S(1)}, f32[4,8,128,128]{3,2,1,0:T(8,128)S(1)}, f32[4,8,128,128]{3,2,1,0:T(8,128)}, f32[4,8,128,128]{3,2,1,0:T(...) custom-call(bf16[256,256]{1,0:T(8,128)(2,1)S(1)} %copy-done.2, ...), custom_call_target="tpu_custom_call", output_to_operand_aliasing={{0}: (11, {}), {1}: (12, {}), {2}: (13, {}), {3}: (14, {})} | custom-call | flops 2147483648 | bytes 25165824 | tf_op jit(solution)/shard_map/pallas_call | solution.py:245
  192.2 2.4 collective-permute-start.19
  194.8 1.2 collective-permute-start.21
  196.2 1.2 add.158
  197.8 22.6 %collective-permute-done.21 = f32[2,8,128,128]{3,2,1,0:T(8,128)S(1)} collective-permute-done((f32[2,8,128,128]{3,2,1,0:T(8,128)S(1)}, f32[2,8,128,128]{3,2,1,0:T(8,128)S(1)}, u32[]{:S(2)}, u32[]{:S(2)}) %collective-permute-start.21) | collective-permute-done | bytes 1048608 | tf_op jit(solution)/shard_map/ppermute | solution.py:273
  220.4 1.2 add_add_fusion
  221.6 1.8 select_add_fusion.1
  223.6 1.1 collective-permute-start.24
  224.7 1.5 collective-permute-start.25
  226.2 2.7 collective-permute-start.23
  228.9 1.2 collective-permute-start.26
  230.1 42.0 %collective-permute-done.26 = f32[2,8,128,128]{3,2,1,0:T(8,128)} collective-permute-done((f32[2,8,128,128]{3,2,1,0:T(8,128)}, f32[2,8,128,128]{3,2,1,0:T(8,128)}, u32[]{:S(2)}, u32[]{:S(2)}) %collective-permute-start.26) | collective-permute-done | bytes 1048608 | tf_op jit(solution)/shard_map/ppermute | solution.py:273
  272.1 1.3 add.166
  273.5 3.7 %select_add_fusion = f32[4,8,128,128]{3,2,1,0:T(8,128)S(1)} fusion(f32[4,8,128,128]{3,2,1,0:T(8,128)} %copy-done.4, f32[4,8,128,128]{3,2,1,0:T(8,128)} %collective-permute-done.25, f32[4,8,128,128]{3,2,1,0:T(8,128)} %collective-permute-done.23, f32[4,8,128,128]{3,2,1,0:T(8,128)} %collective-permute-done.24, pred[]{:T(512)S(6)} %eq.16), kind=kLoop, calls=%fused_computation.8 | loop fusion | flops 2097152 | bytes 10485761 | tf_op jit(solution)/shard_map/add | solution.py:364
  277.3 1.2 slice_bitcast_fusion.4
  278.5 3.0 collective-permute-start.28
  281.4 1.3 slice_bitcast_fusion
  284.8 1.4 collective-permute-start.30
  286.7 27.3 %collective-permute-done.28 = f32[8,128,128]{2,1,0:T(8,128)} collective-permute-done((f32[8,128,128]{2,1,0:T(8,128)}, f32[8,128,128]{2,1,0:T(8,128)}, u32[]{:S(2)}, u32[]{:S(2)}) %collective-permute-start.28) | collective-permute-done | bytes 524320 | tf_op jit(solution)/shard_map/ppermute | solution.py:273
  314.0 1.1 fusion.2
  315.1 11.2 %collective-permute-done.30 = f32[8,128,128]{2,1,0:T(8,128)} collective-permute-done((f32[8,128,128]{2,1,0:T(8,128)}, f32[8,128,128]{2,1,0:T(8,128)}, u32[]{:S(2)}, u32[]{:S(2)}) %collective-permute-start.30) | collective-permute-done | bytes 524320 | tf_op jit(solution)/shard_map/ppermute | solution.py:273
  326.3 1.3 add_bitcast_fusion
  328.7 1.8 maximum_select_fusion
  330.5 1.5 copy.14
  (88 shorter events, 12.7 us)
Async XLA Ops:
  0.6 2.0 copy-start.9
  2.0 25.1 %collective-permute-start = (f32[2,8,128,128]{3,2,1,0:T(8,128)S(1)}, f32[2,8,128,128]{3,2,1,0:T(8,128)}, u32[]{:S(2)}, u32[]{:S(2)}) collective-permute-start(f32[2,8,128,128]{3,2,1,0:T(8,128)S(1)} %dynamic-slice_bitcast_fusion), channel_id=1, source_target_pairs={{2,0},{3,1},{0,2},{1,3},{6,4},{7,5},{4,6},{5,7},{10,8},{11,9},{8,1... | collective-permute-start | bytes 3145736 | tf_op jit(solution)/shard_map/ppermute | solution.py:273
  3.5 47.2 %copy-start.5 = (f32[1,8,128,128]{3,2,1,0:T(8,128)}, f32[1,8,128,128]{3,2,1,0:T(8,128)S(1)}, u32[]{:S(2)}) copy-start(f32[1,8,128,128]{3,2,1,0:T(8,128)S(1)} %get-tuple-element.111) | copy-start | bytes 1572868
  3.5 25.9 %collective-permute-start.1 = (f32[8,128,128]{2,1,0:T(8,128)S(1)}, f32[8,128,128]{2,1,0:T(8,128)S(1)}, u32[]{:S(2)}, u32[]{:S(2)}) collective-permute-start(f32[8,128,128]{2,1,0:T(8,128)S(1)} %bitcast.45), channel_id=1, source_target_pairs={{8,0},{9,1},{10,2},{11,3},{12,4},{13,5},{14,6},{15,7},{0,8},{1,9},... | collective-permute-start | bytes 1572872 | tf_op jit(solution)/shard_map/ppermute | solution.py:273
  6.1 24.6 %collective-permute-start.3 = (f32[8,128,128]{2,1,0:T(8,128)}, f32[8,128,128]{2,1,0:T(8,128)S(1)}, u32[]{:S(2)}, u32[]{:S(2)}) collective-permute-start(f32[8,128,128]{2,1,0:T(8,128)} %get-tuple-element.110), channel_id=1, source_target_pairs={{4,0},{5,1},{6,2},{7,3},{0,4},{1,5},{2,6},{3,7},{12,8},{13,9},{14,... | collective-permute-start | bytes 1572872 | tf_op jit(solution)/shard_map/ppermute | solution.py:273
  6.6 44.1 %collective-permute-start.2 = (f32[8,128,128]{2,1,0:T(8,128)}, f32[8,128,128]{2,1,0:T(8,128)S(1)}, u32[]{:S(2)}, u32[]{:S(2)}) collective-permute-start(f32[8,128,128]{2,1,0:T(8,128)} %get-tuple-element.110), channel_id=1, source_target_pairs={{12,0},{13,1},{14,2},{15,3},{8,4},{9,5},{10,6},{11,7},{4,8},{5,9},... | collective-permute-start | bytes 1572872 | tf_op jit(solution)/shard_map/ppermute | solution.py:273
  29.4 21.3 %copy-start.6 = (f32[8,128,128]{2,1,0:T(8,128)}, f32[8,128,128]{2,1,0:T(8,128)S(1)}, u32[]{:S(2)}) copy-start(f32[8,128,128]{2,1,0:T(8,128)S(1)} %collective-permute-done.1) | copy-start | bytes 1572868
  30.7 20.1 %copy-start.7 = (f32[8,128,128]{2,1,0:T(8,128)}, f32[8,128,128]{2,1,0:T(8,128)S(1)}, u32[]{:S(2)}) copy-start(f32[8,128,128]{2,1,0:T(8,128)S(1)} %collective-permute-done.3) | copy-start | bytes 1572868
  50.7 0.8 copy-start.8
  51.5 57.1 %copy-start.11 = (bf16[16,8,128]{2,1,0:T(8,128)(2,1)S(1)}, bf16[16,8,128]{2,1,0:T(8,128)(2,1)}, u32[]{:S(2)}) copy-start(bf16[16,8,128]{2,1,0:T(8,128)(2,1)} %constant.155.clone.1) | copy-start | bytes 98308
  51.5 57.7 %copy-start.10 = (bf16[16,8,128]{2,1,0:T(8,128)(2,1)S(1)}, bf16[16,8,128]{2,1,0:T(8,128)(2,1)}, u32[]{:S(2)}) copy-start(bf16[16,8,128]{2,1,0:T(8,128)(2,1)} %constant.154.clone.1) | copy-start | bytes 98308
  51.7 54.4 %collective-permute-start.6 = (f32[4,8,128,128]{3,2,1,0:T(8,128)S(1)}, f32[4,8,128,128]{3,2,1,0:T(8,128)S(1)}, u32[]{:S(2)}, u32[]{:S(2)}) collective-permute-start(f32[4,8,128,128]{3,2,1,0:T(8,128)S(1)} %pad_maximum_fusion), channel_id=1, source_target_pairs={{17,0},{0,1},{19,2},{2,3},{21,4},{4,5},{23,6},{6,7},{25,8},{8,9},{... | collective-permute-start | bytes 6291464 | tf_op jit(solution)/shard_map/ppermute | solution.py:287
  51.8 54.3 %collective-permute-start.5 = (f32[4,8,128,128]{3,2,1,0:T(8,128)S(1)}, f32[4,8,128,128]{3,2,1,0:T(8,128)}, u32[]{:S(2)}, u32[]{:S(2)}) collective-permute-start(f32[4,8,128,128]{3,2,1,0:T(8,128)S(1)} %pad_maximum_fusion), channel_id=1, source_target_pairs={{16,0},{18,2},{20,4},{22,6},{24,8},{26,10},{28,12},{30,14},{0,16},... | collective-permute-start | bytes 6291464 | tf_op jit(solution)/shard_map/ppermute | solution.py:287
  55.2 50.9 %collective-permute-start.4 = (f32[4,8,128,128]{3,2,1,0:T(8,128)S(1)}, f32[4,8,128,128]{3,2,1,0:T(8,128)}, u32[]{:S(2)}, u32[]{:S(2)}) collective-permute-start(f32[4,8,128,128]{3,2,1,0:T(8,128)S(1)} %pad_maximum_fusion), channel_id=1, source_target_pairs={{2,0},{3,1},{0,2},{1,3},{6,4},{7,5},{4,6},{5,7},{10,8},{11,9},{8,1... | collective-permute-start | bytes 6291464 | tf_op jit(solution)/shard_map/ppermute | solution.py:273
  56.8 45.1 %collective-permute-start.7 = (f32[2,8,128,128]{3,2,1,0:T(8,128)S(1)}, f32[2,8,128,128]{3,2,1,0:T(8,128)}, u32[]{:S(2)}, u32[]{:S(2)}) collective-permute-start(f32[2,8,128,128]{3,2,1,0:T(8,128)S(1)} %get-tuple-element.55), channel_id=1, source_target_pairs={{8,0},{9,1},{10,2},{11,3},{12,4},{13,5},{14,6},{15,7},{0,8},{1,9},... | collective-permute-start | bytes 3145736 | tf_op jit(solution)/shard_map/ppermute | solution.py:273
  56.8 49.3 %collective-permute-start.8 = (f32[2,8,128,128]{3,2,1,0:T(8,128)S(1)}, f32[2,8,128,128]{3,2,1,0:T(8,128)}, u32[]{:S(2)}, u32[]{:S(2)}) collective-permute-start(f32[2,8,128,128]{3,2,1,0:T(8,128)S(1)} %get-tuple-element.56.refs_4_), channel_id=1, source_target_pairs={{4,0},{5,1},{6,2},{7,3},{0,4},{1,5},{2,6},{3,7},{12,8},{13,9},{14,... | collective-permute-start | bytes 3145736 | tf_op jit(solution)/shard_map/ppermute | solution.py:273
  106.1 28.3 %collective-permute-start.9 = (f32[4,8,128,128]{3,2,1,0:T(8,128)}, f32[4,8,128,128]{3,2,1,0:T(8,128)}, u32[]{:S(2)}, u32[]{:S(2)}) collective-permute-start(f32[4,8,128,128]{3,2,1,0:T(8,128)} %collective-permute-done.5), channel_id=1, source_target_pairs={{2,0},{0,2},{6,4},{4,6},{10,8},{8,10},{14,12},{12,14},{18,16},{16,... | collective-permute-start | bytes 6291464 | tf_op jit(solution)/shard_map/ppermute | solution.py:277
  109.9 23.9 %collective-permute-start.13 = (f32[2,8,128,128]{3,2,1,0:T(8,128)}, f32[2,8,128,128]{3,2,1,0:T(8,128)}, u32[]{:S(2)}, u32[]{:S(2)}) collective-permute-start(f32[2,8,128,128]{3,2,1,0:T(8,128)} %collective-permute-done.7.refs_5_), channel_id=1, source_target_pairs={{4,0},{5,1},{6,2},{7,3},{0,4},{1,5},{2,6},{3,7},{12,8},{13,9},{14,... | collective-permute-start | bytes 3145736 | tf_op jit(solution)/shard_map/ppermute | solution.py:273
  111.3 28.0 %collective-permute-start.10 = (f32[4,8,128,128]{3,2,1,0:T(8,128)}, f32[4,8,128,128]{3,2,1,0:T(8,128)}, u32[]{:S(2)}, u32[]{:S(2)}) collective-permute-start(f32[4,8,128,128]{3,2,1,0:T(8,128)} %collective-permute-done.4), channel_id=1, source_target_pairs={{17,0},{0,1},{19,2},{2,3},{21,4},{4,5},{23,6},{6,7},{25,8},{8,9},{... | collective-permute-start | bytes 6291464 | tf_op jit(solution)/shard_map/ppermute | solution.py:287
  118.1 21.2 %collective-permute-start.14 = (f32[2,8,128,128]{3,2,1,0:T(8,128)}, f32[2,8,128,128]{3,2,1,0:T(8,128)}, u32[]{:S(2)}, u32[]{:S(2)}) collective-permute-start(f32[2,8,128,128]{3,2,1,0:T(8,128)} %collective-permute-done.8.refs_4_), channel_id=1, source_target_pairs={{1,0},{0,1},{3,2},{2,3},{5,4},{4,5},{7,6},{6,7},{9,8},{8,9},{11,10... | collective-permute-start | bytes 3145736 | tf_op jit(solution)/shard_map/ppermute | solution.py:273
  133.8 5.5 %collective-permute-start.15 = (f32[2,8,128,128]{3,2,1,0:T(8,128)}, f32[2,8,128,128]{3,2,1,0:T(8,128)}, u32[]{:S(2)}, u32[]{:S(2)}) collective-permute-start(f32[2,8,128,128]{3,2,1,0:T(8,128)} %collective-permute-done.13.refs_5_), channel_id=1, source_target_pairs={{1,0},{0,1},{3,2},{2,3},{5,4},{4,5},{7,6},{6,7},{9,8},{8,9},{11,10... | collective-permute-start | bytes 3145736 | tf_op jit(solution)/shard_map/ppermute | solution.py:273
  133.9 14.6 %collective-permute-start.11 = (f32[2,8,128,128]{3,2,1,0:T(8,128)S(1)}, f32[2,8,128,128]{3,2,1,0:T(8,128)}, u32[]{:S(2)}, u32[]{:S(2)}) collective-permute-start(f32[2,8,128,128]{3,2,1,0:T(8,128)S(1)} %get-tuple-element.56.refs_4_), channel_id=1, source_target_pairs={{1,0},{0,1},{3,2},{2,3},{5,4},{4,5},{7,6},{6,7},{9,8},{8,9},{11,10... | collective-permute-start | bytes 3145736 | tf_op jit(solution)/shard_map/ppermute | solution.py:273
  134.4 14.0 %collective-permute-start.12 = (f32[2,8,128,128]{3,2,1,0:T(8,128)}, f32[2,8,128,128]{3,2,1,0:T(8,128)}, u32[]{:S(2)}, u32[]{:S(2)}) collective-permute-start(f32[2,8,128,128]{3,2,1,0:T(8,128)} %collective-permute-done.7.refs_5_), channel_id=1, source_target_pairs={{1,0},{0,1},{3,2},{2,3},{5,4},{4,5},{7,6},{6,7},{9,8},{8,9},{11,10... | collective-permute-start | bytes 3145736 | tf_op jit(solution)/shard_map/ppermute | solution.py:273
  137.2 2.1 copy-start.2
  137.2 2.1 copy-start.3
  139.3 18.1 %slice-start = ((s8[8388608]{0:T(1024)(128)(4,1)}), s8[4194304]{0:T(1024)(128)(4,1)S(1)}, s32[]{:S(2)}) async-start(s8[8388608]{0:T(1024)(128)(4,1)} %bitcast.43), calls=%async_computation | async-start | bytes 8388608
  148.4 8.9 %slice-start.1 = ((s8[8388608]{0:T(1024)(128)(4,1)}), s8[4194304]{0:T(1024)(128)(4,1)S(1)}, s32[]{:S(2)}) async-start(s8[8388608]{0:T(1024)(128)(4,1)} %bitcast.43), calls=%async_computation.1 | async-start | bytes 8388608
  167.4 2.0 copy-start
  169.4 2.2 copy-start.1
  181.7 10.3 %collective-permute-start.16 = (f32[2,8,128,128]{3,2,1,0:T(8,128)S(1)}, f32[2,8,128,128]{3,2,1,0:T(8,128)S(1)}, u32[]{:S(2)}, u32[]{:S(2)}) collective-permute-start(f32[2,8,128,128]{3,2,1,0:T(8,128)S(1)} %get-tuple-element.78), channel_id=1, source_target_pairs={{1,0},{0,1},{3,2},{2,3},{5,4},{4,5},{7,6},{6,7},{9,8},{8,9},{11,10... | collective-permute-start | bytes 3145736 | tf_op jit(solution)/shard_map/ppermute | solution.py:273
  181.7 10.3 %collective-permute-start.17 = (f32[2,8,128,128]{3,2,1,0:T(8,128)S(1)}, f32[2,8,128,128]{3,2,1,0:T(8,128)S(1)}, u32[]{:S(2)}, u32[]{:S(2)}) collective-permute-start(f32[2,8,128,128]{3,2,1,0:T(8,128)S(1)} %get-tuple-element.79), channel_id=1, source_target_pairs={{1,0},{0,1},{3,2},{2,3},{5,4},{4,5},{7,6},{6,7},{9,8},{8,9},{11,10... | collective-permute-start | bytes 3145736 | tf_op jit(solution)/shard_map/ppermute | solution.py:273
  192.0 29.6 %collective-permute-start.18 = (f32[4,8,128,128]{3,2,1,0:T(8,128)S(1)}, f32[4,8,128,128]{3,2,1,0:T(8,128)S(1)}, u32[]{:S(2)}, u32[]{:S(2)}) collective-permute-start(f32[4,8,128,128]{3,2,1,0:T(8,128)S(1)} %get-tuple-element.80), channel_id=1, source_target_pairs={{0,17},{1,0},{2,19},{3,2},{4,21},{5,4},{6,23},{7,6},{8,25},{9,8},{... | collective-permute-start | bytes 6291464 | tf_op jit(solution)/shard_map/ppermute | solution.py:287
  192.2 31.2 %collective-permute-start.19 = (f32[4,8,128,128]{3,2,1,0:T(8,128)S(1)}, f32[4,8,128,128]{3,2,1,0:T(8,128)S(1)}, u32[]{:S(2)}, u32[]{:S(2)}) collective-permute-start(f32[4,8,128,128]{3,2,1,0:T(8,128)S(1)} %get-tuple-element.81), channel_id=1, source_target_pairs={{2,0},{0,2},{6,4},{4,6},{10,8},{8,10},{14,12},{12,14},{18,16},{16,... | collective-permute-start | bytes 6291464 | tf_op jit(solution)/shard_map/ppermute | solution.py:277
  194.6 3.1 collective-permute-start.20
  194.8 25.6 %collective-permute-start.21 = (f32[2,8,128,128]{3,2,1,0:T(8,128)S(1)}, f32[2,8,128,128]{3,2,1,0:T(8,128)S(1)}, u32[]{:S(2)}, u32[]{:S(2)}) collective-permute-start(f32[2,8,128,128]{3,2,1,0:T(8,128)S(1)} %add.160), channel_id=1, source_target_pairs={{4,0},{5,1},{6,2},{7,3},{0,4},{1,5},{2,6},{3,7},{12,8},{13,9},{14,... | collective-permute-start | bytes 3145736 | tf_op jit(solution)/shard_map/ppermute | solution.py:273
  196.0 24.4 %collective-permute-start.22 = (f32[2,8,128,128]{3,2,1,0:T(8,128)S(1)}, f32[2,8,128,128]{3,2,1,0:T(8,128)S(1)}, u32[]{:S(2)}, u32[]{:S(2)}) collective-permute-start(f32[2,8,128,128]{3,2,1,0:T(8,128)S(1)} %get-tuple-element.91), channel_id=1, source_target_pairs={{1,0},{0,1},{3,2},{2,3},{5,4},{4,5},{7,6},{6,7},{9,8},{8,9},{11,10... | collective-permute-start | bytes 3145736 | tf_op jit(solution)/shard_map/ppermute | solution.py:273
  223.6 49.8 %copy-start.4 = (f32[4,8,128,128]{3,2,1,0:T(8,128)}, f32[4,8,128,128]{3,2,1,0:T(8,128)S(1)}, u32[]{:S(2)}) copy-start(f32[4,8,128,128]{3,2,1,0:T(8,128)S(1)} %add.157) | copy-start | bytes 6291460
  223.6 49.8 %collective-permute-start.24 = (f32[4,8,128,128]{3,2,1,0:T(8,128)}, f32[4,8,128,128]{3,2,1,0:T(8,128)}, u32[]{:S(2)}, u32[]{:S(2)}) collective-permute-start(f32[4,8,128,128]{3,2,1,0:T(8,128)} %get-tuple-element.93), channel_id=1, source_target_pairs={{0,17},{1,0},{2,19},{3,2},{4,21},{5,4},{6,23},{7,6},{8,25},{9,8},{... | collective-permute-start | bytes 6291464 | tf_op jit(solution)/shard_map/ppermute | solution.py:287
  224.7 48.8 %collective-permute-start.25 = (f32[4,8,128,128]{3,2,1,0:T(8,128)}, f32[4,8,128,128]{3,2,1,0:T(8,128)}, u32[]{:S(2)}, u32[]{:S(2)}) collective-permute-start(f32[4,8,128,128]{3,2,1,0:T(8,128)} %select_add_fusion.1), channel_id=1, source_target_pairs={{2,0},{3,1},{0,2},{1,3},{6,4},{7,5},{4,6},{5,7},{10,8},{11,9},{8,1... | collective-permute-start | bytes 6291464 | tf_op jit(solution)/shard_map/ppermute | solution.py:273
  226.2 47.3 %collective-permute-start.23 = (f32[4,8,128,128]{3,2,1,0:T(8,128)S(1)}, f32[4,8,128,128]{3,2,1,0:T(8,128)}, u32[]{:S(2)}, u32[]{:S(2)}) collective-permute-start(f32[4,8,128,128]{3,2,1,0:T(8,128)S(1)} %add.157), channel_id=1, source_target_pairs={{0,16},{2,18},{4,20},{6,22},{8,24},{10,26},{12,28},{14,30},{16,0},... | collective-permute-start | bytes 6291464 | tf_op jit(solution)/shard_map/ppermute | solution.py:287
  228.9 43.2 %collective-permute-start.26 = (f32[2,8,128,128]{3,2,1,0:T(8,128)}, f32[2,8,128,128]{3,2,1,0:T(8,128)}, u32[]{:S(2)}, u32[]{:S(2)}) collective-permute-start(f32[2,8,128,128]{3,2,1,0:T(8,128)} %add.158), channel_id=1, source_target_pairs={{4,0},{5,1},{6,2},{7,3},{0,4},{1,5},{2,6},{3,7},{12,8},{13,9},{14,... | collective-permute-start | bytes 3145736 | tf_op jit(solution)/shard_map/ppermute | solution.py:273
  230.1 47.1 %collective-permute-start.27 = (f32[2,8,128,128]{3,2,1,0:T(8,128)}, f32[2,8,128,128]{3,2,1,0:T(8,128)}, u32[]{:S(2)}, u32[]{:S(2)}) collective-permute-start(f32[2,8,128,128]{3,2,1,0:T(8,128)} %add_add_fusion), channel_id=1, source_target_pairs={{8,0},{9,1},{10,2},{11,3},{12,4},{13,5},{14,6},{15,7},{0,8},{1,9},... | collective-permute-start | bytes 3145736 | tf_op jit(solution)/shard_map/ppermute | solution.py:273
  278.5 35.5 %collective-permute-start.28 = (f32[8,128,128]{2,1,0:T(8,128)}, f32[8,128,128]{2,1,0:T(8,128)}, u32[]{:S(2)}, u32[]{:S(2)}) collective-permute-start(f32[8,128,128]{2,1,0:T(8,128)} %get-tuple-element.101), channel_id=1, source_target_pairs={{8,0},{9,1},{10,2},{11,3},{12,4},{13,5},{14,6},{15,7},{0,8},{1,9},... | collective-permute-start | bytes 1572872 | tf_op jit(solution)/shard_map/ppermute | solution.py:273
  283.8 44.9 %collective-permute-start.31 = (f32[2,8,128,128]{3,2,1,0:T(8,128)}, f32[2,8,128,128]{3,2,1,0:T(8,128)}, u32[]{:S(2)}, u32[]{:S(2)}) collective-permute-start(f32[2,8,128,128]{3,2,1,0:T(8,128)} %maximum_select_fusion.3), channel_id=1, source_target_pairs={{2,0},{3,1},{0,2},{1,3},{6,4},{7,5},{4,6},{5,7},{10,8},{11,9},{8,1... | collective-permute-start | bytes 3145736 | tf_op jit(solution)/shard_map/ppermute | solution.py:273
  284.8 41.6 %collective-permute-start.30 = (f32[8,128,128]{2,1,0:T(8,128)}, f32[8,128,128]{2,1,0:T(8,128)}, u32[]{:S(2)}, u32[]{:S(2)}) collective-permute-start(f32[8,128,128]{2,1,0:T(8,128)} %get-tuple-element.102), channel_id=1, source_target_pairs={{12,0},{13,1},{14,2},{15,3},{8,4},{9,5},{10,6},{11,7},{4,8},{5,9},... | collective-permute-start | bytes 1572872 | tf_op jit(solution)/shard_map/ppermute | solution.py:273
  286.1 40.2 %collective-permute-start.29 = (f32[8,128,128]{2,1,0:T(8,128)}, f32[8,128,128]{2,1,0:T(8,128)}, u32[]{:S(2)}, u32[]{:S(2)}) collective-permute-start(f32[8,128,128]{2,1,0:T(8,128)} %get-tuple-element.103), channel_id=1, source_target_pairs={{4,0},{5,1},{6,2},{7,3},{0,4},{1,5},{2,6},{3,7},{12,8},{13,9},{14,... | collective-permute-start | bytes 1572872 | tf_op jit(solution)/shard_map/ppermute | solution.py:273

commit v6 on v1

--- a/solution.py
+++ b/solution.py
@@ -3,8 +3,11 @@
 
 import jax
 import jax.numpy as jnp
+import ml_dtypes
 import numpy as np
 from jax import lax
+from jax.experimental import pallas as pl
+from jax.experimental.pallas import tpu as pltpu
 from jax.sharding import PartitionSpec as P
 
 STEPS = 2
@@ -77,10 +80,419 @@
     return own_acc, part_acc
 
 
+def two_terms(values):
+    high = values.astype(jnp.bfloat16)
+    return high, (values - high.astype(jnp.float32)).astype(jnp.bfloat16)
+
+
+def table_terms(length):
+    table = cas_table(length)
+    high = table.astype(ml_dtypes.bfloat16)
+    low = (table - high.astype(np.float32)).astype(ml_dtypes.bfloat16)
+    return high, low
+
+
+def from_left(high, low, xp=np):
+    return xp.concatenate([xp.concatenate([high, high], 1), xp.concatenate([low, low], 1)], 0)
+
+
+def product(left, right):
+    return jnp.dot(left, right, preferred_element_type=jnp.float32)
+
+
+def along_x(rows, right):
+    high, low = two_terms(rows)
+    both = product(jnp.concatenate([high, low], 1), right)
+    return both[:, : both.shape[1] // 2] + both[:, both.shape[1] // 2 :]
+
+
+def along_y(columns, left):
+    high, low = two_terms(columns)
+    both = product(left, jnp.concatenate([high, low], 0))
+    return both[: both.shape[0] // 2] + both[both.shape[0] // 2 :]
+
+
+def steps_of(late):
+    steps = []
+    for core in range(2):
+        for x, z in [(1, 0), (1, 1), (1, 2), (0, 3), (1, 3)] if late else [(0, 0), (0, 1), (0, 2)]:
+            steps.append((2 * core + x, z, 4 + 4 * core + z, x))
+    return steps
+
+
+EARLY, LATE = steps_of(False), steps_of(True)
+
+
+def slabs_of(steps):
+    return [(z >> 1) * 8 + (z & 1) * 4 + x * 2 + own // 2 for own, z, part, x in steps]
+
+
+def used(steps):
+    return sorted({step[0] for step in steps} | {step[2] for step in steps})
+
+
+def to_field(pair_ref, out_ref, right, left):
+    rows, length = pair_ref.shape[0], pair_ref.shape[1]
+    for r in range(0, rows, 2):
+        block = along_x(pair_ref[pl.ds(r, 2)].reshape(2 * length, length), right)
+        block = along_y(jnp.concatenate([block[:length], block[length:]], 1), left)
+        out_ref[pl.ds(r, length, stride=rows), :] = block[:, :length]
+        out_ref[pl.ds(r + 1, length, stride=rows), :] = block[:, length:]
+
+
+def from_field(field_ref, pot_ref, right, left):
+    rows, length = pot_ref.shape[0], pot_ref.shape[1]
+    for r in range(0, rows, 2):
+        block = jnp.concatenate(
+            [field_ref[pl.ds(r + k, length, stride=rows), :] for k in range(2)], 1
+        )
+        block = along_y(block, left)
+        block = jnp.concatenate([block[:, :length], block[:, length:]], 0)
+        pot_ref[pl.ds(r, 2)] = along_x(block, right).reshape(2, length, length)
+
+
+def make_pairs(steps, turn, pieces, pair_ref):
+    for k, (own, _, part, _) in enumerate(steps):
+
+        @pl.when(turn == k)
+        def _(own=own, part=part):
+            pair_ref[...] = pieces[own][0] * pieces[part][0]
+
+
+def make_terms(steps, turn, pieces, outs, pot_ref):
+    for k, (own, _, part, _) in enumerate(steps):
+
+        @pl.when(turn == k)
+        def _(own=own, part=part):
+            outs[own][0] = pot_ref[...] * pieces[part][0]
+            outs[part][0] = pot_ref[...] * pieces[own][0]
+
+
+def gather_kernel(steps, right_ref, left_ref, *refs):
+    pieces, out_ref, pair_ref = dict(zip(used(steps), refs)), refs[-2], refs[-1]
+    make_pairs(steps, pl.program_id(0), pieces, pair_ref)
+    rows, length = pair_ref.shape[0], pair_ref.shape[1]
+    to_field(pair_ref, out_ref.reshape(rows * length, length), right_ref[...], left_ref[...])
+
+
+def late_kernel(
+    steps, right_ref, left_ref, z_left_ref, z_back_ref, square_ref, early_ref, *refs
+):
+    names = used(steps)
+    pieces, early_out = dict(zip(names, refs)), refs[len(names)]
+    outs = dict(zip(names, refs[len(names) + 1 :]))
+    own_ref, part_ref, field_ref, middle_ref, in_sems, out_sems, middle_sems = refs[-7:]
+    rows, length = own_ref.shape[1], own_ref.shape[2]
+    count, part = len(steps), middle_ref.shape[1]
+
+    def blocks(k, arrays):
+        own, z, part, x = steps[k]
+        return [(arrays[own].at[z], own_ref.at[k]), (arrays[part].at[x], part_ref.at[k])]
+
+    for k in range(count):
+        for j, (block, held) in enumerate(blocks(k, pieces)):
+            pltpu.make_async_copy(block, held, in_sems.at[j, k]).start()
+    middle_in = pltpu.make_async_copy(early_ref, middle_ref, middle_sems.at[0])
+    middle_in.start()
+
+    @pl.loop(0, count)
+    def _(k):
+        pltpu.make_async_copy(pieces[names[0]].at[0], own_ref.at[k], in_sems.at[0, k]).wait()
+        pltpu.make_async_copy(pieces[names[0]].at[0], part_ref.at[k], in_sems.at[1, k]).wait()
+        out_ref = field_ref.at[k]
+        for r in range(0, rows, 2):
+            pair = own_ref[k, pl.ds(r, 2)] * part_ref[k, pl.ds(r, 2)]
+            block = along_x(pair.reshape(2 * length, length), right_ref[...])
+            block = along_y(
+                jnp.concatenate([block[:length], block[length:]], 1), left_ref[...]
+            )
+            out_ref[pl.ds(r, length, stride=rows), :] = block[:, :length]
+            out_ref[pl.ds(r + 1, length, stride=rows), :] = block[:, length:]
+
+    middle_in.wait()
+    group = 8
+    scale = coulomb_scale / float(length**3)
+
+    @pl.loop(0, length // group)
+    def _(i):
+        for k in range(0, group, 2):
+            columns, factors, spans = [], [], []
+            for j in range(2):
+                y = i * group + k + j
+                spans.append(pl.ds(pl.multiple_of(y * rows, rows), rows))
+                late = field_ref[:, spans[j], :].reshape(count * rows, length)
+                columns.append(jnp.concatenate([middle_ref[y], late], 0))
+                wave = frequency(y, length)
+                total = square_ref[...] + wave * wave
+                factors.append(jnp.where(total > 0, scale / jnp.maximum(total, 1.0), 0.0))
+            block = along_y(jnp.concatenate(columns, 1), z_left_ref[...])
+            block = along_y(block * jnp.concatenate(factors, 1), z_back_ref[...])
+            for j in range(2):
+                piece = block[:, j * length : (j + 1) * length]
+                middle_ref[i * group + k + j] = piece[:part]
+                field_ref[:, spans[j], :] = piece[part:].reshape(count, rows, length)
+
+    middle_out = pltpu.make_async_copy(middle_ref, early_out, middle_sems.at[1])
+    middle_out.start()
+
+    @pl.loop(0, count)
+    def _(k):
+        in_ref = field_ref.at[k]
+        for r in range(0, rows, 2):
+            block = jnp.concatenate(
+                [in_ref[pl.ds(r + j, length, stride=rows), :] for j in range(2)], 1
+            )
+            block = along_y(block, left_ref[...])
+            block = jnp.concatenate([block[:, :length], block[:, length:]], 0)
+            block = along_x(block, right_ref[...]).reshape(2, length, length)
+            span = pl.ds(r, 2)
+            own_term = block * part_ref[k, span]
+            part_ref[k, span] = block * own_ref[k, span]
+            own_ref[k, span] = own_term
+        for turn in range(count):
+
+            @pl.when(k == turn)
+            def _(turn=turn):
+                for j, (block, held) in enumerate(blocks(turn, outs)):
+                    pltpu.make_async_copy(held, block, out_sems.at[j, turn]).start()
+
+    for k in range(count):
+        for j, (block, held) in enumerate(blocks(k, outs)):
+            pltpu.make_async_copy(held, block, out_sems.at[j, k]).wait()
+    middle_out.wait()
+
+
+def scatter_kernel(steps, right_ref, left_ref, field_ref, *refs):
+    names = used(steps)
+    pieces, outs = dict(zip(names, refs)), dict(zip(names, refs[-1 - len(names) : -1]))
+    pot_ref = refs[-1]
+    rows, length = pot_ref.shape[0], pot_ref.shape[1]
+    flat = field_ref.reshape(rows * length, length)
+    from_field(flat, pot_ref, right_ref[...], left_ref[...])
+    make_terms(steps, pl.program_id(0), pieces, outs, pot_ref)
+
+
+def piece_specs(steps, rows, length, starts=(0,)):
+    def spec(name):
+        visits = []
+        for start in starts:
+            for turn, (own, z, part, x) in enumerate(steps):
+                if name in (own, part):
+                    visits.append((start + turn, z if name == own else x))
+
+        def index(i):
+            block = visits[0][1]
+            for (_, before), (turn, after) in zip(visits, visits[1:]):
+                block = block + jnp.where(i >= turn, after - before, 0)
+            return (block, 0, 0, 0)
+
+        return pl.BlockSpec((1, rows, length, length), index)
+
+    return [spec(name) for name in used(steps)]
+
+
+def fixed_spec(shape):
+    return pl.BlockSpec(shape, lambda i: (0,) * len(shape))
+
+
+def settings(megabytes):
+    return pltpu.CompilerParams(
+        dimension_semantics=("arbitrary",), vmem_limit_bytes=megabytes * 2**20
+    )
+
+
+def cost(cells, length, fields, transforms):
+    return pl.CostEstimate(
+        flops=transforms * 8 * cells * length, bytes_accessed=4 * fields * cells, transcendentals=0
+    )
+
+
+def gather_part(right, left, pieces, steps):
+    rows, length = pieces[0].shape[1], pieces[0].shape[2]
+    count = len(steps)
+    return pl.pallas_call(
+        functools.partial(gather_kernel, steps),
+        grid=(count,),
+        in_specs=[fixed_spec(right.shape), fixed_spec(left.shape)]
+        + piece_specs(steps, rows, length),
+        out_specs=pl.BlockSpec((length, rows, length), lambda i: (0, i, 0)),
+        out_shape=jax.ShapeDtypeStruct((length, count * rows, length), jnp.float32),
+        scratch_shapes=[pltpu.VMEM((rows, length, length), jnp.float32)],
+        compiler_params=settings(20),
+        cost_estimate=cost(count * rows * length * length, length, 3, 2),
+    )(right, left, *[pieces[name] for name in used(steps)])
+
+
+def late_part(right, left, z_left, z_back, square, early, pieces, steps):
+    rows, length = pieces[0].shape[1], pieces[0].shape[2]
+    names = used(steps)
+    count = len(steps)
+    tables = [right, left, z_left, z_back, square]
+    anywhere = pl.BlockSpec(memory_space=pl.ANY)
+    early, *outs = pl.pallas_call(
+        functools.partial(late_kernel, steps),
+        in_specs=[pl.BlockSpec(memory_space=pltpu.VMEM)] * len(tables)
+        + [anywhere] * (1 + len(names)),
+        out_specs=[anywhere] * (1 + len(names)),
+        out_shape=[jax.ShapeDtypeStruct(early.shape, jnp.float32)]
+        + [jax.ShapeDtypeStruct(pieces[name].shape, jnp.float32) for name in names],
+        scratch_shapes=[
+            pltpu.VMEM((count, rows, length, length), jnp.float32),
+            pltpu.VMEM((count, rows, length, length), jnp.float32),
+            pltpu.VMEM((count, rows * length, length), jnp.float32),
+            pltpu.VMEM(early.shape, jnp.float32),
+            pltpu.SemaphoreType.DMA((2, count)),
+            pltpu.SemaphoreType.DMA((2, count)),
+            pltpu.SemaphoreType.DMA((2,)),
+        ],
+        compiler_params=pltpu.CompilerParams(vmem_limit_bytes=32 * 2**20),
+        cost_estimate=cost(length**3, length, 4, 5),
+    )(*tables, early, *[pieces[name] for name in names])
+    return early, dict(zip(names, outs))
+
+
+def scatter_part(right, left, field, pieces, steps, held):
+    rows, length = pieces[0].shape[1], pieces[0].shape[2]
+    names = used(steps)
+    specs = piece_specs(steps, rows, length)
+    kept = [name for name in names if name in held]
+    outs = pl.pallas_call(
+        functools.partial(scatter_kernel, steps),
+        grid=(len(steps),),
+        in_specs=[
+            fixed_spec(right.shape), fixed_spec(left.shape),
+            pl.BlockSpec((length, rows, length), lambda i: (0, i, 0)),
+        ]
+        + specs
+        + [pl.BlockSpec(memory_space=pl.ANY)] * len(kept),
+        out_specs=specs,
+        out_shape=[jax.ShapeDtypeStruct(pieces[name].shape, jnp.float32) for name in names],
+        input_output_aliases={
+            3 + len(names) + k: names.index(name) for k, name in enumerate(kept)
+        },
+        scratch_shapes=[pltpu.VMEM((rows, length, length), jnp.float32)],
+        compiler_params=settings(32),
+        cost_estimate=cost(len(steps) * rows * length * length, length, 5, 2),
+    )(right, left, field, *[pieces[name] for name in names], *[held[name] for name in kept])
+    return dict(zip(names, outs))
+
+
+def whole_fields(own, partners, groups, slabs):
+    length = own.shape[3]
+    rows = own.shape[1]
+    plane = own.shape[2:]
+    me = lax.axis_index("slab")
+    part_half, own_band, part_low = (me >> 3) & 1, (me >> 2) & 1, (me >> 1) & 1
+
+    at_home = ((me & 1) + 1) % groups == 0
+
+    def swap(block, mask):
+        return lax.ppermute(block, "slab", [(i ^ mask, i) for i in range(slabs)])
+
+    def swap_away(block, mask):
+        away = [i for i in range(slabs) if ((i & 1) + 1) % groups != 0]
+        return lax.ppermute(block, "slab", [(i ^ mask, i) for i in away])
+
+    def across(block, flip, back):
+        route = []
+        for b in range(groups):
+            for i in range(slabs):
+                source = ((b + 1 + (i & 1)) % groups) * slabs + (i ^ flip)
+                target = b * slabs + i
+                if source != target:
+                    route.append((target, source) if back else (source, target))
+        return lax.ppermute(block, ("band", "slab"), route)
+
+    def pick(block, position, axis=0):
+        return lax.dynamic_index_in_dim(block, position, axis, keepdims=False)
+
+    def ordered(position, mine, other, axis=0):
+        shape = [1] * (mine.ndim + 1)
+        shape[axis] = 2
+        first = lax.iota(jnp.int32, 2).reshape(shape) == position
+        return jnp.where(first, jnp.expand_dims(mine, axis), jnp.expand_dims(other, axis))
+
+    def together(*blocks):
+        return lax.optimization_barrier(blocks)
+
+    high, low = table_terms(length)
+    left = jnp.asarray(from_left(high, low))
+    right = jnp.asarray(from_left(high, low).T)
+    slab_of = me ^ jnp.asarray(np.array(slabs_of(EARLY) + slabs_of(LATE), np.int32))
+    z_high, z_low = [
+        jnp.take(jnp.asarray(term).reshape(slabs, rows, length), slab_of, axis=0).reshape(
+            length, length
+        )
+        for term in (high, low)
+    ]
+    z_left, z_back = from_left(z_high.T, z_low.T, jnp), from_left(z_high, z_low, jnp)
+    waves = frequency(lax.iota(jnp.int32, length), length)
+    square = waves[:, None] * waves[:, None] + waves[None] * waves[None]
+
+    kept, passed = pick(own, own_band), pick(own, 1 - own_band)
+    from_z = [swap(kept, 8), swap(passed, 12), swap(passed, 4)]
+    parts = partners.reshape((2, 2) + partners.shape[1:])
+    parts, parts_x = pick(parts, part_low, 1), swap(pick(parts, 1 - part_low, 1), 2)
+    kept_near = jnp.stack([pick(parts, part_half), pick(parts_x, part_half)])
+    leaving = jnp.stack([pick(parts, 1 - part_half), pick(parts_x, 1 - part_half)])
+    kept_near, leaving, *from_z = together(kept_near, leaving, *from_z)
+    got_near, kept_far = swap(leaving, 8), swap(kept_near, 4)
+    bands = jnp.stack([kept, from_z[2], from_z[0], from_z[1]])
+    bands_x = swap(bands, 2)
+    first, second = across(bands, 0, False), across(bands, 1, False)
+    bands_x, first, second, got_near, kept_far = together(
+        bands_x, first, second, got_near, kept_far
+    )
+    got_far = swap(got_near, 4)
+    first_x, second_x = swap_away(first, 2), across(bands_x, 1, False)
+    parts = [kept_near, kept_far, got_near]
+    parts_c = [swap(part, 1) for part in parts]
+    first = jnp.where(at_home, bands, first)
+    early = [first, None, second, None] + parts + [None] + parts_c + [None]
+    field_early = gather_part(right, left, early, EARLY)
+    got_far, first_x, second_x, field_early = together(got_far, first_x, second_x, field_early)
+    first_x = jnp.where(at_home, bands_x, first_x)
+    pieces = [first, first_x, second, second_x] + parts + [got_far] + parts_c + [swap(got_far, 1)]
+    field_early, outs = late_part(
+        right, left, z_left, z_back, square, field_early, pieces, LATE
+    )
+    got_far = outs[7] + swap(outs[11], 1)
+    got_far, field_early = together(got_far, field_early)
+    got_near = swap(got_far, 4)
+    first = swap_away(outs[1], 2)
+    bands_x = across(outs[3], 1, True) + jnp.where(at_home, outs[1], 0.0)
+    outs = scatter_part(right, left, field_early, pieces, EARLY, outs)
+    names = sorted(outs)
+    got_near, first, bands_x, *blocks = together(
+        got_near, first, bands_x, *[outs[name] for name in names]
+    )
+    outs = dict(zip(names, blocks))
+    got_near = got_near + outs[6] + swap(outs[10], 1)
+    kept_far = outs[5] + swap(outs[9], 1)
+    kept_near = outs[4] + swap(outs[8], 1)
+    first, second = outs[0] + first, outs[2]
+    leaving = swap(got_near, 8)
+    kept_near = kept_near + swap(kept_far, 4)
+    terms = [across(first, 0, True), across(second, 1, True), swap(bands_x, 2)]
+    terms.append(jnp.where(at_home, first, 0.0))
+    kept_near, leaving, *terms = together(kept_near, leaving, *terms)
+    bands = [sum(term[z] for term in terms) for z in range(4)]
+    parts_x = swap(ordered(part_half, kept_near[1], leaving[1]), 2)
+    from_z = [swap(bands[2], 8), swap(bands[3], 12), swap(bands[1], 4)]
+    parts = ordered(part_low, ordered(part_half, kept_near[0], leaving[0]), parts_x, 1)
+    parts, *from_z = together(parts.reshape(partners.shape), *from_z)
+    return ordered(own_band, bands[0] + from_z[0], from_z[1] + from_z[2]), parts
+
+
 def solution(mesh):
     groups, slabs = mesh.shape["band"], mesh.shape["slab"]
     spec = P("band", "slab", None, None)
+
+    def shards(own, partners):
+        if slabs == 16 and own.shape[0] == 2 and partners.shape[0] == 4 and STEPS == 2:
+            return whole_fields(own, partners, groups, slabs)
+        return pencils(own, partners, groups, slabs)
+
     return jax.shard_map(
-        functools.partial(pencils, groups=groups, slabs=slabs),
-        mesh=mesh, in_specs=(spec, spec), out_specs=(spec, spec), check_vma=False,
-    )
+        shards, mesh=mesh, in_specs=(spec, spec), out_specs=(spec, spec), check_vma=False
+    )

time: 469 us -> 312 us (0.67); the launches traced: 468 us -> 306 us
  waiting for transfers between devices: 356 us -> 198 us
  matrix products: 46.6 us -> 0 us
  Pallas kernels: 0 us -> 38.6 us
  local copies, waits for them, and re-layouts: 30.9 us -> 11.9 us
  starting transfers between devices: 24.6 us -> 39 us
  other arithmetic: 9.47 us -> 17.1 us
    all_to_all x4 -> x0, waiting for transfers between devices: 312 us -> none  [the longest x2 157 us: pencils(): lax.all_to_all(field, 'slab', split_axis=1, concat_axis=2, tiled=True)]
    ppermute x2 -> x32, waiting for transfers between devices: 44.4 us -> 198 us  [the longest x24 188 us: swap(): return lax.ppermute(block, 'slab', [(i ^ mask, i) for i in range(slabs)])]
    dot_general x12 -> x0, matrix products: 46.6 us -> none  [apply_table(): return jnp.einsum(pattern, field, table, precision=precision)]
    pallas_call x0 -> x3, Pallas kernels: none -> 38.6 us  [the longest x1 25.5 us: late_part(): pl.pallas_call(functools.partial(late_kernel, steps), in_specs=[pl.BlockS...]
    ppermute x2 -> x32, starting transfers between devices: 3.17 us -> 39 us  [the longest x24 23.9 us: swap(): return lax.ppermute(block, 'slab', [(i ^ mask, i) for i in range(slabs)])]
    transpose x4 -> x0, local copies, waits for them, and re-layouts: 21.6 us -> none  [apply_table(): return jnp.einsum(pattern, field, table, precision=precision)]
    all_to_all x4 -> x0, starting transfers between devices: 21.4 us -> none  [the longest x2 11.3 us: pencils(): lax.all_to_all(field, 'slab', split_axis=2, concat_axis=1, tiled=True)]
    select_n x1 -> x6, other arithmetic: 0.17 us -> 11.4 us  [the longest x3 5.69 us: ordered(): jnp.where(first, jnp.expand_dims(mine, axis), jnp.expand_dims(other, axis))]
  transfers between devices with their start and end apart: 6 -> 32, of which waited for: 6 -> 17; matrix products, arithmetic and copies ran while one was open for 13% -> 5% of each run, Pallas kernels for 0% -> 4%
where the time goes in v6:
time: 312 us; the launch traced here: 306 us
  waiting for transfers between devices  198 us (63%)
  starting transfers between devices  39 us (12%)
  Pallas kernels  38.6 us (12%)
  other arithmetic  17.1 us (5%)
  local copies, waits for them, and re-layouts  11.9 us (4%)
    ppermute x24, waiting for transfers between devices, swap(): return lax.ppermute(block, 'slab', [(i ^ mask, i) for i in range(slabs)])  188 us
    pallas_call x1, Pallas kernels, late_part(): pl.pallas_call(functools.partial(late_kernel, steps), in_specs=[pl.BlockS...  25.5 us
    ppermute x24, starting transfers between devices, swap(): return lax.ppermute(block, 'slab', [(i ^ mask, i) for i in range(slabs)])  23.9 us
    ppermute x6, waiting for transfers between devices, across(): return lax.ppermute(block, ('band', 'slab'), route)  9.75 us
    ppermute x6, starting transfers between devices, across(): return lax.ppermute(block, ('band', 'slab'), route)  9.27 us
    pallas_call x1, Pallas kernels, scatter_part(): pl.pallas_call(functools.partial(scatter_kernel, steps), grid=(len(steps)...  6.96 us
  transfers between devices with their start and end apart: 32, of which 17 were waited for; matrix products, arithmetic and copies ran while one was open for 5% of the time, Pallas kernels for 4%

profile of v6, /device:TPU:10, one launch (start us, length us, event | category | flops | bytes accessed | tf_op | source)
XLA Modules:
  0.0 305.6 jit_solution(7553356052761016784)
XLA Ops:
  0.6 1.4 dynamic-slice_bitcast_fusion
  3.5 2.6 collective-permute-start.1
  7.0 1.3 dynamic-slice_bitcast_fusion.2
  8.3 18.8 %collective-permute-done = f32[2,8,128,128]{3,2,1,0:T(8,128)} collective-permute-done((f32[2,8,128,128]{3,2,1,0:T(8,128)S(1)}, f32[2,8,128,128]{3,2,1,0:T(8,128)}, u32[]{:S(2)}, u32[]{:S(2)}) %collective-permute-start) | collective-permute-done | bytes 1048608 | tf_op jit(solution)/shard_map/ppermute | solution.py:390
  27.1 1.3 constant_dynamic-slice_fusion
  29.4 1.2 collective-permute-done.3
  30.7 20.0 %collective-permute-done.2 = f32[8,128,128]{2,1,0:T(8,128)S(1)} collective-permute-done((f32[8,128,128]{2,1,0:T(8,128)}, f32[8,128,128]{2,1,0:T(8,128)S(1)}, u32[]{:S(2)}, u32[]{:S(2)}) %collective-permute-start.2) | collective-permute-done | bytes 524320 | tf_op jit(solution)/shard_map/ppermute | solution.py:390
  51.0 3.4 %collective-permute-start.5 = (f32[4,8,128,128]{3,2,1,0:T(8,128)S(1)}, f32[4,8,128,128]{3,2,1,0:T(8,128)}, u32[]{:S(2)}, u32[]{:S(2)}) collective-permute-start(f32[4,8,128,128]{3,2,1,0:T(8,128)S(1)} %pad_maximum_fusion), channel_id=1, source_target_pairs={{16,0},{18,2},{20,4},{22,6},{24,8},{26,10},{28,12},{30,14},{0,16},... | collective-permute-start | bytes 6291464 | tf_op jit(solution)/shard_map/ppermute | solution.py:404
  54.4 1.6 collective-permute-start.4
  56.0 3.8 %collective-permute-start.8 = (f32[2,8,128,128]{3,2,1,0:T(8,128)S(1)}, f32[2,8,128,128]{3,2,1,0:T(8,128)}, u32[]{:S(2)}, u32[]{:S(2)}) collective-permute-start(f32[2,8,128,128]{3,2,1,0:T(8,128)S(1)} %get-tuple-element.65.refs_2_.refs_4_), channel_id=1, source_target_pairs={{4,0},{5,1},{6,2},{7,3},{0,4},{1,5},{2,6},{3,7},{12,8},{13,9},{14,... | collective-permute-start | bytes 3145736 | tf_op jit(solution)/shard_map/ppermute | solution.py:390
  59.8 41.4 %collective-permute-done.7.refs_4_.refs_6_ = f32[2,8,128,128]{3,2,1,0:T(8,128)} collective-permute-done((f32[2,8,128,128]{3,2,1,0:T(8,128)S(1)}, f32[2,8,128,128]{3,2,1,0:T(8,128)}, u32[]{:S(2)}, u32[]{:S(2)}) %collective-permute-start.7) | collective-permute-done | bytes 1048608 | tf_op jit(solution)/shard_map/ppermute | solution.py:390
  101.3 4.2 %collective-permute-done.8.refs_3_.refs_5_ = f32[2,8,128,128]{3,2,1,0:T(8,128)} collective-permute-done((f32[2,8,128,128]{3,2,1,0:T(8,128)S(1)}, f32[2,8,128,128]{3,2,1,0:T(8,128)}, u32[]{:S(2)}, u32[]{:S(2)}) %collective-permute-start.8) | collective-permute-done | bytes 1048608 | tf_op jit(solution)/shard_map/ppermute | solution.py:390
  105.4 1.3 copy-done.2
  106.7 2.4 collective-permute-start.10
  109.9 1.0 copy-done.5
  110.8 1.3 collective-permute-start.9
  113.4 2.0 broadcast_select_fusion.2.refs_0_
  115.4 0.9 collective-permute-done.14.refs_7_.refs_10_
  116.4 6.1 %shard_map.86.early_ref = f32[128,48,128]{2,1,0:T(8,128)S(1)} custom-call(bf16[256,256]{1,0:T(8,128)(2,1)S(1)} %copy-done.10, bf16[256,256]{1,0:T(8,128)(2,1)S(1)} %copy-done.11, f32[4,8,128,128]{3,2,1,0:T(8,128)S(1)} %broadcast_select_fusion.2.refs_0_, f32[4,8,128,128]{3,2,1,0:T(8,128)S(1)} %copy-done.3, ...), custom_call_target="tpu_custom_call" | custom-call | flops 1610612736 | bytes 9437184 | tf_op jit(solution)/shard_map/pallas_call | solution.py:313
  122.5 1.7 copy-done.8
  124.2 12.5 %collective-permute-done.9.refs_7_ = f32[2,8,128,128]{3,2,1,0:T(8,128)} collective-permute-done((f32[2,8,128,128]{3,2,1,0:T(8,128)}, f32[2,8,128,128]{3,2,1,0:T(8,128)}, u32[]{:S(2)}, u32[]{:S(2)}) %collective-permute-start.9) | collective-permute-done | bytes 1048608 | tf_op jit(solution)/shard_map/ppermute | solution.py:390
  137.1 3.3 %broadcast_select_fusion.1.refs_1_ = f32[4,8,128,128]{3,2,1,0:T(8,128)} fusion(f32[4,8,128,128]{3,2,1,0:T(8,128)} %collective-permute-done.4, f32[4,8,128,128]{3,2,1,0:T(8,128)} %collective-permute-done.10, pred[]{:T(512)S(6)} %eq.42), kind=kLoop, calls=%fused_computation.11 | loop fusion | flops 524288 | bytes 6291457 | tf_op jit(solution)/shard_map/jit(_where)/select_n | solution.py:454
  140.4 25.5 %shard_map.87 = (f32[128,48,128]{2,1,0:T(8,128)}, f32[4,8,128,128]{3,2,1,0:T(8,128)S(1)}, f32[4,8,128,128]{3,2,1,0:T(8,128)S(1)}, f32[4,8,128,128]{3,2,1,0:T(8,1...) custom-call(bf16[256,256]{1,0:T(8,128)(2,1)S(1)} %copy-done.10, ...), custom_call_target="tpu_custom_call" | custom-call | flops 10737418240 | bytes 33554432 | tf_op jit(solution)/shard_map/pallas_call | solution.py:332
  166.0 1.7 collective-permute-start.19
  167.7 3.4 %collective-permute-start.18 = (f32[4,8,128,128]{3,2,1,0:T(8,128)S(1)}, f32[4,8,128,128]{3,2,1,0:T(8,128)S(1)}, u32[]{:S(2)}, u32[]{:S(2)}) collective-permute-start(f32[4,8,128,128]{3,2,1,0:T(8,128)S(1)} %get-tuple-element.79), channel_id=1, source_target_pairs={{2,0},{0,2},{6,4},{4,6},{10,8},{8,10},{14,12},{12,14},{18,16},{16,... | collective-permute-start | bytes 6291464 | tf_op jit(solution)/shard_map/ppermute | solution.py:394
  171.8 1.4 collective-permute-start.17
  173.2 1.6 copy-done.9
  174.8 7.0 %shard_map.88 = (f32[4,8,128,128]{3,2,1,0:T(8,128)S(1)}, f32[4,8,128,128]{3,2,1,0:T(8,128)S(1)}, f32[2,8,128,128]{3,2,1,0:T(8,128)S(1)}, f32[2,8,128,128]{3,2,1,...) custom-call(bf16[256,256]{1,0:T(8,128)(2,1)S(1)} %copy-done.10, ...), custom_call_target="tpu_custom_call", output_to_operand_aliasing={{0}: (11, {}), {1}: (12, {}), {2}: (13, {}), {3}: (14, {}),... | custom-call | flops 1610612736 | bytes 15728640 | tf_op jit(solution)/shard_map/pallas_call | solution.py:359
  181.8 9.7 %collective-permute-done.19 = f32[4,8,128,128]{3,2,1,0:T(8,128)S(1)} collective-permute-done((f32[4,8,128,128]{3,2,1,0:T(8,128)}, f32[4,8,128,128]{3,2,1,0:T(8,128)S(1)}, u32[]{:S(2)}, u32[]{:S(2)}) %collective-permute-start.19) | collective-permute-done | bytes 2097184 | tf_op jit(solution)/shard_map/ppermute | solution.py:404
  191.8 5.3 %collective-permute-done.17 = f32[2,8,128,128]{3,2,1,0:T(8,128)S(1)} collective-permute-done((f32[2,8,128,128]{3,2,1,0:T(8,128)S(1)}, f32[2,8,128,128]{3,2,1,0:T(8,128)S(1)}, u32[]{:S(2)}, u32[]{:S(2)}) %collective-permute-start.17) | collective-permute-done | bytes 1048608 | tf_op jit(solution)/shard_map/ppermute | solution.py:390
  197.6 1.6 collective-permute-start.26
  199.2 1.5 collective-permute-start.27
  201.1 2.4 collective-permute-start.25
  203.6 1.4 collective-permute-start.22
  205.3 41.7 %collective-permute-done.22 = f32[2,8,128,128]{3,2,1,0:T(8,128)S(1)} collective-permute-done((f32[2,8,128,128]{3,2,1,0:T(8,128)S(1)}, f32[2,8,128,128]{3,2,1,0:T(8,128)S(1)}, u32[]{:S(2)}, u32[]{:S(2)}) %collective-permute-start.22) | collective-permute-done | bytes 1048608 | tf_op jit(solution)/shard_map/ppermute | solution.py:390
  247.2 2.5 collective-permute-done.24
  249.8 1.7 broadcast_select_fusion.5
  251.5 1.5 collective-permute-start.28
  253.0 1.3 add_bitcast_fusion
  254.3 3.7 %collective-permute-start.31 = (f32[8,128,128]{2,1,0:T(8,128)}, f32[8,128,128]{2,1,0:T(8,128)}, u32[]{:S(2)}, u32[]{:S(2)}) collective-permute-start(f32[8,128,128]{2,1,0:T(8,128)} %get-tuple-element.123), channel_id=1, source_target_pairs={{4,0},{5,1},{6,2},{7,3},{0,4},{1,5},{2,6},{3,7},{12,8},{13,9},{14,... | collective-permute-start | bytes 1572872 | tf_op jit(solution)/shard_map/ppermute | solution.py:390
  258.2 2.2 collective-permute-start.29
  260.6 14.6 %collective-permute-done.28 = f32[2,8,128,128]{3,2,1,0:T(8,128)} collective-permute-done((f32[2,8,128,128]{3,2,1,0:T(8,128)}, f32[2,8,128,128]{3,2,1,0:T(8,128)}, u32[]{:S(2)}, u32[]{:S(2)}) %collective-permute-start.28) | collective-permute-done | bytes 1048608 | tf_op jit(solution)/shard_map/ppermute | solution.py:390
  275.2 2.9 bitcast_select_fusion
  278.2 17.5 %collective-permute-done.30 = f32[8,128,128]{2,1,0:T(8,128)} collective-permute-done((f32[8,128,128]{2,1,0:T(8,128)}, f32[8,128,128]{2,1,0:T(8,128)}, u32[]{:S(2)}, u32[]{:S(2)}) %collective-permute-start.30) | collective-permute-done | bytes 524320 | tf_op jit(solution)/shard_map/ppermute | solution.py:390
  295.7 5.8 %collective-permute-done.29 = f32[8,128,128]{2,1,0:T(8,128)} collective-permute-done((f32[8,128,128]{2,1,0:T(8,128)}, f32[8,128,128]{2,1,0:T(8,128)}, u32[]{:S(2)}, u32[]{:S(2)}) %collective-permute-start.29) | collective-permute-done | bytes 524320 | tf_op jit(solution)/shard_map/ppermute | solution.py:390
  301.5 1.6 bitcast_add_fusion
  303.2 1.3 add.189
  304.4 1.2 broadcast_select_fusion.3
  (94 shorter events, 8.9 us)
Async XLA Ops:
  0.6 2.0 copy-start.15
  2.0 25.1 %collective-permute-start = (f32[2,8,128,128]{3,2,1,0:T(8,128)S(1)}, f32[2,8,128,128]{3,2,1,0:T(8,128)}, u32[]{:S(2)}, u32[]{:S(2)}) collective-permute-start(f32[2,8,128,128]{3,2,1,0:T(8,128)S(1)} %dynamic-slice_bitcast_fusion), channel_id=1, source_target_pairs={{2,0},{3,1},{0,2},{1,3},{6,4},{7,5},{4,6},{5,7},{10,8},{11,9},{8,1... | collective-permute-start | bytes 3145736 | tf_op jit(solution)/shard_map/ppermute | solution.py:390
  3.5 25.9 %collective-permute-start.1 = (f32[8,128,128]{2,1,0:T(8,128)S(1)}, f32[8,128,128]{2,1,0:T(8,128)S(1)}, u32[]{:S(2)}, u32[]{:S(2)}) collective-permute-start(f32[8,128,128]{2,1,0:T(8,128)S(1)} %bitcast.43), channel_id=1, source_target_pairs={{8,0},{9,1},{10,2},{11,3},{12,4},{13,5},{14,6},{15,7},{0,8},{1,9},... | collective-permute-start | bytes 1572872 | tf_op jit(solution)/shard_map/ppermute | solution.py:390
  6.1 24.6 %collective-permute-start.3 = (f32[8,128,128]{2,1,0:T(8,128)}, f32[8,128,128]{2,1,0:T(8,128)S(1)}, u32[]{:S(2)}, u32[]{:S(2)}) collective-permute-start(f32[8,128,128]{2,1,0:T(8,128)} %get-tuple-element.132), channel_id=1, source_target_pairs={{4,0},{5,1},{6,2},{7,3},{0,4},{1,5},{2,6},{3,7},{12,8},{13,9},{14,... | collective-permute-start | bytes 1572872 | tf_op jit(solution)/shard_map/ppermute | solution.py:390
  6.6 44.1 %collective-permute-start.2 = (f32[8,128,128]{2,1,0:T(8,128)}, f32[8,128,128]{2,1,0:T(8,128)S(1)}, u32[]{:S(2)}, u32[]{:S(2)}) collective-permute-start(f32[8,128,128]{2,1,0:T(8,128)} %get-tuple-element.132), channel_id=1, source_target_pairs={{12,0},{13,1},{14,2},{15,3},{8,4},{9,5},{10,6},{11,7},{4,8},{5,9},... | collective-permute-start | bytes 1572872 | tf_op jit(solution)/shard_map/ppermute | solution.py:390
  50.7 61.5 %copy-start.18 = (s32[16]{0:T(128)S(1)}, s32[16]{0:T(128)}, u32[]{:S(2)}) copy-start(s32[16]{0:T(128)} %constant.121.clone) | copy-start | bytes 196
  50.7 61.5 %copy-start.17 = (bf16[16,8,128]{2,1,0:T(8,128)(2,1)S(1)}, bf16[16,8,128]{2,1,0:T(8,128)(2,1)}, u32[]{:S(2)}) copy-start(bf16[16,8,128]{2,1,0:T(8,128)(2,1)} %constant.127.clone.1) | copy-start | bytes 98308
  50.7 62.1 %copy-start.16 = (bf16[16,8,128]{2,1,0:T(8,128)(2,1)S(1)}, bf16[16,8,128]{2,1,0:T(8,128)(2,1)}, u32[]{:S(2)}) copy-start(bf16[16,8,128]{2,1,0:T(8,128)(2,1)} %constant.126.clone.1) | copy-start | bytes 98308
  50.9 54.5 %collective-permute-start.6 = (f32[4,8,128,128]{3,2,1,0:T(8,128)S(1)}, f32[4,8,128,128]{3,2,1,0:T(8,128)S(1)}, u32[]{:S(2)}, u32[]{:S(2)}) collective-permute-start(f32[4,8,128,128]{3,2,1,0:T(8,128)S(1)} %pad_maximum_fusion), channel_id=1, source_target_pairs={{17,0},{0,1},{19,2},{2,3},{21,4},{4,5},{23,6},{6,7},{25,8},{8,9},{... | collective-permute-start | bytes 6291464 | tf_op jit(solution)/shard_map/ppermute | solution.py:404
  51.0 55.7 %collective-permute-start.5 = (f32[4,8,128,128]{3,2,1,0:T(8,128)S(1)}, f32[4,8,128,128]{3,2,1,0:T(8,128)}, u32[]{:S(2)}, u32[]{:S(2)}) collective-permute-start(f32[4,8,128,128]{3,2,1,0:T(8,128)S(1)} %pad_maximum_fusion), channel_id=1, source_target_pairs={{16,0},{18,2},{20,4},{22,6},{24,8},{26,10},{28,12},{30,14},{0,16},... | collective-permute-start | bytes 6291464 | tf_op jit(solution)/shard_map/ppermute | solution.py:404
  54.4 52.3 %collective-permute-start.4 = (f32[4,8,128,128]{3,2,1,0:T(8,128)S(1)}, f32[4,8,128,128]{3,2,1,0:T(8,128)}, u32[]{:S(2)}, u32[]{:S(2)}) collective-permute-start(f32[4,8,128,128]{3,2,1,0:T(8,128)S(1)} %pad_maximum_fusion), channel_id=1, source_target_pairs={{2,0},{3,1},{0,2},{1,3},{6,4},{7,5},{4,6},{5,7},{10,8},{11,9},{8,1... | collective-permute-start | bytes 6291464 | tf_op jit(solution)/shard_map/ppermute | solution.py:390
  56.0 45.3 %collective-permute-start.7 = (f32[2,8,128,128]{3,2,1,0:T(8,128)S(1)}, f32[2,8,128,128]{3,2,1,0:T(8,128)}, u32[]{:S(2)}, u32[]{:S(2)}) collective-permute-start(f32[2,8,128,128]{3,2,1,0:T(8,128)S(1)} %get-tuple-element.64), channel_id=1, source_target_pairs={{8,0},{9,1},{10,2},{11,3},{12,4},{13,5},{14,6},{15,7},{0,8},{1,9},... | collective-permute-start | bytes 3145736 | tf_op jit(solution)/shard_map/ppermute | solution.py:390
  56.0 49.4 %collective-permute-start.8 = (f32[2,8,128,128]{3,2,1,0:T(8,128)S(1)}, f32[2,8,128,128]{3,2,1,0:T(8,128)}, u32[]{:S(2)}, u32[]{:S(2)}) collective-permute-start(f32[2,8,128,128]{3,2,1,0:T(8,128)S(1)} %get-tuple-element.65.refs_2_.refs_4_), channel_id=1, source_target_pairs={{4,0},{5,1},{6,2},{7,3},{0,4},{1,5},{2,6},{3,7},{12,8},{13,9},{14,... | collective-permute-start | bytes 3145736 | tf_op jit(solution)/shard_map/ppermute | solution.py:390
  101.2 8.6 %collective-permute-start.12 = (f32[2,8,128,128]{3,2,1,0:T(8,128)S(1)}, f32[2,8,128,128]{3,2,1,0:T(8,128)S(1)}, u32[]{:S(2)}, u32[]{:S(2)}) collective-permute-start(f32[2,8,128,128]{3,2,1,0:T(8,128)S(1)} %get-tuple-element.65.refs_2_.refs_4_), channel_id=1, source_target_pairs={{1,0},{0,1},{3,2},{2,3},{5,4},{4,5},{7,6},{6,7},{9,8},{8,9},{11,10... | collective-permute-start | bytes 3145736 | tf_op jit(solution)/shard_map/ppermute | solution.py:390
  106.7 30.0 %collective-permute-start.10 = (f32[4,8,128,128]{3,2,1,0:T(8,128)}, f32[4,8,128,128]{3,2,1,0:T(8,128)}, u32[]{:S(2)}, u32[]{:S(2)}) collective-permute-start(f32[4,8,128,128]{3,2,1,0:T(8,128)} %collective-permute-done.5), channel_id=1, source_target_pairs={{2,0},{0,2},{6,4},{4,6},{10,8},{8,10},{14,12},{12,14},{18,16},{16,... | collective-permute-start | bytes 6291464 | tf_op jit(solution)/shard_map/ppermute | solution.py:394
  109.2 27.5 %collective-permute-start.11 = (f32[4,8,128,128]{3,2,1,0:T(8,128)}, f32[4,8,128,128]{3,2,1,0:T(8,128)}, u32[]{:S(2)}, u32[]{:S(2)}) collective-permute-start(f32[4,8,128,128]{3,2,1,0:T(8,128)} %collective-permute-done.4), channel_id=1, source_target_pairs={{17,0},{0,1},{19,2},{2,3},{21,4},{4,5},{23,6},{6,7},{25,8},{8,9},{... | collective-permute-start | bytes 6291464 | tf_op jit(solution)/shard_map/ppermute | solution.py:404
  109.2 6.2 %collective-permute-start.13 = (f32[2,8,128,128]{3,2,1,0:T(8,128)}, f32[2,8,128,128]{3,2,1,0:T(8,128)}, u32[]{:S(2)}, u32[]{:S(2)}) collective-permute-start(f32[2,8,128,128]{3,2,1,0:T(8,128)} %collective-permute-done.8.refs_3_.refs_5_), channel_id=1, source_target_pairs={{1,0},{0,1},{3,2},{2,3},{5,4},{4,5},{7,6},{6,7},{9,8},{8,9},{11,10... | collective-permute-start | bytes 3145736 | tf_op jit(solution)/shard_map/ppermute | solution.py:390
  109.9 6.5 %collective-permute-start.14 = (f32[2,8,128,128]{3,2,1,0:T(8,128)}, f32[2,8,128,128]{3,2,1,0:T(8,128)}, u32[]{:S(2)}, u32[]{:S(2)}) collective-permute-start(f32[2,8,128,128]{3,2,1,0:T(8,128)} %collective-permute-done.7.refs_4_.refs_6_), channel_id=1, source_target_pairs={{1,0},{0,1},{3,2},{2,3},{5,4},{4,5},{7,6},{6,7},{9,8},{8,9},{11,10... | collective-permute-start | bytes 3145736 | tf_op jit(solution)/shard_map/ppermute | solution.py:390
  110.8 25.9 %collective-permute-start.9 = (f32[2,8,128,128]{3,2,1,0:T(8,128)}, f32[2,8,128,128]{3,2,1,0:T(8,128)}, u32[]{:S(2)}, u32[]{:S(2)}) collective-permute-start(f32[2,8,128,128]{3,2,1,0:T(8,128)} %collective-permute-done.7.refs_4_.refs_6_), channel_id=1, source_target_pairs={{4,0},{5,1},{6,2},{7,3},{0,4},{1,5},{2,6},{3,7},{12,8},{13,9},{14,... | collective-permute-start | bytes 3145736 | tf_op jit(solution)/shard_map/ppermute | solution.py:390
  113.4 3.0 copy-start.3
  113.4 3.0 copy-start.6
  113.4 3.0 copy-start.10
  113.4 3.0 copy-start.11
  115.4 7.1 %copy-start = (f32[4,8,128,128]{3,2,1,0:T(8,128)}, f32[4,8,128,128]{3,2,1,0:T(8,128)S(1)}, u32[]{:S(2)}) copy-start(f32[4,8,128,128]{3,2,1,0:T(8,128)S(1)} %broadcast_select_fusion.2.refs_0_) | copy-start | bytes 6291460
  122.5 1.7 copy-start.8
  136.7 3.7 %collective-permute-start.15 = (f32[2,8,128,128]{3,2,1,0:T(8,128)}, f32[2,8,128,128]{3,2,1,0:T(8,128)S(1)}, u32[]{:S(2)}, u32[]{:S(2)}) collective-permute-start(f32[2,8,128,128]{3,2,1,0:T(8,128)} %collective-permute-done.9.refs_7_), channel_id=1, source_target_pairs={{1,0},{0,1},{3,2},{2,3},{5,4},{4,5},{7,6},{6,7},{9,8},{8,9},{11,10... | collective-permute-start | bytes 3145736 | tf_op jit(solution)/shard_map/ppermute | solution.py:390
  137.1 3.4 %copy-start.7 = (f32[2,8,128,128]{3,2,1,0:T(8,128)S(1)}, f32[2,8,128,128]{3,2,1,0:T(8,128)}, u32[]{:S(2)}) copy-start(f32[2,8,128,128]{3,2,1,0:T(8,128)} %copy-done.5) | copy-start | bytes 3145732
  140.4 32.8 %copy-start.4 = (f32[4,8,128,128]{3,2,1,0:T(8,128)S(1)}, f32[4,8,128,128]{3,2,1,0:T(8,128)}, u32[]{:S(2)}) copy-start(f32[4,8,128,128]{3,2,1,0:T(8,128)} %copy-done.2) | copy-start | bytes 6291460
  166.0 7.3 %copy-start.1 = (f32[4,8,128,128]{3,2,1,0:T(8,128)S(1)}, f32[4,8,128,128]{3,2,1,0:T(8,128)}, u32[]{:S(2)}) copy-start(f32[4,8,128,128]{3,2,1,0:T(8,128)} %copy-done) | copy-start | bytes 6291460
  166.0 25.5 %collective-permute-start.19 = (f32[4,8,128,128]{3,2,1,0:T(8,128)}, f32[4,8,128,128]{3,2,1,0:T(8,128)S(1)}, u32[]{:S(2)}, u32[]{:S(2)}) collective-permute-start(f32[4,8,128,128]{3,2,1,0:T(8,128)} %get-tuple-element.80), channel_id=1, source_target_pairs={{0,17},{1,0},{2,19},{3,2},{4,21},{5,4},{6,23},{7,6},{8,25},{9,8},{... | collective-permute-start | bytes 6291464 | tf_op jit(solution)/shard_map/ppermute | solution.py:404
  167.7 4.0 %collective-permute-start.16 = (f32[2,8,128,128]{3,2,1,0:T(8,128)S(1)}, f32[2,8,128,128]{3,2,1,0:T(8,128)S(1)}, u32[]{:S(2)}, u32[]{:S(2)}) collective-permute-start(f32[2,8,128,128]{3,2,1,0:T(8,128)S(1)} %get-tuple-element.76), channel_id=1, source_target_pairs={{1,0},{0,1},{3,2},{2,3},{5,4},{4,5},{7,6},{6,7},{9,8},{8,9},{11,10... | collective-permute-start | bytes 3145736 | tf_op jit(solution)/shard_map/ppermute | solution.py:390
  167.7 29.4 %collective-permute-start.18 = (f32[4,8,128,128]{3,2,1,0:T(8,128)S(1)}, f32[4,8,128,128]{3,2,1,0:T(8,128)S(1)}, u32[]{:S(2)}, u32[]{:S(2)}) collective-permute-start(f32[4,8,128,128]{3,2,1,0:T(8,128)S(1)} %get-tuple-element.79), channel_id=1, source_target_pairs={{2,0},{0,2},{6,4},{4,6},{10,8},{8,10},{14,12},{12,14},{18,16},{16,... | collective-permute-start | bytes 6291464 | tf_op jit(solution)/shard_map/ppermute | solution.py:394
  171.8 25.3 %collective-permute-start.17 = (f32[2,8,128,128]{3,2,1,0:T(8,128)S(1)}, f32[2,8,128,128]{3,2,1,0:T(8,128)S(1)}, u32[]{:S(2)}, u32[]{:S(2)}) collective-permute-start(f32[2,8,128,128]{3,2,1,0:T(8,128)S(1)} %add.164), channel_id=1, source_target_pairs={{4,0},{5,1},{6,2},{7,3},{0,4},{1,5},{2,6},{3,7},{12,8},{13,9},{14,... | collective-permute-start | bytes 3145736 | tf_op jit(solution)/shard_map/ppermute | solution.py:390
  197.1 4.0 %collective-permute-start.21 = (f32[2,8,128,128]{3,2,1,0:T(8,128)S(1)}, f32[2,8,128,128]{3,2,1,0:T(8,128)S(1)}, u32[]{:S(2)}, u32[]{:S(2)}) collective-permute-start(f32[2,8,128,128]{3,2,1,0:T(8,128)S(1)} %get-tuple-element.101), channel_id=1, source_target_pairs={{1,0},{0,1},{3,2},{2,3},{5,4},{4,5},{7,6},{6,7},{9,8},{8,9},{11,10... | collective-permute-start | bytes 3145736 | tf_op jit(solution)/shard_map/ppermute | solution.py:390
  197.1 8.1 %collective-permute-start.20 = (f32[2,8,128,128]{3,2,1,0:T(8,128)S(1)}, f32[2,8,128,128]{3,2,1,0:T(8,128)S(1)}, u32[]{:S(2)}, u32[]{:S(2)}) collective-permute-start(f32[2,8,128,128]{3,2,1,0:T(8,128)S(1)} %get-tuple-element.99), channel_id=1, source_target_pairs={{1,0},{0,1},{3,2},{2,3},{5,4},{4,5},{7,6},{6,7},{9,8},{8,9},{11,10... | collective-permute-start | bytes 3145736 | tf_op jit(solution)/shard_map/ppermute | solution.py:390
  197.6 6.0 %collective-permute-start.23 = (f32[2,8,128,128]{3,2,1,0:T(8,128)S(1)}, f32[2,8,128,128]{3,2,1,0:T(8,128)S(1)}, u32[]{:S(2)}, u32[]{:S(2)}) collective-permute-start(f32[2,8,128,128]{3,2,1,0:T(8,128)S(1)} %get-tuple-element.104), channel_id=1, source_target_pairs={{1,0},{0,1},{3,2},{2,3},{5,4},{4,5},{7,6},{6,7},{9,8},{8,9},{11,10... | collective-permute-start | bytes 3145736 | tf_op jit(solution)/shard_map/ppermute | solution.py:390
  197.6 52.0 %collective-permute-start.26 = (f32[4,8,128,128]{3,2,1,0:T(8,128)S(1)}, f32[4,8,128,128]{3,2,1,0:T(8,128)S(1)}, u32[]{:S(2)}, u32[]{:S(2)}) collective-permute-start(f32[4,8,128,128]{3,2,1,0:T(8,128)S(1)} %get-tuple-element.107), channel_id=1, source_target_pairs={{0,17},{1,0},{2,19},{3,2},{4,21},{5,4},{6,23},{7,6},{8,25},{9,8},{... | collective-permute-start | bytes 6291464 | tf_op jit(solution)/shard_map/ppermute | solution.py:404
  199.2 50.4 %collective-permute-start.27 = (f32[4,8,128,128]{3,2,1,0:T(8,128)S(1)}, f32[4,8,128,128]{3,2,1,0:T(8,128)S(1)}, u32[]{:S(2)}, u32[]{:S(2)}) collective-permute-start(f32[4,8,128,128]{3,2,1,0:T(8,128)S(1)} %select_add_fusion), channel_id=1, source_target_pairs={{2,0},{3,1},{0,2},{1,3},{6,4},{7,5},{4,6},{5,7},{10,8},{11,9},{8,1... | collective-permute-start | bytes 6291464 | tf_op jit(solution)/shard_map/ppermute | solution.py:390
  201.1 48.6 %collective-permute-start.25 = (f32[4,8,128,128]{3,2,1,0:T(8,128)S(1)}, f32[4,8,128,128]{3,2,1,0:T(8,128)S(1)}, u32[]{:S(2)}, u32[]{:S(2)}) collective-permute-start(f32[4,8,128,128]{3,2,1,0:T(8,128)S(1)} %get-tuple-element.120), channel_id=1, source_target_pairs={{0,16},{2,18},{4,20},{6,22},{8,24},{10,26},{12,28},{14,30},{16,0},... | collective-permute-start | bytes 6291464 | tf_op jit(solution)/shard_map/ppermute | solution.py:404
  203.6 43.4 %collective-permute-start.22 = (f32[2,8,128,128]{3,2,1,0:T(8,128)S(1)}, f32[2,8,128,128]{3,2,1,0:T(8,128)S(1)}, u32[]{:S(2)}, u32[]{:S(2)}) collective-permute-start(f32[2,8,128,128]{3,2,1,0:T(8,128)S(1)} %add.167), channel_id=1, source_target_pairs={{4,0},{5,1},{6,2},{7,3},{0,4},{1,5},{2,6},{3,7},{12,8},{13,9},{14,... | collective-permute-start | bytes 3145736 | tf_op jit(solution)/shard_map/ppermute | solution.py:390
  205.2 44.4 %collective-permute-start.24 = (f32[2,8,128,128]{3,2,1,0:T(8,128)S(1)}, f32[2,8,128,128]{3,2,1,0:T(8,128)S(1)}, u32[]{:S(2)}, u32[]{:S(2)}) collective-permute-start(f32[2,8,128,128]{3,2,1,0:T(8,128)S(1)} %add_add_fusion), channel_id=1, source_target_pairs={{8,0},{9,1},{10,2},{11,3},{12,4},{13,5},{14,6},{15,7},{0,8},{1,9},... | collective-permute-start | bytes 3145736 | tf_op jit(solution)/shard_map/ppermute | solution.py:390
  249.6 3.4 %copy-start.12 = (f32[4,8,128,128]{3,2,1,0:T(8,128)}, f32[4,8,128,128]{3,2,1,0:T(8,128)S(1)}, u32[]{:S(2)}) copy-start(f32[4,8,128,128]{3,2,1,0:T(8,128)S(1)} %collective-permute-done.26) | copy-start | bytes 6291460
  249.6 3.4 %copy-start.13 = (f32[4,8,128,128]{3,2,1,0:T(8,128)}, f32[4,8,128,128]{3,2,1,0:T(8,128)S(1)}, u32[]{:S(2)}) copy-start(f32[4,8,128,128]{3,2,1,0:T(8,128)S(1)} %collective-permute-done.27) | copy-start | bytes 6291460
  249.7 3.3 %copy-start.14 = (f32[4,8,128,128]{3,2,1,0:T(8,128)}, f32[4,8,128,128]{3,2,1,0:T(8,128)S(1)}, u32[]{:S(2)}) copy-start(f32[4,8,128,128]{3,2,1,0:T(8,128)S(1)} %collective-permute-done.25) | copy-start | bytes 6291460
  251.5 23.7 %collective-permute-start.28 = (f32[2,8,128,128]{3,2,1,0:T(8,128)}, f32[2,8,128,128]{3,2,1,0:T(8,128)}, u32[]{:S(2)}, u32[]{:S(2)}) collective-permute-start(f32[2,8,128,128]{3,2,1,0:T(8,128)} %get-tuple-element.141), channel_id=1, source_target_pairs={{2,0},{3,1},{0,2},{1,3},{6,4},{7,5},{4,6},{5,7},{10,8},{11,9},{8,1... | collective-permute-start | bytes 3145736 | tf_op jit(solution)/shard_map/ppermute | solution.py:390
  254.3 23.9 %collective-permute-start.31 = (f32[8,128,128]{2,1,0:T(8,128)}, f32[8,128,128]{2,1,0:T(8,128)}, u32[]{:S(2)}, u32[]{:S(2)}) collective-permute-start(f32[8,128,128]{2,1,0:T(8,128)} %get-tuple-element.123), channel_id=1, source_target_pairs={{4,0},{5,1},{6,2},{7,3},{0,4},{1,5},{2,6},{3,7},{12,8},{13,9},{14,... | collective-permute-start | bytes 1572872 | tf_op jit(solution)/shard_map/ppermute | solution.py:390
  258.1 37.6 %collective-permute-start.30 = (f32[8,128,128]{2,1,0:T(8,128)}, f32[8,128,128]{2,1,0:T(8,128)}, u32[]{:S(2)}, u32[]{:S(2)}) collective-permute-start(f32[8,128,128]{2,1,0:T(8,128)} %get-tuple-element.124), channel_id=1, source_target_pairs={{12,0},{13,1},{14,2},{15,3},{8,4},{9,5},{10,6},{11,7},{4,8},{5,9},... | collective-permute-start | bytes 1572872 | tf_op jit(solution)/shard_map/ppermute | solution.py:390
  258.2 43.3 %collective-permute-start.29 = (f32[8,128,128]{2,1,0:T(8,128)}, f32[8,128,128]{2,1,0:T(8,128)}, u32[]{:S(2)}, u32[]{:S(2)}) collective-permute-start(f32[8,128,128]{2,1,0:T(8,128)} %get-tuple-element.125), channel_id=1, source_target_pairs={{8,0},{9,1},{10,2},{11,3},{12,4},{13,5},{14,6},{15,7},{0,8},{1,9},... | collective-permute-start | bytes 1572872 | tf_op jit(solution)/shard_map/ppermute | solution.py:390
  (3 other events, 3.9 us)

commit v7 on v6

--- a/solution.py
+++ b/solution.py
@@ -176,7 +176,8 @@
 
 
 def late_kernel(
-    steps, right_ref, left_ref, z_left_ref, z_back_ref, square_ref, early_ref, *refs
+    steps, groups, right_ref, left_ref, z_left_ref, z_back_ref, square_ref, early_ref, home_ref,
+    *refs,
 ):
     names = used(steps)
     pieces, early_out = dict(zip(names, refs)), refs[len(names)]
@@ -189,13 +190,27 @@
         own, z, part, x = steps[k]
         return [(arrays[own].at[z], own_ref.at[k]), (arrays[part].at[x], part_ref.at[k])]
 
-    for k in range(count):
-        for j, (block, held) in enumerate(blocks(k, pieces)):
-            pltpu.make_async_copy(block, held, in_sems.at[j, k]).start()
+    def fetch(turns, arrays):
+        for k in turns:
+            for j, (block, held) in enumerate(blocks(k, arrays)):
+                pltpu.make_async_copy(block, held, in_sems.at[j, k]).start()
+
+    chosen = [k for k in range(count) if steps[k][0] == 1]
+    fetch([k for k in range(count) if k not in chosen], pieces)
+    at_home = lax.rem(lax.rem(lax.axis_index("slab"), 2) + 1, groups) == 0
+
+    @pl.when(at_home)
+    def _():
+        fetch(chosen, {**pieces, 1: home_ref})
+
+    @pl.when(jnp.logical_not(at_home))
+    def _():
+        fetch(chosen, pieces)
+
     middle_in = pltpu.make_async_copy(early_ref, middle_ref, middle_sems.at[0])
     middle_in.start()
 
-    @pl.loop(0, count)
+    @pl.loop(0, count, unroll=5)
     def _(k):
         pltpu.make_async_copy(pieces[names[0]].at[0], own_ref.at[k], in_sems.at[0, k]).wait()
         pltpu.make_async_copy(pieces[names[0]].at[0], part_ref.at[k], in_sems.at[1, k]).wait()
@@ -210,7 +225,7 @@
             out_ref[pl.ds(r + 1, length, stride=rows), :] = block[:, length:]
 
     middle_in.wait()
-    group = 8
+    group = 32
     scale = coulomb_scale / float(length**3)
 
     @pl.loop(0, length // group)
@@ -235,7 +250,7 @@
     middle_out = pltpu.make_async_copy(middle_ref, early_out, middle_sems.at[1])
     middle_out.start()
 
-    @pl.loop(0, count)
+    @pl.loop(0, count, unroll=5)
     def _(k):
         in_ref = field_ref.at[k]
         for r in range(0, rows, 2):
@@ -323,16 +338,16 @@
     )(right, left, *[pieces[name] for name in used(steps)])
 
 
-def late_part(right, left, z_left, z_back, square, early, pieces, steps):
+def late_part(right, left, z_left, z_back, square, early, home, pieces, steps, groups):
     rows, length = pieces[0].shape[1], pieces[0].shape[2]
     names = used(steps)
     count = len(steps)
     tables = [right, left, z_left, z_back, square]
     anywhere = pl.BlockSpec(memory_space=pl.ANY)
     early, *outs = pl.pallas_call(
-        functools.partial(late_kernel, steps),
+        functools.partial(late_kernel, steps, groups),
         in_specs=[pl.BlockSpec(memory_space=pltpu.VMEM)] * len(tables)
-        + [anywhere] * (1 + len(names)),
+        + [anywhere] * (2 + len(names)),
         out_specs=[anywhere] * (1 + len(names)),
         out_shape=[jax.ShapeDtypeStruct(early.shape, jnp.float32)]
         + [jax.ShapeDtypeStruct(pieces[name].shape, jnp.float32) for name in names],
@@ -347,7 +362,7 @@
         ],
         compiler_params=pltpu.CompilerParams(vmem_limit_bytes=32 * 2**20),
         cost_estimate=cost(length**3, length, 4, 5),
-    )(*tables, early, *[pieces[name] for name in names])
+    )(*tables, early, home, *[pieces[name] for name in names])
     return early, dict(zip(names, outs))
 
 
@@ -430,9 +445,11 @@
     square = waves[:, None] * waves[:, None] + waves[None] * waves[None]
 
     kept, passed = pick(own, own_band), pick(own, 1 - own_band)
+    parts = partners.reshape((2, 2) + partners.shape[1:])
+    parts_x = pick(parts, 1 - part_low, 1)
+    kept, passed, parts_x = together(kept, passed, parts_x)
     from_z = [swap(kept, 8), swap(passed, 12), swap(passed, 4)]
-    parts = partners.reshape((2, 2) + partners.shape[1:])
-    parts, parts_x = pick(parts, part_low, 1), swap(pick(parts, 1 - part_low, 1), 2)
+    parts, parts_x = pick(parts, part_low, 1), swap(parts_x, 2)
     kept_near = jnp.stack([pick(parts, part_half), pick(parts_x, part_half)])
     leaving = jnp.stack([pick(parts, 1 - part_half), pick(parts_x, 1 - part_half)])
     kept_near, leaving, *from_z = together(kept_near, leaving, *from_z)
@@ -443,18 +460,17 @@
     bands_x, first, second, got_near, kept_far = together(
         bands_x, first, second, got_near, kept_far
     )
+    first_x, second_x = swap_away(first, 2), across(bands_x, 1, False)
     got_far = swap(got_near, 4)
-    first_x, second_x = swap_away(first, 2), across(bands_x, 1, False)
     parts = [kept_near, kept_far, got_near]
     parts_c = [swap(part, 1) for part in parts]
     first = jnp.where(at_home, bands, first)
     early = [first, None, second, None] + parts + [None] + parts_c + [None]
     field_early = gather_part(right, left, early, EARLY)
     got_far, first_x, second_x, field_early = together(got_far, first_x, second_x, field_early)
-    first_x = jnp.where(at_home, bands_x, first_x)
     pieces = [first, first_x, second, second_x] + parts + [got_far] + parts_c + [swap(got_far, 1)]
     field_early, outs = late_part(
-        right, left, z_left, z_back, square, field_early, pieces, LATE
+        right, left, z_left, z_back, square, field_early, bands_x, pieces, LATE, groups
     )
     got_far = outs[7] + swap(outs[11], 1)
     got_far, field_early = together(got_far, field_early)
@@ -463,9 +479,7 @@
     bands_x = across(outs[3], 1, True) + jnp.where(at_home, outs[1], 0.0)
     outs = scatter_part(right, left, field_early, pieces, EARLY, outs)
     names = sorted(outs)
-    got_near, first, bands_x, *blocks = together(
-        got_near, first, bands_x, *[outs[name] for name in names]
-    )
+    first, bands_x, *blocks = together(first, bands_x, *[outs[name] for name in names])
     outs = dict(zip(names, blocks))
     got_near = got_near + outs[6] + swap(outs[10], 1)
     kept_far = outs[5] + swap(outs[9], 1)
@@ -477,11 +491,13 @@
     terms.append(jnp.where(at_home, first, 0.0))
     kept_near, leaving, *terms = together(kept_near, leaving, *terms)
     bands = [sum(term[z] for term in terms) for z in range(4)]
+    kept_near, leaving, *bands = together(kept_near, leaving, *bands)
+    from_z = [swap(bands[2], 8), swap(bands[3], 12), swap(bands[1], 4)]
     parts_x = swap(ordered(part_half, kept_near[1], leaving[1]), 2)
-    from_z = [swap(bands[2], 8), swap(bands[3], 12), swap(bands[1], 4)]
     parts = ordered(part_low, ordered(part_half, kept_near[0], leaving[0]), parts_x, 1)
     parts, *from_z = together(parts.reshape(partners.shape), *from_z)
-    return ordered(own_band, bands[0] + from_z[0], from_z[1] + from_z[2]), parts
+    own_out = ordered(own_band, bands[0], from_z[1]) + ordered(own_band, from_z[0], from_z[2])
+    return own_out, parts
 
 
 def solution(mesh):

time: 312 us -> 298 us (0.955); the launches traced: 306 us -> 298 us
  other arithmetic: 17.1 us -> 11.5 us
    ppermute x2, waiting for transfers between devices: 0.01 us -> 3.75 us  [swap_away(): return lax.ppermute(block, 'slab', [(i ^ mask, i) for i in away])]
    select_n x1 -> x0, other arithmetic: 3.35 us -> none  [whole_fields(): first_x = jnp.where(at_home, bands_x, first_x)]
    unnamed x38 -> x34, local copies, waits for them, and re-layouts: 5.62 us -> 6.95 us
  transfers between devices with their start and end apart: 32 -> 32, of which waited for: 17 -> 18; matrix products, arithmetic and copies ran while one was open for 5% -> 4% of each run, Pallas kernels for 4% -> 4%
where the time goes in v7:
time: 298 us
  waiting for transfers between devices  200 us (67%)
  starting transfers between devices  36.4 us (12%)
  Pallas kernels  35.7 us (12%)
  local copies, waits for them, and re-layouts  13.2 us (4%)
  other arithmetic  11.5 us (4%)
    ppermute x24, waiting for transfers between devices, swap(): return lax.ppermute(block, 'slab', [(i ^ mask, i) for i in range(slabs)])  188 us
    pallas_call x1, Pallas kernels, late_part(): pl.pallas_call(functools.partial(late_kernel, steps, groups), in_specs=[p...  22.6 us
    ppermute x24, starting transfers between devices, swap(): return lax.ppermute(block, 'slab', [(i ^ mask, i) for i in range(slabs)])  22.1 us
    ppermute x6, starting transfers between devices, across(): return lax.ppermute(block, ('band', 'slab'), route)  8.49 us
    ppermute x6, waiting for transfers between devices, across(): return lax.ppermute(block, ('band', 'slab'), route)  7.66 us
    pallas_call x1, Pallas kernels, scatter_part(): pl.pallas_call(functools.partial(scatter_kernel, steps), grid=(len(steps)...  6.96 us
    unnamed x34, local copies, waits for them, and re-layouts  6.95 us
    pallas_call x1, Pallas kernels, gather_part(): pl.pallas_call(functools.partial(gather_kernel, steps), grid=(count,), in...  6.13 us
  transfers between devices with their start and end apart: 32, of which 18 were waited for; matrix products, arithmetic and copies ran while one was open for 4% of the time, Pallas kernels for 4%

profile of v7, /device:TPU:10, one launch (start us, length us, event | category | flops | bytes accessed | tf_op | source)
XLA Modules:
  0.0 297.5 jit_solution(15374468479141567111)
XLA Ops:
  0.6 1.4 dynamic-slice_bitcast_fusion
  2.2 0.9 dynamic-slice_bitcast_fusion.3
  3.6 2.6 collective-permute-start.1
  7.1 1.3 dynamic-slice_bitcast_fusion.1
  8.4 19.7 %collective-permute-done = f32[2,8,128,128]{3,2,1,0:T(8,128)} collective-permute-done((f32[2,8,128,128]{3,2,1,0:T(8,128)S(1)}, f32[2,8,128,128]{3,2,1,0:T(8,128)}, u32[]{:S(2)}, u32[]{:S(2)}) %collective-permute-start) | collective-permute-done | bytes 1048608 | tf_op jit(solution)/shard_map/ppermute | solution.py:405
  28.1 1.3 constant_dynamic-slice_fusion
  29.6 1.2 collective-permute-done.3
  30.7 20.0 %collective-permute-done.2 = f32[8,128,128]{2,1,0:T(8,128)S(1)} collective-permute-done((f32[8,128,128]{2,1,0:T(8,128)}, f32[8,128,128]{2,1,0:T(8,128)S(1)}, u32[]{:S(2)}, u32[]{:S(2)}) %collective-permute-start.2) | collective-permute-done | bytes 524320 | tf_op jit(solution)/shard_map/ppermute | solution.py:405
  51.1 3.4 %collective-permute-start.5 = (f32[4,8,128,128]{3,2,1,0:T(8,128)S(1)}, f32[4,8,128,128]{3,2,1,0:T(8,128)}, u32[]{:S(2)}, u32[]{:S(2)}) collective-permute-start(f32[4,8,128,128]{3,2,1,0:T(8,128)S(1)} %pad_maximum_fusion), channel_id=1, source_target_pairs={{16,0},{18,2},{20,4},{22,6},{24,8},{26,10},{28,12},{30,14},{0,16},... | collective-permute-start | bytes 6291464 | tf_op jit(solution)/shard_map/ppermute | solution.py:419
  54.5 1.6 collective-permute-start.4
  56.0 3.8 %collective-permute-start.8 = (f32[2,8,128,128]{3,2,1,0:T(8,128)S(1)}, f32[2,8,128,128]{3,2,1,0:T(8,128)}, u32[]{:S(2)}, u32[]{:S(2)}) collective-permute-start(f32[2,8,128,128]{3,2,1,0:T(8,128)S(1)} %get-tuple-element.76.refs_2_.refs_4_), channel_id=1, source_target_pairs={{4,0},{5,1},{6,2},{7,3},{0,4},{1,5},{2,6},{3,7},{12,8},{13,9},{14,... | collective-permute-start | bytes 3145736 | tf_op jit(solution)/shard_map/ppermute | solution.py:405
  59.9 41.3 %collective-permute-done.7.refs_4_.refs_6_ = f32[2,8,128,128]{3,2,1,0:T(8,128)} collective-permute-done((f32[2,8,128,128]{3,2,1,0:T(8,128)S(1)}, f32[2,8,128,128]{3,2,1,0:T(8,128)}, u32[]{:S(2)}, u32[]{:S(2)}) %collective-permute-start.7) | collective-permute-done | bytes 1048608 | tf_op jit(solution)/shard_map/ppermute | solution.py:405
  101.2 4.2 %collective-permute-done.8.refs_3_.refs_5_ = f32[2,8,128,128]{3,2,1,0:T(8,128)} collective-permute-done((f32[2,8,128,128]{3,2,1,0:T(8,128)S(1)}, f32[2,8,128,128]{3,2,1,0:T(8,128)}, u32[]{:S(2)}, u32[]{:S(2)}) %collective-permute-start.8) | collective-permute-done | bytes 1048608 | tf_op jit(solution)/shard_map/ppermute | solution.py:405
  105.4 1.3 copy-done.2
  106.7 2.4 collective-permute-start.10
  109.8 1.0 copy-done.5
  110.8 1.3 collective-permute-start.9
  112.1 2.0 broadcast_select_fusion.1.refs_0_
  114.8 1.5 collective-permute-done.14.refs_7_.refs_10_
  116.3 6.1 %shard_map.86.early_ref = f32[128,48,128]{2,1,0:T(8,128)S(1)} custom-call(bf16[256,256]{1,0:T(8,128)(2,1)S(1)} %copy-done.11, bf16[256,256]{1,0:T(8,128)(2,1)S(1)} %copy-done.12, f32[4,8,128,128]{3,2,1,0:T(8,128)S(1)} %broadcast_select_fusion.1.refs_0_, f32[4,8,128,128]{3,2,1,0:T(8,128)S(1)} %copy-done.3, ...), custom_call_target="tpu_custom_call" | custom-call | flops 1610612736 | bytes 9437184 | tf_op jit(solution)/shard_map/pallas_call | solution.py:328
  122.5 1.7 copy-done.9
  124.1 12.5 %collective-permute-done.9.refs_7_ = f32[2,8,128,128]{3,2,1,0:T(8,128)} collective-permute-done((f32[2,8,128,128]{3,2,1,0:T(8,128)}, f32[2,8,128,128]{3,2,1,0:T(8,128)}, u32[]{:S(2)}, u32[]{:S(2)}) %collective-permute-start.9) | collective-permute-done | bytes 1048608 | tf_op jit(solution)/shard_map/ppermute | solution.py:405
  138.2 1.3 collective-permute-done.15.refs_11_
  139.5 1.2 copy-done.7
  140.8 22.6 %shard_map.87 = (f32[128,48,128]{2,1,0:T(8,128)}, f32[4,8,128,128]{3,2,1,0:T(8,128)S(1)}, f32[4,8,128,128]{3,2,1,0:T(8,128)S(1)}, f32[4,8,128,128]{3,2,1,0:T(8,1...) custom-call(bf16[256,256]{1,0:T(8,128)(2,1)S(1)} %copy-done.11, ...), custom_call_target="tpu_custom_call" | custom-call | flops 10737418240 | bytes 33554432 | tf_op jit(solution)/shard_map/pallas_call | solution.py:347
  163.4 1.3 collective-permute-start.17
  164.7 3.4 %collective-permute-start.16 = (f32[4,8,128,128]{3,2,1,0:T(8,128)S(1)}, f32[4,8,128,128]{3,2,1,0:T(8,128)S(1)}, u32[]{:S(2)}, u32[]{:S(2)}) collective-permute-start(f32[4,8,128,128]{3,2,1,0:T(8,128)S(1)} %get-tuple-element.86), channel_id=1, source_target_pairs={{2,0},{0,2},{6,4},{4,6},{10,8},{8,10},{14,12},{12,14},{18,16},{16,... | collective-permute-start | bytes 6291464 | tf_op jit(solution)/shard_map/ppermute | solution.py:409
  168.2 2.6 collective-permute-done.18
  171.0 1.4 collective-permute-start.22
  172.4 1.6 copy-done.10
  174.0 7.0 %shard_map.88 = (f32[4,8,128,128]{3,2,1,0:T(8,128)S(1)}, f32[4,8,128,128]{3,2,1,0:T(8,128)S(1)}, f32[2,8,128,128]{3,2,1,0:T(8,128)S(1)}, f32[2,8,128,128]{3,2,1,...) custom-call(bf16[256,256]{1,0:T(8,128)(2,1)S(1)} %copy-done.11, ...), custom_call_target="tpu_custom_call", output_to_operand_aliasing={{0}: (11, {}), {1}: (12, {}), {2}: (13, {}), {3}: (14, {}),... | custom-call | flops 1610612736 | bytes 15728640 | tf_op jit(solution)/shard_map/pallas_call | solution.py:374
  180.9 7.6 %collective-permute-done.17 = f32[4,8,128,128]{3,2,1,0:T(8,128)S(1)} collective-permute-done((f32[4,8,128,128]{3,2,1,0:T(8,128)}, f32[4,8,128,128]{3,2,1,0:T(8,128)S(1)}, u32[]{:S(2)}, u32[]{:S(2)}) %collective-permute-start.17) | collective-permute-done | bytes 2097184 | tf_op jit(solution)/shard_map/ppermute | solution.py:419
  188.9 3.7 %collective-permute-done.16 = f32[4,8,128,128]{3,2,1,0:T(8,128)S(1)} collective-permute-done((f32[4,8,128,128]{3,2,1,0:T(8,128)S(1)}, f32[4,8,128,128]{3,2,1,0:T(8,128)S(1)}, u32[]{:S(2)}, u32[]{:S(2)}) %collective-permute-start.16) | collective-permute-done | bytes 2097184 | tf_op jit(solution)/shard_map/ppermute | solution.py:409
  193.2 0.8 collective-permute-start.26
  194.4 1.9 collective-permute-done.22
  196.8 2.9 collective-permute-start.25
  199.8 1.4 collective-permute-start.21
  201.5 41.1 %collective-permute-done.21 = f32[2,8,128,128]{3,2,1,0:T(8,128)S(1)} collective-permute-done((f32[2,8,128,128]{3,2,1,0:T(8,128)S(1)}, f32[2,8,128,128]{3,2,1,0:T(8,128)S(1)}, u32[]{:S(2)}, u32[]{:S(2)}) %collective-permute-start.21) | collective-permute-done | bytes 1048608 | tf_op jit(solution)/shard_map/ppermute | solution.py:405
  242.7 2.5 collective-permute-done.24
  245.2 1.8 add_bitcast_fusion
  247.5 1.6 collective-permute-start.28
  249.0 3.3 %collective-permute-start.29 = (f32[8,128,128]{2,1,0:T(8,128)}, f32[8,128,128]{2,1,0:T(8,128)}, u32[]{:S(2)}, u32[]{:S(2)}) collective-permute-start(f32[8,128,128]{2,1,0:T(8,128)} %get-tuple-element.128), channel_id=1, source_target_pairs={{8,0},{9,1},{10,2},{11,3},{12,4},{13,5},{14,6},{15,7},{0,8},{1,9},... | collective-permute-start | bytes 1572872 | tf_op jit(solution)/shard_map/ppermute | solution.py:405
  252.4 1.9 collective-permute-start.30
  254.4 15.9 %collective-permute-done.28 = f32[2,8,128,128]{3,2,1,0:T(8,128)} collective-permute-done((f32[2,8,128,128]{3,2,1,0:T(8,128)S(1)}, f32[2,8,128,128]{3,2,1,0:T(8,128)}, u32[]{:S(2)}, u32[]{:S(2)}) %collective-permute-start.28) | collective-permute-done | bytes 1048608 | tf_op jit(solution)/shard_map/ppermute | solution.py:405
  270.3 2.9 bitcast_select_fusion
  273.2 10.9 %collective-permute-done.29 = f32[8,128,128]{2,1,0:T(8,128)} collective-permute-done((f32[8,128,128]{2,1,0:T(8,128)}, f32[8,128,128]{2,1,0:T(8,128)}, u32[]{:S(2)}, u32[]{:S(2)}) %collective-permute-start.29) | collective-permute-done | bytes 524320 | tf_op jit(solution)/shard_map/ppermute | solution.py:405
  284.1 10.9 %collective-permute-done.30 = f32[8,128,128]{2,1,0:T(8,128)} collective-permute-done((f32[8,128,128]{2,1,0:T(8,128)}, f32[8,128,128]{2,1,0:T(8,128)}, u32[]{:S(2)}, u32[]{:S(2)}) %collective-permute-start.30) | collective-permute-done | bytes 524320 | tf_op jit(solution)/shard_map/ppermute | solution.py:405
  295.0 2.5 select_add_fusion.1
  (87 shorter events, 8.0 us)
Async XLA Ops:
  0.6 1.5 copy-start.13
  3.0 25.0 %collective-permute-start = (f32[2,8,128,128]{3,2,1,0:T(8,128)S(1)}, f32[2,8,128,128]{3,2,1,0:T(8,128)}, u32[]{:S(2)}, u32[]{:S(2)}) collective-permute-start(f32[2,8,128,128]{3,2,1,0:T(8,128)S(1)} %dynamic-slice_bitcast_fusion), channel_id=1, source_target_pairs={{2,0},{3,1},{0,2},{1,3},{6,4},{7,5},{4,6},{5,7},{10,8},{11,9},{8,1... | collective-permute-start | bytes 3145736 | tf_op jit(solution)/shard_map/ppermute | solution.py:405
  3.6 26.0 %collective-permute-start.1 = (f32[8,128,128]{2,1,0:T(8,128)S(1)}, f32[8,128,128]{2,1,0:T(8,128)S(1)}, u32[]{:S(2)}, u32[]{:S(2)}) collective-permute-start(f32[8,128,128]{2,1,0:T(8,128)S(1)} %get-tuple-element.69), channel_id=1, source_target_pairs={{8,0},{9,1},{10,2},{11,3},{12,4},{13,5},{14,6},{15,7},{0,8},{1,9},... | collective-permute-start | bytes 1572872 | tf_op jit(solution)/shard_map/ppermute | solution.py:405
  6.2 24.6 %collective-permute-start.3 = (f32[8,128,128]{2,1,0:T(8,128)}, f32[8,128,128]{2,1,0:T(8,128)S(1)}, u32[]{:S(2)}, u32[]{:S(2)}) collective-permute-start(f32[8,128,128]{2,1,0:T(8,128)} %get-tuple-element.71), channel_id=1, source_target_pairs={{4,0},{5,1},{6,2},{7,3},{0,4},{1,5},{2,6},{3,7},{12,8},{13,9},{14,... | collective-permute-start | bytes 1572872 | tf_op jit(solution)/shard_map/ppermute | solution.py:405
  6.6 44.1 %collective-permute-start.2 = (f32[8,128,128]{2,1,0:T(8,128)}, f32[8,128,128]{2,1,0:T(8,128)S(1)}, u32[]{:S(2)}, u32[]{:S(2)}) collective-permute-start(f32[8,128,128]{2,1,0:T(8,128)} %get-tuple-element.71), channel_id=1, source_target_pairs={{12,0},{13,1},{14,2},{15,3},{8,4},{9,5},{10,6},{11,7},{4,8},{5,9},... | collective-permute-start | bytes 1572872 | tf_op jit(solution)/shard_map/ppermute | solution.py:405
  51.0 54.4 %collective-permute-start.6 = (f32[4,8,128,128]{3,2,1,0:T(8,128)S(1)}, f32[4,8,128,128]{3,2,1,0:T(8,128)S(1)}, u32[]{:S(2)}, u32[]{:S(2)}) collective-permute-start(f32[4,8,128,128]{3,2,1,0:T(8,128)S(1)} %pad_maximum_fusion), channel_id=1, source_target_pairs={{17,0},{0,1},{19,2},{2,3},{21,4},{4,5},{23,6},{6,7},{25,8},{8,9},{... | collective-permute-start | bytes 6291464 | tf_op jit(solution)/shard_map/ppermute | solution.py:419
  51.1 55.6 %collective-permute-start.5 = (f32[4,8,128,128]{3,2,1,0:T(8,128)S(1)}, f32[4,8,128,128]{3,2,1,0:T(8,128)}, u32[]{:S(2)}, u32[]{:S(2)}) collective-permute-start(f32[4,8,128,128]{3,2,1,0:T(8,128)S(1)} %pad_maximum_fusion), channel_id=1, source_target_pairs={{16,0},{18,2},{20,4},{22,6},{24,8},{26,10},{28,12},{30,14},{0,16},... | collective-permute-start | bytes 6291464 | tf_op jit(solution)/shard_map/ppermute | solution.py:419
  54.5 52.2 %collective-permute-start.4 = (f32[4,8,128,128]{3,2,1,0:T(8,128)S(1)}, f32[4,8,128,128]{3,2,1,0:T(8,128)}, u32[]{:S(2)}, u32[]{:S(2)}) collective-permute-start(f32[4,8,128,128]{3,2,1,0:T(8,128)S(1)} %pad_maximum_fusion), channel_id=1, source_target_pairs={{2,0},{3,1},{0,2},{1,3},{6,4},{7,5},{4,6},{5,7},{10,8},{11,9},{8,1... | collective-permute-start | bytes 6291464 | tf_op jit(solution)/shard_map/ppermute | solution.py:405
  56.0 45.1 %collective-permute-start.7 = (f32[2,8,128,128]{3,2,1,0:T(8,128)S(1)}, f32[2,8,128,128]{3,2,1,0:T(8,128)}, u32[]{:S(2)}, u32[]{:S(2)}) collective-permute-start(f32[2,8,128,128]{3,2,1,0:T(8,128)S(1)} %get-tuple-element.75), channel_id=1, source_target_pairs={{8,0},{9,1},{10,2},{11,3},{12,4},{13,5},{14,6},{15,7},{0,8},{1,9},... | collective-permute-start | bytes 3145736 | tf_op jit(solution)/shard_map/ppermute | solution.py:405
  56.0 49.3 %collective-permute-start.8 = (f32[2,8,128,128]{3,2,1,0:T(8,128)S(1)}, f32[2,8,128,128]{3,2,1,0:T(8,128)}, u32[]{:S(2)}, u32[]{:S(2)}) collective-permute-start(f32[2,8,128,128]{3,2,1,0:T(8,128)S(1)} %get-tuple-element.76.refs_2_.refs_4_), channel_id=1, source_target_pairs={{4,0},{5,1},{6,2},{7,3},{0,4},{1,5},{2,6},{3,7},{12,8},{13,9},{14,... | collective-permute-start | bytes 3145736 | tf_op jit(solution)/shard_map/ppermute | solution.py:405
  101.2 8.6 %collective-permute-start.12 = (f32[2,8,128,128]{3,2,1,0:T(8,128)S(1)}, f32[2,8,128,128]{3,2,1,0:T(8,128)S(1)}, u32[]{:S(2)}, u32[]{:S(2)}) collective-permute-start(f32[2,8,128,128]{3,2,1,0:T(8,128)S(1)} %get-tuple-element.76.refs_2_.refs_4_), channel_id=1, source_target_pairs={{1,0},{0,1},{3,2},{2,3},{5,4},{4,5},{7,6},{6,7},{9,8},{8,9},{11,10... | collective-permute-start | bytes 3145736 | tf_op jit(solution)/shard_map/ppermute | solution.py:405
  105.3 1.3 copy-start.2
  106.7 30.0 %collective-permute-start.10 = (f32[4,8,128,128]{3,2,1,0:T(8,128)}, f32[4,8,128,128]{3,2,1,0:T(8,128)}, u32[]{:S(2)}, u32[]{:S(2)}) collective-permute-start(f32[4,8,128,128]{3,2,1,0:T(8,128)} %collective-permute-done.5), channel_id=1, source_target_pairs={{2,0},{0,2},{6,4},{4,6},{10,8},{8,10},{14,12},{12,14},{18,16},{16,... | collective-permute-start | bytes 6291464 | tf_op jit(solution)/shard_map/ppermute | solution.py:409
  109.1 27.5 %collective-permute-start.11 = (f32[4,8,128,128]{3,2,1,0:T(8,128)}, f32[4,8,128,128]{3,2,1,0:T(8,128)}, u32[]{:S(2)}, u32[]{:S(2)}) collective-permute-start(f32[4,8,128,128]{3,2,1,0:T(8,128)} %collective-permute-done.4.home_ref), channel_id=1, source_target_pairs={{17,0},{0,1},{19,2},{2,3},{21,4},{4,5},{23,6},{6,7},{25,8},{8,9},{... | collective-permute-start | bytes 6291464 | tf_op jit(solution)/shard_map/ppermute | solution.py:419
  109.2 5.6 %collective-permute-start.13 = (f32[2,8,128,128]{3,2,1,0:T(8,128)}, f32[2,8,128,128]{3,2,1,0:T(8,128)}, u32[]{:S(2)}, u32[]{:S(2)}) collective-permute-start(f32[2,8,128,128]{3,2,1,0:T(8,128)} %collective-permute-done.8.refs_3_.refs_5_), channel_id=1, source_target_pairs={{1,0},{0,1},{3,2},{2,3},{5,4},{4,5},{7,6},{6,7},{9,8},{8,9},{11,10... | collective-permute-start | bytes 3145736 | tf_op jit(solution)/shard_map/ppermute | solution.py:405
  109.8 6.5 %collective-permute-start.14 = (f32[2,8,128,128]{3,2,1,0:T(8,128)}, f32[2,8,128,128]{3,2,1,0:T(8,128)}, u32[]{:S(2)}, u32[]{:S(2)}) collective-permute-start(f32[2,8,128,128]{3,2,1,0:T(8,128)} %collective-permute-done.7.refs_4_.refs_6_), channel_id=1, source_target_pairs={{1,0},{0,1},{3,2},{2,3},{5,4},{4,5},{7,6},{6,7},{9,8},{8,9},{11,10... | collective-permute-start | bytes 3145736 | tf_op jit(solution)/shard_map/ppermute | solution.py:405
  110.8 25.9 %collective-permute-start.9 = (f32[2,8,128,128]{3,2,1,0:T(8,128)}, f32[2,8,128,128]{3,2,1,0:T(8,128)}, u32[]{:S(2)}, u32[]{:S(2)}) collective-permute-start(f32[2,8,128,128]{3,2,1,0:T(8,128)} %collective-permute-done.7.refs_4_.refs_6_), channel_id=1, source_target_pairs={{4,0},{5,1},{6,2},{7,3},{0,4},{1,5},{2,6},{3,7},{12,8},{13,9},{14,... | collective-permute-start | bytes 3145736 | tf_op jit(solution)/shard_map/ppermute | solution.py:405
  112.1 4.2 %copy-start.3 = (f32[4,8,128,128]{3,2,1,0:T(8,128)S(1)}, f32[4,8,128,128]{3,2,1,0:T(8,128)}, u32[]{:S(2)}) copy-start(f32[4,8,128,128]{3,2,1,0:T(8,128)} %copy-done.2) | copy-start | bytes 6291460
  112.1 4.2 %copy-start.6 = (f32[2,8,128,128]{3,2,1,0:T(8,128)S(1)}, f32[2,8,128,128]{3,2,1,0:T(8,128)}, u32[]{:S(2)}) copy-start(f32[2,8,128,128]{3,2,1,0:T(8,128)} %copy-done.5) | copy-start | bytes 3145732
  112.1 4.2 %copy-start.11 = (bf16[256,256]{1,0:T(8,128)(2,1)S(1)}, bf16[256,256]{1,0:T(8,128)(2,1)}, u32[]{:S(2)}) copy-start(bf16[256,256]{1,0:T(8,128)(2,1)} %constant.120.clone.right_ref) | copy-start | bytes 393220
  112.1 4.2 %copy-start.12 = (bf16[256,256]{1,0:T(8,128)(2,1)S(1)}, bf16[256,256]{1,0:T(8,128)(2,1)}, u32[]{:S(2)}) copy-start(bf16[256,256]{1,0:T(8,128)(2,1)} %constant.119.clone.left_ref) | copy-start | bytes 393220
  114.1 8.3 %copy-start = (f32[4,8,128,128]{3,2,1,0:T(8,128)}, f32[4,8,128,128]{3,2,1,0:T(8,128)S(1)}, u32[]{:S(2)}) copy-start(f32[4,8,128,128]{3,2,1,0:T(8,128)S(1)} %broadcast_select_fusion.1.refs_0_) | copy-start | bytes 6291460
  114.1 22.5 %copy-start.16 = (s32[16]{0:T(128)S(1)}, s32[16]{0:T(128)}, u32[]{:S(2)}) copy-start(s32[16]{0:T(128)} %constant.121.clone) | copy-start | bytes 196
  114.1 22.6 %copy-start.15 = (bf16[16,8,128]{2,1,0:T(8,128)(2,1)S(1)}, bf16[16,8,128]{2,1,0:T(8,128)(2,1)}, u32[]{:S(2)}) copy-start(bf16[16,8,128]{2,1,0:T(8,128)(2,1)} %constant.127.clone.1) | copy-start | bytes 98308
  114.2 23.1 %copy-start.14 = (bf16[16,8,128]{2,1,0:T(8,128)(2,1)S(1)}, bf16[16,8,128]{2,1,0:T(8,128)(2,1)}, u32[]{:S(2)}) copy-start(bf16[16,8,128]{2,1,0:T(8,128)(2,1)} %constant.126.clone.1) | copy-start | bytes 98308
  122.5 1.7 copy-start.9
  136.7 2.9 collective-permute-start.15
  139.5 1.2 copy-start.7
  140.8 31.6 %copy-start.4 = (f32[4,8,128,128]{3,2,1,0:T(8,128)S(1)}, f32[4,8,128,128]{3,2,1,0:T(8,128)}, u32[]{:S(2)}) copy-start(f32[4,8,128,128]{3,2,1,0:T(8,128)} %copy-done.2) | copy-start | bytes 6291460
  163.4 9.0 %copy-start.1 = (f32[4,8,128,128]{3,2,1,0:T(8,128)S(1)}, f32[4,8,128,128]{3,2,1,0:T(8,128)}, u32[]{:S(2)}) copy-start(f32[4,8,128,128]{3,2,1,0:T(8,128)} %copy-done) | copy-start | bytes 6291460
  163.4 9.0 %copy-start.8 = (f32[2,8,128,128]{3,2,1,0:T(8,128)S(1)}, f32[2,8,128,128]{3,2,1,0:T(8,128)}, u32[]{:S(2)}) copy-start(f32[2,8,128,128]{3,2,1,0:T(8,128)} %copy-done.5) | copy-start | bytes 3145732
  163.4 25.2 %collective-permute-start.17 = (f32[4,8,128,128]{3,2,1,0:T(8,128)}, f32[4,8,128,128]{3,2,1,0:T(8,128)S(1)}, u32[]{:S(2)}, u32[]{:S(2)}) collective-permute-start(f32[4,8,128,128]{3,2,1,0:T(8,128)} %get-tuple-element.87), channel_id=1, source_target_pairs={{0,17},{1,0},{2,19},{3,2},{4,21},{5,4},{6,23},{7,6},{8,25},{9,8},{... | collective-permute-start | bytes 6291464 | tf_op jit(solution)/shard_map/ppermute | solution.py:419
  164.7 27.9 %collective-permute-start.16 = (f32[4,8,128,128]{3,2,1,0:T(8,128)S(1)}, f32[4,8,128,128]{3,2,1,0:T(8,128)S(1)}, u32[]{:S(2)}, u32[]{:S(2)}) collective-permute-start(f32[4,8,128,128]{3,2,1,0:T(8,128)S(1)} %get-tuple-element.86), channel_id=1, source_target_pairs={{2,0},{0,2},{6,4},{4,6},{10,8},{8,10},{14,12},{12,14},{18,16},{16,... | collective-permute-start | bytes 6291464 | tf_op jit(solution)/shard_map/ppermute | solution.py:409
  168.1 2.7 collective-permute-start.18
  171.0 25.3 %collective-permute-start.22 = (f32[2,8,128,128]{3,2,1,0:T(8,128)S(1)}, f32[2,8,128,128]{3,2,1,0:T(8,128)S(1)}, u32[]{:S(2)}, u32[]{:S(2)}) collective-permute-start(f32[2,8,128,128]{3,2,1,0:T(8,128)S(1)} %add.162), channel_id=1, source_target_pairs={{4,0},{5,1},{6,2},{7,3},{0,4},{1,5},{2,6},{3,7},{12,8},{13,9},{14,... | collective-permute-start | bytes 3145736 | tf_op jit(solution)/shard_map/ppermute | solution.py:405
  172.4 1.6 copy-start.10
  192.6 4.1 %collective-permute-start.20 = (f32[2,8,128,128]{3,2,1,0:T(8,128)S(1)}, f32[2,8,128,128]{3,2,1,0:T(8,128)S(1)}, u32[]{:S(2)}, u32[]{:S(2)}) collective-permute-start(f32[2,8,128,128]{3,2,1,0:T(8,128)S(1)} %get-tuple-element.111), channel_id=1, source_target_pairs={{1,0},{0,1},{3,2},{2,3},{5,4},{4,5},{7,6},{6,7},{9,8},{8,9},{11,10... | collective-permute-start | bytes 3145736 | tf_op jit(solution)/shard_map/ppermute | solution.py:405
  192.6 8.7 %collective-permute-start.19 = (f32[2,8,128,128]{3,2,1,0:T(8,128)S(1)}, f32[2,8,128,128]{3,2,1,0:T(8,128)S(1)}, u32[]{:S(2)}, u32[]{:S(2)}) collective-permute-start(f32[2,8,128,128]{3,2,1,0:T(8,128)S(1)} %get-tuple-element.109), channel_id=1, source_target_pairs={{1,0},{0,1},{3,2},{2,3},{5,4},{4,5},{7,6},{6,7},{9,8},{8,9},{11,10... | collective-permute-start | bytes 3145736 | tf_op jit(solution)/shard_map/ppermute | solution.py:405
  193.2 6.6 %collective-permute-start.23 = (f32[2,8,128,128]{3,2,1,0:T(8,128)S(1)}, f32[2,8,128,128]{3,2,1,0:T(8,128)S(1)}, u32[]{:S(2)}, u32[]{:S(2)}) collective-permute-start(f32[2,8,128,128]{3,2,1,0:T(8,128)S(1)} %get-tuple-element.114), channel_id=1, source_target_pairs={{1,0},{0,1},{3,2},{2,3},{5,4},{4,5},{7,6},{6,7},{9,8},{8,9},{11,10... | collective-permute-start | bytes 3145736 | tf_op jit(solution)/shard_map/ppermute | solution.py:405
  193.2 52.0 %collective-permute-start.26 = (f32[4,8,128,128]{3,2,1,0:T(8,128)S(1)}, f32[4,8,128,128]{3,2,1,0:T(8,128)S(1)}, u32[]{:S(2)}, u32[]{:S(2)}) collective-permute-start(f32[4,8,128,128]{3,2,1,0:T(8,128)S(1)} %get-tuple-element.117), channel_id=1, source_target_pairs={{0,17},{1,0},{2,19},{3,2},{4,21},{5,4},{6,23},{7,6},{8,25},{9,8},{... | collective-permute-start | bytes 6291464 | tf_op jit(solution)/shard_map/ppermute | solution.py:419
  196.2 48.9 %collective-permute-start.27 = (f32[4,8,128,128]{3,2,1,0:T(8,128)S(1)}, f32[4,8,128,128]{3,2,1,0:T(8,128)S(1)}, u32[]{:S(2)}, u32[]{:S(2)}) collective-permute-start(f32[4,8,128,128]{3,2,1,0:T(8,128)S(1)} %select_add_fusion), channel_id=1, source_target_pairs={{2,0},{3,1},{0,2},{1,3},{6,4},{7,5},{4,6},{5,7},{10,8},{11,9},{8,1... | collective-permute-start | bytes 6291464 | tf_op jit(solution)/shard_map/ppermute | solution.py:405
  196.8 48.4 %collective-permute-start.25 = (f32[4,8,128,128]{3,2,1,0:T(8,128)S(1)}, f32[4,8,128,128]{3,2,1,0:T(8,128)S(1)}, u32[]{:S(2)}, u32[]{:S(2)}) collective-permute-start(f32[4,8,128,128]{3,2,1,0:T(8,128)S(1)} %get-tuple-element.136), channel_id=1, source_target_pairs={{0,16},{2,18},{4,20},{6,22},{8,24},{10,26},{12,28},{14,30},{16,0},... | collective-permute-start | bytes 6291464 | tf_op jit(solution)/shard_map/ppermute | solution.py:419
  199.8 42.7 %collective-permute-start.21 = (f32[2,8,128,128]{3,2,1,0:T(8,128)S(1)}, f32[2,8,128,128]{3,2,1,0:T(8,128)S(1)}, u32[]{:S(2)}, u32[]{:S(2)}) collective-permute-start(f32[2,8,128,128]{3,2,1,0:T(8,128)S(1)} %add.164), channel_id=1, source_target_pairs={{4,0},{5,1},{6,2},{7,3},{0,4},{1,5},{2,6},{3,7},{12,8},{13,9},{14,... | collective-permute-start | bytes 3145736 | tf_op jit(solution)/shard_map/ppermute | solution.py:405
  201.4 43.8 %collective-permute-start.24 = (f32[2,8,128,128]{3,2,1,0:T(8,128)S(1)}, f32[2,8,128,128]{3,2,1,0:T(8,128)S(1)}, u32[]{:S(2)}, u32[]{:S(2)}) collective-permute-start(f32[2,8,128,128]{3,2,1,0:T(8,128)S(1)} %add_add_fusion), channel_id=1, source_target_pairs={{8,0},{9,1},{10,2},{11,3},{12,4},{13,5},{14,6},{15,7},{0,8},{1,9},... | collective-permute-start | bytes 3145736 | tf_op jit(solution)/shard_map/ppermute | solution.py:405
  247.5 22.8 %collective-permute-start.28 = (f32[2,8,128,128]{3,2,1,0:T(8,128)S(1)}, f32[2,8,128,128]{3,2,1,0:T(8,128)}, u32[]{:S(2)}, u32[]{:S(2)}) collective-permute-start(f32[2,8,128,128]{3,2,1,0:T(8,128)S(1)} %get-tuple-element.158), channel_id=1, source_target_pairs={{2,0},{3,1},{0,2},{1,3},{6,4},{7,5},{4,6},{5,7},{10,8},{11,9},{8,1... | collective-permute-start | bytes 3145736 | tf_op jit(solution)/shard_map/ppermute | solution.py:405
  249.0 35.1 %collective-permute-start.29 = (f32[8,128,128]{2,1,0:T(8,128)}, f32[8,128,128]{2,1,0:T(8,128)}, u32[]{:S(2)}, u32[]{:S(2)}) collective-permute-start(f32[8,128,128]{2,1,0:T(8,128)} %get-tuple-element.128), channel_id=1, source_target_pairs={{8,0},{9,1},{10,2},{11,3},{12,4},{13,5},{14,6},{15,7},{0,8},{1,9},... | collective-permute-start | bytes 1572872 | tf_op jit(solution)/shard_map/ppermute | solution.py:405
  252.4 42.6 %collective-permute-start.30 = (f32[8,128,128]{2,1,0:T(8,128)}, f32[8,128,128]{2,1,0:T(8,128)}, u32[]{:S(2)}, u32[]{:S(2)}) collective-permute-start(f32[8,128,128]{2,1,0:T(8,128)} %get-tuple-element.129), channel_id=1, source_target_pairs={{12,0},{13,1},{14,2},{15,3},{8,4},{9,5},{10,6},{11,7},{4,8},{5,9},... | collective-permute-start | bytes 1572872 | tf_op jit(solution)/shard_map/ppermute | solution.py:405
  254.3 40.8 %collective-permute-start.31 = (f32[8,128,128]{2,1,0:T(8,128)S(1)}, f32[8,128,128]{2,1,0:T(8,128)}, u32[]{:S(2)}, u32[]{:S(2)}) collective-permute-start(f32[8,128,128]{2,1,0:T(8,128)S(1)} %get-tuple-element.130), channel_id=1, source_target_pairs={{4,0},{5,1},{6,2},{7,3},{0,4},{1,5},{2,6},{3,7},{12,8},{13,9},{14,... | collective-permute-start | bytes 1572872 | tf_op jit(solution)/shard_map/ppermute | solution.py:405
  (1 other events, 1.0 us)

commit v8 on v7

--- a/solution.py
+++ b/solution.py
@@ -196,7 +196,6 @@
                 pltpu.make_async_copy(block, held, in_sems.at[j, k]).start()
 
     chosen = [k for k in range(count) if steps[k][0] == 1]
-    fetch([k for k in range(count) if k not in chosen], pieces)
     at_home = lax.rem(lax.rem(lax.axis_index("slab"), 2) + 1, groups) == 0
 
     @pl.when(at_home)
@@ -207,6 +206,7 @@
     def _():
         fetch(chosen, pieces)
 
+    fetch([k for k in range(count) if k not in chosen], pieces)
     middle_in = pltpu.make_async_copy(early_ref, middle_ref, middle_sems.at[0])
     middle_in.start()
 

time: 298 us -> 297 us (level)
  no operation moved by 1% of the time
where the time goes in v8:
time: 297 us; the launch traced here: 296 us
  waiting for transfers between devices  200 us (67%)
  starting transfers between devices  36.4 us (12%)
  Pallas kernels  34.3 us (12%)
  local copies, waits for them, and re-layouts  13.2 us (4%)
  other arithmetic  11.5 us (4%)
    ppermute x24, waiting for transfers between devices, swap(): return lax.ppermute(block, 'slab', [(i ^ mask, i) for i in range(slabs)])  188 us
    ppermute x24, starting transfers between devices, swap(): return lax.ppermute(block, 'slab', [(i ^ mask, i) for i in range(slabs)])  22.1 us
    pallas_call x1, Pallas kernels, late_part(): pl.pallas_call(functools.partial(late_kernel, steps, groups), in_specs=[p...  21.2 us
    ppermute x6, starting transfers between devices, across(): return lax.ppermute(block, ('band', 'slab'), route)  8.48 us
    ppermute x6, waiting for transfers between devices, across(): return lax.ppermute(block, ('band', 'slab'), route)  7.66 us
    pallas_call x1, Pallas kernels, scatter_part(): pl.pallas_call(functools.partial(scatter_kernel, steps), grid=(len(steps)...  6.96 us
    unnamed x34, local copies, waits for them, and re-layouts  6.95 us
    pallas_call x1, Pallas kernels, gather_part(): pl.pallas_call(functools.partial(gather_kernel, steps), grid=(count,), in...  6.13 us
  transfers between devices with their start and end apart: 32, of which 18 were waited for; matrix products, arithmetic and copies ran while one was open for 4% of the time, Pallas kernels for 4%

profile of v8, /device:TPU:10, one launch (start us, length us, event | category | flops | bytes accessed | tf_op | source)
XLA Modules:
  0.0 296.1 jit_solution(2308022990231277532)
XLA Ops:
  0.6 1.4 dynamic-slice_bitcast_fusion
  2.2 0.9 dynamic-slice_bitcast_fusion.3
  3.6 2.6 collective-permute-start.1
  7.1 1.3 dynamic-slice_bitcast_fusion.1
  8.4 19.7 %collective-permute-done = f32[2,8,128,128]{3,2,1,0:T(8,128)} collective-permute-done((f32[2,8,128,128]{3,2,1,0:T(8,128)S(1)}, f32[2,8,128,128]{3,2,1,0:T(8,128)}, u32[]{:S(2)}, u32[]{:S(2)}) %collective-permute-start) | collective-permute-done | bytes 1048608 | tf_op jit(solution)/shard_map/ppermute | solution.py:405
  28.1 1.3 constant_dynamic-slice_fusion
  29.6 1.2 collective-permute-done.3
  30.7 20.0 %collective-permute-done.2 = f32[8,128,128]{2,1,0:T(8,128)S(1)} collective-permute-done((f32[8,128,128]{2,1,0:T(8,128)}, f32[8,128,128]{2,1,0:T(8,128)S(1)}, u32[]{:S(2)}, u32[]{:S(2)}) %collective-permute-start.2) | collective-permute-done | bytes 524320 | tf_op jit(solution)/shard_map/ppermute | solution.py:405
  51.1 3.4 %collective-permute-start.5 = (f32[4,8,128,128]{3,2,1,0:T(8,128)S(1)}, f32[4,8,128,128]{3,2,1,0:T(8,128)}, u32[]{:S(2)}, u32[]{:S(2)}) collective-permute-start(f32[4,8,128,128]{3,2,1,0:T(8,128)S(1)} %pad_maximum_fusion), channel_id=1, source_target_pairs={{16,0},{18,2},{20,4},{22,6},{24,8},{26,10},{28,12},{30,14},{0,16},... | collective-permute-start | bytes 6291464 | tf_op jit(solution)/shard_map/ppermute | solution.py:419
  54.5 1.6 collective-permute-start.4
  56.0 3.8 %collective-permute-start.8 = (f32[2,8,128,128]{3,2,1,0:T(8,128)S(1)}, f32[2,8,128,128]{3,2,1,0:T(8,128)}, u32[]{:S(2)}, u32[]{:S(2)}) collective-permute-start(f32[2,8,128,128]{3,2,1,0:T(8,128)S(1)} %get-tuple-element.76.refs_2_.refs_4_), channel_id=1, source_target_pairs={{4,0},{5,1},{6,2},{7,3},{0,4},{1,5},{2,6},{3,7},{12,8},{13,9},{14,... | collective-permute-start | bytes 3145736 | tf_op jit(solution)/shard_map/ppermute | solution.py:405
  59.9 41.3 %collective-permute-done.7.refs_4_.refs_6_ = f32[2,8,128,128]{3,2,1,0:T(8,128)} collective-permute-done((f32[2,8,128,128]{3,2,1,0:T(8,128)S(1)}, f32[2,8,128,128]{3,2,1,0:T(8,128)}, u32[]{:S(2)}, u32[]{:S(2)}) %collective-permute-start.7) | collective-permute-done | bytes 1048608 | tf_op jit(solution)/shard_map/ppermute | solution.py:405
  101.2 4.2 %collective-permute-done.8.refs_3_.refs_5_ = f32[2,8,128,128]{3,2,1,0:T(8,128)} collective-permute-done((f32[2,8,128,128]{3,2,1,0:T(8,128)S(1)}, f32[2,8,128,128]{3,2,1,0:T(8,128)}, u32[]{:S(2)}, u32[]{:S(2)}) %collective-permute-start.8) | collective-permute-done | bytes 1048608 | tf_op jit(solution)/shard_map/ppermute | solution.py:405
  105.4 1.3 copy-done.2
  106.7 2.4 collective-permute-start.10
  109.8 1.0 copy-done.5
  110.8 1.3 collective-permute-start.9
  112.1 2.0 broadcast_select_fusion.1.refs_0_
  114.8 1.5 collective-permute-done.14.refs_7_.refs_10_
  116.3 6.1 %shard_map.86.early_ref = f32[128,48,128]{2,1,0:T(8,128)S(1)} custom-call(bf16[256,256]{1,0:T(8,128)(2,1)S(1)} %copy-done.11, bf16[256,256]{1,0:T(8,128)(2,1)S(1)} %copy-done.12, f32[4,8,128,128]{3,2,1,0:T(8,128)S(1)} %broadcast_select_fusion.1.refs_0_, f32[4,8,128,128]{3,2,1,0:T(8,128)S(1)} %copy-done.3, ...), custom_call_target="tpu_custom_call" | custom-call | flops 1610612736 | bytes 9437184 | tf_op jit(solution)/shard_map/pallas_call | solution.py:328
  122.5 1.7 copy-done.9
  124.1 12.5 %collective-permute-done.9.refs_7_ = f32[2,8,128,128]{3,2,1,0:T(8,128)} collective-permute-done((f32[2,8,128,128]{3,2,1,0:T(8,128)}, f32[2,8,128,128]{3,2,1,0:T(8,128)}, u32[]{:S(2)}, u32[]{:S(2)}) %collective-permute-start.9) | collective-permute-done | bytes 1048608 | tf_op jit(solution)/shard_map/ppermute | solution.py:405
  138.2 1.3 collective-permute-done.15.refs_11_
  139.5 1.2 copy-done.7
  140.8 21.2 %shard_map.87 = (f32[128,48,128]{2,1,0:T(8,128)}, f32[4,8,128,128]{3,2,1,0:T(8,128)S(1)}, f32[4,8,128,128]{3,2,1,0:T(8,128)S(1)}, f32[4,8,128,128]{3,2,1,0:T(8,1...) custom-call(bf16[256,256]{1,0:T(8,128)(2,1)S(1)} %copy-done.11, ...), custom_call_target="tpu_custom_call" | custom-call | flops 10737418240 | bytes 33554432 | tf_op jit(solution)/shard_map/pallas_call | solution.py:347
  162.0 1.3 collective-permute-start.17
  163.3 3.4 %collective-permute-start.16 = (f32[4,8,128,128]{3,2,1,0:T(8,128)S(1)}, f32[4,8,128,128]{3,2,1,0:T(8,128)S(1)}, u32[]{:S(2)}, u32[]{:S(2)}) collective-permute-start(f32[4,8,128,128]{3,2,1,0:T(8,128)S(1)} %get-tuple-element.86), channel_id=1, source_target_pairs={{2,0},{0,2},{6,4},{4,6},{10,8},{8,10},{14,12},{12,14},{18,16},{16,... | collective-permute-start | bytes 6291464 | tf_op jit(solution)/shard_map/ppermute | solution.py:409
  166.8 2.6 collective-permute-done.18
  169.6 1.4 collective-permute-start.22
  171.0 1.6 copy-done.10
  172.6 7.0 %shard_map.88 = (f32[4,8,128,128]{3,2,1,0:T(8,128)S(1)}, f32[4,8,128,128]{3,2,1,0:T(8,128)S(1)}, f32[2,8,128,128]{3,2,1,0:T(8,128)S(1)}, f32[2,8,128,128]{3,2,1,...) custom-call(bf16[256,256]{1,0:T(8,128)(2,1)S(1)} %copy-done.11, ...), custom_call_target="tpu_custom_call", output_to_operand_aliasing={{0}: (11, {}), {1}: (12, {}), {2}: (13, {}), {3}: (14, {}),... | custom-call | flops 1610612736 | bytes 15728640 | tf_op jit(solution)/shard_map/pallas_call | solution.py:374
  179.5 7.6 %collective-permute-done.17 = f32[4,8,128,128]{3,2,1,0:T(8,128)S(1)} collective-permute-done((f32[4,8,128,128]{3,2,1,0:T(8,128)}, f32[4,8,128,128]{3,2,1,0:T(8,128)S(1)}, u32[]{:S(2)}, u32[]{:S(2)}) %collective-permute-start.17) | collective-permute-done | bytes 2097184 | tf_op jit(solution)/shard_map/ppermute | solution.py:419
  187.5 3.7 %collective-permute-done.16 = f32[4,8,128,128]{3,2,1,0:T(8,128)S(1)} collective-permute-done((f32[4,8,128,128]{3,2,1,0:T(8,128)S(1)}, f32[4,8,128,128]{3,2,1,0:T(8,128)S(1)}, u32[]{:S(2)}, u32[]{:S(2)}) %collective-permute-start.16) | collective-permute-done | bytes 2097184 | tf_op jit(solution)/shard_map/ppermute | solution.py:409
  191.7 0.7 collective-permute-start.26
  192.9 1.9 collective-permute-done.22
  195.4 2.9 collective-permute-start.25
  198.4 1.4 collective-permute-start.21
  200.1 41.1 %collective-permute-done.21 = f32[2,8,128,128]{3,2,1,0:T(8,128)S(1)} collective-permute-done((f32[2,8,128,128]{3,2,1,0:T(8,128)S(1)}, f32[2,8,128,128]{3,2,1,0:T(8,128)S(1)}, u32[]{:S(2)}, u32[]{:S(2)}) %collective-permute-start.21) | collective-permute-done | bytes 1048608 | tf_op jit(solution)/shard_map/ppermute | solution.py:405
  241.3 2.5 collective-permute-done.24
  243.8 1.8 add_bitcast_fusion
  246.1 1.6 collective-permute-start.28
  247.6 3.3 %collective-permute-start.29 = (f32[8,128,128]{2,1,0:T(8,128)}, f32[8,128,128]{2,1,0:T(8,128)}, u32[]{:S(2)}, u32[]{:S(2)}) collective-permute-start(f32[8,128,128]{2,1,0:T(8,128)} %get-tuple-element.128), channel_id=1, source_target_pairs={{8,0},{9,1},{10,2},{11,3},{12,4},{13,5},{14,6},{15,7},{0,8},{1,9},... | collective-permute-start | bytes 1572872 | tf_op jit(solution)/shard_map/ppermute | solution.py:405
  251.0 1.9 collective-permute-start.30
  253.0 16.0 %collective-permute-done.28 = f32[2,8,128,128]{3,2,1,0:T(8,128)} collective-permute-done((f32[2,8,128,128]{3,2,1,0:T(8,128)S(1)}, f32[2,8,128,128]{3,2,1,0:T(8,128)}, u32[]{:S(2)}, u32[]{:S(2)}) %collective-permute-start.28) | collective-permute-done | bytes 1048608 | tf_op jit(solution)/shard_map/ppermute | solution.py:405
  268.9 2.9 bitcast_select_fusion
  271.8 10.9 %collective-permute-done.29 = f32[8,128,128]{2,1,0:T(8,128)} collective-permute-done((f32[8,128,128]{2,1,0:T(8,128)}, f32[8,128,128]{2,1,0:T(8,128)}, u32[]{:S(2)}, u32[]{:S(2)}) %collective-permute-start.29) | collective-permute-done | bytes 524320 | tf_op jit(solution)/shard_map/ppermute | solution.py:405
  282.7 10.9 %collective-permute-done.30 = f32[8,128,128]{2,1,0:T(8,128)} collective-permute-done((f32[8,128,128]{2,1,0:T(8,128)}, f32[8,128,128]{2,1,0:T(8,128)}, u32[]{:S(2)}, u32[]{:S(2)}) %collective-permute-start.30) | collective-permute-done | bytes 524320 | tf_op jit(solution)/shard_map/ppermute | solution.py:405
  293.6 2.5 select_add_fusion.1
  (87 shorter events, 8.0 us)
Async XLA Ops:
  0.6 1.5 copy-start.13
  3.0 25.0 %collective-permute-start = (f32[2,8,128,128]{3,2,1,0:T(8,128)S(1)}, f32[2,8,128,128]{3,2,1,0:T(8,128)}, u32[]{:S(2)}, u32[]{:S(2)}) collective-permute-start(f32[2,8,128,128]{3,2,1,0:T(8,128)S(1)} %dynamic-slice_bitcast_fusion), channel_id=1, source_target_pairs={{2,0},{3,1},{0,2},{1,3},{6,4},{7,5},{4,6},{5,7},{10,8},{11,9},{8,1... | collective-permute-start | bytes 3145736 | tf_op jit(solution)/shard_map/ppermute | solution.py:405
  3.6 26.0 %collective-permute-start.1 = (f32[8,128,128]{2,1,0:T(8,128)S(1)}, f32[8,128,128]{2,1,0:T(8,128)S(1)}, u32[]{:S(2)}, u32[]{:S(2)}) collective-permute-start(f32[8,128,128]{2,1,0:T(8,128)S(1)} %get-tuple-element.69), channel_id=1, source_target_pairs={{8,0},{9,1},{10,2},{11,3},{12,4},{13,5},{14,6},{15,7},{0,8},{1,9},... | collective-permute-start | bytes 1572872 | tf_op jit(solution)/shard_map/ppermute | solution.py:405
  6.2 24.6 %collective-permute-start.3 = (f32[8,128,128]{2,1,0:T(8,128)}, f32[8,128,128]{2,1,0:T(8,128)S(1)}, u32[]{:S(2)}, u32[]{:S(2)}) collective-permute-start(f32[8,128,128]{2,1,0:T(8,128)} %get-tuple-element.71), channel_id=1, source_target_pairs={{4,0},{5,1},{6,2},{7,3},{0,4},{1,5},{2,6},{3,7},{12,8},{13,9},{14,... | collective-permute-start | bytes 1572872 | tf_op jit(solution)/shard_map/ppermute | solution.py:405
  6.6 44.1 %collective-permute-start.2 = (f32[8,128,128]{2,1,0:T(8,128)}, f32[8,128,128]{2,1,0:T(8,128)S(1)}, u32[]{:S(2)}, u32[]{:S(2)}) collective-permute-start(f32[8,128,128]{2,1,0:T(8,128)} %get-tuple-element.71), channel_id=1, source_target_pairs={{12,0},{13,1},{14,2},{15,3},{8,4},{9,5},{10,6},{11,7},{4,8},{5,9},... | collective-permute-start | bytes 1572872 | tf_op jit(solution)/shard_map/ppermute | solution.py:405
  51.0 54.4 %collective-permute-start.6 = (f32[4,8,128,128]{3,2,1,0:T(8,128)S(1)}, f32[4,8,128,128]{3,2,1,0:T(8,128)S(1)}, u32[]{:S(2)}, u32[]{:S(2)}) collective-permute-start(f32[4,8,128,128]{3,2,1,0:T(8,128)S(1)} %pad_maximum_fusion), channel_id=1, source_target_pairs={{17,0},{0,1},{19,2},{2,3},{21,4},{4,5},{23,6},{6,7},{25,8},{8,9},{... | collective-permute-start | bytes 6291464 | tf_op jit(solution)/shard_map/ppermute | solution.py:419
  51.1 55.6 %collective-permute-start.5 = (f32[4,8,128,128]{3,2,1,0:T(8,128)S(1)}, f32[4,8,128,128]{3,2,1,0:T(8,128)}, u32[]{:S(2)}, u32[]{:S(2)}) collective-permute-start(f32[4,8,128,128]{3,2,1,0:T(8,128)S(1)} %pad_maximum_fusion), channel_id=1, source_target_pairs={{16,0},{18,2},{20,4},{22,6},{24,8},{26,10},{28,12},{30,14},{0,16},... | collective-permute-start | bytes 6291464 | tf_op jit(solution)/shard_map/ppermute | solution.py:419
  54.5 52.2 %collective-permute-start.4 = (f32[4,8,128,128]{3,2,1,0:T(8,128)S(1)}, f32[4,8,128,128]{3,2,1,0:T(8,128)}, u32[]{:S(2)}, u32[]{:S(2)}) collective-permute-start(f32[4,8,128,128]{3,2,1,0:T(8,128)S(1)} %pad_maximum_fusion), channel_id=1, source_target_pairs={{2,0},{3,1},{0,2},{1,3},{6,4},{7,5},{4,6},{5,7},{10,8},{11,9},{8,1... | collective-permute-start | bytes 6291464 | tf_op jit(solution)/shard_map/ppermute | solution.py:405
  56.0 45.1 %collective-permute-start.7 = (f32[2,8,128,128]{3,2,1,0:T(8,128)S(1)}, f32[2,8,128,128]{3,2,1,0:T(8,128)}, u32[]{:S(2)}, u32[]{:S(2)}) collective-permute-start(f32[2,8,128,128]{3,2,1,0:T(8,128)S(1)} %get-tuple-element.75), channel_id=1, source_target_pairs={{8,0},{9,1},{10,2},{11,3},{12,4},{13,5},{14,6},{15,7},{0,8},{1,9},... | collective-permute-start | bytes 3145736 | tf_op jit(solution)/shard_map/ppermute | solution.py:405
  56.0 49.3 %collective-permute-start.8 = (f32[2,8,128,128]{3,2,1,0:T(8,128)S(1)}, f32[2,8,128,128]{3,2,1,0:T(8,128)}, u32[]{:S(2)}, u32[]{:S(2)}) collective-permute-start(f32[2,8,128,128]{3,2,1,0:T(8,128)S(1)} %get-tuple-element.76.refs_2_.refs_4_), channel_id=1, source_target_pairs={{4,0},{5,1},{6,2},{7,3},{0,4},{1,5},{2,6},{3,7},{12,8},{13,9},{14,... | collective-permute-start | bytes 3145736 | tf_op jit(solution)/shard_map/ppermute | solution.py:405
  101.2 8.6 %collective-permute-start.12 = (f32[2,8,128,128]{3,2,1,0:T(8,128)S(1)}, f32[2,8,128,128]{3,2,1,0:T(8,128)S(1)}, u32[]{:S(2)}, u32[]{:S(2)}) collective-permute-start(f32[2,8,128,128]{3,2,1,0:T(8,128)S(1)} %get-tuple-element.76.refs_2_.refs_4_), channel_id=1, source_target_pairs={{1,0},{0,1},{3,2},{2,3},{5,4},{4,5},{7,6},{6,7},{9,8},{8,9},{11,10... | collective-permute-start | bytes 3145736 | tf_op jit(solution)/shard_map/ppermute | solution.py:405
  105.3 1.3 copy-start.2
  106.7 30.0 %collective-permute-start.10 = (f32[4,8,128,128]{3,2,1,0:T(8,128)}, f32[4,8,128,128]{3,2,1,0:T(8,128)}, u32[]{:S(2)}, u32[]{:S(2)}) collective-permute-start(f32[4,8,128,128]{3,2,1,0:T(8,128)} %collective-permute-done.5), channel_id=1, source_target_pairs={{2,0},{0,2},{6,4},{4,6},{10,8},{8,10},{14,12},{12,14},{18,16},{16,... | collective-permute-start | bytes 6291464 | tf_op jit(solution)/shard_map/ppermute | solution.py:409
  109.1 27.5 %collective-permute-start.11 = (f32[4,8,128,128]{3,2,1,0:T(8,128)}, f32[4,8,128,128]{3,2,1,0:T(8,128)}, u32[]{:S(2)}, u32[]{:S(2)}) collective-permute-start(f32[4,8,128,128]{3,2,1,0:T(8,128)} %collective-permute-done.4.home_ref), channel_id=1, source_target_pairs={{17,0},{0,1},{19,2},{2,3},{21,4},{4,5},{23,6},{6,7},{25,8},{8,9},{... | collective-permute-start | bytes 6291464 | tf_op jit(solution)/shard_map/ppermute | solution.py:419
  109.2 5.6 %collective-permute-start.13 = (f32[2,8,128,128]{3,2,1,0:T(8,128)}, f32[2,8,128,128]{3,2,1,0:T(8,128)}, u32[]{:S(2)}, u32[]{:S(2)}) collective-permute-start(f32[2,8,128,128]{3,2,1,0:T(8,128)} %collective-permute-done.8.refs_3_.refs_5_), channel_id=1, source_target_pairs={{1,0},{0,1},{3,2},{2,3},{5,4},{4,5},{7,6},{6,7},{9,8},{8,9},{11,10... | collective-permute-start | bytes 3145736 | tf_op jit(solution)/shard_map/ppermute | solution.py:405
  109.8 6.5 %collective-permute-start.14 = (f32[2,8,128,128]{3,2,1,0:T(8,128)}, f32[2,8,128,128]{3,2,1,0:T(8,128)}, u32[]{:S(2)}, u32[]{:S(2)}) collective-permute-start(f32[2,8,128,128]{3,2,1,0:T(8,128)} %collective-permute-done.7.refs_4_.refs_6_), channel_id=1, source_target_pairs={{1,0},{0,1},{3,2},{2,3},{5,4},{4,5},{7,6},{6,7},{9,8},{8,9},{11,10... | collective-permute-start | bytes 3145736 | tf_op jit(solution)/shard_map/ppermute | solution.py:405
  110.8 25.9 %collective-permute-start.9 = (f32[2,8,128,128]{3,2,1,0:T(8,128)}, f32[2,8,128,128]{3,2,1,0:T(8,128)}, u32[]{:S(2)}, u32[]{:S(2)}) collective-permute-start(f32[2,8,128,128]{3,2,1,0:T(8,128)} %collective-permute-done.7.refs_4_.refs_6_), channel_id=1, source_target_pairs={{4,0},{5,1},{6,2},{7,3},{0,4},{1,5},{2,6},{3,7},{12,8},{13,9},{14,... | collective-permute-start | bytes 3145736 | tf_op jit(solution)/shard_map/ppermute | solution.py:405
  112.1 4.2 %copy-start.3 = (f32[4,8,128,128]{3,2,1,0:T(8,128)S(1)}, f32[4,8,128,128]{3,2,1,0:T(8,128)}, u32[]{:S(2)}) copy-start(f32[4,8,128,128]{3,2,1,0:T(8,128)} %copy-done.2) | copy-start | bytes 6291460
  112.1 4.2 %copy-start.6 = (f32[2,8,128,128]{3,2,1,0:T(8,128)S(1)}, f32[2,8,128,128]{3,2,1,0:T(8,128)}, u32[]{:S(2)}) copy-start(f32[2,8,128,128]{3,2,1,0:T(8,128)} %copy-done.5) | copy-start | bytes 3145732
  112.1 4.2 %copy-start.11 = (bf16[256,256]{1,0:T(8,128)(2,1)S(1)}, bf16[256,256]{1,0:T(8,128)(2,1)}, u32[]{:S(2)}) copy-start(bf16[256,256]{1,0:T(8,128)(2,1)} %constant.120.clone.right_ref) | copy-start | bytes 393220
  112.1 4.2 %copy-start.12 = (bf16[256,256]{1,0:T(8,128)(2,1)S(1)}, bf16[256,256]{1,0:T(8,128)(2,1)}, u32[]{:S(2)}) copy-start(bf16[256,256]{1,0:T(8,128)(2,1)} %constant.119.clone.left_ref) | copy-start | bytes 393220
  114.1 8.3 %copy-start = (f32[4,8,128,128]{3,2,1,0:T(8,128)}, f32[4,8,128,128]{3,2,1,0:T(8,128)S(1)}, u32[]{:S(2)}) copy-start(f32[4,8,128,128]{3,2,1,0:T(8,128)S(1)} %broadcast_select_fusion.1.refs_0_) | copy-start | bytes 6291460
  114.1 22.5 %copy-start.16 = (s32[16]{0:T(128)S(1)}, s32[16]{0:T(128)}, u32[]{:S(2)}) copy-start(s32[16]{0:T(128)} %constant.121.clone) | copy-start | bytes 196
  114.1 22.6 %copy-start.15 = (bf16[16,8,128]{2,1,0:T(8,128)(2,1)S(1)}, bf16[16,8,128]{2,1,0:T(8,128)(2,1)}, u32[]{:S(2)}) copy-start(bf16[16,8,128]{2,1,0:T(8,128)(2,1)} %constant.127.clone.1) | copy-start | bytes 98308
  114.2 23.1 %copy-start.14 = (bf16[16,8,128]{2,1,0:T(8,128)(2,1)S(1)}, bf16[16,8,128]{2,1,0:T(8,128)(2,1)}, u32[]{:S(2)}) copy-start(bf16[16,8,128]{2,1,0:T(8,128)(2,1)} %constant.126.clone.1) | copy-start | bytes 98308
  122.5 1.7 copy-start.9
  136.7 2.9 collective-permute-start.15
  139.5 1.2 copy-start.7
  140.8 30.2 %copy-start.4 = (f32[4,8,128,128]{3,2,1,0:T(8,128)S(1)}, f32[4,8,128,128]{3,2,1,0:T(8,128)}, u32[]{:S(2)}) copy-start(f32[4,8,128,128]{3,2,1,0:T(8,128)} %copy-done.2) | copy-start | bytes 6291460
  162.0 9.0 %copy-start.1 = (f32[4,8,128,128]{3,2,1,0:T(8,128)S(1)}, f32[4,8,128,128]{3,2,1,0:T(8,128)}, u32[]{:S(2)}) copy-start(f32[4,8,128,128]{3,2,1,0:T(8,128)} %copy-done) | copy-start | bytes 6291460
  162.0 9.0 %copy-start.8 = (f32[2,8,128,128]{3,2,1,0:T(8,128)S(1)}, f32[2,8,128,128]{3,2,1,0:T(8,128)}, u32[]{:S(2)}) copy-start(f32[2,8,128,128]{3,2,1,0:T(8,128)} %copy-done.5) | copy-start | bytes 3145732
  162.0 25.2 %collective-permute-start.17 = (f32[4,8,128,128]{3,2,1,0:T(8,128)}, f32[4,8,128,128]{3,2,1,0:T(8,128)S(1)}, u32[]{:S(2)}, u32[]{:S(2)}) collective-permute-start(f32[4,8,128,128]{3,2,1,0:T(8,128)} %get-tuple-element.87), channel_id=1, source_target_pairs={{0,17},{1,0},{2,19},{3,2},{4,21},{5,4},{6,23},{7,6},{8,25},{9,8},{... | collective-permute-start | bytes 6291464 | tf_op jit(solution)/shard_map/ppermute | solution.py:419
  163.3 27.9 %collective-permute-start.16 = (f32[4,8,128,128]{3,2,1,0:T(8,128)S(1)}, f32[4,8,128,128]{3,2,1,0:T(8,128)S(1)}, u32[]{:S(2)}, u32[]{:S(2)}) collective-permute-start(f32[4,8,128,128]{3,2,1,0:T(8,128)S(1)} %get-tuple-element.86), channel_id=1, source_target_pairs={{2,0},{0,2},{6,4},{4,6},{10,8},{8,10},{14,12},{12,14},{18,16},{16,... | collective-permute-start | bytes 6291464 | tf_op jit(solution)/shard_map/ppermute | solution.py:409
  166.7 2.7 collective-permute-start.18
  169.6 25.3 %collective-permute-start.22 = (f32[2,8,128,128]{3,2,1,0:T(8,128)S(1)}, f32[2,8,128,128]{3,2,1,0:T(8,128)S(1)}, u32[]{:S(2)}, u32[]{:S(2)}) collective-permute-start(f32[2,8,128,128]{3,2,1,0:T(8,128)S(1)} %add.162), channel_id=1, source_target_pairs={{4,0},{5,1},{6,2},{7,3},{0,4},{1,5},{2,6},{3,7},{12,8},{13,9},{14,... | collective-permute-start | bytes 3145736 | tf_op jit(solution)/shard_map/ppermute | solution.py:405
  171.0 1.6 copy-start.10
  191.2 4.1 %collective-permute-start.20 = (f32[2,8,128,128]{3,2,1,0:T(8,128)S(1)}, f32[2,8,128,128]{3,2,1,0:T(8,128)S(1)}, u32[]{:S(2)}, u32[]{:S(2)}) collective-permute-start(f32[2,8,128,128]{3,2,1,0:T(8,128)S(1)} %get-tuple-element.111), channel_id=1, source_target_pairs={{1,0},{0,1},{3,2},{2,3},{5,4},{4,5},{7,6},{6,7},{9,8},{8,9},{11,10... | collective-permute-start | bytes 3145736 | tf_op jit(solution)/shard_map/ppermute | solution.py:405
  191.2 8.7 %collective-permute-start.19 = (f32[2,8,128,128]{3,2,1,0:T(8,128)S(1)}, f32[2,8,128,128]{3,2,1,0:T(8,128)S(1)}, u32[]{:S(2)}, u32[]{:S(2)}) collective-permute-start(f32[2,8,128,128]{3,2,1,0:T(8,128)S(1)} %get-tuple-element.109), channel_id=1, source_target_pairs={{1,0},{0,1},{3,2},{2,3},{5,4},{4,5},{7,6},{6,7},{9,8},{8,9},{11,10... | collective-permute-start | bytes 3145736 | tf_op jit(solution)/shard_map/ppermute | solution.py:405
  191.7 6.6 %collective-permute-start.23 = (f32[2,8,128,128]{3,2,1,0:T(8,128)S(1)}, f32[2,8,128,128]{3,2,1,0:T(8,128)S(1)}, u32[]{:S(2)}, u32[]{:S(2)}) collective-permute-start(f32[2,8,128,128]{3,2,1,0:T(8,128)S(1)} %get-tuple-element.114), channel_id=1, source_target_pairs={{1,0},{0,1},{3,2},{2,3},{5,4},{4,5},{7,6},{6,7},{9,8},{8,9},{11,10... | collective-permute-start | bytes 3145736 | tf_op jit(solution)/shard_map/ppermute | solution.py:405
  191.7 52.0 %collective-permute-start.26 = (f32[4,8,128,128]{3,2,1,0:T(8,128)S(1)}, f32[4,8,128,128]{3,2,1,0:T(8,128)S(1)}, u32[]{:S(2)}, u32[]{:S(2)}) collective-permute-start(f32[4,8,128,128]{3,2,1,0:T(8,128)S(1)} %get-tuple-element.117), channel_id=1, source_target_pairs={{0,17},{1,0},{2,19},{3,2},{4,21},{5,4},{6,23},{7,6},{8,25},{9,8},{... | collective-permute-start | bytes 6291464 | tf_op jit(solution)/shard_map/ppermute | solution.py:419
  194.8 48.9 %collective-permute-start.27 = (f32[4,8,128,128]{3,2,1,0:T(8,128)S(1)}, f32[4,8,128,128]{3,2,1,0:T(8,128)S(1)}, u32[]{:S(2)}, u32[]{:S(2)}) collective-permute-start(f32[4,8,128,128]{3,2,1,0:T(8,128)S(1)} %select_add_fusion), channel_id=1, source_target_pairs={{2,0},{3,1},{0,2},{1,3},{6,4},{7,5},{4,6},{5,7},{10,8},{11,9},{8,1... | collective-permute-start | bytes 6291464 | tf_op jit(solution)/shard_map/ppermute | solution.py:405
  195.4 48.4 %collective-permute-start.25 = (f32[4,8,128,128]{3,2,1,0:T(8,128)S(1)}, f32[4,8,128,128]{3,2,1,0:T(8,128)S(1)}, u32[]{:S(2)}, u32[]{:S(2)}) collective-permute-start(f32[4,8,128,128]{3,2,1,0:T(8,128)S(1)} %get-tuple-element.136), channel_id=1, source_target_pairs={{0,16},{2,18},{4,20},{6,22},{8,24},{10,26},{12,28},{14,30},{16,0},... | collective-permute-start | bytes 6291464 | tf_op jit(solution)/shard_map/ppermute | solution.py:419
  198.4 42.8 %collective-permute-start.21 = (f32[2,8,128,128]{3,2,1,0:T(8,128)S(1)}, f32[2,8,128,128]{3,2,1,0:T(8,128)S(1)}, u32[]{:S(2)}, u32[]{:S(2)}) collective-permute-start(f32[2,8,128,128]{3,2,1,0:T(8,128)S(1)} %add.164), channel_id=1, source_target_pairs={{4,0},{5,1},{6,2},{7,3},{0,4},{1,5},{2,6},{3,7},{12,8},{13,9},{14,... | collective-permute-start | bytes 3145736 | tf_op jit(solution)/shard_map/ppermute | solution.py:405
  200.0 43.8 %collective-permute-start.24 = (f32[2,8,128,128]{3,2,1,0:T(8,128)S(1)}, f32[2,8,128,128]{3,2,1,0:T(8,128)S(1)}, u32[]{:S(2)}, u32[]{:S(2)}) collective-permute-start(f32[2,8,128,128]{3,2,1,0:T(8,128)S(1)} %add_add_fusion), channel_id=1, source_target_pairs={{8,0},{9,1},{10,2},{11,3},{12,4},{13,5},{14,6},{15,7},{0,8},{1,9},... | collective-permute-start | bytes 3145736 | tf_op jit(solution)/shard_map/ppermute | solution.py:405
  246.1 22.8 %collective-permute-start.28 = (f32[2,8,128,128]{3,2,1,0:T(8,128)S(1)}, f32[2,8,128,128]{3,2,1,0:T(8,128)}, u32[]{:S(2)}, u32[]{:S(2)}) collective-permute-start(f32[2,8,128,128]{3,2,1,0:T(8,128)S(1)} %get-tuple-element.158), channel_id=1, source_target_pairs={{2,0},{3,1},{0,2},{1,3},{6,4},{7,5},{4,6},{5,7},{10,8},{11,9},{8,1... | collective-permute-start | bytes 3145736 | tf_op jit(solution)/shard_map/ppermute | solution.py:405
  247.6 35.0 %collective-permute-start.29 = (f32[8,128,128]{2,1,0:T(8,128)}, f32[8,128,128]{2,1,0:T(8,128)}, u32[]{:S(2)}, u32[]{:S(2)}) collective-permute-start(f32[8,128,128]{2,1,0:T(8,128)} %get-tuple-element.128), channel_id=1, source_target_pairs={{8,0},{9,1},{10,2},{11,3},{12,4},{13,5},{14,6},{15,7},{0,8},{1,9},... | collective-permute-start | bytes 1572872 | tf_op jit(solution)/shard_map/ppermute | solution.py:405
  251.0 42.6 %collective-permute-start.30 = (f32[8,128,128]{2,1,0:T(8,128)}, f32[8,128,128]{2,1,0:T(8,128)}, u32[]{:S(2)}, u32[]{:S(2)}) collective-permute-start(f32[8,128,128]{2,1,0:T(8,128)} %get-tuple-element.129), channel_id=1, source_target_pairs={{12,0},{13,1},{14,2},{15,3},{8,4},{9,5},{10,6},{11,7},{4,8},{5,9},... | collective-permute-start | bytes 1572872 | tf_op jit(solution)/shard_map/ppermute | solution.py:405
  252.8 40.8 %collective-permute-start.31 = (f32[8,128,128]{2,1,0:T(8,128)S(1)}, f32[8,128,128]{2,1,0:T(8,128)}, u32[]{:S(2)}, u32[]{:S(2)}) collective-permute-start(f32[8,128,128]{2,1,0:T(8,128)S(1)} %get-tuple-element.130), channel_id=1, source_target_pairs={{4,0},{5,1},{6,2},{7,3},{0,4},{1,5},{2,6},{3,7},{12,8},{13,9},{14,... | collective-permute-start | bytes 1572872 | tf_op jit(solution)/shard_map/ppermute | solution.py:405
  (1 other events, 1.0 us)

commit v9 on v8

--- a/solution.py
+++ b/solution.py
@@ -463,7 +463,9 @@
     first_x, second_x = swap_away(first, 2), across(bands_x, 1, False)
     got_far = swap(got_near, 4)
     parts = [kept_near, kept_far, got_near]
-    parts_c = [swap(part, 1) for part in parts]
+    parts_c = [
+        pltpu.with_memory_space_constraint(swap(part, 1), pltpu.HBM) for part in parts
+    ]
     first = jnp.where(at_home, bands, first)
     early = [first, None, second, None] + parts + [None] + parts_c + [None]
     field_early = gather_part(right, left, early, EARLY)

time: 297 us -> 294 us (0.990)
    unnamed x34 -> x32, local copies, waits for them, and re-layouts: 6.95 us -> 5.6 us
where the time goes in v9:
time: 294 us
  waiting for transfers between devices  200 us (68%)
  starting transfers between devices  36.4 us (12%)
  Pallas kernels  33.3 us (11%)
  local copies, waits for them, and re-layouts  11.9 us (4%)
  other arithmetic  11.7 us (4%)
    ppermute x24, waiting for transfers between devices, swap(): return lax.ppermute(block, 'slab', [(i ^ mask, i) for i in range(slabs)])  188 us
    ppermute x24, starting transfers between devices, swap(): return lax.ppermute(block, 'slab', [(i ^ mask, i) for i in range(slabs)])  22.2 us
    pallas_call x1, Pallas kernels, late_part(): pl.pallas_call(functools.partial(late_kernel, steps, groups), in_specs=[p...  20.6 us
    ppermute x6, starting transfers between devices, across(): return lax.ppermute(block, ('band', 'slab'), route)  8.43 us
    ppermute x6, waiting for transfers between devices, across(): return lax.ppermute(block, ('band', 'slab'), route)  7.67 us
    pallas_call x1, Pallas kernels, scatter_part(): pl.pallas_call(functools.partial(scatter_kernel, steps), grid=(len(steps)...  6.34 us
    pallas_call x1, Pallas kernels, gather_part(): pl.pallas_call(functools.partial(gather_kernel, steps), grid=(count,), in...  6.31 us
  transfers between devices with their start and end apart: 32, of which 18 were waited for; matrix products, arithmetic and copies ran while one was open for 4% of the time, Pallas kernels for 4%

profile of v9, /device:TPU:10, one launch (start us, length us, event | category | flops | bytes accessed | tf_op | source)
XLA Modules:
  0.0 293.9 jit_solution(1560497647423284142)
XLA Ops:
  0.6 1.4 dynamic-slice_bitcast_fusion
  2.2 0.9 dynamic-slice_bitcast_fusion.3
  3.6 2.6 collective-permute-start.1
  7.1 1.3 dynamic-slice_bitcast_fusion.1
  8.4 19.7 %collective-permute-done = f32[2,8,128,128]{3,2,1,0:T(8,128)} collective-permute-done((f32[2,8,128,128]{3,2,1,0:T(8,128)S(1)}, f32[2,8,128,128]{3,2,1,0:T(8,128)}, u32[]{:S(2)}, u32[]{:S(2)}) %collective-permute-start) | collective-permute-done | bytes 1048608 | tf_op jit(solution)/shard_map/ppermute | solution.py:405
  28.1 1.3 constant_dynamic-slice_fusion
  29.6 1.2 collective-permute-done.3
  30.7 20.0 %collective-permute-done.2 = f32[8,128,128]{2,1,0:T(8,128)S(1)} collective-permute-done((f32[8,128,128]{2,1,0:T(8,128)}, f32[8,128,128]{2,1,0:T(8,128)S(1)}, u32[]{:S(2)}, u32[]{:S(2)}) %collective-permute-start.2) | collective-permute-done | bytes 524320 | tf_op jit(solution)/shard_map/ppermute | solution.py:405
  51.6 3.4 %collective-permute-start.5 = (f32[4,8,128,128]{3,2,1,0:T(8,128)S(1)}, f32[4,8,128,128]{3,2,1,0:T(8,128)}, u32[]{:S(2)}, u32[]{:S(2)}) collective-permute-start(f32[4,8,128,128]{3,2,1,0:T(8,128)S(1)} %pad_maximum_fusion), channel_id=1, source_target_pairs={{16,0},{18,2},{20,4},{22,6},{24,8},{26,10},{28,12},{30,14},{0,16},... | collective-permute-start | bytes 6291464 | tf_op jit(solution)/shard_map/ppermute | solution.py:419
  55.0 1.6 collective-permute-start.4
  56.6 3.8 %collective-permute-start.8 = (f32[2,8,128,128]{3,2,1,0:T(8,128)S(1)}, f32[2,8,128,128]{3,2,1,0:T(8,128)}, u32[]{:S(2)}, u32[]{:S(2)}) collective-permute-start(f32[2,8,128,128]{3,2,1,0:T(8,128)S(1)} %get-tuple-element.76.refs_2_.refs_4_), channel_id=1, source_target_pairs={{4,0},{5,1},{6,2},{7,3},{0,4},{1,5},{2,6},{3,7},{12,8},{13,9},{14,... | collective-permute-start | bytes 3145736 | tf_op jit(solution)/shard_map/ppermute | solution.py:405
  60.4 41.3 %collective-permute-done.7.refs_4_.refs_6_ = f32[2,8,128,128]{3,2,1,0:T(8,128)} collective-permute-done((f32[2,8,128,128]{3,2,1,0:T(8,128)S(1)}, f32[2,8,128,128]{3,2,1,0:T(8,128)}, u32[]{:S(2)}, u32[]{:S(2)}) %collective-permute-start.7) | collective-permute-done | bytes 1048608 | tf_op jit(solution)/shard_map/ppermute | solution.py:405
  101.8 4.2 %collective-permute-done.8.refs_3_.refs_5_ = f32[2,8,128,128]{3,2,1,0:T(8,128)} collective-permute-done((f32[2,8,128,128]{3,2,1,0:T(8,128)S(1)}, f32[2,8,128,128]{3,2,1,0:T(8,128)}, u32[]{:S(2)}, u32[]{:S(2)}) %collective-permute-start.8) | collective-permute-done | bytes 1048608 | tf_op jit(solution)/shard_map/ppermute | solution.py:405
  105.9 1.3 copy-done.2
  107.3 2.4 collective-permute-start.10
  109.8 0.6 collective-permute-start.13
  110.4 1.4 collective-permute-start.9
  111.8 2.2 broadcast_select_fusion.1.refs_0_
  114.1 1.3 collective-permute-done.13.refs_6_.refs_9_
  115.4 1.5 collective-permute-done.14.refs_7_.refs_10_
  116.9 6.3 %shard_map.86.early_ref = f32[128,48,128]{2,1,0:T(8,128)S(1)} custom-call(bf16[256,256]{1,0:T(8,128)(2,1)S(1)} %copy-done.7, bf16[256,256]{1,0:T(8,128)(2,1)S(1)} %copy-done.8, f32[4,8,128,128]{3,2,1,0:T(8,128)S(1)} %broadcast_select_fusion.1.refs_0_, f32[4,8,128,128]{3,2,1,0:T(8,128)S(1)} %copy-done.3, ...), custom_call_target="tpu_custom_call" | custom-call | flops 1610612736 | bytes 9437184 | tf_op jit(solution)/shard_map/pallas_call | solution.py:328
  123.2 1.6 copy-done.6
  124.8 11.4 %collective-permute-done.9.refs_7_ = f32[2,8,128,128]{3,2,1,0:T(8,128)} collective-permute-done((f32[2,8,128,128]{3,2,1,0:T(8,128)}, f32[2,8,128,128]{3,2,1,0:T(8,128)}, u32[]{:S(2)}, u32[]{:S(2)}) %collective-permute-start.9) | collective-permute-done | bytes 1048608 | tf_op jit(solution)/shard_map/ppermute | solution.py:405
  137.8 1.3 collective-permute-done.15.refs_11_
  139.2 20.6 %shard_map.87 = (f32[128,48,128]{2,1,0:T(8,128)}, f32[4,8,128,128]{3,2,1,0:T(8,128)S(1)}, f32[4,8,128,128]{3,2,1,0:T(8,128)S(1)}, f32[4,8,128,128]{3,2,1,0:T(8,1...) custom-call(bf16[256,256]{1,0:T(8,128)(2,1)S(1)} %copy-done.7, ...), custom_call_target="tpu_custom_call" | custom-call | flops 10737418240 | bytes 33554432 | tf_op jit(solution)/shard_map/pallas_call | solution.py:347
  159.8 1.3 collective-permute-start.17
  161.1 3.4 %collective-permute-start.16 = (f32[4,8,128,128]{3,2,1,0:T(8,128)S(1)}, f32[4,8,128,128]{3,2,1,0:T(8,128)S(1)}, u32[]{:S(2)}, u32[]{:S(2)}) collective-permute-start(f32[4,8,128,128]{3,2,1,0:T(8,128)S(1)} %get-tuple-element.86), channel_id=1, source_target_pairs={{2,0},{0,2},{6,4},{4,6},{10,8},{8,10},{14,12},{12,14},{18,16},{16,... | collective-permute-start | bytes 6291464 | tf_op jit(solution)/shard_map/ppermute | solution.py:409
  164.6 2.6 collective-permute-done.18
  167.4 1.4 collective-permute-start.22
  168.8 1.9 copy-done.5
  170.7 6.3 %shard_map.88 = (f32[4,8,128,128]{3,2,1,0:T(8,128)S(1)}, f32[4,8,128,128]{3,2,1,0:T(8,128)S(1)}, f32[2,8,128,128]{3,2,1,0:T(8,128)S(1)}, f32[2,8,128,128]{3,2,1,...) custom-call(bf16[256,256]{1,0:T(8,128)(2,1)S(1)} %copy-done.7, ...), custom_call_target="tpu_custom_call", output_to_operand_aliasing={{0}: (11, {}), {1}: (12, {}), {2}: (13, {}), {3}: (14, {}),... | custom-call | flops 1610612736 | bytes 15728640 | tf_op jit(solution)/shard_map/pallas_call | solution.py:374
  177.0 7.7 %collective-permute-done.17 = f32[4,8,128,128]{3,2,1,0:T(8,128)S(1)} collective-permute-done((f32[4,8,128,128]{3,2,1,0:T(8,128)S(1)}, f32[4,8,128,128]{3,2,1,0:T(8,128)S(1)}, u32[]{:S(2)}, u32[]{:S(2)}) %collective-permute-start.17) | collective-permute-done | bytes 2097184 | tf_op jit(solution)/shard_map/ppermute | solution.py:419
  185.0 4.1 %collective-permute-done.16 = f32[4,8,128,128]{3,2,1,0:T(8,128)S(1)} collective-permute-done((f32[4,8,128,128]{3,2,1,0:T(8,128)S(1)}, f32[4,8,128,128]{3,2,1,0:T(8,128)S(1)}, u32[]{:S(2)}, u32[]{:S(2)}) %collective-permute-start.16) | collective-permute-done | bytes 2097184 | tf_op jit(solution)/shard_map/ppermute | solution.py:409
  189.6 0.8 collective-permute-start.26
  190.8 1.9 collective-permute-done.22
  193.2 2.9 collective-permute-start.25
  196.2 1.4 collective-permute-start.21
  197.9 41.1 %collective-permute-done.21 = f32[2,8,128,128]{3,2,1,0:T(8,128)S(1)} collective-permute-done((f32[2,8,128,128]{3,2,1,0:T(8,128)S(1)}, f32[2,8,128,128]{3,2,1,0:T(8,128)S(1)}, u32[]{:S(2)}, u32[]{:S(2)}) %collective-permute-start.21) | collective-permute-done | bytes 1048608 | tf_op jit(solution)/shard_map/ppermute | solution.py:405
  239.1 2.5 collective-permute-done.24
  241.6 1.8 add_bitcast_fusion
  243.9 1.6 collective-permute-start.28
  245.4 3.3 %collective-permute-start.29 = (f32[8,128,128]{2,1,0:T(8,128)}, f32[8,128,128]{2,1,0:T(8,128)}, u32[]{:S(2)}, u32[]{:S(2)}) collective-permute-start(f32[8,128,128]{2,1,0:T(8,128)} %get-tuple-element.128), channel_id=1, source_target_pairs={{8,0},{9,1},{10,2},{11,3},{12,4},{13,5},{14,6},{15,7},{0,8},{1,9},... | collective-permute-start | bytes 1572872 | tf_op jit(solution)/shard_map/ppermute | solution.py:405
  248.8 1.9 collective-permute-start.30
  250.8 16.0 %collective-permute-done.28 = f32[2,8,128,128]{3,2,1,0:T(8,128)} collective-permute-done((f32[2,8,128,128]{3,2,1,0:T(8,128)S(1)}, f32[2,8,128,128]{3,2,1,0:T(8,128)}, u32[]{:S(2)}, u32[]{:S(2)}) %collective-permute-start.28) | collective-permute-done | bytes 1048608 | tf_op jit(solution)/shard_map/ppermute | solution.py:405
  266.7 2.9 bitcast_select_fusion
  269.6 10.9 %collective-permute-done.29 = f32[8,128,128]{2,1,0:T(8,128)} collective-permute-done((f32[8,128,128]{2,1,0:T(8,128)}, f32[8,128,128]{2,1,0:T(8,128)}, u32[]{:S(2)}, u32[]{:S(2)}) %collective-permute-start.29) | collective-permute-done | bytes 524320 | tf_op jit(solution)/shard_map/ppermute | solution.py:405
  280.5 10.9 %collective-permute-done.30 = f32[8,128,128]{2,1,0:T(8,128)} collective-permute-done((f32[8,128,128]{2,1,0:T(8,128)}, f32[8,128,128]{2,1,0:T(8,128)}, u32[]{:S(2)}, u32[]{:S(2)}) %collective-permute-start.30) | collective-permute-done | bytes 524320 | tf_op jit(solution)/shard_map/ppermute | solution.py:405
  291.4 2.5 select_add_fusion.1
  (85 shorter events, 7.3 us)
Async XLA Ops:
  0.6 1.5 copy-start.12
  3.0 25.0 %collective-permute-start = (f32[2,8,128,128]{3,2,1,0:T(8,128)S(1)}, f32[2,8,128,128]{3,2,1,0:T(8,128)}, u32[]{:S(2)}, u32[]{:S(2)}) collective-permute-start(f32[2,8,128,128]{3,2,1,0:T(8,128)S(1)} %dynamic-slice_bitcast_fusion), channel_id=1, source_target_pairs={{2,0},{3,1},{0,2},{1,3},{6,4},{7,5},{4,6},{5,7},{10,8},{11,9},{8,1... | collective-permute-start | bytes 3145736 | tf_op jit(solution)/shard_map/ppermute | solution.py:405
  3.6 26.0 %collective-permute-start.1 = (f32[8,128,128]{2,1,0:T(8,128)S(1)}, f32[8,128,128]{2,1,0:T(8,128)S(1)}, u32[]{:S(2)}, u32[]{:S(2)}) collective-permute-start(f32[8,128,128]{2,1,0:T(8,128)S(1)} %get-tuple-element.69), channel_id=1, source_target_pairs={{8,0},{9,1},{10,2},{11,3},{12,4},{13,5},{14,6},{15,7},{0,8},{1,9},... | collective-permute-start | bytes 1572872 | tf_op jit(solution)/shard_map/ppermute | solution.py:405
  6.2 24.6 %collective-permute-start.3 = (f32[8,128,128]{2,1,0:T(8,128)}, f32[8,128,128]{2,1,0:T(8,128)S(1)}, u32[]{:S(2)}, u32[]{:S(2)}) collective-permute-start(f32[8,128,128]{2,1,0:T(8,128)} %get-tuple-element.71), channel_id=1, source_target_pairs={{4,0},{5,1},{6,2},{7,3},{0,4},{1,5},{2,6},{3,7},{12,8},{13,9},{14,... | collective-permute-start | bytes 1572872 | tf_op jit(solution)/shard_map/ppermute | solution.py:405
  6.6 44.1 %collective-permute-start.2 = (f32[8,128,128]{2,1,0:T(8,128)}, f32[8,128,128]{2,1,0:T(8,128)S(1)}, u32[]{:S(2)}, u32[]{:S(2)}) collective-permute-start(f32[8,128,128]{2,1,0:T(8,128)} %get-tuple-element.71), channel_id=1, source_target_pairs={{12,0},{13,1},{14,2},{15,3},{8,4},{9,5},{10,6},{11,7},{4,8},{5,9},... | collective-permute-start | bytes 1572872 | tf_op jit(solution)/shard_map/ppermute | solution.py:405
  30.7 20.3 %copy-start.10 = (f32[8,128,128]{2,1,0:T(8,128)}, f32[8,128,128]{2,1,0:T(8,128)S(1)}, u32[]{:S(2)}) copy-start(f32[8,128,128]{2,1,0:T(8,128)S(1)} %collective-permute-done.3) | copy-start | bytes 1572868
  50.8 0.8 copy-start.11
  51.6 54.3 %collective-permute-start.6 = (f32[4,8,128,128]{3,2,1,0:T(8,128)S(1)}, f32[4,8,128,128]{3,2,1,0:T(8,128)S(1)}, u32[]{:S(2)}, u32[]{:S(2)}) collective-permute-start(f32[4,8,128,128]{3,2,1,0:T(8,128)S(1)} %pad_maximum_fusion), channel_id=1, source_target_pairs={{17,0},{0,1},{19,2},{2,3},{21,4},{4,5},{23,6},{6,7},{25,8},{8,9},{... | collective-permute-start | bytes 6291464 | tf_op jit(solution)/shard_map/ppermute | solution.py:419
  51.6 55.6 %collective-permute-start.5 = (f32[4,8,128,128]{3,2,1,0:T(8,128)S(1)}, f32[4,8,128,128]{3,2,1,0:T(8,128)}, u32[]{:S(2)}, u32[]{:S(2)}) collective-permute-start(f32[4,8,128,128]{3,2,1,0:T(8,128)S(1)} %pad_maximum_fusion), channel_id=1, source_target_pairs={{16,0},{18,2},{20,4},{22,6},{24,8},{26,10},{28,12},{30,14},{0,16},... | collective-permute-start | bytes 6291464 | tf_op jit(solution)/shard_map/ppermute | solution.py:419
  55.0 52.2 %collective-permute-start.4 = (f32[4,8,128,128]{3,2,1,0:T(8,128)S(1)}, f32[4,8,128,128]{3,2,1,0:T(8,128)}, u32[]{:S(2)}, u32[]{:S(2)}) collective-permute-start(f32[4,8,128,128]{3,2,1,0:T(8,128)S(1)} %pad_maximum_fusion), channel_id=1, source_target_pairs={{2,0},{3,1},{0,2},{1,3},{6,4},{7,5},{4,6},{5,7},{10,8},{11,9},{8,1... | collective-permute-start | bytes 6291464 | tf_op jit(solution)/shard_map/ppermute | solution.py:405
  56.6 45.2 %collective-permute-start.7 = (f32[2,8,128,128]{3,2,1,0:T(8,128)S(1)}, f32[2,8,128,128]{3,2,1,0:T(8,128)}, u32[]{:S(2)}, u32[]{:S(2)}) collective-permute-start(f32[2,8,128,128]{3,2,1,0:T(8,128)S(1)} %get-tuple-element.75), channel_id=1, source_target_pairs={{8,0},{9,1},{10,2},{11,3},{12,4},{13,5},{14,6},{15,7},{0,8},{1,9},... | collective-permute-start | bytes 3145736 | tf_op jit(solution)/shard_map/ppermute | solution.py:405
  56.6 49.3 %collective-permute-start.8 = (f32[2,8,128,128]{3,2,1,0:T(8,128)S(1)}, f32[2,8,128,128]{3,2,1,0:T(8,128)}, u32[]{:S(2)}, u32[]{:S(2)}) collective-permute-start(f32[2,8,128,128]{3,2,1,0:T(8,128)S(1)} %get-tuple-element.76.refs_2_.refs_4_), channel_id=1, source_target_pairs={{4,0},{5,1},{6,2},{7,3},{0,4},{1,5},{2,6},{3,7},{12,8},{13,9},{14,... | collective-permute-start | bytes 3145736 | tf_op jit(solution)/shard_map/ppermute | solution.py:405
  101.8 8.6 %collective-permute-start.12 = (f32[2,8,128,128]{3,2,1,0:T(8,128)S(1)}, f32[2,8,128,128]{3,2,1,0:T(8,128)S(1)}, u32[]{:S(2)}, u32[]{:S(2)}) collective-permute-start(f32[2,8,128,128]{3,2,1,0:T(8,128)S(1)} %get-tuple-element.76.refs_2_.refs_4_), channel_id=1, source_target_pairs={{1,0},{0,1},{3,2},{2,3},{5,4},{4,5},{7,6},{6,7},{9,8},{8,9},{11,10... | collective-permute-start | bytes 3145736 | tf_op jit(solution)/shard_map/ppermute | solution.py:405
  105.9 1.3 copy-start.2
  107.3 29.0 %collective-permute-start.10 = (f32[4,8,128,128]{3,2,1,0:T(8,128)}, f32[4,8,128,128]{3,2,1,0:T(8,128)}, u32[]{:S(2)}, u32[]{:S(2)}) collective-permute-start(f32[4,8,128,128]{3,2,1,0:T(8,128)} %collective-permute-done.5), channel_id=1, source_target_pairs={{2,0},{0,2},{6,4},{4,6},{10,8},{8,10},{14,12},{12,14},{18,16},{16,... | collective-permute-start | bytes 6291464 | tf_op jit(solution)/shard_map/ppermute | solution.py:409
  109.7 26.6 %collective-permute-start.11 = (f32[4,8,128,128]{3,2,1,0:T(8,128)}, f32[4,8,128,128]{3,2,1,0:T(8,128)}, u32[]{:S(2)}, u32[]{:S(2)}) collective-permute-start(f32[4,8,128,128]{3,2,1,0:T(8,128)} %collective-permute-done.4.home_ref), channel_id=1, source_target_pairs={{17,0},{0,1},{19,2},{2,3},{21,4},{4,5},{23,6},{6,7},{25,8},{8,9},{... | collective-permute-start | bytes 6291464 | tf_op jit(solution)/shard_map/ppermute | solution.py:419
  109.8 5.6 %collective-permute-start.13 = (f32[2,8,128,128]{3,2,1,0:T(8,128)}, f32[2,8,128,128]{3,2,1,0:T(8,128)}, u32[]{:S(2)}, u32[]{:S(2)}) collective-permute-start(f32[2,8,128,128]{3,2,1,0:T(8,128)} %collective-permute-done.8.refs_3_.refs_5_), channel_id=1, source_target_pairs={{1,0},{0,1},{3,2},{2,3},{5,4},{4,5},{7,6},{6,7},{9,8},{8,9},{11,10... | collective-permute-start | bytes 3145736 | tf_op jit(solution)/shard_map/ppermute | solution.py:405
  110.4 6.5 %collective-permute-start.14 = (f32[2,8,128,128]{3,2,1,0:T(8,128)}, f32[2,8,128,128]{3,2,1,0:T(8,128)}, u32[]{:S(2)}, u32[]{:S(2)}) collective-permute-start(f32[2,8,128,128]{3,2,1,0:T(8,128)} %collective-permute-done.7.refs_4_.refs_6_), channel_id=1, source_target_pairs={{1,0},{0,1},{3,2},{2,3},{5,4},{4,5},{7,6},{6,7},{9,8},{8,9},{11,10... | collective-permute-start | bytes 3145736 | tf_op jit(solution)/shard_map/ppermute | solution.py:405
  110.4 3.6 %copy-start.9 = (f32[2,8,128,128]{3,2,1,0:T(8,128)}, f32[2,8,128,128]{3,2,1,0:T(8,128)S(1)}, u32[]{:S(2)}) copy-start(f32[2,8,128,128]{3,2,1,0:T(8,128)S(1)} %collective-permute-done.12.refs_5_.refs_8_) | copy-start | bytes 3145732
  110.4 25.9 %collective-permute-start.9 = (f32[2,8,128,128]{3,2,1,0:T(8,128)}, f32[2,8,128,128]{3,2,1,0:T(8,128)}, u32[]{:S(2)}, u32[]{:S(2)}) collective-permute-start(f32[2,8,128,128]{3,2,1,0:T(8,128)} %collective-permute-done.7.refs_4_.refs_6_), channel_id=1, source_target_pairs={{4,0},{5,1},{6,2},{7,3},{0,4},{1,5},{2,6},{3,7},{12,8},{13,9},{14,... | collective-permute-start | bytes 3145736 | tf_op jit(solution)/shard_map/ppermute | solution.py:405
  111.8 5.1 %copy-start.3 = (f32[4,8,128,128]{3,2,1,0:T(8,128)S(1)}, f32[4,8,128,128]{3,2,1,0:T(8,128)}, u32[]{:S(2)}) copy-start(f32[4,8,128,128]{3,2,1,0:T(8,128)} %copy-done.2) | copy-start | bytes 6291460
  111.8 5.1 %copy-start.7 = (bf16[256,256]{1,0:T(8,128)(2,1)S(1)}, bf16[256,256]{1,0:T(8,128)(2,1)}, u32[]{:S(2)}) copy-start(bf16[256,256]{1,0:T(8,128)(2,1)} %constant.120.clone.right_ref) | copy-start | bytes 393220
  111.8 5.1 %copy-start.8 = (bf16[256,256]{1,0:T(8,128)(2,1)S(1)}, bf16[256,256]{1,0:T(8,128)(2,1)}, u32[]{:S(2)}) copy-start(bf16[256,256]{1,0:T(8,128)(2,1)} %constant.119.clone.left_ref) | copy-start | bytes 393220
  114.0 9.2 %copy-start = (f32[4,8,128,128]{3,2,1,0:T(8,128)}, f32[4,8,128,128]{3,2,1,0:T(8,128)S(1)}, u32[]{:S(2)}) copy-start(f32[4,8,128,128]{3,2,1,0:T(8,128)S(1)} %broadcast_select_fusion.1.refs_0_) | copy-start | bytes 6291460
  114.0 22.2 %copy-start.15 = (s32[16]{0:T(128)S(1)}, s32[16]{0:T(128)}, u32[]{:S(2)}) copy-start(s32[16]{0:T(128)} %constant.121.clone) | copy-start | bytes 196
  114.1 22.3 %copy-start.14 = (bf16[16,8,128]{2,1,0:T(8,128)(2,1)S(1)}, bf16[16,8,128]{2,1,0:T(8,128)(2,1)}, u32[]{:S(2)}) copy-start(bf16[16,8,128]{2,1,0:T(8,128)(2,1)} %constant.127.clone.1) | copy-start | bytes 98308
  114.1 22.8 %copy-start.13 = (bf16[16,8,128]{2,1,0:T(8,128)(2,1)S(1)}, bf16[16,8,128]{2,1,0:T(8,128)(2,1)}, u32[]{:S(2)}) copy-start(bf16[16,8,128]{2,1,0:T(8,128)(2,1)} %constant.126.clone.1) | copy-start | bytes 98308
  123.2 1.6 copy-start.6
  136.3 2.9 collective-permute-start.15
  139.2 29.6 %copy-start.4 = (f32[4,8,128,128]{3,2,1,0:T(8,128)S(1)}, f32[4,8,128,128]{3,2,1,0:T(8,128)}, u32[]{:S(2)}) copy-start(f32[4,8,128,128]{3,2,1,0:T(8,128)} %copy-done.2) | copy-start | bytes 6291460
  159.8 9.0 %copy-start.1 = (f32[4,8,128,128]{3,2,1,0:T(8,128)S(1)}, f32[4,8,128,128]{3,2,1,0:T(8,128)}, u32[]{:S(2)}) copy-start(f32[4,8,128,128]{3,2,1,0:T(8,128)} %copy-done) | copy-start | bytes 6291460
  159.8 24.9 %collective-permute-start.17 = (f32[4,8,128,128]{3,2,1,0:T(8,128)S(1)}, f32[4,8,128,128]{3,2,1,0:T(8,128)S(1)}, u32[]{:S(2)}, u32[]{:S(2)}) collective-permute-start(f32[4,8,128,128]{3,2,1,0:T(8,128)S(1)} %get-tuple-element.87), channel_id=1, source_target_pairs={{0,17},{1,0},{2,19},{3,2},{4,21},{5,4},{6,23},{7,6},{8,25},{9,8},{... | collective-permute-start | bytes 6291464 | tf_op jit(solution)/shard_map/ppermute | solution.py:419
  161.1 27.9 %collective-permute-start.16 = (f32[4,8,128,128]{3,2,1,0:T(8,128)S(1)}, f32[4,8,128,128]{3,2,1,0:T(8,128)S(1)}, u32[]{:S(2)}, u32[]{:S(2)}) collective-permute-start(f32[4,8,128,128]{3,2,1,0:T(8,128)S(1)} %get-tuple-element.86), channel_id=1, source_target_pairs={{2,0},{0,2},{6,4},{4,6},{10,8},{8,10},{14,12},{12,14},{18,16},{16,... | collective-permute-start | bytes 6291464 | tf_op jit(solution)/shard_map/ppermute | solution.py:409
  164.5 2.7 collective-permute-start.18
  167.4 25.3 %collective-permute-start.22 = (f32[2,8,128,128]{3,2,1,0:T(8,128)S(1)}, f32[2,8,128,128]{3,2,1,0:T(8,128)S(1)}, u32[]{:S(2)}, u32[]{:S(2)}) collective-permute-start(f32[2,8,128,128]{3,2,1,0:T(8,128)S(1)} %add.162), channel_id=1, source_target_pairs={{4,0},{5,1},{6,2},{7,3},{0,4},{1,5},{2,6},{3,7},{12,8},{13,9},{14,... | collective-permute-start | bytes 3145736 | tf_op jit(solution)/shard_map/ppermute | solution.py:405
  168.8 1.9 copy-start.5
  189.0 4.1 %collective-permute-start.20 = (f32[2,8,128,128]{3,2,1,0:T(8,128)S(1)}, f32[2,8,128,128]{3,2,1,0:T(8,128)S(1)}, u32[]{:S(2)}, u32[]{:S(2)}) collective-permute-start(f32[2,8,128,128]{3,2,1,0:T(8,128)S(1)} %get-tuple-element.111), channel_id=1, source_target_pairs={{1,0},{0,1},{3,2},{2,3},{5,4},{4,5},{7,6},{6,7},{9,8},{8,9},{11,10... | collective-permute-start | bytes 3145736 | tf_op jit(solution)/shard_map/ppermute | solution.py:405
  189.0 8.7 %collective-permute-start.19 = (f32[2,8,128,128]{3,2,1,0:T(8,128)S(1)}, f32[2,8,128,128]{3,2,1,0:T(8,128)S(1)}, u32[]{:S(2)}, u32[]{:S(2)}) collective-permute-start(f32[2,8,128,128]{3,2,1,0:T(8,128)S(1)} %get-tuple-element.109), channel_id=1, source_target_pairs={{1,0},{0,1},{3,2},{2,3},{5,4},{4,5},{7,6},{6,7},{9,8},{8,9},{11,10... | collective-permute-start | bytes 3145736 | tf_op jit(solution)/shard_map/ppermute | solution.py:405
  189.6 6.6 %collective-permute-start.23 = (f32[2,8,128,128]{3,2,1,0:T(8,128)S(1)}, f32[2,8,128,128]{3,2,1,0:T(8,128)S(1)}, u32[]{:S(2)}, u32[]{:S(2)}) collective-permute-start(f32[2,8,128,128]{3,2,1,0:T(8,128)S(1)} %get-tuple-element.114), channel_id=1, source_target_pairs={{1,0},{0,1},{3,2},{2,3},{5,4},{4,5},{7,6},{6,7},{9,8},{8,9},{11,10... | collective-permute-start | bytes 3145736 | tf_op jit(solution)/shard_map/ppermute | solution.py:405
  189.6 52.0 %collective-permute-start.26 = (f32[4,8,128,128]{3,2,1,0:T(8,128)S(1)}, f32[4,8,128,128]{3,2,1,0:T(8,128)S(1)}, u32[]{:S(2)}, u32[]{:S(2)}) collective-permute-start(f32[4,8,128,128]{3,2,1,0:T(8,128)S(1)} %get-tuple-element.117), channel_id=1, source_target_pairs={{0,17},{1,0},{2,19},{3,2},{4,21},{5,4},{6,23},{7,6},{8,25},{9,8},{... | collective-permute-start | bytes 6291464 | tf_op jit(solution)/shard_map/ppermute | solution.py:419
  192.6 48.9 %collective-permute-start.27 = (f32[4,8,128,128]{3,2,1,0:T(8,128)S(1)}, f32[4,8,128,128]{3,2,1,0:T(8,128)S(1)}, u32[]{:S(2)}, u32[]{:S(2)}) collective-permute-start(f32[4,8,128,128]{3,2,1,0:T(8,128)S(1)} %select_add_fusion), channel_id=1, source_target_pairs={{2,0},{3,1},{0,2},{1,3},{6,4},{7,5},{4,6},{5,7},{10,8},{11,9},{8,1... | collective-permute-start | bytes 6291464 | tf_op jit(solution)/shard_map/ppermute | solution.py:405
  193.2 48.4 %collective-permute-start.25 = (f32[4,8,128,128]{3,2,1,0:T(8,128)S(1)}, f32[4,8,128,128]{3,2,1,0:T(8,128)S(1)}, u32[]{:S(2)}, u32[]{:S(2)}) collective-permute-start(f32[4,8,128,128]{3,2,1,0:T(8,128)S(1)} %get-tuple-element.136), channel_id=1, source_target_pairs={{0,16},{2,18},{4,20},{6,22},{8,24},{10,26},{12,28},{14,30},{16,0},... | collective-permute-start | bytes 6291464 | tf_op jit(solution)/shard_map/ppermute | solution.py:419
  196.2 42.7 %collective-permute-start.21 = (f32[2,8,128,128]{3,2,1,0:T(8,128)S(1)}, f32[2,8,128,128]{3,2,1,0:T(8,128)S(1)}, u32[]{:S(2)}, u32[]{:S(2)}) collective-permute-start(f32[2,8,128,128]{3,2,1,0:T(8,128)S(1)} %add.164), channel_id=1, source_target_pairs={{4,0},{5,1},{6,2},{7,3},{0,4},{1,5},{2,6},{3,7},{12,8},{13,9},{14,... | collective-permute-start | bytes 3145736 | tf_op jit(solution)/shard_map/ppermute | solution.py:405
  197.8 43.8 %collective-permute-start.24 = (f32[2,8,128,128]{3,2,1,0:T(8,128)S(1)}, f32[2,8,128,128]{3,2,1,0:T(8,128)S(1)}, u32[]{:S(2)}, u32[]{:S(2)}) collective-permute-start(f32[2,8,128,128]{3,2,1,0:T(8,128)S(1)} %add_add_fusion), channel_id=1, source_target_pairs={{8,0},{9,1},{10,2},{11,3},{12,4},{13,5},{14,6},{15,7},{0,8},{1,9},... | collective-permute-start | bytes 3145736 | tf_op jit(solution)/shard_map/ppermute | solution.py:405
  243.9 22.8 %collective-permute-start.28 = (f32[2,8,128,128]{3,2,1,0:T(8,128)S(1)}, f32[2,8,128,128]{3,2,1,0:T(8,128)}, u32[]{:S(2)}, u32[]{:S(2)}) collective-permute-start(f32[2,8,128,128]{3,2,1,0:T(8,128)S(1)} %get-tuple-element.158), channel_id=1, source_target_pairs={{2,0},{3,1},{0,2},{1,3},{6,4},{7,5},{4,6},{5,7},{10,8},{11,9},{8,1... | collective-permute-start | bytes 3145736 | tf_op jit(solution)/shard_map/ppermute | solution.py:405
  245.4 35.0 %collective-permute-start.29 = (f32[8,128,128]{2,1,0:T(8,128)}, f32[8,128,128]{2,1,0:T(8,128)}, u32[]{:S(2)}, u32[]{:S(2)}) collective-permute-start(f32[8,128,128]{2,1,0:T(8,128)} %get-tuple-element.128), channel_id=1, source_target_pairs={{8,0},{9,1},{10,2},{11,3},{12,4},{13,5},{14,6},{15,7},{0,8},{1,9},... | collective-permute-start | bytes 1572872 | tf_op jit(solution)/shard_map/ppermute | solution.py:405
  248.8 42.6 %collective-permute-start.30 = (f32[8,128,128]{2,1,0:T(8,128)}, f32[8,128,128]{2,1,0:T(8,128)}, u32[]{:S(2)}, u32[]{:S(2)}) collective-permute-start(f32[8,128,128]{2,1,0:T(8,128)} %get-tuple-element.129), channel_id=1, source_target_pairs={{12,0},{13,1},{14,2},{15,3},{8,4},{9,5},{10,6},{11,7},{4,8},{5,9},... | collective-permute-start | bytes 1572872 | tf_op jit(solution)/shard_map/ppermute | solution.py:405
  250.6 40.8 %collective-permute-start.31 = (f32[8,128,128]{2,1,0:T(8,128)S(1)}, f32[8,128,128]{2,1,0:T(8,128)}, u32[]{:S(2)}, u32[]{:S(2)}) collective-permute-start(f32[8,128,128]{2,1,0:T(8,128)S(1)} %get-tuple-element.130), channel_id=1, source_target_pairs={{4,0},{5,1},{6,2},{7,3},{0,4},{1,5},{2,6},{3,7},{12,8},{13,9},{14,... | collective-permute-start | bytes 1572872 | tf_op jit(solution)/shard_map/ppermute | solution.py:405

commit v10 on v9

--- a/solution.py
+++ b/solution.py
@@ -462,6 +462,7 @@
     )
     first_x, second_x = swap_away(first, 2), across(bands_x, 1, False)
     got_far = swap(got_near, 4)
+    second = pltpu.with_memory_space_constraint(second, pltpu.HBM)
     parts = [kept_near, kept_far, got_near]
     parts_c = [
         pltpu.with_memory_space_constraint(swap(part, 1), pltpu.HBM) for part in parts

time: 294 us -> 293 us (level)
  transfers between devices with their start and end apart: 32 -> 32, of which waited for: 18 -> 18; matrix products, arithmetic and copies ran while one was open for 4% -> 4% of each run, Pallas kernels for 4% -> 5%
where the time goes in v10:
time: 293 us
  waiting for transfers between devices  199 us (68%)
  starting transfers between devices  36.1 us (12%)
  Pallas kernels  34.1 us (12%)
  other arithmetic  11.6 us (4%)
  local copies, waits for them, and re-layouts  10.6 us (4%)
    ppermute x24, waiting for transfers between devices, swap(): return lax.ppermute(block, 'slab', [(i ^ mask, i) for i in range(slabs)])  188 us
    ppermute x24, starting transfers between devices, swap(): return lax.ppermute(block, 'slab', [(i ^ mask, i) for i in range(slabs)])  21.8 us
    pallas_call x1, Pallas kernels, late_part(): pl.pallas_call(functools.partial(late_kernel, steps, groups), in_specs=[p...  20.5 us
    ppermute x6, starting transfers between devices, across(): return lax.ppermute(block, ('band', 'slab'), route)  8.43 us
    ppermute x6, waiting for transfers between devices, across(): return lax.ppermute(block, ('band', 'slab'), route)  7.14 us
    pallas_call x1, Pallas kernels, scatter_part(): pl.pallas_call(functools.partial(scatter_kernel, steps), grid=(len(steps)...  6.87 us
    pallas_call x1, Pallas kernels, gather_part(): pl.pallas_call(functools.partial(gather_kernel, steps), grid=(count,), in...  6.73 us
  transfers between devices with their start and end apart: 32, of which 18 were waited for; matrix products, arithmetic and copies ran while one was open for 4% of the time, Pallas kernels for 5%

profile of v10, /device:TPU:10, one launch (start us, length us, event | category | flops | bytes accessed | tf_op | source)
XLA Modules:
  0.0 292.5 jit_solution(1279269663764235031)
XLA Ops:
  0.6 1.4 dynamic-slice_bitcast_fusion
  2.2 0.9 dynamic-slice_bitcast_fusion.3
  3.6 2.6 collective-permute-start.1
  7.1 1.3 dynamic-slice_bitcast_fusion.1
  8.4 19.7 %collective-permute-done = f32[2,8,128,128]{3,2,1,0:T(8,128)} collective-permute-done((f32[2,8,128,128]{3,2,1,0:T(8,128)S(1)}, f32[2,8,128,128]{3,2,1,0:T(8,128)}, u32[]{:S(2)}, u32[]{:S(2)}) %collective-permute-start) | collective-permute-done | bytes 1048608 | tf_op jit(solution)/shard_map/ppermute | solution.py:405
  28.1 1.3 constant_dynamic-slice_fusion
  29.6 1.2 collective-permute-done.3
  30.7 20.0 %collective-permute-done.2 = f32[8,128,128]{2,1,0:T(8,128)S(1)} collective-permute-done((f32[8,128,128]{2,1,0:T(8,128)}, f32[8,128,128]{2,1,0:T(8,128)S(1)}, u32[]{:S(2)}, u32[]{:S(2)}) %collective-permute-start.2) | collective-permute-done | bytes 524320 | tf_op jit(solution)/shard_map/ppermute | solution.py:405
  51.0 0.6 copy-done.9
  51.6 3.4 %collective-permute-start.5 = (f32[4,8,128,128]{3,2,1,0:T(8,128)S(1)}, f32[4,8,128,128]{3,2,1,0:T(8,128)}, u32[]{:S(2)}, u32[]{:S(2)}) collective-permute-start(f32[4,8,128,128]{3,2,1,0:T(8,128)S(1)} %pad_maximum_fusion), channel_id=1, source_target_pairs={{16,0},{18,2},{20,4},{22,6},{24,8},{26,10},{28,12},{30,14},{0,16},... | collective-permute-start | bytes 6291464 | tf_op jit(solution)/shard_map/ppermute | solution.py:419
  55.0 1.6 collective-permute-start.4
  56.6 3.8 %collective-permute-start.8 = (f32[2,8,128,128]{3,2,1,0:T(8,128)S(1)}, f32[2,8,128,128]{3,2,1,0:T(8,128)}, u32[]{:S(2)}, u32[]{:S(2)}) collective-permute-start(f32[2,8,128,128]{3,2,1,0:T(8,128)S(1)} %get-tuple-element.76.refs_2_.refs_4_), channel_id=1, source_target_pairs={{4,0},{5,1},{6,2},{7,3},{0,4},{1,5},{2,6},{3,7},{12,8},{13,9},{14,... | collective-permute-start | bytes 3145736 | tf_op jit(solution)/shard_map/ppermute | solution.py:405
  60.4 41.4 %collective-permute-done.7.refs_4_.refs_6_ = f32[2,8,128,128]{3,2,1,0:T(8,128)} collective-permute-done((f32[2,8,128,128]{3,2,1,0:T(8,128)S(1)}, f32[2,8,128,128]{3,2,1,0:T(8,128)}, u32[]{:S(2)}, u32[]{:S(2)}) %collective-permute-start.7) | collective-permute-done | bytes 1048608 | tf_op jit(solution)/shard_map/ppermute | solution.py:405
  101.8 4.2 %collective-permute-done.8.refs_3_.refs_5_ = f32[2,8,128,128]{3,2,1,0:T(8,128)} collective-permute-done((f32[2,8,128,128]{3,2,1,0:T(8,128)S(1)}, f32[2,8,128,128]{3,2,1,0:T(8,128)}, u32[]{:S(2)}, u32[]{:S(2)}) %collective-permute-start.8) | collective-permute-done | bytes 1048608 | tf_op jit(solution)/shard_map/ppermute | solution.py:405
  105.9 2.4 collective-permute-start.10
  108.5 0.6 collective-permute-start.13
  109.1 1.4 collective-permute-start.9
  110.5 2.1 broadcast_select_fusion.1.refs_0_
  112.7 1.4 collective-permute-done.13.refs_6_.refs_9_
  114.1 1.5 collective-permute-done.14.refs_7_.refs_10_
  115.6 6.7 %shard_map.86.early_ref = f32[128,48,128]{2,1,0:T(8,128)S(1)} custom-call(bf16[256,256]{1,0:T(8,128)(2,1)S(1)} %copy-done.4, bf16[256,256]{1,0:T(8,128)(2,1)S(1)} %copy-done.5, f32[4,8,128,128]{3,2,1,0:T(8,128)S(1)} %broadcast_select_fusion.1.refs_0_, f32[4,8,128,128]{3,2,1,0:T(8,128)} %copy-done.6, ...), custom_call_target="tpu_custom_call" | custom-call | flops 1610612736 | bytes 9437184 | tf_op jit(solution)/shard_map/pallas_call | solution.py:328
  122.4 1.6 copy-done.3
  124.0 11.1 %collective-permute-done.9.refs_7_ = f32[2,8,128,128]{3,2,1,0:T(8,128)} collective-permute-done((f32[2,8,128,128]{3,2,1,0:T(8,128)}, f32[2,8,128,128]{3,2,1,0:T(8,128)}, u32[]{:S(2)}, u32[]{:S(2)}) %collective-permute-start.9) | collective-permute-done | bytes 1048608 | tf_op jit(solution)/shard_map/ppermute | solution.py:405
  136.6 1.3 collective-permute-done.15.refs_11_
  137.9 20.5 %shard_map.87 = (f32[128,48,128]{2,1,0:T(8,128)}, f32[4,8,128,128]{3,2,1,0:T(8,128)S(1)}, f32[4,8,128,128]{3,2,1,0:T(8,128)S(1)}, f32[4,8,128,128]{3,2,1,0:T(8,1...) custom-call(bf16[256,256]{1,0:T(8,128)(2,1)S(1)} %copy-done.4, ...), custom_call_target="tpu_custom_call" | custom-call | flops 10737418240 | bytes 33554432 | tf_op jit(solution)/shard_map/pallas_call | solution.py:347
  158.4 1.3 collective-permute-start.17
  159.7 3.4 %collective-permute-start.16 = (f32[4,8,128,128]{3,2,1,0:T(8,128)S(1)}, f32[4,8,128,128]{3,2,1,0:T(8,128)S(1)}, u32[]{:S(2)}, u32[]{:S(2)}) collective-permute-start(f32[4,8,128,128]{3,2,1,0:T(8,128)S(1)} %get-tuple-element.86), channel_id=1, source_target_pairs={{2,0},{0,2},{6,4},{4,6},{10,8},{8,10},{14,12},{12,14},{18,16},{16,... | collective-permute-start | bytes 6291464 | tf_op jit(solution)/shard_map/ppermute | solution.py:409
  163.2 2.6 collective-permute-done.18
  166.0 1.4 collective-permute-start.22
  167.4 1.9 copy-done.2
  169.3 6.9 %shard_map.88 = (f32[4,8,128,128]{3,2,1,0:T(8,128)S(1)}, f32[4,8,128,128]{3,2,1,0:T(8,128)S(1)}, f32[2,8,128,128]{3,2,1,0:T(8,128)S(1)}, f32[2,8,128,128]{3,2,1,...) custom-call(bf16[256,256]{1,0:T(8,128)(2,1)S(1)} %copy-done.4, ...), custom_call_target="tpu_custom_call", output_to_operand_aliasing={{0}: (11, {}), {1}: (12, {}), {2}: (13, {}), {3}: (14, {}),... | custom-call | flops 1610612736 | bytes 15728640 | tf_op jit(solution)/shard_map/pallas_call | solution.py:374
  176.2 7.1 %collective-permute-done.17 = f32[4,8,128,128]{3,2,1,0:T(8,128)S(1)} collective-permute-done((f32[4,8,128,128]{3,2,1,0:T(8,128)S(1)}, f32[4,8,128,128]{3,2,1,0:T(8,128)S(1)}, u32[]{:S(2)}, u32[]{:S(2)}) %collective-permute-start.17) | collective-permute-done | bytes 2097184 | tf_op jit(solution)/shard_map/ppermute | solution.py:419
  183.6 4.1 %collective-permute-done.16 = f32[4,8,128,128]{3,2,1,0:T(8,128)S(1)} collective-permute-done((f32[4,8,128,128]{3,2,1,0:T(8,128)S(1)}, f32[4,8,128,128]{3,2,1,0:T(8,128)S(1)}, u32[]{:S(2)}, u32[]{:S(2)}) %collective-permute-start.16) | collective-permute-done | bytes 2097184 | tf_op jit(solution)/shard_map/ppermute | solution.py:409
  188.2 0.8 collective-permute-start.26
  189.4 1.9 collective-permute-done.22
  191.8 2.9 collective-permute-start.25
  194.8 1.4 collective-permute-start.21
  196.7 41.4 %collective-permute-done.21 = f32[2,8,128,128]{3,2,1,0:T(8,128)S(1)} collective-permute-done((f32[2,8,128,128]{3,2,1,0:T(8,128)S(1)}, f32[2,8,128,128]{3,2,1,0:T(8,128)S(1)}, u32[]{:S(2)}, u32[]{:S(2)}) %collective-permute-start.21) | collective-permute-done | bytes 1048608 | tf_op jit(solution)/shard_map/ppermute | solution.py:405
  238.3 2.5 collective-permute-done.24
  240.8 1.8 add_bitcast_fusion
  243.1 1.0 collective-permute-start.28
  244.1 3.3 %collective-permute-start.29 = (f32[8,128,128]{2,1,0:T(8,128)}, f32[8,128,128]{2,1,0:T(8,128)}, u32[]{:S(2)}, u32[]{:S(2)}) collective-permute-start(f32[8,128,128]{2,1,0:T(8,128)} %get-tuple-element.128), channel_id=1, source_target_pairs={{8,0},{9,1},{10,2},{11,3},{12,4},{13,5},{14,6},{15,7},{0,8},{1,9},... | collective-permute-start | bytes 1572872 | tf_op jit(solution)/shard_map/ppermute | solution.py:405
  247.4 1.9 collective-permute-start.30
  249.4 16.7 %collective-permute-done.28 = f32[2,8,128,128]{3,2,1,0:T(8,128)} collective-permute-done((f32[2,8,128,128]{3,2,1,0:T(8,128)S(1)}, f32[2,8,128,128]{3,2,1,0:T(8,128)}, u32[]{:S(2)}, u32[]{:S(2)}) %collective-permute-start.28) | collective-permute-done | bytes 1048608 | tf_op jit(solution)/shard_map/ppermute | solution.py:405
  266.0 2.9 bitcast_select_fusion
  268.9 10.2 %collective-permute-done.29 = f32[8,128,128]{2,1,0:T(8,128)} collective-permute-done((f32[8,128,128]{2,1,0:T(8,128)}, f32[8,128,128]{2,1,0:T(8,128)}, u32[]{:S(2)}, u32[]{:S(2)}) %collective-permute-start.29) | collective-permute-done | bytes 524320 | tf_op jit(solution)/shard_map/ppermute | solution.py:405
  279.1 10.9 %collective-permute-done.30 = f32[8,128,128]{2,1,0:T(8,128)} collective-permute-done((f32[8,128,128]{2,1,0:T(8,128)}, f32[8,128,128]{2,1,0:T(8,128)}, u32[]{:S(2)}, u32[]{:S(2)}) %collective-permute-start.30) | collective-permute-done | bytes 524320 | tf_op jit(solution)/shard_map/ppermute | solution.py:405
  290.0 2.5 select_add_fusion.1
  (81 shorter events, 6.9 us)
Async XLA Ops:
  0.6 1.5 copy-start.10
  3.0 25.0 %collective-permute-start = (f32[2,8,128,128]{3,2,1,0:T(8,128)S(1)}, f32[2,8,128,128]{3,2,1,0:T(8,128)}, u32[]{:S(2)}, u32[]{:S(2)}) collective-permute-start(f32[2,8,128,128]{3,2,1,0:T(8,128)S(1)} %dynamic-slice_bitcast_fusion), channel_id=1, source_target_pairs={{2,0},{3,1},{0,2},{1,3},{6,4},{7,5},{4,6},{5,7},{10,8},{11,9},{8,1... | collective-permute-start | bytes 3145736 | tf_op jit(solution)/shard_map/ppermute | solution.py:405
  3.6 26.0 %collective-permute-start.1 = (f32[8,128,128]{2,1,0:T(8,128)S(1)}, f32[8,128,128]{2,1,0:T(8,128)S(1)}, u32[]{:S(2)}, u32[]{:S(2)}) collective-permute-start(f32[8,128,128]{2,1,0:T(8,128)S(1)} %get-tuple-element.69), channel_id=1, source_target_pairs={{8,0},{9,1},{10,2},{11,3},{12,4},{13,5},{14,6},{15,7},{0,8},{1,9},... | collective-permute-start | bytes 1572872 | tf_op jit(solution)/shard_map/ppermute | solution.py:405
  6.2 24.6 %collective-permute-start.3 = (f32[8,128,128]{2,1,0:T(8,128)}, f32[8,128,128]{2,1,0:T(8,128)S(1)}, u32[]{:S(2)}, u32[]{:S(2)}) collective-permute-start(f32[8,128,128]{2,1,0:T(8,128)} %get-tuple-element.71), channel_id=1, source_target_pairs={{4,0},{5,1},{6,2},{7,3},{0,4},{1,5},{2,6},{3,7},{12,8},{13,9},{14,... | collective-permute-start | bytes 1572872 | tf_op jit(solution)/shard_map/ppermute | solution.py:405
  6.6 44.1 %collective-permute-start.2 = (f32[8,128,128]{2,1,0:T(8,128)}, f32[8,128,128]{2,1,0:T(8,128)S(1)}, u32[]{:S(2)}, u32[]{:S(2)}) collective-permute-start(f32[8,128,128]{2,1,0:T(8,128)} %get-tuple-element.71), channel_id=1, source_target_pairs={{12,0},{13,1},{14,2},{15,3},{8,4},{9,5},{10,6},{11,7},{4,8},{5,9},... | collective-permute-start | bytes 1572872 | tf_op jit(solution)/shard_map/ppermute | solution.py:405
  30.7 20.3 %copy-start.8 = (f32[8,128,128]{2,1,0:T(8,128)}, f32[8,128,128]{2,1,0:T(8,128)S(1)}, u32[]{:S(2)}) copy-start(f32[8,128,128]{2,1,0:T(8,128)S(1)} %collective-permute-done.3) | copy-start | bytes 1572868
  50.8 0.8 copy-start.9
  51.6 54.4 %collective-permute-start.6 = (f32[4,8,128,128]{3,2,1,0:T(8,128)S(1)}, f32[4,8,128,128]{3,2,1,0:T(8,128)S(1)}, u32[]{:S(2)}, u32[]{:S(2)}) collective-permute-start(f32[4,8,128,128]{3,2,1,0:T(8,128)S(1)} %pad_maximum_fusion), channel_id=1, source_target_pairs={{17,0},{0,1},{19,2},{2,3},{21,4},{4,5},{23,6},{6,7},{25,8},{8,9},{... | collective-permute-start | bytes 6291464 | tf_op jit(solution)/shard_map/ppermute | solution.py:419
  51.6 54.3 %collective-permute-start.5 = (f32[4,8,128,128]{3,2,1,0:T(8,128)S(1)}, f32[4,8,128,128]{3,2,1,0:T(8,128)}, u32[]{:S(2)}, u32[]{:S(2)}) collective-permute-start(f32[4,8,128,128]{3,2,1,0:T(8,128)S(1)} %pad_maximum_fusion), channel_id=1, source_target_pairs={{16,0},{18,2},{20,4},{22,6},{24,8},{26,10},{28,12},{30,14},{0,16},... | collective-permute-start | bytes 6291464 | tf_op jit(solution)/shard_map/ppermute | solution.py:419
  55.0 50.9 %collective-permute-start.4 = (f32[4,8,128,128]{3,2,1,0:T(8,128)S(1)}, f32[4,8,128,128]{3,2,1,0:T(8,128)}, u32[]{:S(2)}, u32[]{:S(2)}) collective-permute-start(f32[4,8,128,128]{3,2,1,0:T(8,128)S(1)} %pad_maximum_fusion), channel_id=1, source_target_pairs={{2,0},{3,1},{0,2},{1,3},{6,4},{7,5},{4,6},{5,7},{10,8},{11,9},{8,1... | collective-permute-start | bytes 6291464 | tf_op jit(solution)/shard_map/ppermute | solution.py:405
  56.6 45.2 %collective-permute-start.7 = (f32[2,8,128,128]{3,2,1,0:T(8,128)S(1)}, f32[2,8,128,128]{3,2,1,0:T(8,128)}, u32[]{:S(2)}, u32[]{:S(2)}) collective-permute-start(f32[2,8,128,128]{3,2,1,0:T(8,128)S(1)} %get-tuple-element.75), channel_id=1, source_target_pairs={{8,0},{9,1},{10,2},{11,3},{12,4},{13,5},{14,6},{15,7},{0,8},{1,9},... | collective-permute-start | bytes 3145736 | tf_op jit(solution)/shard_map/ppermute | solution.py:405
  56.6 49.3 %collective-permute-start.8 = (f32[2,8,128,128]{3,2,1,0:T(8,128)S(1)}, f32[2,8,128,128]{3,2,1,0:T(8,128)}, u32[]{:S(2)}, u32[]{:S(2)}) collective-permute-start(f32[2,8,128,128]{3,2,1,0:T(8,128)S(1)} %get-tuple-element.76.refs_2_.refs_4_), channel_id=1, source_target_pairs={{4,0},{5,1},{6,2},{7,3},{0,4},{1,5},{2,6},{3,7},{12,8},{13,9},{14,... | collective-permute-start | bytes 3145736 | tf_op jit(solution)/shard_map/ppermute | solution.py:405
  101.8 7.3 %collective-permute-start.12 = (f32[2,8,128,128]{3,2,1,0:T(8,128)S(1)}, f32[2,8,128,128]{3,2,1,0:T(8,128)S(1)}, u32[]{:S(2)}, u32[]{:S(2)}) collective-permute-start(f32[2,8,128,128]{3,2,1,0:T(8,128)S(1)} %get-tuple-element.76.refs_2_.refs_4_), channel_id=1, source_target_pairs={{1,0},{0,1},{3,2},{2,3},{5,4},{4,5},{7,6},{6,7},{9,8},{8,9},{11,10... | collective-permute-start | bytes 3145736 | tf_op jit(solution)/shard_map/ppermute | solution.py:405
  105.9 3.2 %copy-start.6 = (f32[4,8,128,128]{3,2,1,0:T(8,128)}, f32[4,8,128,128]{3,2,1,0:T(8,128)S(1)}, u32[]{:S(2)}) copy-start(f32[4,8,128,128]{3,2,1,0:T(8,128)S(1)} %collective-permute-done.6.refs_1_.refs_2_) | copy-start | bytes 6291460
  105.9 29.1 %collective-permute-start.10 = (f32[4,8,128,128]{3,2,1,0:T(8,128)}, f32[4,8,128,128]{3,2,1,0:T(8,128)}, u32[]{:S(2)}, u32[]{:S(2)}) collective-permute-start(f32[4,8,128,128]{3,2,1,0:T(8,128)} %collective-permute-done.5), channel_id=1, source_target_pairs={{2,0},{0,2},{6,4},{4,6},{10,8},{8,10},{14,12},{12,14},{18,16},{16,... | collective-permute-start | bytes 6291464 | tf_op jit(solution)/shard_map/ppermute | solution.py:409
  108.4 26.6 %collective-permute-start.11 = (f32[4,8,128,128]{3,2,1,0:T(8,128)}, f32[4,8,128,128]{3,2,1,0:T(8,128)}, u32[]{:S(2)}, u32[]{:S(2)}) collective-permute-start(f32[4,8,128,128]{3,2,1,0:T(8,128)} %collective-permute-done.4.home_ref), channel_id=1, source_target_pairs={{17,0},{0,1},{19,2},{2,3},{21,4},{4,5},{23,6},{6,7},{25,8},{8,9},{... | collective-permute-start | bytes 6291464 | tf_op jit(solution)/shard_map/ppermute | solution.py:419
  108.5 5.6 %collective-permute-start.13 = (f32[2,8,128,128]{3,2,1,0:T(8,128)}, f32[2,8,128,128]{3,2,1,0:T(8,128)}, u32[]{:S(2)}, u32[]{:S(2)}) collective-permute-start(f32[2,8,128,128]{3,2,1,0:T(8,128)} %collective-permute-done.8.refs_3_.refs_5_), channel_id=1, source_target_pairs={{1,0},{0,1},{3,2},{2,3},{5,4},{4,5},{7,6},{6,7},{9,8},{8,9},{11,10... | collective-permute-start | bytes 3145736 | tf_op jit(solution)/shard_map/ppermute | solution.py:405
  109.1 6.5 %collective-permute-start.14 = (f32[2,8,128,128]{3,2,1,0:T(8,128)}, f32[2,8,128,128]{3,2,1,0:T(8,128)}, u32[]{:S(2)}, u32[]{:S(2)}) collective-permute-start(f32[2,8,128,128]{3,2,1,0:T(8,128)} %collective-permute-done.7.refs_4_.refs_6_), channel_id=1, source_target_pairs={{1,0},{0,1},{3,2},{2,3},{5,4},{4,5},{7,6},{6,7},{9,8},{8,9},{11,10... | collective-permute-start | bytes 3145736 | tf_op jit(solution)/shard_map/ppermute | solution.py:405
  109.1 3.5 %copy-start.7 = (f32[2,8,128,128]{3,2,1,0:T(8,128)}, f32[2,8,128,128]{3,2,1,0:T(8,128)S(1)}, u32[]{:S(2)}) copy-start(f32[2,8,128,128]{3,2,1,0:T(8,128)S(1)} %collective-permute-done.12.refs_5_.refs_8_) | copy-start | bytes 3145732
  109.1 25.9 %collective-permute-start.9 = (f32[2,8,128,128]{3,2,1,0:T(8,128)}, f32[2,8,128,128]{3,2,1,0:T(8,128)}, u32[]{:S(2)}, u32[]{:S(2)}) collective-permute-start(f32[2,8,128,128]{3,2,1,0:T(8,128)} %collective-permute-done.7.refs_4_.refs_6_), channel_id=1, source_target_pairs={{4,0},{5,1},{6,2},{7,3},{0,4},{1,5},{2,6},{3,7},{12,8},{13,9},{14,... | collective-permute-start | bytes 3145736 | tf_op jit(solution)/shard_map/ppermute | solution.py:405
  110.5 5.1 %copy-start.4 = (bf16[256,256]{1,0:T(8,128)(2,1)S(1)}, bf16[256,256]{1,0:T(8,128)(2,1)}, u32[]{:S(2)}) copy-start(bf16[256,256]{1,0:T(8,128)(2,1)} %constant.120.clone.right_ref) | copy-start | bytes 393220
  110.5 5.1 %copy-start.5 = (bf16[256,256]{1,0:T(8,128)(2,1)S(1)}, bf16[256,256]{1,0:T(8,128)(2,1)}, u32[]{:S(2)}) copy-start(bf16[256,256]{1,0:T(8,128)(2,1)} %constant.119.clone.left_ref) | copy-start | bytes 393220
  112.6 9.7 %copy-start = (f32[4,8,128,128]{3,2,1,0:T(8,128)}, f32[4,8,128,128]{3,2,1,0:T(8,128)S(1)}, u32[]{:S(2)}) copy-start(f32[4,8,128,128]{3,2,1,0:T(8,128)S(1)} %broadcast_select_fusion.1.refs_0_) | copy-start | bytes 6291460
  112.6 22.4 %copy-start.13 = (s32[16]{0:T(128)S(1)}, s32[16]{0:T(128)}, u32[]{:S(2)}) copy-start(s32[16]{0:T(128)} %constant.121.clone) | copy-start | bytes 196
  112.7 22.4 %copy-start.12 = (bf16[16,8,128]{2,1,0:T(8,128)(2,1)S(1)}, bf16[16,8,128]{2,1,0:T(8,128)(2,1)}, u32[]{:S(2)}) copy-start(bf16[16,8,128]{2,1,0:T(8,128)(2,1)} %constant.127.clone.1) | copy-start | bytes 98308
  112.7 23.0 %copy-start.11 = (bf16[16,8,128]{2,1,0:T(8,128)(2,1)S(1)}, bf16[16,8,128]{2,1,0:T(8,128)(2,1)}, u32[]{:S(2)}) copy-start(bf16[16,8,128]{2,1,0:T(8,128)(2,1)} %constant.126.clone.1) | copy-start | bytes 98308
  122.3 1.6 copy-start.3
  135.0 2.9 collective-permute-start.15
  158.4 9.0 %copy-start.1 = (f32[4,8,128,128]{3,2,1,0:T(8,128)S(1)}, f32[4,8,128,128]{3,2,1,0:T(8,128)}, u32[]{:S(2)}) copy-start(f32[4,8,128,128]{3,2,1,0:T(8,128)} %copy-done) | copy-start | bytes 6291460
  158.4 24.9 %collective-permute-start.17 = (f32[4,8,128,128]{3,2,1,0:T(8,128)S(1)}, f32[4,8,128,128]{3,2,1,0:T(8,128)S(1)}, u32[]{:S(2)}, u32[]{:S(2)}) collective-permute-start(f32[4,8,128,128]{3,2,1,0:T(8,128)S(1)} %get-tuple-element.87), channel_id=1, source_target_pairs={{0,17},{1,0},{2,19},{3,2},{4,21},{5,4},{6,23},{7,6},{8,25},{9,8},{... | collective-permute-start | bytes 6291464 | tf_op jit(solution)/shard_map/ppermute | solution.py:419
  159.7 27.9 %collective-permute-start.16 = (f32[4,8,128,128]{3,2,1,0:T(8,128)S(1)}, f32[4,8,128,128]{3,2,1,0:T(8,128)S(1)}, u32[]{:S(2)}, u32[]{:S(2)}) collective-permute-start(f32[4,8,128,128]{3,2,1,0:T(8,128)S(1)} %get-tuple-element.86), channel_id=1, source_target_pairs={{2,0},{0,2},{6,4},{4,6},{10,8},{8,10},{14,12},{12,14},{18,16},{16,... | collective-permute-start | bytes 6291464 | tf_op jit(solution)/shard_map/ppermute | solution.py:409
  163.1 2.7 collective-permute-start.18
  166.0 25.3 %collective-permute-start.22 = (f32[2,8,128,128]{3,2,1,0:T(8,128)S(1)}, f32[2,8,128,128]{3,2,1,0:T(8,128)S(1)}, u32[]{:S(2)}, u32[]{:S(2)}) collective-permute-start(f32[2,8,128,128]{3,2,1,0:T(8,128)S(1)} %add.162), channel_id=1, source_target_pairs={{4,0},{5,1},{6,2},{7,3},{0,4},{1,5},{2,6},{3,7},{12,8},{13,9},{14,... | collective-permute-start | bytes 3145736 | tf_op jit(solution)/shard_map/ppermute | solution.py:405
  167.4 1.9 copy-start.2
  187.7 4.1 %collective-permute-start.20 = (f32[2,8,128,128]{3,2,1,0:T(8,128)S(1)}, f32[2,8,128,128]{3,2,1,0:T(8,128)S(1)}, u32[]{:S(2)}, u32[]{:S(2)}) collective-permute-start(f32[2,8,128,128]{3,2,1,0:T(8,128)S(1)} %get-tuple-element.111), channel_id=1, source_target_pairs={{1,0},{0,1},{3,2},{2,3},{5,4},{4,5},{7,6},{6,7},{9,8},{8,9},{11,10... | collective-permute-start | bytes 3145736 | tf_op jit(solution)/shard_map/ppermute | solution.py:405
  187.7 8.7 %collective-permute-start.19 = (f32[2,8,128,128]{3,2,1,0:T(8,128)S(1)}, f32[2,8,128,128]{3,2,1,0:T(8,128)S(1)}, u32[]{:S(2)}, u32[]{:S(2)}) collective-permute-start(f32[2,8,128,128]{3,2,1,0:T(8,128)S(1)} %get-tuple-element.109), channel_id=1, source_target_pairs={{1,0},{0,1},{3,2},{2,3},{5,4},{4,5},{7,6},{6,7},{9,8},{8,9},{11,10... | collective-permute-start | bytes 3145736 | tf_op jit(solution)/shard_map/ppermute | solution.py:405
  188.2 6.6 %collective-permute-start.23 = (f32[2,8,128,128]{3,2,1,0:T(8,128)S(1)}, f32[2,8,128,128]{3,2,1,0:T(8,128)S(1)}, u32[]{:S(2)}, u32[]{:S(2)}) collective-permute-start(f32[2,8,128,128]{3,2,1,0:T(8,128)S(1)} %get-tuple-element.114), channel_id=1, source_target_pairs={{1,0},{0,1},{3,2},{2,3},{5,4},{4,5},{7,6},{6,7},{9,8},{8,9},{11,10... | collective-permute-start | bytes 3145736 | tf_op jit(solution)/shard_map/ppermute | solution.py:405
  188.2 52.6 %collective-permute-start.26 = (f32[4,8,128,128]{3,2,1,0:T(8,128)S(1)}, f32[4,8,128,128]{3,2,1,0:T(8,128)S(1)}, u32[]{:S(2)}, u32[]{:S(2)}) collective-permute-start(f32[4,8,128,128]{3,2,1,0:T(8,128)S(1)} %get-tuple-element.117), channel_id=1, source_target_pairs={{0,17},{1,0},{2,19},{3,2},{4,21},{5,4},{6,23},{7,6},{8,25},{9,8},{... | collective-permute-start | bytes 6291464 | tf_op jit(solution)/shard_map/ppermute | solution.py:419
  191.3 49.5 %collective-permute-start.27 = (f32[4,8,128,128]{3,2,1,0:T(8,128)S(1)}, f32[4,8,128,128]{3,2,1,0:T(8,128)S(1)}, u32[]{:S(2)}, u32[]{:S(2)}) collective-permute-start(f32[4,8,128,128]{3,2,1,0:T(8,128)S(1)} %select_add_fusion), channel_id=1, source_target_pairs={{2,0},{3,1},{0,2},{1,3},{6,4},{7,5},{4,6},{5,7},{10,8},{11,9},{8,1... | collective-permute-start | bytes 6291464 | tf_op jit(solution)/shard_map/ppermute | solution.py:405
  191.8 49.0 %collective-permute-start.25 = (f32[4,8,128,128]{3,2,1,0:T(8,128)S(1)}, f32[4,8,128,128]{3,2,1,0:T(8,128)S(1)}, u32[]{:S(2)}, u32[]{:S(2)}) collective-permute-start(f32[4,8,128,128]{3,2,1,0:T(8,128)S(1)} %get-tuple-element.136), channel_id=1, source_target_pairs={{0,16},{2,18},{4,20},{6,22},{8,24},{10,26},{12,28},{14,30},{16,0},... | collective-permute-start | bytes 6291464 | tf_op jit(solution)/shard_map/ppermute | solution.py:419
  194.8 43.3 %collective-permute-start.21 = (f32[2,8,128,128]{3,2,1,0:T(8,128)S(1)}, f32[2,8,128,128]{3,2,1,0:T(8,128)S(1)}, u32[]{:S(2)}, u32[]{:S(2)}) collective-permute-start(f32[2,8,128,128]{3,2,1,0:T(8,128)S(1)} %add.164), channel_id=1, source_target_pairs={{4,0},{5,1},{6,2},{7,3},{0,4},{1,5},{2,6},{3,7},{12,8},{13,9},{14,... | collective-permute-start | bytes 3145736 | tf_op jit(solution)/shard_map/ppermute | solution.py:405
  196.4 44.4 %collective-permute-start.24 = (f32[2,8,128,128]{3,2,1,0:T(8,128)S(1)}, f32[2,8,128,128]{3,2,1,0:T(8,128)S(1)}, u32[]{:S(2)}, u32[]{:S(2)}) collective-permute-start(f32[2,8,128,128]{3,2,1,0:T(8,128)S(1)} %add_add_fusion), channel_id=1, source_target_pairs={{8,0},{9,1},{10,2},{11,3},{12,4},{13,5},{14,6},{15,7},{0,8},{1,9},... | collective-permute-start | bytes 3145736 | tf_op jit(solution)/shard_map/ppermute | solution.py:405
  243.1 22.9 %collective-permute-start.28 = (f32[2,8,128,128]{3,2,1,0:T(8,128)S(1)}, f32[2,8,128,128]{3,2,1,0:T(8,128)}, u32[]{:S(2)}, u32[]{:S(2)}) collective-permute-start(f32[2,8,128,128]{3,2,1,0:T(8,128)S(1)} %get-tuple-element.158), channel_id=1, source_target_pairs={{2,0},{3,1},{0,2},{1,3},{6,4},{7,5},{4,6},{5,7},{10,8},{11,9},{8,1... | collective-permute-start | bytes 3145736 | tf_op jit(solution)/shard_map/ppermute | solution.py:405
  244.1 35.0 %collective-permute-start.29 = (f32[8,128,128]{2,1,0:T(8,128)}, f32[8,128,128]{2,1,0:T(8,128)}, u32[]{:S(2)}, u32[]{:S(2)}) collective-permute-start(f32[8,128,128]{2,1,0:T(8,128)} %get-tuple-element.128), channel_id=1, source_target_pairs={{8,0},{9,1},{10,2},{11,3},{12,4},{13,5},{14,6},{15,7},{0,8},{1,9},... | collective-permute-start | bytes 1572872 | tf_op jit(solution)/shard_map/ppermute | solution.py:405
  247.4 42.6 %collective-permute-start.30 = (f32[8,128,128]{2,1,0:T(8,128)}, f32[8,128,128]{2,1,0:T(8,128)}, u32[]{:S(2)}, u32[]{:S(2)}) collective-permute-start(f32[8,128,128]{2,1,0:T(8,128)} %get-tuple-element.129), channel_id=1, source_target_pairs={{12,0},{13,1},{14,2},{15,3},{8,4},{9,5},{10,6},{11,7},{4,8},{5,9},... | collective-permute-start | bytes 1572872 | tf_op jit(solution)/shard_map/ppermute | solution.py:405
  249.3 40.8 %collective-permute-start.31 = (f32[8,128,128]{2,1,0:T(8,128)S(1)}, f32[8,128,128]{2,1,0:T(8,128)}, u32[]{:S(2)}, u32[]{:S(2)}) collective-permute-start(f32[8,128,128]{2,1,0:T(8,128)S(1)} %get-tuple-element.130), channel_id=1, source_target_pairs={{4,0},{5,1},{6,2},{7,3},{0,4},{1,5},{2,6},{3,7},{12,8},{13,9},{14,... | collective-permute-start | bytes 1572872 | tf_op jit(solution)/shard_map/ppermute | solution.py:405

commit v11 on v10

--- a/solution.py
+++ b/solution.py
@@ -210,7 +210,7 @@
     middle_in = pltpu.make_async_copy(early_ref, middle_ref, middle_sems.at[0])
     middle_in.start()
 
-    @pl.loop(0, count, unroll=5)
+    @pl.loop(0, count, unroll=10)
     def _(k):
         pltpu.make_async_copy(pieces[names[0]].at[0], own_ref.at[k], in_sems.at[0, k]).wait()
         pltpu.make_async_copy(pieces[names[0]].at[0], part_ref.at[k], in_sems.at[1, k]).wait()
@@ -225,7 +225,7 @@
             out_ref[pl.ds(r + 1, length, stride=rows), :] = block[:, length:]
 
     middle_in.wait()
-    group = 32
+    group = 64
     scale = coulomb_scale / float(length**3)
 
     @pl.loop(0, length // group)
@@ -250,7 +250,7 @@
     middle_out = pltpu.make_async_copy(middle_ref, early_out, middle_sems.at[1])
     middle_out.start()
 
-    @pl.loop(0, count, unroll=5)
+    @pl.loop(0, count, unroll=10)
     def _(k):
         in_ref = field_ref.at[k]
         for r in range(0, rows, 2):

time: 293 us -> 292 us (level)
  no operation moved by 1% of the time
where the time goes in v11:
time: 292 us
  waiting for transfers between devices  200 us (68%)
  starting transfers between devices  35.9 us (12%)
  Pallas kernels  33.2 us (11%)
  other arithmetic  11.6 us (4%)
  local copies, waits for them, and re-layouts  10.6 us (4%)
    ppermute x24, waiting for transfers between devices, swap(): return lax.ppermute(block, 'slab', [(i ^ mask, i) for i in range(slabs)])  188 us
    ppermute x24, starting transfers between devices, swap(): return lax.ppermute(block, 'slab', [(i ^ mask, i) for i in range(slabs)])  21.8 us
    pallas_call x1, Pallas kernels, late_part(): pl.pallas_call(functools.partial(late_kernel, steps, groups), in_specs=[p...  19.6 us
    ppermute x6, starting transfers between devices, across(): return lax.ppermute(block, ('band', 'slab'), route)  8.2 us
    ppermute x6, waiting for transfers between devices, across(): return lax.ppermute(block, ('band', 'slab'), route)  7.15 us
    pallas_call x1, Pallas kernels, scatter_part(): pl.pallas_call(functools.partial(scatter_kernel, steps), grid=(len(steps)...  6.87 us
    pallas_call x1, Pallas kernels, gather_part(): pl.pallas_call(functools.partial(gather_kernel, steps), grid=(count,), in...  6.73 us
  transfers between devices with their start and end apart: 32, of which 18 were waited for; matrix products, arithmetic and copies ran while one was open for 4% of the time, Pallas kernels for 5%

profile of v11, /device:TPU:10, one launch (start us, length us, event | category | flops | bytes accessed | tf_op | source)
XLA Modules:
  0.0 291.8 jit_solution(3301248297953436092)
XLA Ops:
  0.6 1.4 dynamic-slice_bitcast_fusion
  2.2 0.9 dynamic-slice_bitcast_fusion.3
  3.6 2.6 collective-permute-start.1
  7.1 1.3 dynamic-slice_bitcast_fusion.1
  8.4 19.7 %collective-permute-done = f32[2,8,128,128]{3,2,1,0:T(8,128)} collective-permute-done((f32[2,8,128,128]{3,2,1,0:T(8,128)S(1)}, f32[2,8,128,128]{3,2,1,0:T(8,128)}, u32[]{:S(2)}, u32[]{:S(2)}) %collective-permute-start) | collective-permute-done | bytes 1048608 | tf_op jit(solution)/shard_map/ppermute | solution.py:405
  28.1 1.3 constant_dynamic-slice_fusion
  29.6 1.2 collective-permute-done.3
  30.7 20.0 %collective-permute-done.2 = f32[8,128,128]{2,1,0:T(8,128)S(1)} collective-permute-done((f32[8,128,128]{2,1,0:T(8,128)}, f32[8,128,128]{2,1,0:T(8,128)S(1)}, u32[]{:S(2)}, u32[]{:S(2)}) %collective-permute-start.2) | collective-permute-done | bytes 524320 | tf_op jit(solution)/shard_map/ppermute | solution.py:405
  51.0 0.6 copy-done.9
  51.6 3.4 %collective-permute-start.5 = (f32[4,8,128,128]{3,2,1,0:T(8,128)S(1)}, f32[4,8,128,128]{3,2,1,0:T(8,128)}, u32[]{:S(2)}, u32[]{:S(2)}) collective-permute-start(f32[4,8,128,128]{3,2,1,0:T(8,128)S(1)} %pad_maximum_fusion), channel_id=1, source_target_pairs={{16,0},{18,2},{20,4},{22,6},{24,8},{26,10},{28,12},{30,14},{0,16},... | collective-permute-start | bytes 6291464 | tf_op jit(solution)/shard_map/ppermute | solution.py:419
  55.0 1.6 collective-permute-start.4
  56.6 3.8 %collective-permute-start.8 = (f32[2,8,128,128]{3,2,1,0:T(8,128)S(1)}, f32[2,8,128,128]{3,2,1,0:T(8,128)}, u32[]{:S(2)}, u32[]{:S(2)}) collective-permute-start(f32[2,8,128,128]{3,2,1,0:T(8,128)S(1)} %get-tuple-element.76.refs_2_.refs_4_), channel_id=1, source_target_pairs={{4,0},{5,1},{6,2},{7,3},{0,4},{1,5},{2,6},{3,7},{12,8},{13,9},{14,... | collective-permute-start | bytes 3145736 | tf_op jit(solution)/shard_map/ppermute | solution.py:405
  60.4 41.4 %collective-permute-done.7.refs_4_.refs_6_ = f32[2,8,128,128]{3,2,1,0:T(8,128)} collective-permute-done((f32[2,8,128,128]{3,2,1,0:T(8,128)S(1)}, f32[2,8,128,128]{3,2,1,0:T(8,128)}, u32[]{:S(2)}, u32[]{:S(2)}) %collective-permute-start.7) | collective-permute-done | bytes 1048608 | tf_op jit(solution)/shard_map/ppermute | solution.py:405
  101.8 4.2 %collective-permute-done.8.refs_3_.refs_5_ = f32[2,8,128,128]{3,2,1,0:T(8,128)} collective-permute-done((f32[2,8,128,128]{3,2,1,0:T(8,128)S(1)}, f32[2,8,128,128]{3,2,1,0:T(8,128)}, u32[]{:S(2)}, u32[]{:S(2)}) %collective-permute-start.8) | collective-permute-done | bytes 1048608 | tf_op jit(solution)/shard_map/ppermute | solution.py:405
  105.9 2.4 collective-permute-start.10
  108.5 0.6 collective-permute-start.13
  109.1 1.4 collective-permute-start.9
  110.5 2.1 broadcast_select_fusion.1.refs_0_
  112.7 1.4 collective-permute-done.13.refs_6_.refs_9_
  114.1 1.5 collective-permute-done.14.refs_7_.refs_10_
  115.6 6.7 %shard_map.86.early_ref = f32[128,48,128]{2,1,0:T(8,128)S(1)} custom-call(bf16[256,256]{1,0:T(8,128)(2,1)S(1)} %copy-done.4, bf16[256,256]{1,0:T(8,128)(2,1)S(1)} %copy-done.5, f32[4,8,128,128]{3,2,1,0:T(8,128)S(1)} %broadcast_select_fusion.1.refs_0_, f32[4,8,128,128]{3,2,1,0:T(8,128)} %copy-done.6, ...), custom_call_target="tpu_custom_call" | custom-call | flops 1610612736 | bytes 9437184 | tf_op jit(solution)/shard_map/pallas_call | solution.py:328
  122.4 1.6 copy-done.3
  124.0 11.1 %collective-permute-done.9.refs_7_ = f32[2,8,128,128]{3,2,1,0:T(8,128)} collective-permute-done((f32[2,8,128,128]{3,2,1,0:T(8,128)}, f32[2,8,128,128]{3,2,1,0:T(8,128)}, u32[]{:S(2)}, u32[]{:S(2)}) %collective-permute-start.9) | collective-permute-done | bytes 1048608 | tf_op jit(solution)/shard_map/ppermute | solution.py:405
  136.6 1.3 collective-permute-done.15.refs_11_
  137.9 19.6 %shard_map.87 = (f32[128,48,128]{2,1,0:T(8,128)}, f32[4,8,128,128]{3,2,1,0:T(8,128)S(1)}, f32[4,8,128,128]{3,2,1,0:T(8,128)S(1)}, f32[4,8,128,128]{3,2,1,0:T(8,1...) custom-call(bf16[256,256]{1,0:T(8,128)(2,1)S(1)} %copy-done.4, ...), custom_call_target="tpu_custom_call" | custom-call | flops 10737418240 | bytes 33554432 | tf_op jit(solution)/shard_map/pallas_call | solution.py:347
  157.5 1.3 collective-permute-start.17
  158.8 3.4 %collective-permute-start.16 = (f32[4,8,128,128]{3,2,1,0:T(8,128)S(1)}, f32[4,8,128,128]{3,2,1,0:T(8,128)S(1)}, u32[]{:S(2)}, u32[]{:S(2)}) collective-permute-start(f32[4,8,128,128]{3,2,1,0:T(8,128)S(1)} %get-tuple-element.86), channel_id=1, source_target_pairs={{2,0},{0,2},{6,4},{4,6},{10,8},{8,10},{14,12},{12,14},{18,16},{16,... | collective-permute-start | bytes 6291464 | tf_op jit(solution)/shard_map/ppermute | solution.py:409
  162.3 2.6 collective-permute-done.18
  165.1 1.4 collective-permute-start.22
  166.5 1.9 copy-done.2
  168.4 6.9 %shard_map.88 = (f32[4,8,128,128]{3,2,1,0:T(8,128)S(1)}, f32[4,8,128,128]{3,2,1,0:T(8,128)S(1)}, f32[2,8,128,128]{3,2,1,0:T(8,128)S(1)}, f32[2,8,128,128]{3,2,1,...) custom-call(bf16[256,256]{1,0:T(8,128)(2,1)S(1)} %copy-done.4, ...), custom_call_target="tpu_custom_call", output_to_operand_aliasing={{0}: (11, {}), {1}: (12, {}), {2}: (13, {}), {3}: (14, {}),... | custom-call | flops 1610612736 | bytes 15728640 | tf_op jit(solution)/shard_map/pallas_call | solution.py:374
  175.2 7.1 %collective-permute-done.17 = f32[4,8,128,128]{3,2,1,0:T(8,128)S(1)} collective-permute-done((f32[4,8,128,128]{3,2,1,0:T(8,128)S(1)}, f32[4,8,128,128]{3,2,1,0:T(8,128)S(1)}, u32[]{:S(2)}, u32[]{:S(2)}) %collective-permute-start.17) | collective-permute-done | bytes 2097184 | tf_op jit(solution)/shard_map/ppermute | solution.py:419
  182.7 4.1 %collective-permute-done.16 = f32[4,8,128,128]{3,2,1,0:T(8,128)S(1)} collective-permute-done((f32[4,8,128,128]{3,2,1,0:T(8,128)S(1)}, f32[4,8,128,128]{3,2,1,0:T(8,128)S(1)}, u32[]{:S(2)}, u32[]{:S(2)}) %collective-permute-start.16) | collective-permute-done | bytes 2097184 | tf_op jit(solution)/shard_map/ppermute | solution.py:409
  187.3 0.7 collective-permute-start.26
  188.5 1.9 collective-permute-done.22
  190.9 2.6 collective-permute-start.25
  193.7 1.4 collective-permute-start.21
  195.6 41.7 %collective-permute-done.21 = f32[2,8,128,128]{3,2,1,0:T(8,128)S(1)} collective-permute-done((f32[2,8,128,128]{3,2,1,0:T(8,128)S(1)}, f32[2,8,128,128]{3,2,1,0:T(8,128)S(1)}, u32[]{:S(2)}, u32[]{:S(2)}) %collective-permute-start.21) | collective-permute-done | bytes 1048608 | tf_op jit(solution)/shard_map/ppermute | solution.py:405
  237.4 2.5 collective-permute-done.24
  239.9 1.8 add_bitcast_fusion
  242.2 1.0 collective-permute-start.28
  243.1 3.3 %collective-permute-start.29 = (f32[8,128,128]{2,1,0:T(8,128)}, f32[8,128,128]{2,1,0:T(8,128)}, u32[]{:S(2)}, u32[]{:S(2)}) collective-permute-start(f32[8,128,128]{2,1,0:T(8,128)} %get-tuple-element.128), channel_id=1, source_target_pairs={{8,0},{9,1},{10,2},{11,3},{12,4},{13,5},{14,6},{15,7},{0,8},{1,9},... | collective-permute-start | bytes 1572872 | tf_op jit(solution)/shard_map/ppermute | solution.py:405
  246.5 1.9 collective-permute-start.30
  248.5 16.9 %collective-permute-done.28 = f32[2,8,128,128]{3,2,1,0:T(8,128)} collective-permute-done((f32[2,8,128,128]{3,2,1,0:T(8,128)S(1)}, f32[2,8,128,128]{3,2,1,0:T(8,128)}, u32[]{:S(2)}, u32[]{:S(2)}) %collective-permute-start.28) | collective-permute-done | bytes 1048608 | tf_op jit(solution)/shard_map/ppermute | solution.py:405
  265.3 2.9 bitcast_select_fusion
  268.2 10.2 %collective-permute-done.29 = f32[8,128,128]{2,1,0:T(8,128)} collective-permute-done((f32[8,128,128]{2,1,0:T(8,128)}, f32[8,128,128]{2,1,0:T(8,128)}, u32[]{:S(2)}, u32[]{:S(2)}) %collective-permute-start.29) | collective-permute-done | bytes 524320 | tf_op jit(solution)/shard_map/ppermute | solution.py:405
  278.4 10.9 %collective-permute-done.30 = f32[8,128,128]{2,1,0:T(8,128)} collective-permute-done((f32[8,128,128]{2,1,0:T(8,128)}, f32[8,128,128]{2,1,0:T(8,128)}, u32[]{:S(2)}, u32[]{:S(2)}) %collective-permute-start.30) | collective-permute-done | bytes 524320 | tf_op jit(solution)/shard_map/ppermute | solution.py:405
  289.3 2.5 select_add_fusion.1
  (81 shorter events, 6.9 us)
Async XLA Ops:
  0.6 1.5 copy-start.10
  3.0 25.0 %collective-permute-start = (f32[2,8,128,128]{3,2,1,0:T(8,128)S(1)}, f32[2,8,128,128]{3,2,1,0:T(8,128)}, u32[]{:S(2)}, u32[]{:S(2)}) collective-permute-start(f32[2,8,128,128]{3,2,1,0:T(8,128)S(1)} %dynamic-slice_bitcast_fusion), channel_id=1, source_target_pairs={{2,0},{3,1},{0,2},{1,3},{6,4},{7,5},{4,6},{5,7},{10,8},{11,9},{8,1... | collective-permute-start | bytes 3145736 | tf_op jit(solution)/shard_map/ppermute | solution.py:405
  3.6 26.0 %collective-permute-start.1 = (f32[8,128,128]{2,1,0:T(8,128)S(1)}, f32[8,128,128]{2,1,0:T(8,128)S(1)}, u32[]{:S(2)}, u32[]{:S(2)}) collective-permute-start(f32[8,128,128]{2,1,0:T(8,128)S(1)} %get-tuple-element.69), channel_id=1, source_target_pairs={{8,0},{9,1},{10,2},{11,3},{12,4},{13,5},{14,6},{15,7},{0,8},{1,9},... | collective-permute-start | bytes 1572872 | tf_op jit(solution)/shard_map/ppermute | solution.py:405
  6.2 24.6 %collective-permute-start.3 = (f32[8,128,128]{2,1,0:T(8,128)}, f32[8,128,128]{2,1,0:T(8,128)S(1)}, u32[]{:S(2)}, u32[]{:S(2)}) collective-permute-start(f32[8,128,128]{2,1,0:T(8,128)} %get-tuple-element.71), channel_id=1, source_target_pairs={{4,0},{5,1},{6,2},{7,3},{0,4},{1,5},{2,6},{3,7},{12,8},{13,9},{14,... | collective-permute-start | bytes 1572872 | tf_op jit(solution)/shard_map/ppermute | solution.py:405
  6.6 44.1 %collective-permute-start.2 = (f32[8,128,128]{2,1,0:T(8,128)}, f32[8,128,128]{2,1,0:T(8,128)S(1)}, u32[]{:S(2)}, u32[]{:S(2)}) collective-permute-start(f32[8,128,128]{2,1,0:T(8,128)} %get-tuple-element.71), channel_id=1, source_target_pairs={{12,0},{13,1},{14,2},{15,3},{8,4},{9,5},{10,6},{11,7},{4,8},{5,9},... | collective-permute-start | bytes 1572872 | tf_op jit(solution)/shard_map/ppermute | solution.py:405
  30.7 20.3 %copy-start.8 = (f32[8,128,128]{2,1,0:T(8,128)}, f32[8,128,128]{2,1,0:T(8,128)S(1)}, u32[]{:S(2)}) copy-start(f32[8,128,128]{2,1,0:T(8,128)S(1)} %collective-permute-done.3) | copy-start | bytes 1572868
  50.8 0.8 copy-start.9
  51.6 54.4 %collective-permute-start.6 = (f32[4,8,128,128]{3,2,1,0:T(8,128)S(1)}, f32[4,8,128,128]{3,2,1,0:T(8,128)S(1)}, u32[]{:S(2)}, u32[]{:S(2)}) collective-permute-start(f32[4,8,128,128]{3,2,1,0:T(8,128)S(1)} %pad_maximum_fusion), channel_id=1, source_target_pairs={{17,0},{0,1},{19,2},{2,3},{21,4},{4,5},{23,6},{6,7},{25,8},{8,9},{... | collective-permute-start | bytes 6291464 | tf_op jit(solution)/shard_map/ppermute | solution.py:419
  51.6 54.3 %collective-permute-start.5 = (f32[4,8,128,128]{3,2,1,0:T(8,128)S(1)}, f32[4,8,128,128]{3,2,1,0:T(8,128)}, u32[]{:S(2)}, u32[]{:S(2)}) collective-permute-start(f32[4,8,128,128]{3,2,1,0:T(8,128)S(1)} %pad_maximum_fusion), channel_id=1, source_target_pairs={{16,0},{18,2},{20,4},{22,6},{24,8},{26,10},{28,12},{30,14},{0,16},... | collective-permute-start | bytes 6291464 | tf_op jit(solution)/shard_map/ppermute | solution.py:419
  55.0 50.9 %collective-permute-start.4 = (f32[4,8,128,128]{3,2,1,0:T(8,128)S(1)}, f32[4,8,128,128]{3,2,1,0:T(8,128)}, u32[]{:S(2)}, u32[]{:S(2)}) collective-permute-start(f32[4,8,128,128]{3,2,1,0:T(8,128)S(1)} %pad_maximum_fusion), channel_id=1, source_target_pairs={{2,0},{3,1},{0,2},{1,3},{6,4},{7,5},{4,6},{5,7},{10,8},{11,9},{8,1... | collective-permute-start | bytes 6291464 | tf_op jit(solution)/shard_map/ppermute | solution.py:405
  56.6 45.2 %collective-permute-start.7 = (f32[2,8,128,128]{3,2,1,0:T(8,128)S(1)}, f32[2,8,128,128]{3,2,1,0:T(8,128)}, u32[]{:S(2)}, u32[]{:S(2)}) collective-permute-start(f32[2,8,128,128]{3,2,1,0:T(8,128)S(1)} %get-tuple-element.75), channel_id=1, source_target_pairs={{8,0},{9,1},{10,2},{11,3},{12,4},{13,5},{14,6},{15,7},{0,8},{1,9},... | collective-permute-start | bytes 3145736 | tf_op jit(solution)/shard_map/ppermute | solution.py:405
  56.6 49.3 %collective-permute-start.8 = (f32[2,8,128,128]{3,2,1,0:T(8,128)S(1)}, f32[2,8,128,128]{3,2,1,0:T(8,128)}, u32[]{:S(2)}, u32[]{:S(2)}) collective-permute-start(f32[2,8,128,128]{3,2,1,0:T(8,128)S(1)} %get-tuple-element.76.refs_2_.refs_4_), channel_id=1, source_target_pairs={{4,0},{5,1},{6,2},{7,3},{0,4},{1,5},{2,6},{3,7},{12,8},{13,9},{14,... | collective-permute-start | bytes 3145736 | tf_op jit(solution)/shard_map/ppermute | solution.py:405
  101.8 7.3 %collective-permute-start.12 = (f32[2,8,128,128]{3,2,1,0:T(8,128)S(1)}, f32[2,8,128,128]{3,2,1,0:T(8,128)S(1)}, u32[]{:S(2)}, u32[]{:S(2)}) collective-permute-start(f32[2,8,128,128]{3,2,1,0:T(8,128)S(1)} %get-tuple-element.76.refs_2_.refs_4_), channel_id=1, source_target_pairs={{1,0},{0,1},{3,2},{2,3},{5,4},{4,5},{7,6},{6,7},{9,8},{8,9},{11,10... | collective-permute-start | bytes 3145736 | tf_op jit(solution)/shard_map/ppermute | solution.py:405
  105.9 3.2 %copy-start.6 = (f32[4,8,128,128]{3,2,1,0:T(8,128)}, f32[4,8,128,128]{3,2,1,0:T(8,128)S(1)}, u32[]{:S(2)}) copy-start(f32[4,8,128,128]{3,2,1,0:T(8,128)S(1)} %collective-permute-done.6.refs_1_.refs_2_) | copy-start | bytes 6291460
  105.9 29.1 %collective-permute-start.10 = (f32[4,8,128,128]{3,2,1,0:T(8,128)}, f32[4,8,128,128]{3,2,1,0:T(8,128)}, u32[]{:S(2)}, u32[]{:S(2)}) collective-permute-start(f32[4,8,128,128]{3,2,1,0:T(8,128)} %collective-permute-done.5), channel_id=1, source_target_pairs={{2,0},{0,2},{6,4},{4,6},{10,8},{8,10},{14,12},{12,14},{18,16},{16,... | collective-permute-start | bytes 6291464 | tf_op jit(solution)/shard_map/ppermute | solution.py:409
  108.4 26.6 %collective-permute-start.11 = (f32[4,8,128,128]{3,2,1,0:T(8,128)}, f32[4,8,128,128]{3,2,1,0:T(8,128)}, u32[]{:S(2)}, u32[]{:S(2)}) collective-permute-start(f32[4,8,128,128]{3,2,1,0:T(8,128)} %collective-permute-done.4.home_ref), channel_id=1, source_target_pairs={{17,0},{0,1},{19,2},{2,3},{21,4},{4,5},{23,6},{6,7},{25,8},{8,9},{... | collective-permute-start | bytes 6291464 | tf_op jit(solution)/shard_map/ppermute | solution.py:419
  108.5 5.6 %collective-permute-start.13 = (f32[2,8,128,128]{3,2,1,0:T(8,128)}, f32[2,8,128,128]{3,2,1,0:T(8,128)}, u32[]{:S(2)}, u32[]{:S(2)}) collective-permute-start(f32[2,8,128,128]{3,2,1,0:T(8,128)} %collective-permute-done.8.refs_3_.refs_5_), channel_id=1, source_target_pairs={{1,0},{0,1},{3,2},{2,3},{5,4},{4,5},{7,6},{6,7},{9,8},{8,9},{11,10... | collective-permute-start | bytes 3145736 | tf_op jit(solution)/shard_map/ppermute | solution.py:405
  109.1 6.5 %collective-permute-start.14 = (f32[2,8,128,128]{3,2,1,0:T(8,128)}, f32[2,8,128,128]{3,2,1,0:T(8,128)}, u32[]{:S(2)}, u32[]{:S(2)}) collective-permute-start(f32[2,8,128,128]{3,2,1,0:T(8,128)} %collective-permute-done.7.refs_4_.refs_6_), channel_id=1, source_target_pairs={{1,0},{0,1},{3,2},{2,3},{5,4},{4,5},{7,6},{6,7},{9,8},{8,9},{11,10... | collective-permute-start | bytes 3145736 | tf_op jit(solution)/shard_map/ppermute | solution.py:405
  109.1 3.5 %copy-start.7 = (f32[2,8,128,128]{3,2,1,0:T(8,128)}, f32[2,8,128,128]{3,2,1,0:T(8,128)S(1)}, u32[]{:S(2)}) copy-start(f32[2,8,128,128]{3,2,1,0:T(8,128)S(1)} %collective-permute-done.12.refs_5_.refs_8_) | copy-start | bytes 3145732
  109.1 25.9 %collective-permute-start.9 = (f32[2,8,128,128]{3,2,1,0:T(8,128)}, f32[2,8,128,128]{3,2,1,0:T(8,128)}, u32[]{:S(2)}, u32[]{:S(2)}) collective-permute-start(f32[2,8,128,128]{3,2,1,0:T(8,128)} %collective-permute-done.7.refs_4_.refs_6_), channel_id=1, source_target_pairs={{4,0},{5,1},{6,2},{7,3},{0,4},{1,5},{2,6},{3,7},{12,8},{13,9},{14,... | collective-permute-start | bytes 3145736 | tf_op jit(solution)/shard_map/ppermute | solution.py:405
  110.5 5.1 %copy-start.4 = (bf16[256,256]{1,0:T(8,128)(2,1)S(1)}, bf16[256,256]{1,0:T(8,128)(2,1)}, u32[]{:S(2)}) copy-start(bf16[256,256]{1,0:T(8,128)(2,1)} %constant.120.clone.right_ref) | copy-start | bytes 393220
  110.5 5.1 %copy-start.5 = (bf16[256,256]{1,0:T(8,128)(2,1)S(1)}, bf16[256,256]{1,0:T(8,128)(2,1)}, u32[]{:S(2)}) copy-start(bf16[256,256]{1,0:T(8,128)(2,1)} %constant.119.clone.left_ref) | copy-start | bytes 393220
  112.6 9.7 %copy-start = (f32[4,8,128,128]{3,2,1,0:T(8,128)}, f32[4,8,128,128]{3,2,1,0:T(8,128)S(1)}, u32[]{:S(2)}) copy-start(f32[4,8,128,128]{3,2,1,0:T(8,128)S(1)} %broadcast_select_fusion.1.refs_0_) | copy-start | bytes 6291460
  112.6 22.4 %copy-start.13 = (s32[16]{0:T(128)S(1)}, s32[16]{0:T(128)}, u32[]{:S(2)}) copy-start(s32[16]{0:T(128)} %constant.121.clone) | copy-start | bytes 196
  112.7 22.4 %copy-start.12 = (bf16[16,8,128]{2,1,0:T(8,128)(2,1)S(1)}, bf16[16,8,128]{2,1,0:T(8,128)(2,1)}, u32[]{:S(2)}) copy-start(bf16[16,8,128]{2,1,0:T(8,128)(2,1)} %constant.127.clone.1) | copy-start | bytes 98308
  112.7 23.0 %copy-start.11 = (bf16[16,8,128]{2,1,0:T(8,128)(2,1)S(1)}, bf16[16,8,128]{2,1,0:T(8,128)(2,1)}, u32[]{:S(2)}) copy-start(bf16[16,8,128]{2,1,0:T(8,128)(2,1)} %constant.126.clone.1) | copy-start | bytes 98308
  122.3 1.6 copy-start.3
  135.0 2.9 collective-permute-start.15
  157.5 9.0 %copy-start.1 = (f32[4,8,128,128]{3,2,1,0:T(8,128)S(1)}, f32[4,8,128,128]{3,2,1,0:T(8,128)}, u32[]{:S(2)}) copy-start(f32[4,8,128,128]{3,2,1,0:T(8,128)} %copy-done) | copy-start | bytes 6291460
  157.5 24.9 %collective-permute-start.17 = (f32[4,8,128,128]{3,2,1,0:T(8,128)S(1)}, f32[4,8,128,128]{3,2,1,0:T(8,128)S(1)}, u32[]{:S(2)}, u32[]{:S(2)}) collective-permute-start(f32[4,8,128,128]{3,2,1,0:T(8,128)S(1)} %get-tuple-element.87), channel_id=1, source_target_pairs={{0,17},{1,0},{2,19},{3,2},{4,21},{5,4},{6,23},{7,6},{8,25},{9,8},{... | collective-permute-start | bytes 6291464 | tf_op jit(solution)/shard_map/ppermute | solution.py:419
  158.8 27.9 %collective-permute-start.16 = (f32[4,8,128,128]{3,2,1,0:T(8,128)S(1)}, f32[4,8,128,128]{3,2,1,0:T(8,128)S(1)}, u32[]{:S(2)}, u32[]{:S(2)}) collective-permute-start(f32[4,8,128,128]{3,2,1,0:T(8,128)S(1)} %get-tuple-element.86), channel_id=1, source_target_pairs={{2,0},{0,2},{6,4},{4,6},{10,8},{8,10},{14,12},{12,14},{18,16},{16,... | collective-permute-start | bytes 6291464 | tf_op jit(solution)/shard_map/ppermute | solution.py:409
  162.2 2.7 collective-permute-start.18
  165.1 25.3 %collective-permute-start.22 = (f32[2,8,128,128]{3,2,1,0:T(8,128)S(1)}, f32[2,8,128,128]{3,2,1,0:T(8,128)S(1)}, u32[]{:S(2)}, u32[]{:S(2)}) collective-permute-start(f32[2,8,128,128]{3,2,1,0:T(8,128)S(1)} %add.162), channel_id=1, source_target_pairs={{4,0},{5,1},{6,2},{7,3},{0,4},{1,5},{2,6},{3,7},{12,8},{13,9},{14,... | collective-permute-start | bytes 3145736 | tf_op jit(solution)/shard_map/ppermute | solution.py:405
  166.5 1.9 copy-start.2
  186.7 4.1 %collective-permute-start.20 = (f32[2,8,128,128]{3,2,1,0:T(8,128)S(1)}, f32[2,8,128,128]{3,2,1,0:T(8,128)S(1)}, u32[]{:S(2)}, u32[]{:S(2)}) collective-permute-start(f32[2,8,128,128]{3,2,1,0:T(8,128)S(1)} %get-tuple-element.111), channel_id=1, source_target_pairs={{1,0},{0,1},{3,2},{2,3},{5,4},{4,5},{7,6},{6,7},{9,8},{8,9},{11,10... | collective-permute-start | bytes 3145736 | tf_op jit(solution)/shard_map/ppermute | solution.py:405
  186.7 8.5 %collective-permute-start.19 = (f32[2,8,128,128]{3,2,1,0:T(8,128)S(1)}, f32[2,8,128,128]{3,2,1,0:T(8,128)S(1)}, u32[]{:S(2)}, u32[]{:S(2)}) collective-permute-start(f32[2,8,128,128]{3,2,1,0:T(8,128)S(1)} %get-tuple-element.109), channel_id=1, source_target_pairs={{1,0},{0,1},{3,2},{2,3},{5,4},{4,5},{7,6},{6,7},{9,8},{8,9},{11,10... | collective-permute-start | bytes 3145736 | tf_op jit(solution)/shard_map/ppermute | solution.py:405
  187.3 6.4 %collective-permute-start.23 = (f32[2,8,128,128]{3,2,1,0:T(8,128)S(1)}, f32[2,8,128,128]{3,2,1,0:T(8,128)S(1)}, u32[]{:S(2)}, u32[]{:S(2)}) collective-permute-start(f32[2,8,128,128]{3,2,1,0:T(8,128)S(1)} %get-tuple-element.114), channel_id=1, source_target_pairs={{1,0},{0,1},{3,2},{2,3},{5,4},{4,5},{7,6},{6,7},{9,8},{8,9},{11,10... | collective-permute-start | bytes 3145736 | tf_op jit(solution)/shard_map/ppermute | solution.py:405
  187.3 52.6 %collective-permute-start.26 = (f32[4,8,128,128]{3,2,1,0:T(8,128)S(1)}, f32[4,8,128,128]{3,2,1,0:T(8,128)S(1)}, u32[]{:S(2)}, u32[]{:S(2)}) collective-permute-start(f32[4,8,128,128]{3,2,1,0:T(8,128)S(1)} %get-tuple-element.117), channel_id=1, source_target_pairs={{0,17},{1,0},{2,19},{3,2},{4,21},{5,4},{6,23},{7,6},{8,25},{9,8},{... | collective-permute-start | bytes 6291464 | tf_op jit(solution)/shard_map/ppermute | solution.py:419
  190.3 49.5 %collective-permute-start.27 = (f32[4,8,128,128]{3,2,1,0:T(8,128)S(1)}, f32[4,8,128,128]{3,2,1,0:T(8,128)S(1)}, u32[]{:S(2)}, u32[]{:S(2)}) collective-permute-start(f32[4,8,128,128]{3,2,1,0:T(8,128)S(1)} %select_add_fusion), channel_id=1, source_target_pairs={{2,0},{3,1},{0,2},{1,3},{6,4},{7,5},{4,6},{5,7},{10,8},{11,9},{8,1... | collective-permute-start | bytes 6291464 | tf_op jit(solution)/shard_map/ppermute | solution.py:405
  190.9 49.0 %collective-permute-start.25 = (f32[4,8,128,128]{3,2,1,0:T(8,128)S(1)}, f32[4,8,128,128]{3,2,1,0:T(8,128)S(1)}, u32[]{:S(2)}, u32[]{:S(2)}) collective-permute-start(f32[4,8,128,128]{3,2,1,0:T(8,128)S(1)} %get-tuple-element.136), channel_id=1, source_target_pairs={{0,16},{2,18},{4,20},{6,22},{8,24},{10,26},{12,28},{14,30},{16,0},... | collective-permute-start | bytes 6291464 | tf_op jit(solution)/shard_map/ppermute | solution.py:419
  193.7 43.5 %collective-permute-start.21 = (f32[2,8,128,128]{3,2,1,0:T(8,128)S(1)}, f32[2,8,128,128]{3,2,1,0:T(8,128)S(1)}, u32[]{:S(2)}, u32[]{:S(2)}) collective-permute-start(f32[2,8,128,128]{3,2,1,0:T(8,128)S(1)} %add.164), channel_id=1, source_target_pairs={{4,0},{5,1},{6,2},{7,3},{0,4},{1,5},{2,6},{3,7},{12,8},{13,9},{14,... | collective-permute-start | bytes 3145736 | tf_op jit(solution)/shard_map/ppermute | solution.py:405
  195.2 44.6 %collective-permute-start.24 = (f32[2,8,128,128]{3,2,1,0:T(8,128)S(1)}, f32[2,8,128,128]{3,2,1,0:T(8,128)S(1)}, u32[]{:S(2)}, u32[]{:S(2)}) collective-permute-start(f32[2,8,128,128]{3,2,1,0:T(8,128)S(1)} %add_add_fusion), channel_id=1, source_target_pairs={{8,0},{9,1},{10,2},{11,3},{12,4},{13,5},{14,6},{15,7},{0,8},{1,9},... | collective-permute-start | bytes 3145736 | tf_op jit(solution)/shard_map/ppermute | solution.py:405
  242.2 23.2 %collective-permute-start.28 = (f32[2,8,128,128]{3,2,1,0:T(8,128)S(1)}, f32[2,8,128,128]{3,2,1,0:T(8,128)}, u32[]{:S(2)}, u32[]{:S(2)}) collective-permute-start(f32[2,8,128,128]{3,2,1,0:T(8,128)S(1)} %get-tuple-element.158), channel_id=1, source_target_pairs={{2,0},{3,1},{0,2},{1,3},{6,4},{7,5},{4,6},{5,7},{10,8},{11,9},{8,1... | collective-permute-start | bytes 3145736 | tf_op jit(solution)/shard_map/ppermute | solution.py:405
  243.1 35.3 %collective-permute-start.29 = (f32[8,128,128]{2,1,0:T(8,128)}, f32[8,128,128]{2,1,0:T(8,128)}, u32[]{:S(2)}, u32[]{:S(2)}) collective-permute-start(f32[8,128,128]{2,1,0:T(8,128)} %get-tuple-element.128), channel_id=1, source_target_pairs={{8,0},{9,1},{10,2},{11,3},{12,4},{13,5},{14,6},{15,7},{0,8},{1,9},... | collective-permute-start | bytes 1572872 | tf_op jit(solution)/shard_map/ppermute | solution.py:405
  246.5 42.8 %collective-permute-start.30 = (f32[8,128,128]{2,1,0:T(8,128)}, f32[8,128,128]{2,1,0:T(8,128)}, u32[]{:S(2)}, u32[]{:S(2)}) collective-permute-start(f32[8,128,128]{2,1,0:T(8,128)} %get-tuple-element.129), channel_id=1, source_target_pairs={{12,0},{13,1},{14,2},{15,3},{8,4},{9,5},{10,6},{11,7},{4,8},{5,9},... | collective-permute-start | bytes 1572872 | tf_op jit(solution)/shard_map/ppermute | solution.py:405
  248.4 41.0 %collective-permute-start.31 = (f32[8,128,128]{2,1,0:T(8,128)S(1)}, f32[8,128,128]{2,1,0:T(8,128)}, u32[]{:S(2)}, u32[]{:S(2)}) collective-permute-start(f32[8,128,128]{2,1,0:T(8,128)S(1)} %get-tuple-element.130), channel_id=1, source_target_pairs={{4,0},{5,1},{6,2},{7,3},{0,4},{1,5},{2,6},{3,7},{12,8},{13,9},{14,... | collective-permute-start | bytes 1572872 | tf_op jit(solution)/shard_map/ppermute | solution.py:405
